TPU v7x, 256 devices: a whole 4x4x8 slice. The times are simulated.
256 devices in a mesh: leaf: 256 (over x, y, z, core).
Axes of the slice: x: 4, y: 4, z: 8, core: 2. Of those that a mesh axis runs over, the one named last changes fastest.
Arguments:
- right_side: bfloat16 [262144, 256], P('leaf'), may hold values from -6 to 6
- leaf_inv: bfloat16 [262144, 1024], P('leaf'), may hold values from -0.1875 to 0.1875
- right_basis: bfloat16 [4, 262144, 256], P(None, 'leaf'), may hold values from -0.0234375 to 0.0234375
- left_basis: bfloat16 [4, 262144, 256], P(None, 'leaf'), may hold values from -0.375 to 0.375
- reduced_first: float32 [512, 512], P('leaf'), may hold values from -0.25 to 0.25
- reduced_second: float32 [1024, 512], P('leaf'), may hold values from -0.25 to 0.25
- reduced_third: float32 [2048, 512], P('leaf'), may hold values from -0.25 to 0.25
- reduced_fourth: float32 [4096, 512], P('leaf'), may hold values from -0.25 to 0.25
Outputs:
- solution: float32 [262144, 256], P('leaf')
All inputs are finite; a program needn't handle non-finite values.
Results may differ from a plain program's by a relative error of at most 0.0003.
Values sent between devices are 32-bit elements; how exact they have to be, the bound alone decides.
No kernel may reach another device: no remote copies, remote signals or barrier semaphores. Data moves between devices by JAX's collectives and lax.ppermute only.
A program may use at most 64 MiB of HBM per device.

v0:
```python
import jax
import jax.numpy as jnp
from jax import lax
from jax.experimental import pallas as pl
from jax.experimental.pallas import tpu as pltpu
from jax.sharding import Mesh, PartitionSpec as P

AXES = ("xh", "xl", "yh", "yl", "z", "c")
SIZES = (2, 2, 2, 2, 8, 2)
Z = 8
STEPS = 4
F32 = jnp.float32
BF16 = jnp.bfloat16
PAIRS = ((3, 4), (2, 4), (1, 4), (2, 3), (1, 3), (1, 2))


def dot(a, b, dims):
    return lax.dot_general(a, b, ((dims[0], dims[1]), ((), ())), preferred_element_type=F32)


def fdot(a, b, dims):
    return lax.dot_general(
        a, b, ((dims[0], dims[1]), ((), ())), precision=lax.Precision.HIGH, preferred_element_type=F32
    )


def pack_kernel(a_ref, b_ref, c_ref, d_ref, out_ref):
    for z in range(Z):
        out_ref[z, 0:16, :] = a_ref[...]
        out_ref[z, 16:24, :] = b_ref[...]
        out_ref[z, 24:28, :] = c_ref[...]
        out_ref[z, 28:30, :] = d_ref[...]
        out_ref[z, 30:32, :] = jnp.zeros((2, 512), F32)


def pack(k4, k3, k2, k1):
    return pl.pallas_call(pack_kernel, out_shape=jax.ShapeDtypeStruct((Z, 32, 512), F32), name="pack")(k4, k3, k2, k1)


def leaf_kernel(core_ref, inv_hbm, rhs_hbm, v_hbm, w_hbm, x_ref, keep_ref, give_ref, inv_ref, rhs_ref, v_ref, w_ref, high_ref, low_ref, sems):
    rows = 1024 // STEPS
    count = [0]

    def load(src, dst):
        copy = pltpu.make_async_copy(src, dst, sems.at[count[0]])
        count[0] += 1
        copy.start()
        return copy

    wait_w, wait_v = {}, {}
    wait_w[4] = load(w_hbm.at[3], w_ref.at[2])
    wait_v[3] = load(v_hbm.at[2], v_ref.at[2])
    wait_v[2] = load(v_hbm.at[1], v_ref.at[1])
    wait_v[1] = load(v_hbm.at[0], v_ref.at[0])
    wait_w[3] = load(w_hbm.at[2], w_ref.at[1])
    wait_w[2] = load(w_hbm.at[1], w_ref.at[0])
    wait_rhs = load(rhs_hbm, rhs_ref)
    parts = [pl.ds(step * rows, rows) for step in range(STEPS)]
    wait_inv = [load(inv_hbm.at[part], inv_ref.at[part]) for part in parts]
    wait_v[4] = load(v_hbm.at[3], v_ref.at[3])
    first = core_ref[0] == 0

    def store(n, value):
        low, high = value[:128], value[128:]
        keep_ref[:, n] = jnp.where(first, low, high).reshape(Z, 16, 256)
        give_ref[:, n] = jnp.where(first, high, low).reshape(Z, 16, 256)

    done = set()

    def ready(waits, level):
        if (id(waits), level) not in done:
            done.add((id(waits), level))
            waits[level].wait()

    turned = {}
    for n, (j, k) in enumerate(PAIRS):
        ready(wait_w, k)
        if k not in turned:
            turned[k] = w_ref[k - 2].T
        ready(wait_v, j)
        store(4 + n, dot(turned[k], v_ref[j - 1], ((1,), (0,))))
    wait_rhs.wait()
    rhs = rhs_ref[...]
    rhs_turned = rhs.T
    for step, part in enumerate(parts):
        wait_inv[step].wait()
        inv = inv_ref[part, :]
        x_ref[part, :] = jnp.dot(inv, rhs, preferred_element_type=F32)
        xt = dot(rhs_turned, inv, ((1,), (1,)))
        high = xt.astype(BF16)
        high_ref[:, part] = high
        low_ref[:, part] = (xt - high.astype(F32)).astype(BF16)
    for n, j in enumerate((4, 3, 2, 1)):
        ready(wait_v, j)
        v = v_ref[j - 1]
        store(n, dot(high_ref[...], v, ((1,), (0,))) + dot(low_ref[...], v, ((1,), (0,))))


def leaf(core, leaf_inv, right_side, right_basis, left_basis):
    any_space = pl.BlockSpec(memory_space=pl.ANY)
    return pl.pallas_call(
        leaf_kernel,
        in_specs=[pl.BlockSpec(memory_space=pltpu.SMEM)] + [any_space] * 4,
        out_shape=[
            jax.ShapeDtypeStruct((1024, 256), F32),
            jax.ShapeDtypeStruct((Z, 10, 16, 256), F32),
            jax.ShapeDtypeStruct((Z, 10, 16, 256), F32),
        ],
        scratch_shapes=[
            pltpu.VMEM((1024, 1024), BF16),
            pltpu.VMEM((1024, 256), BF16),
            pltpu.VMEM((4, 1024, 256), BF16),
            pltpu.VMEM((3, 1024, 256), BF16),
            pltpu.VMEM((256, 1024), BF16),
            pltpu.VMEM((256, 1024), BF16),
            pltpu.SemaphoreType.DMA((8 + STEPS,)),
        ],
        name="leaf",
    )(core.reshape(1), leaf_inv, right_side, right_basis, left_basis)


def finish_kernel(core_ref, w_ref, x_ref, own_ref, other_ref, out_ref, high_ref, low_ref):
    first = core_ref[0] == 0

    @pl.when(pl.program_id(0) == 0)
    def _():
        for n in range(4):
            own = own_ref[:, n].reshape(128, 256)
            other = other_ref[:, n].reshape(128, 256)
            m = jnp.concatenate([jnp.where(first, own, other), jnp.where(first, other, own)], axis=0)
            high = m.astype(BF16)
            high_ref[n] = high
            low_ref[n] = (m - high.astype(F32)).astype(BF16)

    total = x_ref[...]
    for n, level in enumerate((4, 3, 2, 1)):
        w = w_ref[level - 1]
        total = total - (dot(w, high_ref[n], ((1,), (1,))) + dot(w, low_ref[n], ((1,), (1,))))
    out_ref[...] = total


def finish(core, left_basis, x, own, other):
    rows = 1024 // STEPS
    whole = pl.BlockSpec((Z, 4, 16, 256), lambda s: (0, 0, 0, 0))
    return pl.pallas_call(
        finish_kernel,
        grid=(STEPS,),
        in_specs=[
            pl.BlockSpec(memory_space=pltpu.SMEM),
            pl.BlockSpec((4, rows, 256), lambda s: (0, s, 0)),
            pl.BlockSpec((rows, 256), lambda s: (s, 0)),
            whole,
            whole,
        ],
        out_specs=pl.BlockSpec((rows, 256), lambda s: (s, 0)),
        out_shape=jax.ShapeDtypeStruct((1024, 256), F32),
        scratch_shapes=[pltpu.VMEM((4, 256, 256), BF16), pltpu.VMEM((4, 256, 256), BF16)],
        name="finish",
    )(core.reshape(1), left_basis, x, own, other)


def partner(block, axis):
    return lax.ppermute(block, axis, [(0, 1), (1, 0)])


def ordered(bit, own, other, axis):
    low = jnp.where(bit == 0, own, other)
    high = jnp.where(bit == 0, other, own)
    return jnp.concatenate([low, high], axis=axis)


def exchange(block, axes):
    return lax.all_to_all(block, axes, 0, 0, tiled=True)


def spread(block, axes, count):
    return exchange(jnp.broadcast_to(block[None], (count,) + block.shape), axes)


def local(right_side, leaf_inv, right_basis, left_basis, k1, k2, k3, k4):
    at = {axis: lax.axis_index(axis) for axis in AXES}
    core = at["c"]
    rows = exchange(pack(k4, k3, k2, k1), "z")
    x0, keep, give = leaf(core, leaf_inv, right_side, right_basis, left_basis)
    mine, rows = lax.optimization_barrier((keep + partner(give, "c"), rows))
    sums = exchange(mine, "z").sum(axis=0)

    part4, part3, part2, part1 = rows[:, 0:16], rows[None, :, 16:24], rows[None, :, 24:28], rows[None, :, 28:30]

    def widen(part, axis):
        return ordered(at[axis], part, partner(part, axis), 0)

    part3 = widen(part3, "yl")
    part2 = widen(widen(part2, "yl"), "yh")
    part1 = widen(widen(widen(part1, "yl"), "yh"), "xl")
    other4 = partner(part4, "c")

    def whole(part, other=None):
        if other is None:
            other = partner(part, "c")
        low = jnp.where(core == 0, part, other)
        high = jnp.where(core == 0, other, part)
        return jnp.stack([low, high], axis=-3).reshape(256, 512)

    def both_cores(by_z):
        n = by_z.shape[1]
        half = by_z.transpose(1, 0, 2, 3).reshape(n, 128, 256)
        return ordered(core, half, partner(half, "c"), 1)

    def mix(part, own, axis, other=None):
        stack = ordered(at[axis], own, partner(own, axis), 1)
        return fdot(stack, whole(part, other), ((1,), (1,)))

    def times(m, g):
        return fdot(m, g, ((1,), (0,)))

    g34, g24, g14 = both_cores(spread(sums[4:7], "z", Z))
    shared = sums[7:10]
    shared = shared + partner(shared, "yl")
    shared = jnp.concatenate([shared[:2], shared[2:] + partner(shared[2:], "yh")], axis=0)
    m4 = mix(part4, sums[0], "yl", other4)
    t = sums[1:4] - jnp.stack([times(m4, g34), times(m4, g24), times(m4, g14)])
    g23, g13, g12 = both_cores(spread(shared, "z", Z))
    t = t + partner(t, "yl")
    m3 = mix(part3, t[0], "yh")
    t = t[1:] - jnp.stack([times(m3, g23), times(m3, g13)])
    t = t + partner(t, "yh")
    m2 = mix(part2, t[0], "xl")
    t = t[1] - times(m2, g12)
    t = t + partner(t, "xl")
    m1 = mix(part1, t, "xh")

    last = spread(jnp.stack([m4, m3, m2, m1]), "z", Z)
    return finish(core, left_basis, x0, last, partner(last, "c"))


def solution(mesh):
    fine = Mesh(mesh.devices.reshape(SIZES), AXES)
    row = P(AXES, None)
    level = P(None, AXES, None)
    return jax.shard_map(
        local,
        mesh=fine,
        in_specs=(row, row, level, level, row, row, row, row),
        out_specs=row,
        check_vma=False,
    )
```

profile of v0, /device:TPU:1, one launch (start us, length us, event | category | flops | bytes accessed | tf_op | source)
XLA Modules:
  0.0 169.5 jit_solution(14941158717856294091)
XLA Ops:
  0.0 8.3 %leaf.1 = (f32[1024,256]{1,0:T(8,128)}, f32[8,10,16,256]{3,2,1,0:T(8,128)}, f32[8,10,16,256]{3,2,1,0:T(8,128)}) custom-call(s32[1]{0:T(128)} %bitcast.core_ref, bf16[1024,1024]{1,0:T(8,128)(2,1)} %inv_hbm.1, bf16[1024,256]{1,0:T(8,128)(2,1)} %rhs_hbm.1, bf16[4,1024,256]{2,1,0:T(8,128)(2,1)} %v_hbm.1, bf16[4,1024,256]{2,1,0:T(8,128)(2,1)} %w_ref.1), custom_call_target="tpu_custom_call" | custom-call | tf_op jit(solution)/shard_map/leaf/pallas_call | solution.py:101
  8.3 3.3 %collective-permute-start = (f32[8,10,16,256]{3,2,1,0:T(8,128)}, f32[8,10,16,256]{3,2,1,0:T(8,128)S(1)}, u32[]{:S(2)}, u32[]{:S(2)}) collective-permute-start(f32[8,10,16,256]{3,2,1,0:T(8,128)} %get-tuple-element.12), channel_id=1, source_target_pairs={{0,1},{1,0},{2,3},{3,2},{4,5},{5,4},{6,7},{7,6},{8,9},{9,8},{10,11... | collective-permute-start | bytes 3932168 | tf_op jit(solution)/shard_map/ppermute | solution.py:163
  11.6 1.6 pack.1
  13.2 6.5 %all-to-all-start = ((f32[8,32,512]{2,1,0:T(8,128)}), f32[8,32,512]{2,1,0:T(8,128)S(1)}, u32[]{:S(2)}, u32[]{:S(2)}) async-start(f32[8,32,512]{2,1,0:T(8,128)} %pack.1), calls=%async_computation | async-start | bytes 1048576 | tf_op jit(solution)/shard_map/all_to_all | solution.py:173
  19.7 1.5 add.18
  21.2 16.5 %all-to-all-done = f32[8,32,512]{2,1,0:T(8,128)S(1)} async-done(((f32[8,32,512]{2,1,0:T(8,128)}), f32[8,32,512]{2,1,0:T(8,128)S(1)}, u32[]{:S(2)}, u32[]{:S(2)}) %all-to-all-start) | async-done | bytes 524320 | tf_op jit(solution)/shard_map/all_to_all | solution.py:173
  37.7 1.4 collective-permute-start.18
  39.1 3.6 %all-to-all-start.1 = ((f32[8,10,16,256]{3,2,1,0:T(8,128)}), f32[8,10,16,256]{3,2,1,0:T(8,128)S(1)}, u32[]{:S(2)}, u32[]{:S(2)}) async-start(f32[8,10,16,256]{3,2,1,0:T(8,128)} %add.18), calls=%async_computation.1 | async-start | bytes 2621440 | tf_op jit(solution)/shard_map/all_to_all | solution.py:173
  42.7 0.8 collective-permute-start.2
  43.6 0.2 collective-permute-start.6
  43.7 1.3 collective-permute-start.13
  45.1 2.7 %collective-permute-start.19 = (f32[2,8,2,512]{3,2,1,0:T(2,128)S(1)}, f32[2,8,2,512]{3,2,1,0:T(2,128)S(1)}, u32[]{:S(2)}, u32[]{:S(2)}) collective-permute-start(f32[2,8,2,512]{3,2,1,0:T(2,128)S(1)} %pad_maximum_fusion.11), channel_id=1, source_target_pairs={{0,32},{32,0},{1,33},{33,1},{2,34},{34,2},{3,35},{35,3},{4,36},{36... | collective-permute-start | bytes 196616 | tf_op jit(solution)/shard_map/ppermute | solution.py:163
  47.8 2.1 %collective-permute-done.13 = f32[1,8,4,512]{3,2,1,0:T(4,128)S(1)} collective-permute-done((f32[1,8,4,512]{3,2,1,0:T(4,128)S(1)}, f32[1,8,4,512]{3,2,1,0:T(4,128)S(1)}, u32[]{:S(2)}, u32[]{:S(2)}) %collective-permute-start.13) | collective-permute-done | bytes 65568 | tf_op jit(solution)/shard_map/ppermute | solution.py:163
  50.0 2.7 %collective-permute-start.14 = (f32[2,8,4,512]{3,2,1,0:T(4,128)S(1)}, f32[2,8,4,512]{3,2,1,0:T(4,128)S(1)}, u32[]{:S(2)}, u32[]{:S(2)}) collective-permute-start(f32[2,8,4,512]{3,2,1,0:T(4,128)S(1)} %pad_maximum_fusion.9), channel_id=1, source_target_pairs={{0,32},{32,0},{1,33},{33,1},{2,34},{34,2},{3,35},{35,3},{4,36},{36... | collective-permute-start | bytes 393224 | tf_op jit(solution)/shard_map/ppermute | solution.py:163
  52.7 0.2 collective-permute-done.19
  53.1 1.3 collective-permute-start.20
  54.4 0.7 pad_maximum_fusion.6
  55.1 1.8 %collective-permute-start.7 = (f32[2,8,8,512]{3,2,1,0:T(8,128)}, f32[2,8,8,512]{3,2,1,0:T(8,128)}, u32[]{:S(2)}, u32[]{:S(2)}) collective-permute-start(f32[2,8,8,512]{3,2,1,0:T(8,128)} %pad_maximum_fusion.6), channel_id=1, source_target_pairs={{0,1},{1,0},{2,3},{3,2},{4,5},{5,4},{6,7},{7,6},{8,9},{9,8},{10,11... | collective-permute-start | bytes 786440 | tf_op jit(solution)/shard_map/ppermute | solution.py:163
  57.0 0.8 pad_maximum_fusion.7
  57.8 1.1 collective-permute-start.15
  59.0 0.9 pad_maximum_fusion.8
  59.9 0.8 collective-permute-start.21
  60.7 16.7 %all-to-all-done.1 = f32[8,10,16,256]{3,2,1,0:T(8,128)S(1)} async-done(((f32[8,10,16,256]{3,2,1,0:T(8,128)}), f32[8,10,16,256]{3,2,1,0:T(8,128)S(1)}, u32[]{:S(2)}, u32[]{:S(2)}) %all-to-all-start.1) | async-done | bytes 1310752 | tf_op jit(solution)/shard_map/all_to_all | solution.py:173
  77.6 0.3 collective-permute-start.8
  77.9 2.7 %collective-permute-done.8 = f32[3,16,256]{2,1,0:T(8,128)S(1)} collective-permute-done((f32[3,16,256]{2,1,0:T(8,128)S(1)}, f32[3,16,256]{2,1,0:T(8,128)S(1)}, u32[]{:S(2)}, u32[]{:S(2)}) %collective-permute-start.8) | collective-permute-done | bytes 49184 | tf_op jit(solution)/shard_map/ppermute | solution.py:163
  80.6 0.8 broadcast_in_dim.12
  81.4 3.6 %all-to-all-start.2 = ((f32[8,3,16,256]{3,2,1,0:T(8,128)}), f32[8,3,16,256]{3,2,1,0:T(8,128)S(1)}, u32[]{:S(2)}, u32[]{:S(2)}) async-start(f32[8,3,16,256]{3,2,1,0:T(8,128)} %broadcast_in_dim.12), calls=%async_computation.2 | async-start | bytes 786432 | tf_op jit(solution)/shard_map/all_to_all | solution.py:173
  85.1 0.3 collective-permute-start.1
  85.3 1.0 select_bitcast_fusion.5
  86.3 1.4 collective-permute-done.1
  87.7 2.7 %collective-permute-start.9 = (f32[1,16,256]{2,1,0:T(8,128)S(1)}, f32[1,16,256]{2,1,0:T(8,128)S(1)}, u32[]{:S(2)}, u32[]{:S(2)}) collective-permute-start(f32[1,16,256]{2,1,0:T(8,128)S(1)} %slice.64), channel_id=1, source_target_pairs={{0,32},{32,0},{1,33},{33,1},{2,34},{34,2},{3,35},{35,3},{4,36},{36... | collective-permute-start | bytes 49160 | tf_op jit(solution)/shard_map/ppermute | solution.py:163
  90.5 7.3 %all-to-all-done.2 = f32[8,3,16,256]{3,2,1,0:T(8,128)S(1)} async-done(((f32[8,3,16,256]{3,2,1,0:T(8,128)}), f32[8,3,16,256]{3,2,1,0:T(8,128)S(1)}, u32[]{:S(2)}, u32[]{:S(2)}) %all-to-all-start.2) | async-done | bytes 393248 | tf_op jit(solution)/shard_map/all_to_all | solution.py:173
  97.8 2.7 %collective-permute-start.3 = (f32[3,128,256]{2,1,0:T(8,128)S(1)}, f32[3,128,256]{2,1,0:T(8,128)S(1)}, u32[]{:S(2)}, u32[]{:S(2)}) collective-permute-start(f32[3,128,256]{2,1,0:T(8,128)S(1)} %bitcast.116), channel_id=1, source_target_pairs={{0,1},{1,0},{2,3},{3,2},{4,5},{5,4},{6,7},{7,6},{8,9},{9,8},{10,11... | collective-permute-start | bytes 1179656 | tf_op jit(solution)/shard_map/ppermute | solution.py:163
  100.5 0.3 fusion.19
  100.9 0.8 broadcast_in_dim.14
  101.7 3.5 %all-to-all-start.3 = ((f32[8,3,16,256]{3,2,1,0:T(8,128)}), f32[8,3,16,256]{3,2,1,0:T(8,128)S(1)}, u32[]{:S(2)}, u32[]{:S(2)}) async-start(f32[8,3,16,256]{3,2,1,0:T(8,128)} %broadcast_in_dim.14), calls=%async_computation.3 | async-start | bytes 786432 | tf_op jit(solution)/shard_map/all_to_all | solution.py:173
  105.4 0.2 convolution_bitcast_fusion.3
  105.6 0.2 convolution_bitcast_fusion.4
  105.8 0.3 collective-permute-start.4
  106.2 14.1 %all-to-all-done.3 = f32[8,3,16,256]{3,2,1,0:T(8,128)S(1)} async-done(((f32[8,3,16,256]{3,2,1,0:T(8,128)}), f32[8,3,16,256]{3,2,1,0:T(8,128)S(1)}, u32[]{:S(2)}, u32[]{:S(2)}) %all-to-all-start.3) | async-done | bytes 393248 | tf_op jit(solution)/shard_map/all_to_all | solution.py:173
  120.3 0.5 collective-permute-start.10
  120.9 2.7 %collective-permute-start.5 = (f32[16,256]{1,0:T(8,128)S(1)}, f32[16,256]{1,0:T(8,128)S(1)}, u32[]{:S(2)}, u32[]{:S(2)}) collective-permute-start(f32[16,256]{1,0:T(8,128)S(1)} %slice_bitcast_fusion.5), channel_id=1, source_target_pairs={{0,32},{32,0},{1,33},{33,1},{2,34},{34,2},{3,35},{35,3},{4,36},{36... | collective-permute-start | bytes 49160 | tf_op jit(solution)/shard_map/ppermute | solution.py:163
  123.7 1.4 collective-permute-done.5
  125.1 0.3 fusion.23
  125.5 0.2 convolution_bitcast_fusion.1
  125.8 2.7 %collective-permute-start.11 = (f32[2,16,256]{2,1,0:T(8,128)S(1)}, f32[2,16,256]{2,1,0:T(8,128)S(1)}, u32[]{:S(2)}, u32[]{:S(2)}) collective-permute-start(f32[2,16,256]{2,1,0:T(8,128)S(1)} %slice_subtract_fusion.1), channel_id=1, source_target_pairs={{0,32},{32,0},{1,33},{33,1},{2,34},{34,2},{3,35},{35,3},{4,36},{36... | collective-permute-start | bytes 98312 | tf_op jit(solution)/shard_map/ppermute | solution.py:163
  128.5 1.1 select_bitcast_fusion.3
  129.6 0.6 collective-permute-done.11
  130.2 1.3 collective-permute-start.12
  131.7 0.2 reshape.30
  131.9 1.0 collective-permute-done.12
  132.8 0.3 fusion.27
  133.3 1.3 collective-permute-start.16
  134.6 1.2 select_bitcast_fusion.1
  136.0 2.7 %collective-permute-start.17 = (f32[16,256]{1,0:T(8,128)S(1)}, f32[16,256]{1,0:T(8,128)S(1)}, u32[]{:S(2)}, u32[]{:S(2)}) collective-permute-start(f32[16,256]{1,0:T(8,128)S(1)} %add.23), channel_id=1, source_target_pairs={{0,128},{128,0},{1,129},{129,1},{2,130},{130,2},{3,131},{131,3},{4... | collective-permute-start | bytes 49160 | tf_op jit(solution)/shard_map/ppermute | solution.py:163
  138.7 0.3 pad_maximum_fusion.3
  139.1 0.4 reshape.31
  139.5 0.6 collective-permute-done.17
  140.1 0.3 convolution_bitcast_fusion.5
  140.5 14.6 %all_to_all.25.own_ref = f32[8,4,16,256]{3,2,1,0:T(8,128)S(1)} all-to-all(f32[8,4,16,256]{3,2,1,0:T(8,128)S(1)} %broadcast_in_dim.32), channel_id=1, replica_groups=mesh['xh'=2,'xl'=2,'yh'=2,'yl'=2,'z'=8,'c'=2] {'z'}, dimensions={0} | all-to-all | bytes 1048576 | tf_op jit(solution)/shard_map/all_to_all | solution.py:173
  155.1 6.9 %collective-permute-start.22 = (f32[8,4,16,256]{3,2,1,0:T(8,128)S(1)}, f32[8,4,16,256]{3,2,1,0:T(8,128)S(1)}, u32[]{:S(2)}, u32[]{:S(2)}) collective-permute-start(f32[8,4,16,256]{3,2,1,0:T(8,128)S(1)} %all_to_all.25.own_ref), channel_id=1, source_target_pairs={{0,1},{1,0},{2,3},{3,2},{4,5},{5,4},{6,7},{7,6},{8,9},{9,8},{10,11... | collective-permute-start | bytes 1572872 | tf_op jit(solution)/shard_map/ppermute | solution.py:163
  162.0 1.5 collective-permute-done.22.other_ref
  163.6 0.8 copy-done.2
  164.4 5.1 %finish.1 = f32[1024,256]{1,0:T(8,128)} custom-call(s32[1]{0:T(128)} %bitcast.core_ref, bf16[4,1024,256]{2,1,0:T(8,128)(2,1)} %w_ref.1, f32[1024,256]{1,0:T(8,128)} %get-tuple-element.10.x_ref, f32[8,4,16,256]{3,2,1,0:T(8,128)} %copy-done, f32[8,4,16,256]{3,2,1,0:T(8,128)} %copy-done.2), custom_call_target="tpu_custom_call" | custom-call | tf_op jit(solution)/shard_map/finish/pallas_call | solution.py:145
  (68 shorter events, 2.1 us)
Async XLA Ops:
  8.3 11.4 %copy-start.1 = (f32[8,10,16,256]{3,2,1,0:T(8,128)S(1)}, f32[8,10,16,256]{3,2,1,0:T(8,128)}, u32[]{:S(2)}) copy-start(f32[8,10,16,256]{3,2,1,0:T(8,128)} %get-tuple-element.11) | copy-start | bytes 3932164
  8.3 11.4 %collective-permute-start = (f32[8,10,16,256]{3,2,1,0:T(8,128)}, f32[8,10,16,256]{3,2,1,0:T(8,128)S(1)}, u32[]{:S(2)}, u32[]{:S(2)}) collective-permute-start(f32[8,10,16,256]{3,2,1,0:T(8,128)} %get-tuple-element.12), channel_id=1, source_target_pairs={{0,1},{1,0},{2,3},{3,2},{4,5},{5,4},{6,7},{7,6},{8,9},{9,8},{10,11... | collective-permute-start | bytes 3932168 | tf_op jit(solution)/shard_map/ppermute | solution.py:163
  13.2 24.5 %all-to-all-start = ((f32[8,32,512]{2,1,0:T(8,128)}), f32[8,32,512]{2,1,0:T(8,128)S(1)}, u32[]{:S(2)}, u32[]{:S(2)}) async-start(f32[8,32,512]{2,1,0:T(8,128)} %pack.1), calls=%async_computation | async-start | bytes 1048576 | tf_op jit(solution)/shard_map/all_to_all | solution.py:173
  37.7 7.3 %collective-permute-start.18 = (f32[1,8,2,512]{3,2,1,0:T(2,128)S(1)}, f32[1,8,2,512]{3,2,1,0:T(2,128)S(1)}, u32[]{:S(2)}, u32[]{:S(2)}) collective-permute-start(f32[1,8,2,512]{3,2,1,0:T(2,128)S(1)} %slice_bitcast_fusion.2), channel_id=1, source_target_pairs={{0,16},{16,0},{1,17},{17,1},{2,18},{18,2},{3,19},{19,3},{4,20},{20... | collective-permute-start | bytes 98312 | tf_op jit(solution)/shard_map/ppermute | solution.py:163
  39.1 38.3 %all-to-all-start.1 = ((f32[8,10,16,256]{3,2,1,0:T(8,128)}), f32[8,10,16,256]{3,2,1,0:T(8,128)S(1)}, u32[]{:S(2)}, u32[]{:S(2)}) async-start(f32[8,10,16,256]{3,2,1,0:T(8,128)} %add.18), calls=%async_computation.1 | async-start | bytes 2621440 | tf_op jit(solution)/shard_map/all_to_all | solution.py:173
  42.7 17.9 %collective-permute-start.2 = (f32[8,16,512]{2,1,0:T(8,128)S(1)}, f32[8,16,512]{2,1,0:T(8,128)S(1)}, u32[]{:S(2)}, u32[]{:S(2)}) collective-permute-start(f32[8,16,512]{2,1,0:T(8,128)S(1)} %slice.44), channel_id=1, source_target_pairs={{0,1},{1,0},{2,3},{3,2},{4,5},{5,4},{6,7},{7,6},{8,9},{9,8},{10,11... | collective-permute-start | bytes 786440 | tf_op jit(solution)/shard_map/ppermute | solution.py:163
  43.6 10.8 %collective-permute-start.6 = (f32[1,8,8,512]{3,2,1,0:T(8,128)S(1)}, f32[1,8,8,512]{3,2,1,0:T(8,128)S(1)}, u32[]{:S(2)}, u32[]{:S(2)}) collective-permute-start(f32[1,8,8,512]{3,2,1,0:T(8,128)S(1)} %slice_bitcast_fusion), channel_id=1, source_target_pairs={{0,16},{16,0},{1,17},{17,1},{2,18},{18,2},{3,19},{19,3},{4,20},{20... | collective-permute-start | bytes 393224 | tf_op jit(solution)/shard_map/ppermute | solution.py:163
  43.7 6.2 %collective-permute-start.13 = (f32[1,8,4,512]{3,2,1,0:T(4,128)S(1)}, f32[1,8,4,512]{3,2,1,0:T(4,128)S(1)}, u32[]{:S(2)}, u32[]{:S(2)}) collective-permute-start(f32[1,8,4,512]{3,2,1,0:T(4,128)S(1)} %slice_bitcast_fusion.1), channel_id=1, source_target_pairs={{0,16},{16,0},{1,17},{17,1},{2,18},{18,2},{3,19},{19,3},{4,20},{20... | collective-permute-start | bytes 196616 | tf_op jit(solution)/shard_map/ppermute | solution.py:163
  45.1 7.8 %collective-permute-start.19 = (f32[2,8,2,512]{3,2,1,0:T(2,128)S(1)}, f32[2,8,2,512]{3,2,1,0:T(2,128)S(1)}, u32[]{:S(2)}, u32[]{:S(2)}) collective-permute-start(f32[2,8,2,512]{3,2,1,0:T(2,128)S(1)} %pad_maximum_fusion.11), channel_id=1, source_target_pairs={{0,32},{32,0},{1,33},{33,1},{2,34},{34,2},{3,35},{35,3},{4,36},{36... | collective-permute-start | bytes 196616 | tf_op jit(solution)/shard_map/ppermute | solution.py:163
  50.0 7.0 %collective-permute-start.14 = (f32[2,8,4,512]{3,2,1,0:T(4,128)S(1)}, f32[2,8,4,512]{3,2,1,0:T(4,128)S(1)}, u32[]{:S(2)}, u32[]{:S(2)}) collective-permute-start(f32[2,8,4,512]{3,2,1,0:T(4,128)S(1)} %pad_maximum_fusion.9), channel_id=1, source_target_pairs={{0,32},{32,0},{1,33},{33,1},{2,34},{34,2},{3,35},{35,3},{4,36},{36... | collective-permute-start | bytes 393224 | tf_op jit(solution)/shard_map/ppermute | solution.py:163
  53.1 5.8 %collective-permute-start.20 = (f32[4,8,2,512]{3,2,1,0:T(2,128)S(1)}, f32[4,8,2,512]{3,2,1,0:T(2,128)S(1)}, u32[]{:S(2)}, u32[]{:S(2)}) collective-permute-start(f32[4,8,2,512]{3,2,1,0:T(2,128)S(1)} %pad_maximum_fusion.10), channel_id=1, source_target_pairs={{0,64},{64,0},{1,65},{65,1},{2,66},{66,2},{3,67},{67,3},{4,68},{68... | collective-permute-start | bytes 393224 | tf_op jit(solution)/shard_map/ppermute | solution.py:163
  55.1 30.2 %collective-permute-start.7 = (f32[2,8,8,512]{3,2,1,0:T(8,128)}, f32[2,8,8,512]{3,2,1,0:T(8,128)}, u32[]{:S(2)}, u32[]{:S(2)}) collective-permute-start(f32[2,8,8,512]{3,2,1,0:T(8,128)} %pad_maximum_fusion.6), channel_id=1, source_target_pairs={{0,1},{1,0},{2,3},{3,2},{4,5},{5,4},{6,7},{7,6},{8,9},{9,8},{10,11... | collective-permute-start | bytes 786440 | tf_op jit(solution)/shard_map/ppermute | solution.py:163
  57.8 70.7 %collective-permute-start.15 = (f32[4,8,4,512]{3,2,1,0:T(4,128)}, f32[4,8,4,512]{3,2,1,0:T(4,128)}, u32[]{:S(2)}, u32[]{:S(2)}) collective-permute-start(f32[4,8,4,512]{3,2,1,0:T(4,128)} %pad_maximum_fusion.7), channel_id=1, source_target_pairs={{0,1},{1,0},{2,3},{3,2},{4,5},{5,4},{6,7},{7,6},{8,9},{9,8},{10,11... | collective-permute-start | bytes 786440 | tf_op jit(solution)/shard_map/ppermute | solution.py:163
  59.9 74.7 %collective-permute-start.21 = (f32[8,8,2,512]{3,2,1,0:T(2,128)}, f32[8,8,2,512]{3,2,1,0:T(2,128)}, u32[]{:S(2)}, u32[]{:S(2)}) collective-permute-start(f32[8,8,2,512]{3,2,1,0:T(2,128)} %pad_maximum_fusion.8), channel_id=1, source_target_pairs={{0,1},{1,0},{2,3},{3,2},{4,5},{5,4},{6,7},{7,6},{8,9},{9,8},{10,11... | collective-permute-start | bytes 786440 | tf_op jit(solution)/shard_map/ppermute | solution.py:163
  77.6 3.0 %collective-permute-start.8 = (f32[3,16,256]{2,1,0:T(8,128)S(1)}, f32[3,16,256]{2,1,0:T(8,128)S(1)}, u32[]{:S(2)}, u32[]{:S(2)}) collective-permute-start(f32[3,16,256]{2,1,0:T(8,128)S(1)} %slice.62), channel_id=1, source_target_pairs={{0,16},{16,0},{1,17},{17,1},{2,18},{18,2},{3,19},{19,3},{4,20},{20... | collective-permute-start | bytes 147464 | tf_op jit(solution)/shard_map/ppermute | solution.py:163
  81.4 16.4 %all-to-all-start.2 = ((f32[8,3,16,256]{3,2,1,0:T(8,128)}), f32[8,3,16,256]{3,2,1,0:T(8,128)S(1)}, u32[]{:S(2)}, u32[]{:S(2)}) async-start(f32[8,3,16,256]{3,2,1,0:T(8,128)} %broadcast_in_dim.12), calls=%async_computation.2 | async-start | bytes 786432 | tf_op jit(solution)/shard_map/all_to_all | solution.py:173
  85.1 2.7 %collective-permute-start.1 = (f32[16,256]{1,0:T(8,128)S(1)}, f32[16,256]{1,0:T(8,128)S(1)}, u32[]{:S(2)}, u32[]{:S(2)}) collective-permute-start(f32[16,256]{1,0:T(8,128)S(1)} %slice_bitcast_fusion.6), channel_id=1, source_target_pairs={{0,16},{16,0},{1,17},{17,1},{2,18},{18,2},{3,19},{19,3},{4,20},{20... | collective-permute-start | bytes 49160 | tf_op jit(solution)/shard_map/ppermute | solution.py:163
  87.7 13.1 %collective-permute-start.9 = (f32[1,16,256]{2,1,0:T(8,128)S(1)}, f32[1,16,256]{2,1,0:T(8,128)S(1)}, u32[]{:S(2)}, u32[]{:S(2)}) collective-permute-start(f32[1,16,256]{2,1,0:T(8,128)S(1)} %slice.64), channel_id=1, source_target_pairs={{0,32},{32,0},{1,33},{33,1},{2,34},{34,2},{3,35},{35,3},{4,36},{36... | collective-permute-start | bytes 49160 | tf_op jit(solution)/shard_map/ppermute | solution.py:163
  97.8 7.3 %collective-permute-start.3 = (f32[3,128,256]{2,1,0:T(8,128)S(1)}, f32[3,128,256]{2,1,0:T(8,128)S(1)}, u32[]{:S(2)}, u32[]{:S(2)}) collective-permute-start(f32[3,128,256]{2,1,0:T(8,128)S(1)} %bitcast.116), channel_id=1, source_target_pairs={{0,1},{1,0},{2,3},{3,2},{4,5},{5,4},{6,7},{7,6},{8,9},{9,8},{10,11... | collective-permute-start | bytes 1179656 | tf_op jit(solution)/shard_map/ppermute | solution.py:163
  101.7 18.6 %all-to-all-start.3 = ((f32[8,3,16,256]{3,2,1,0:T(8,128)}), f32[8,3,16,256]{3,2,1,0:T(8,128)S(1)}, u32[]{:S(2)}, u32[]{:S(2)}) async-start(f32[8,3,16,256]{3,2,1,0:T(8,128)} %broadcast_in_dim.14), calls=%async_computation.3 | async-start | bytes 786432 | tf_op jit(solution)/shard_map/all_to_all | solution.py:173
  105.8 15.0 %collective-permute-start.4 = (f32[3,16,256]{2,1,0:T(8,128)S(1)}, f32[3,16,256]{2,1,0:T(8,128)S(1)}, u32[]{:S(2)}, u32[]{:S(2)}) collective-permute-start(f32[3,16,256]{2,1,0:T(8,128)S(1)} %slice_subtract_fusion), channel_id=1, source_target_pairs={{0,16},{16,0},{1,17},{17,1},{2,18},{18,2},{3,19},{19,3},{4,20},{20... | collective-permute-start | bytes 147464 | tf_op jit(solution)/shard_map/ppermute | solution.py:163
  120.3 3.3 %collective-permute-start.10 = (f32[3,128,256]{2,1,0:T(8,128)S(1)}, f32[3,128,256]{2,1,0:T(8,128)S(1)}, u32[]{:S(2)}, u32[]{:S(2)}) collective-permute-start(f32[3,128,256]{2,1,0:T(8,128)S(1)} %bitcast.117), channel_id=1, source_target_pairs={{0,1},{1,0},{2,3},{3,2},{4,5},{5,4},{6,7},{7,6},{8,9},{9,8},{10,11... | collective-permute-start | bytes 1179656 | tf_op jit(solution)/shard_map/ppermute | solution.py:163
  120.9 4.2 %collective-permute-start.5 = (f32[16,256]{1,0:T(8,128)S(1)}, f32[16,256]{1,0:T(8,128)S(1)}, u32[]{:S(2)}, u32[]{:S(2)}) collective-permute-start(f32[16,256]{1,0:T(8,128)S(1)} %slice_bitcast_fusion.5), channel_id=1, source_target_pairs={{0,32},{32,0},{1,33},{33,1},{2,34},{34,2},{3,35},{35,3},{4,36},{36... | collective-permute-start | bytes 49160 | tf_op jit(solution)/shard_map/ppermute | solution.py:163
  125.8 4.4 %collective-permute-start.11 = (f32[2,16,256]{2,1,0:T(8,128)S(1)}, f32[2,16,256]{2,1,0:T(8,128)S(1)}, u32[]{:S(2)}, u32[]{:S(2)}) collective-permute-start(f32[2,16,256]{2,1,0:T(8,128)S(1)} %slice_subtract_fusion.1), channel_id=1, source_target_pairs={{0,32},{32,0},{1,33},{33,1},{2,34},{34,2},{3,35},{35,3},{4,36},{36... | collective-permute-start | bytes 98312 | tf_op jit(solution)/shard_map/ppermute | solution.py:163
  130.2 2.7 %collective-permute-start.12 = (f32[16,256]{1,0:T(8,128)S(1)}, f32[16,256]{1,0:T(8,128)S(1)}, u32[]{:S(2)}, u32[]{:S(2)}) collective-permute-start(f32[16,256]{1,0:T(8,128)S(1)} %slice_bitcast_fusion.4), channel_id=1, source_target_pairs={{0,64},{64,0},{1,65},{65,1},{2,66},{66,2},{3,67},{67,3},{4,68},{68... | collective-permute-start | bytes 49160 | tf_op jit(solution)/shard_map/ppermute | solution.py:163
  133.3 2.7 %collective-permute-start.16 = (f32[16,256]{1,0:T(8,128)S(1)}, f32[16,256]{1,0:T(8,128)S(1)}, u32[]{:S(2)}, u32[]{:S(2)}) collective-permute-start(f32[16,256]{1,0:T(8,128)S(1)} %fusion.34), channel_id=1, source_target_pairs={{0,64},{64,0},{1,65},{65,1},{2,66},{66,2},{3,67},{67,3},{4,68},{68... | collective-permute-start | bytes 49160 | tf_op jit(solution)/shard_map/ppermute | solution.py:163
  136.0 4.1 %collective-permute-start.17 = (f32[16,256]{1,0:T(8,128)S(1)}, f32[16,256]{1,0:T(8,128)S(1)}, u32[]{:S(2)}, u32[]{:S(2)}) collective-permute-start(f32[16,256]{1,0:T(8,128)S(1)} %add.23), channel_id=1, source_target_pairs={{0,128},{128,0},{1,129},{129,1},{2,130},{130,2},{3,131},{131,3},{4... | collective-permute-start | bytes 49160 | tf_op jit(solution)/shard_map/ppermute | solution.py:163
  155.1 8.5 %copy-start = (f32[8,4,16,256]{3,2,1,0:T(8,128)}, f32[8,4,16,256]{3,2,1,0:T(8,128)S(1)}, u32[]{:S(2)}) copy-start(f32[8,4,16,256]{3,2,1,0:T(8,128)S(1)} %all_to_all.25.own_ref) | copy-start | bytes 1572868
  155.1 8.5 %collective-permute-start.22 = (f32[8,4,16,256]{3,2,1,0:T(8,128)S(1)}, f32[8,4,16,256]{3,2,1,0:T(8,128)S(1)}, u32[]{:S(2)}, u32[]{:S(2)}) collective-permute-start(f32[8,4,16,256]{3,2,1,0:T(8,128)S(1)} %all_to_all.25.own_ref), channel_id=1, source_target_pairs={{0,1},{1,0},{2,3},{3,2},{4,5},{5,4},{6,7},{7,6},{8,9},{9,8},{10,11... | collective-permute-start | bytes 1572872 | tf_op jit(solution)/shard_map/ppermute | solution.py:163
  163.6 0.8 copy-start.2
where the time goes:
time: 170 us
  waiting for transfers between devices  66.4 us (39%)
  starting transfers between devices  58.9 us (35%)
  Pallas kernels  15.1 us (9%)
  blocking collectives  14.6 us (9%)
  other arithmetic  8.49 us (5%)
  local copies, waits for them, and re-layouts  3.31 us (2%)
  matrix products  2.3 us (1%)
    all_to_all x4, waiting for transfers between devices, exchange(): return lax.all_to_all(block, axes, 0, 0, tiled=True)  54.7 us
    ppermute x23, starting transfers between devices, partner(): return lax.ppermute(block, axis, [(0, 1), (1, 0)])  41.8 us
    all_to_all x4, starting transfers between devices, exchange(): return lax.all_to_all(block, axes, 0, 0, tiled=True)  17.1 us
    all_to_all x1, blocking collectives, exchange(): return lax.all_to_all(block, axes, 0, 0, tiled=True)  14.6 us
    ppermute x23, waiting for transfers between devices, partner(): return lax.ppermute(block, axis, [(0, 1), (1, 0)])  11.8 us
    pallas_call x1, Pallas kernels, leaf(): pl.pallas_call(leaf_kernel, in_specs=[pl.BlockSpec(memory_space=pltpu.SME...  8.29 us
    pallas_call x1, Pallas kernels, finish(): pl.pallas_call(finish_kernel, grid=(STEPS,), in_specs=[pl.BlockSpec(memor...  5.15 us
    another operation x8, other arithmetic, whole(): return jnp.stack([low, high], axis=-3).reshape(256, 512)  3.83 us
  transfers between devices with their start and end apart: 27, of which 14 were waited for; matrix products, arithmetic and copies ran while one was open for 8% of the time, Pallas kernels for 1%

commit v1 on v0

--- a/solution.py
+++ b/solution.py
@@ -12,6 +12,8 @@
 F32 = jnp.float32
 BF16 = jnp.bfloat16
 PAIRS = ((3, 4), (2, 4), (1, 4), (2, 3), (1, 3), (1, 2))
+DIRECT = (4, (3, 4), (2, 4), (1, 4))
+SHARED = (3, (2, 3), (1, 3), 2, 1, (1, 2))
 
 
 def dot(a, b, dims):
@@ -37,7 +39,10 @@
     return pl.pallas_call(pack_kernel, out_shape=jax.ShapeDtypeStruct((Z, 32, 512), F32), name="pack")(k4, k3, k2, k1)
 
 
-def leaf_kernel(core_ref, inv_hbm, rhs_hbm, v_hbm, w_hbm, x_ref, keep_ref, give_ref, inv_ref, rhs_ref, v_ref, w_ref, high_ref, low_ref, sems):
+def leaf_kernel(
+    place_ref, inv_hbm, rhs_hbm, v_hbm, w_hbm, x_ref, keep_ref, give_ref, keep_shared_ref, give_shared_ref,
+    inv_ref, rhs_ref, v_ref, w_ref, high_ref, low_ref, sems,
+):
     rows = 1024 // STEPS
     count = [0]
 
@@ -58,12 +63,22 @@
     parts = [pl.ds(step * rows, rows) for step in range(STEPS)]
     wait_inv = [load(inv_hbm.at[part], inv_ref.at[part]) for part in parts]
     wait_v[4] = load(v_hbm.at[3], v_ref.at[3])
-    first = core_ref[0] == 0
-
-    def store(n, value):
+    first_core = place_ref[0] == 0
+    first_lanes = place_ref[1] == 0
+
+    def store(name, value):
         low, high = value[:128], value[128:]
-        keep_ref[:, n] = jnp.where(first, low, high).reshape(Z, 16, 256)
-        give_ref[:, n] = jnp.where(first, high, low).reshape(Z, 16, 256)
+        keep = jnp.where(first_core, low, high).reshape(Z, 16, 256)
+        give = jnp.where(first_core, high, low).reshape(Z, 16, 256)
+        if name in DIRECT:
+            keep_ref[:, DIRECT.index(name)] = keep
+            give_ref[:, DIRECT.index(name)] = give
+            return
+        n = SHARED.index(name)
+        for value, ref in ((keep, keep_shared_ref), (give, give_shared_ref)):
+            left, right = value[:, :, :128], value[:, :, 128:]
+            ref[0, :, n] = jnp.where(first_lanes, left, right)
+            ref[1, :, n] = jnp.where(first_lanes, right, left)
 
     done = set()
 
@@ -73,12 +88,12 @@
             waits[level].wait()
 
     turned = {}
-    for n, (j, k) in enumerate(PAIRS):
+    for j, k in PAIRS:
         ready(wait_w, k)
         if k not in turned:
             turned[k] = w_ref[k - 2].T
         ready(wait_v, j)
-        store(4 + n, dot(turned[k], v_ref[j - 1], ((1,), (0,))))
+        store((j, k), dot(turned[k], v_ref[j - 1], ((1,), (0,))))
     wait_rhs.wait()
     rhs = rhs_ref[...]
     rhs_turned = rhs.T
@@ -90,21 +105,23 @@
         high = xt.astype(BF16)
         high_ref[:, part] = high
         low_ref[:, part] = (xt - high.astype(F32)).astype(BF16)
-    for n, j in enumerate((4, 3, 2, 1)):
+    for j in (4, 3, 2, 1):
         ready(wait_v, j)
         v = v_ref[j - 1]
-        store(n, dot(high_ref[...], v, ((1,), (0,))) + dot(low_ref[...], v, ((1,), (0,))))
-
-
-def leaf(core, leaf_inv, right_side, right_basis, left_basis):
+        store(j, dot(high_ref[...], v, ((1,), (0,))) + dot(low_ref[...], v, ((1,), (0,))))
+
+
+def leaf(place, leaf_inv, right_side, right_basis, left_basis):
     any_space = pl.BlockSpec(memory_space=pl.ANY)
     return pl.pallas_call(
         leaf_kernel,
         in_specs=[pl.BlockSpec(memory_space=pltpu.SMEM)] + [any_space] * 4,
         out_shape=[
             jax.ShapeDtypeStruct((1024, 256), F32),
-            jax.ShapeDtypeStruct((Z, 10, 16, 256), F32),
-            jax.ShapeDtypeStruct((Z, 10, 16, 256), F32),
+            jax.ShapeDtypeStruct((Z, 4, 16, 256), F32),
+            jax.ShapeDtypeStruct((Z, 4, 16, 256), F32),
+            jax.ShapeDtypeStruct((2, Z, 6, 16, 128), F32),
+            jax.ShapeDtypeStruct((2, Z, 6, 16, 128), F32),
         ],
         scratch_shapes=[
             pltpu.VMEM((1024, 1024), BF16),
@@ -116,7 +133,7 @@
             pltpu.SemaphoreType.DMA((8 + STEPS,)),
         ],
         name="leaf",
-    )(core.reshape(1), leaf_inv, right_side, right_basis, left_basis)
+    )(place, leaf_inv, right_side, right_basis, left_basis)
 
 
 def finish_kernel(core_ref, w_ref, x_ref, own_ref, other_ref, out_ref, high_ref, low_ref):
@@ -181,10 +198,19 @@
     at = {axis: lax.axis_index(axis) for axis in AXES}
     core = at["c"]
     rows = exchange(pack(k4, k3, k2, k1), "z")
-    x0, keep, give = leaf(core, leaf_inv, right_side, right_basis, left_basis)
-    mine, rows = lax.optimization_barrier((keep + partner(give, "c"), rows))
-    sums = exchange(mine, "z").sum(axis=0)
-
+    x0, keep, give, keep_shared, give_shared = leaf(
+        jnp.stack([core, at["yl"]]), leaf_inv, right_side, right_basis, left_basis
+    )
+    mine = keep + partner(give, "c")
+    got_shared = partner(give_shared, "c")
+    got = partner(keep_shared[1] + got_shared[1], "yl")
+    direct = exchange(mine, "z")
+    pairs = (keep_shared[0] + got_shared[0]) + got
+    upper = at["yh"] == 0
+    fours = pairs[:, 3:]
+    got = partner(jnp.where(upper, fours[:, :, 8:], fours[:, :, :8]), "yh")
+    fours = jnp.where(upper, fours[:, :, :8], fours[:, :, 8:]) + got
+    got, rows = lax.optimization_barrier((got, rows))
     part4, part3, part2, part1 = rows[:, 0:16], rows[None, :, 16:24], rows[None, :, 24:28], rows[None, :, 28:30]
 
     def widen(part, axis):
@@ -202,10 +228,10 @@
         high = jnp.where(core == 0, other, part)
         return jnp.stack([low, high], axis=-3).reshape(256, 512)
 
-    def both_cores(by_z):
-        n = by_z.shape[1]
-        half = by_z.transpose(1, 0, 2, 3).reshape(n, 128, 256)
-        return ordered(core, half, partner(half, "c"), 1)
+    def both_cores(own, other, first, count):
+        own = own[:, first : first + count].reshape(Z * count, -1)
+        other = other[:, first : first + count].reshape(Z * count, -1)
+        return ordered(core, own, other, 0)
 
     def mix(part, own, axis, other=None):
         stack = ordered(at[axis], own, partner(own, axis), 1)
@@ -214,16 +240,44 @@
     def times(m, g):
         return fdot(m, g, ((1,), (0,)))
 
-    g34, g24, g14 = both_cores(spread(sums[4:7], "z", Z))
-    shared = sums[7:10]
-    shared = shared + partner(shared, "yl")
-    shared = jnp.concatenate([shared[:2], shared[2:] + partner(shared[2:], "yh")], axis=0)
-    m4 = mix(part4, sums[0], "yl", other4)
-    t = sums[1:4] - jnp.stack([times(m4, g34), times(m4, g24), times(m4, g14)])
-    g23, g13, g12 = both_cores(spread(shared, "z", Z))
+    def in_lanes(block):
+        zero = jnp.zeros_like(block)
+        first = at["yl"] == 0
+        return jnp.concatenate([jnp.where(first, block, zero), jnp.where(first, zero, block)], axis=1)
+
+    def in_rows(block):
+        zero = jnp.zeros_like(block)
+        return jnp.concatenate([jnp.where(upper, block, zero), jnp.where(upper, zero, block)], axis=0)
+
+    direct = direct.sum(axis=0)
+    to_all = jnp.broadcast_to(jnp.concatenate([direct[1:, :, :128], direct[1:, :, 128:]], axis=0)[None], (Z, 6, 16, 128))
+    mixed = jnp.concatenate(
+        [to_all.reshape(Z, 96, 128), pairs[:, :3].reshape(Z, 48, 128), fours.reshape(Z, 24, 128)], axis=1
+    )
+    mixed = exchange(mixed, "z")
+    m4 = mix(part4, direct[0], "yl", other4)
+    own = mixed[:, :96]
+    other = partner(own, "c")
+    g34, g24, g14 = [
+        jnp.concatenate([both_cores(own, other, 16 * n, 16), both_cores(own, other, 48 + 16 * n, 16)], axis=1)
+        for n in range(3)
+    ]
+    sums = mixed[:, 96:].sum(axis=0)
+    own = spread(jnp.concatenate([sums[16:48], sums[64:72]], axis=0), "z", Z)
+    t = in_lanes(sums[0:16]) - times(m4, g34)
+    got = partner(t, "yl")
+    t = t + got
+    m3 = mix(part3, t, "yh")
+    t2 = in_rows(in_lanes(sums[48:56])) - times(m4, g24)
+    t1 = in_rows(in_lanes(sums[56:64])) - times(m4, g14)
+    other = partner(own, "c")
+    g23, g13 = both_cores(own, other, 0, 16), both_cores(own, other, 16, 16)
+    quarter = jnp.concatenate([own[:, 32:], other[:, 32:]], axis=0)
+    half = ordered(at["yl"], quarter, partner(quarter, "yl"), 2)
+    full = ordered(at["yh"], half, partner(half, "yh"), 1)
+    g12 = ordered(core, full[:Z].reshape(128, 256), full[Z:].reshape(128, 256), 0)
+    t = jnp.stack([t2 - in_lanes(times(m3, g23)), t1 - in_lanes(times(m3, g13))])
     t = t + partner(t, "yl")
-    m3 = mix(part3, t[0], "yh")
-    t = t[1:] - jnp.stack([times(m3, g23), times(m3, g13)])
     t = t + partner(t, "yh")
     m2 = mix(part2, t[0], "xl")
     t = t[1] - times(m2, g12)

time: 170 us -> 166 us (0.976)
  waiting for transfers between devices: 66.4 us -> 54.9 us
  starting transfers between devices: 58.9 us -> 63.5 us
  other arithmetic: 8.49 us -> 12 us
    all_to_all x4, waiting for transfers between devices: 54.7 us -> 33.5 us  [exchange(): return lax.all_to_all(block, axes, 0, 0, tiled=True)]
    ppermute x23 -> x27, waiting for transfers between devices: 11.8 us -> 21.4 us  [partner(): return lax.ppermute(block, axis, [(0, 1), (1, 0)])]
    all_to_all x4, starting transfers between devices: 17.1 us -> 20.8 us  [exchange(): return lax.all_to_all(block, axes, 0, 0, tiled=True)]
    add x3 -> x4, other arithmetic: 1.48 us -> 4.1 us  [the longest x1 1.91 us: local(): mine = keep + partner(give, 'c')]
    ppermute x23 -> x27, starting transfers between devices: 41.8 us -> 42.7 us  [partner(): return lax.ppermute(block, axis, [(0, 1), (1, 0)])]
  transfers between devices with their start and end apart: 27 -> 31, of which waited for: 14 -> 17; matrix products, arithmetic and copies ran while one was open for 8% -> 8% of each run, Pallas kernels for 1% -> 1%
where the time goes in v1:
time: 166 us; the launch traced here: 165 us
  starting transfers between devices  63.5 us (38%)
  waiting for transfers between devices  54.9 us (33%)
  Pallas kernels  15.4 us (9%)
  blocking collectives  14.5 us (9%)
  other arithmetic  12 us (7%)
  local copies, waits for them, and re-layouts  2.4 us (1%)
  matrix products  2.2 us (1%)
    ppermute x27, starting transfers between devices, partner(): return lax.ppermute(block, axis, [(0, 1), (1, 0)])  42.7 us
    all_to_all x4, waiting for transfers between devices, exchange(): return lax.all_to_all(block, axes, 0, 0, tiled=True)  33.5 us
    ppermute x27, waiting for transfers between devices, partner(): return lax.ppermute(block, axis, [(0, 1), (1, 0)])  21.4 us
    all_to_all x4, starting transfers between devices, exchange(): return lax.all_to_all(block, axes, 0, 0, tiled=True)  20.8 us
    all_to_all x1, blocking collectives, exchange(): return lax.all_to_all(block, axes, 0, 0, tiled=True)  14.5 us
    pallas_call x1, Pallas kernels, leaf(): pl.pallas_call(leaf_kernel, in_specs=[pl.BlockSpec(memory_space=pltpu.SME...  8.61 us
    pallas_call x1, Pallas kernels, finish(): pl.pallas_call(finish_kernel, grid=(STEPS,), in_specs=[pl.BlockSpec(memor...  5.15 us
    another operation x8, other arithmetic, whole(): return jnp.stack([low, high], axis=-3).reshape(256, 512)  4.78 us
  transfers between devices with their start and end apart: 31, of which 17 were waited for; matrix products, arithmetic and copies ran while one was open for 8% of the time, Pallas kernels for 1%

profile of v1, /device:TPU:1, one launch (start us, length us, event | category | flops | bytes accessed | tf_op | source)
XLA Modules:
  0.0 165.5 jit_solution(14850488543654725559)
XLA Ops:
  0.0 0.6 pad_add_fusion.place_ref
  0.6 8.6 %leaf.1 = (f32[1024,256]{1,0:T(8,128)}, f32[8,4,16,256]{3,2,1,0:T(8,128)}, f32[8,4,16,256]{3,2,1,0:T(8,128)}, f32[2,8,6,16,128]{4,3,2,1,0:T(8,128)}, f32[2,8,6,16,128]{4,3,2,1,0:T(8,128)}) custom-call(s32[2]{0:T(128)} %pad_add_fusion.place_ref, bf16[1024,1024]{1,0:T(8,128)(2,1)} %inv_hbm.1, bf16[1024,256]{1,0:T(8,128)(2,1)} %rhs_hbm.1, ...), custom_call_target="tpu_custom_call" | custom-call | tf_op jit(solution)/shard_map/leaf/pallas_call | solution.py:116
  9.2 3.3 %collective-permute-start.2 = (f32[2,8,6,16,128]{4,3,2,1,0:T(8,128)}, f32[2,8,6,16,128]{4,3,2,1,0:T(8,128)S(1)}, u32[]{:S(2)}, u32[]{:S(2)}) collective-permute-start(f32[2,8,6,16,128]{4,3,2,1,0:T(8,128)} %get-tuple-element.15), channel_id=1, source_target_pairs={{0,1},{1,0},{2,3},{3,2},{4,5},{5,4},{6,7},{7,6},{8,9},{9,8},{10,11... | collective-permute-start | bytes 2359304 | tf_op jit(solution)/shard_map/ppermute | solution.py:180
  12.5 2.1 %collective-permute-done.2 = f32[2,8,6,16,128]{4,3,2,1,0:T(8,128)S(1)} collective-permute-done((f32[2,8,6,16,128]{4,3,2,1,0:T(8,128)}, f32[2,8,6,16,128]{4,3,2,1,0:T(8,128)S(1)}, u32[]{:S(2)}, u32[]{:S(2)}) %collective-permute-start.2) | collective-permute-done | bytes 786464 | tf_op jit(solution)/shard_map/ppermute | solution.py:180
  14.7 1.1 fusion.4
  15.9 1.6 pack.1
  17.5 7.8 %all-to-all-start.1 = ((f32[8,32,512]{2,1,0:T(8,128)}), f32[8,32,512]{2,1,0:T(8,128)S(1)}, u32[]{:S(2)}, u32[]{:S(2)}) async-start(f32[8,32,512]{2,1,0:T(8,128)} %pack.1), calls=%async_computation.1 | async-start | bytes 1048576 | tf_op jit(solution)/shard_map/all_to_all | solution.py:190
  25.2 0.9 collective-permute-start
  26.3 1.1 fusion.6
  27.4 2.6 %collective-permute-start.4 = (f32[8,3,8,128]{3,2,1,0:T(8,128)S(1)}, f32[8,3,8,128]{3,2,1,0:T(8,128)S(1)}, u32[]{:S(2)}, u32[]{:S(2)}) collective-permute-start(f32[8,3,8,128]{3,2,1,0:T(8,128)S(1)} %slice_select_fusion), channel_id=1, source_target_pairs={{0,32},{32,0},{1,33},{33,1},{2,34},{34,2},{3,35},{35,3},{4,36},{36... | collective-permute-start | bytes 294920 | tf_op jit(solution)/shard_map/ppermute | solution.py:180
  30.0 1.9 %add.33 = f32[8,4,16,256]{3,2,1,0:T(8,128)} add(f32[8,4,16,256]{3,2,1,0:T(8,128)S(1)} %copy-done.3, f32[8,4,16,256]{3,2,1,0:T(8,128)} %collective-permute-done) | non-fusion elementwise | flops 131072 | bytes 1572864 | tf_op jit(solution)/shard_map/add | solution.py:204
  31.9 11.3 %all-to-all-done.1 = f32[8,32,512]{2,1,0:T(8,128)S(1)} async-done(((f32[8,32,512]{2,1,0:T(8,128)}), f32[8,32,512]{2,1,0:T(8,128)S(1)}, u32[]{:S(2)}, u32[]{:S(2)}) %all-to-all-start.1) | async-done | bytes 524320 | tf_op jit(solution)/shard_map/all_to_all | solution.py:190
  43.2 3.5 %all-to-all-start = ((f32[8,4,16,256]{3,2,1,0:T(8,128)}), f32[8,4,16,256]{3,2,1,0:T(8,128)S(1)}, u32[]{:S(2)}, u32[]{:S(2)}) async-start(f32[8,4,16,256]{3,2,1,0:T(8,128)} %add.33), calls=%async_computation | async-start | bytes 1048576 | tf_op jit(solution)/shard_map/all_to_all | solution.py:190
  46.8 0.6 collective-permute-start.5
  47.6 1.3 collective-permute-start.15
  49.1 5.4 %collective-permute-done.22 = f32[1,8,2,512]{3,2,1,0:T(2,128)S(1)} collective-permute-done((f32[1,8,2,512]{3,2,1,0:T(2,128)S(1)}, f32[1,8,2,512]{3,2,1,0:T(2,128)S(1)}, u32[]{:S(2)}, u32[]{:S(2)}) %collective-permute-start.22) | collective-permute-done | bytes 32800 | tf_op jit(solution)/shard_map/ppermute | solution.py:180
  54.5 2.7 %collective-permute-start.23 = (f32[2,8,2,512]{3,2,1,0:T(2,128)S(1)}, f32[2,8,2,512]{3,2,1,0:T(2,128)S(1)}, u32[]{:S(2)}, u32[]{:S(2)}) collective-permute-start(f32[2,8,2,512]{3,2,1,0:T(2,128)S(1)} %pad_maximum_fusion.13), channel_id=1, source_target_pairs={{0,32},{32,0},{1,33},{33,1},{2,34},{34,2},{3,35},{35,3},{4,36},{36... | collective-permute-start | bytes 196616 | tf_op jit(solution)/shard_map/ppermute | solution.py:180
  57.3 0.4 collective-permute-start.16
  57.7 1.5 collective-permute-done.23
  59.3 0.7 pad_maximum_fusion.11
  60.0 1.2 collective-permute-start.24
  61.3 2.4 %collective-permute-start.10 = (f32[2,8,8,512]{3,2,1,0:T(8,128)S(1)}, f32[2,8,8,512]{3,2,1,0:T(8,128)}, u32[]{:S(2)}, u32[]{:S(2)}) collective-permute-start(f32[2,8,8,512]{3,2,1,0:T(8,128)S(1)} %pad_maximum_fusion.5), channel_id=1, source_target_pairs={{0,1},{1,0},{2,3},{3,2},{4,5},{5,4},{6,7},{7,6},{8,9},{9,8},{10,11... | collective-permute-start | bytes 786440 | tf_op jit(solution)/shard_map/ppermute | solution.py:180
  63.7 0.8 all-to-all-done
  64.6 0.3 collective-permute-start.1
  64.9 0.9 pad_maximum_fusion
  65.8 6.2 %all-to-all-start.2 = ((f32[8,168,128]{2,1,0:T(8,128)}), f32[8,168,128]{2,1,0:T(8,128)S(1)}, u32[]{:S(2)}, u32[]{:S(2)}) async-start(f32[8,168,128]{2,1,0:T(8,128)} %pad_maximum_fusion), calls=%async_computation.2 | async-start | bytes 1376256 | tf_op jit(solution)/shard_map/all_to_all | solution.py:190
  72.2 0.7 collective-permute-start.17
  73.2 1.0 select_bitcast_fusion.7
  74.3 0.3 fusion.41
  74.7 1.0 select_bitcast_fusion.5
  75.7 17.7 %all-to-all-done.2 = f32[8,168,128]{2,1,0:T(8,128)S(1)} async-done(((f32[8,168,128]{2,1,0:T(8,128)}), f32[8,168,128]{2,1,0:T(8,128)S(1)}, u32[]{:S(2)}, u32[]{:S(2)}) %all-to-all-start.2) | async-done | bytes 688160 | tf_op jit(solution)/shard_map/all_to_all | solution.py:190
  93.5 0.6 collective-permute-start.6
  94.1 0.7 broadcast_in_dim.32
  94.8 3.4 %all-to-all-start.3 = ((f32[8,40,128]{2,1,0:T(8,128)}), f32[8,40,128]{2,1,0:T(8,128)S(1)}, u32[]{:S(2)}, u32[]{:S(2)}) async-start(f32[8,40,128]{2,1,0:T(8,128)} %broadcast_in_dim.32), calls=%async_computation.3 | async-start | bytes 327680 | tf_op jit(solution)/shard_map/all_to_all | solution.py:190
  98.5 1.4 collective-permute-start.7
  99.9 1.1 select_bitcast_fusion.3
  101.2 3.6 %collective-permute-start.8 = (f32[16,256]{1,0:T(8,128)S(1)}, f32[16,256]{1,0:T(8,128)S(1)}, u32[]{:S(2)}, u32[]{:S(2)}) collective-permute-start(f32[16,256]{1,0:T(8,128)S(1)} %add.40), channel_id=1, source_target_pairs={{0,32},{32,0},{1,33},{33,1},{2,34},{34,2},{3,35},{35,3},{4,36},{36... | collective-permute-start | bytes 49160 | tf_op jit(solution)/shard_map/ppermute | solution.py:180
  104.8 3.6 %all-to-all-done.3 = f32[8,40,128]{2,1,0:T(8,128)S(1)} async-done(((f32[8,40,128]{2,1,0:T(8,128)}), f32[8,40,128]{2,1,0:T(8,128)S(1)}, u32[]{:S(2)}, u32[]{:S(2)}) %all-to-all-start.3) | async-done | bytes 163872 | tf_op jit(solution)/shard_map/all_to_all | solution.py:190
  108.4 0.5 collective-permute-start.11
  108.9 0.3 fusion.45
  109.2 0.7 collective-permute-done.11
  110.6 1.4 collective-permute-start.12
  112.4 1.1 collective-permute-done.12
  113.5 3.6 %collective-permute-start.13 = (f32[2,16,256]{2,1,0:T(8,128)S(1)}, f32[2,16,256]{2,1,0:T(8,128)S(1)}, u32[]{:S(2)}, u32[]{:S(2)}) collective-permute-start(f32[2,16,256]{2,1,0:T(8,128)S(1)} %fusion.73), channel_id=1, source_target_pairs={{0,32},{32,0},{1,33},{33,1},{2,34},{34,2},{3,35},{35,3},{4,36},{36... | collective-permute-start | bytes 98312 | tf_op jit(solution)/shard_map/ppermute | solution.py:180
  117.1 0.4 collective-permute-start.18
  117.5 0.9 collective-permute-done.13
  118.4 0.3 collective-permute-start.14
  118.8 1.7 %collective-permute-done.18 = f32[16,8,128]{2,1,0:T(8,128)S(1)} collective-permute-done((f32[16,8,128]{2,1,0:T(8,128)S(1)}, f32[16,8,128]{2,1,0:T(8,128)S(1)}, u32[]{:S(2)}, u32[]{:S(2)}) %collective-permute-start.18) | collective-permute-done | bytes 65568 | tf_op jit(solution)/shard_map/ppermute | solution.py:180
  120.5 1.3 collective-permute-start.19
  121.9 0.3 fusion.49
  122.2 3.8 %collective-permute-done.19 = f32[16,8,256]{2,1,0:T(8,128)S(1)} collective-permute-done((f32[16,8,256]{2,1,0:T(8,128)S(1)}, f32[16,8,256]{2,1,0:T(8,128)S(1)}, u32[]{:S(2)}, u32[]{:S(2)}) %collective-permute-start.19) | collective-permute-done | bytes 131104 | tf_op jit(solution)/shard_map/ppermute | solution.py:180
  126.2 0.3 collective-permute-start.20
  126.5 1.2 select_bitcast_fusion.1
  127.7 1.4 collective-permute-done.20
  129.1 2.4 %collective-permute-start.21 = (f32[16,256]{1,0:T(8,128)S(1)}, f32[16,256]{1,0:T(8,128)S(1)}, u32[]{:S(2)}, u32[]{:S(2)}) collective-permute-start(f32[16,256]{1,0:T(8,128)S(1)} %add.43), channel_id=1, source_target_pairs={{0,128},{128,0},{1,129},{129,1},{2,130},{130,2},{3,131},{131,3},{4... | collective-permute-start | bytes 49160 | tf_op jit(solution)/shard_map/ppermute | solution.py:180
  131.6 0.3 pad_maximum_fusion.4
  131.9 0.4 reshape.89
  132.3 0.9 collective-permute-done.21
  133.2 0.3 convolution_bitcast_fusion
  133.6 14.5 %all_to_all.25.own_ref = f32[8,4,16,256]{3,2,1,0:T(8,128)S(1)} all-to-all(f32[8,4,16,256]{3,2,1,0:T(8,128)S(1)} %broadcast_in_dim.35), channel_id=1, replica_groups=mesh['xh'=2,'xl'=2,'yh'=2,'yl'=2,'z'=8,'c'=2] {'z'}, dimensions={0} | all-to-all | bytes 1048576 | tf_op jit(solution)/shard_map/all_to_all | solution.py:190
  148.2 9.8 %collective-permute-start.26 = (f32[8,4,16,256]{3,2,1,0:T(8,128)S(1)}, f32[8,4,16,256]{3,2,1,0:T(8,128)S(1)}, u32[]{:S(2)}, u32[]{:S(2)}) collective-permute-start(f32[8,4,16,256]{3,2,1,0:T(8,128)S(1)} %all_to_all.25.own_ref), channel_id=1, source_target_pairs={{0,1},{1,0},{2,3},{3,2},{4,5},{5,4},{6,7},{7,6},{8,9},{9,8},{10,11... | collective-permute-start | bytes 1572872 | tf_op jit(solution)/shard_map/ppermute | solution.py:180
  158.0 1.5 collective-permute-done.26.other_ref
  159.5 0.8 copy-done.4
  160.3 5.2 %finish.1 = f32[1024,256]{1,0:T(8,128)} custom-call(s32[1]{0:T(128)} %bitcast.core_ref, bf16[4,1024,256]{2,1,0:T(8,128)(2,1)} %w_ref.1, f32[1024,256]{1,0:T(8,128)} %get-tuple-element.11.x_ref, f32[8,4,16,256]{3,2,1,0:T(8,128)} %copy-done.1, f32[8,4,16,256]{3,2,1,0:T(8,128)} %copy-done.4), custom_call_target="tpu_custom_call" | custom-call | tf_op jit(solution)/shard_map/finish/pallas_call | solution.py:162
  (96 shorter events, 3.6 us)
Async XLA Ops:
  9.2 17.0 %copy-start.2 = (f32[2,8,6,16,128]{4,3,2,1,0:T(8,128)S(1)}, f32[2,8,6,16,128]{4,3,2,1,0:T(8,128)}, u32[]{:S(2)}) copy-start(f32[2,8,6,16,128]{4,3,2,1,0:T(8,128)} %get-tuple-element.14) | copy-start | bytes 2359300
  9.2 5.4 %collective-permute-start.2 = (f32[2,8,6,16,128]{4,3,2,1,0:T(8,128)}, f32[2,8,6,16,128]{4,3,2,1,0:T(8,128)S(1)}, u32[]{:S(2)}, u32[]{:S(2)}) collective-permute-start(f32[2,8,6,16,128]{4,3,2,1,0:T(8,128)} %get-tuple-element.15), channel_id=1, source_target_pairs={{0,1},{1,0},{2,3},{3,2},{4,5},{5,4},{6,7},{7,6},{8,9},{9,8},{10,11... | collective-permute-start | bytes 2359304 | tf_op jit(solution)/shard_map/ppermute | solution.py:180
  14.7 15.4 %copy-start.3 = (f32[8,4,16,256]{3,2,1,0:T(8,128)S(1)}, f32[8,4,16,256]{3,2,1,0:T(8,128)}, u32[]{:S(2)}) copy-start(f32[8,4,16,256]{3,2,1,0:T(8,128)} %get-tuple-element.12) | copy-start | bytes 1572868
  15.8 10.5 %collective-permute-start.3 = (f32[8,6,16,128]{3,2,1,0:T(8,128)S(1)}, f32[8,6,16,128]{3,2,1,0:T(8,128)}, u32[]{:S(2)}, u32[]{:S(2)}) collective-permute-start(f32[8,6,16,128]{3,2,1,0:T(8,128)S(1)} %fusion.4), channel_id=1, source_target_pairs={{0,16},{16,0},{1,17},{17,1},{2,18},{18,2},{3,19},{19,3},{4,20},{20... | collective-permute-start | bytes 1179656 | tf_op jit(solution)/shard_map/ppermute | solution.py:180
  17.5 25.7 %all-to-all-start.1 = ((f32[8,32,512]{2,1,0:T(8,128)}), f32[8,32,512]{2,1,0:T(8,128)S(1)}, u32[]{:S(2)}, u32[]{:S(2)}) async-start(f32[8,32,512]{2,1,0:T(8,128)} %pack.1), calls=%async_computation.1 | async-start | bytes 1048576 | tf_op jit(solution)/shard_map/all_to_all | solution.py:190
  25.2 4.8 %collective-permute-start = (f32[8,4,16,256]{3,2,1,0:T(8,128)}, f32[8,4,16,256]{3,2,1,0:T(8,128)}, u32[]{:S(2)}, u32[]{:S(2)}) collective-permute-start(f32[8,4,16,256]{3,2,1,0:T(8,128)} %get-tuple-element.13), channel_id=1, source_target_pairs={{0,1},{1,0},{2,3},{3,2},{4,5},{5,4},{6,7},{7,6},{8,9},{9,8},{10,11... | collective-permute-start | bytes 1572872 | tf_op jit(solution)/shard_map/ppermute | solution.py:180
  27.3 21.7 %copy-start = (f32[8,6,16,128]{3,2,1,0:T(8,128)}, f32[8,6,16,128]{3,2,1,0:T(8,128)S(1)}, u32[]{:S(2)}) copy-start(f32[8,6,16,128]{3,2,1,0:T(8,128)S(1)} %fusion.6) | copy-start | bytes 1179652
  27.4 19.3 %collective-permute-start.4 = (f32[8,3,8,128]{3,2,1,0:T(8,128)S(1)}, f32[8,3,8,128]{3,2,1,0:T(8,128)S(1)}, u32[]{:S(2)}, u32[]{:S(2)}) collective-permute-start(f32[8,3,8,128]{3,2,1,0:T(8,128)S(1)} %slice_select_fusion), channel_id=1, source_target_pairs={{0,32},{32,0},{1,33},{33,1},{2,34},{34,2},{3,35},{35,3},{4,36},{36... | collective-permute-start | bytes 294920 | tf_op jit(solution)/shard_map/ppermute | solution.py:180
  43.2 21.4 %all-to-all-start = ((f32[8,4,16,256]{3,2,1,0:T(8,128)}), f32[8,4,16,256]{3,2,1,0:T(8,128)S(1)}, u32[]{:S(2)}, u32[]{:S(2)}) async-start(f32[8,4,16,256]{3,2,1,0:T(8,128)} %add.33), calls=%async_computation | async-start | bytes 1048576 | tf_op jit(solution)/shard_map/all_to_all | solution.py:190
  46.8 26.4 %collective-permute-start.5 = (f32[8,16,512]{2,1,0:T(8,128)S(1)}, f32[8,16,512]{2,1,0:T(8,128)}, u32[]{:S(2)}, u32[]{:S(2)}) collective-permute-start(f32[8,16,512]{2,1,0:T(8,128)S(1)} %slice.147), channel_id=1, source_target_pairs={{0,1},{1,0},{2,3},{3,2},{4,5},{5,4},{6,7},{7,6},{8,9},{9,8},{10,11... | collective-permute-start | bytes 786440 | tf_op jit(solution)/shard_map/ppermute | solution.py:180
  47.4 13.9 %collective-permute-start.9 = (f32[1,8,8,512]{3,2,1,0:T(8,128)S(1)}, f32[1,8,8,512]{3,2,1,0:T(8,128)S(1)}, u32[]{:S(2)}, u32[]{:S(2)}) collective-permute-start(f32[1,8,8,512]{3,2,1,0:T(8,128)S(1)} %slice_bitcast_fusion), channel_id=1, source_target_pairs={{0,16},{16,0},{1,17},{17,1},{2,18},{18,2},{3,19},{19,3},{4,20},{20... | collective-permute-start | bytes 393224 | tf_op jit(solution)/shard_map/ppermute | solution.py:180
  47.6 9.7 %collective-permute-start.15 = (f32[1,8,4,512]{3,2,1,0:T(4,128)S(1)}, f32[1,8,4,512]{3,2,1,0:T(4,128)S(1)}, u32[]{:S(2)}, u32[]{:S(2)}) collective-permute-start(f32[1,8,4,512]{3,2,1,0:T(4,128)S(1)} %slice_bitcast_fusion.1), channel_id=1, source_target_pairs={{0,16},{16,0},{1,17},{17,1},{2,18},{18,2},{3,19},{19,3},{4,20},{20... | collective-permute-start | bytes 196616 | tf_op jit(solution)/shard_map/ppermute | solution.py:180
  48.8 5.6 %collective-permute-start.22 = (f32[1,8,2,512]{3,2,1,0:T(2,128)S(1)}, f32[1,8,2,512]{3,2,1,0:T(2,128)S(1)}, u32[]{:S(2)}, u32[]{:S(2)}) collective-permute-start(f32[1,8,2,512]{3,2,1,0:T(2,128)S(1)} %slice_bitcast_fusion.2), channel_id=1, source_target_pairs={{0,16},{16,0},{1,17},{17,1},{2,18},{18,2},{3,19},{19,3},{4,20},{20... | collective-permute-start | bytes 98312 | tf_op jit(solution)/shard_map/ppermute | solution.py:180
  49.0 15.9 %slice-start = ((f32[8,6,16,128]{3,2,1,0:T(8,128)}), f32[8,3,16,128]{3,2,1,0:T(8,128)S(1)}, s32[]{:S(2)}) async-start(f32[8,6,16,128]{3,2,1,0:T(8,128)} %copy-done), calls=%async_computation.5 | async-start | bytes 393216 | tf_op jit(solution)/shard_map/slice | solution.py:255
  54.5 4.8 %collective-permute-start.23 = (f32[2,8,2,512]{3,2,1,0:T(2,128)S(1)}, f32[2,8,2,512]{3,2,1,0:T(2,128)S(1)}, u32[]{:S(2)}, u32[]{:S(2)}) collective-permute-start(f32[2,8,2,512]{3,2,1,0:T(2,128)S(1)} %pad_maximum_fusion.13), channel_id=1, source_target_pairs={{0,32},{32,0},{1,33},{33,1},{2,34},{34,2},{3,35},{35,3},{4,36},{36... | collective-permute-start | bytes 196616 | tf_op jit(solution)/shard_map/ppermute | solution.py:180
  57.3 14.7 %collective-permute-start.16 = (f32[2,8,4,512]{3,2,1,0:T(4,128)S(1)}, f32[2,8,4,512]{3,2,1,0:T(4,128)S(1)}, u32[]{:S(2)}, u32[]{:S(2)}) collective-permute-start(f32[2,8,4,512]{3,2,1,0:T(4,128)S(1)} %pad_maximum_fusion.9), channel_id=1, source_target_pairs={{0,32},{32,0},{1,33},{33,1},{2,34},{34,2},{3,35},{35,3},{4,36},{36... | collective-permute-start | bytes 393224 | tf_op jit(solution)/shard_map/ppermute | solution.py:180
  60.0 12.8 %collective-permute-start.24 = (f32[4,8,2,512]{3,2,1,0:T(2,128)}, f32[4,8,2,512]{3,2,1,0:T(2,128)S(1)}, u32[]{:S(2)}, u32[]{:S(2)}) collective-permute-start(f32[4,8,2,512]{3,2,1,0:T(2,128)} %pad_maximum_fusion.11), channel_id=1, source_target_pairs={{0,64},{64,0},{1,65},{65,1},{2,66},{66,2},{3,67},{67,3},{4,68},{68... | collective-permute-start | bytes 393224 | tf_op jit(solution)/shard_map/ppermute | solution.py:180
  61.3 13.4 %collective-permute-start.10 = (f32[2,8,8,512]{3,2,1,0:T(8,128)S(1)}, f32[2,8,8,512]{3,2,1,0:T(8,128)}, u32[]{:S(2)}, u32[]{:S(2)}) collective-permute-start(f32[2,8,8,512]{3,2,1,0:T(8,128)S(1)} %pad_maximum_fusion.5), channel_id=1, source_target_pairs={{0,1},{1,0},{2,3},{3,2},{4,5},{5,4},{6,7},{7,6},{8,9},{9,8},{10,11... | collective-permute-start | bytes 786440 | tf_op jit(solution)/shard_map/ppermute | solution.py:180
  64.6 7.4 %collective-permute-start.1 = (f32[16,256]{1,0:T(8,128)S(1)}, f32[16,256]{1,0:T(8,128)S(1)}, u32[]{:S(2)}, u32[]{:S(2)}) collective-permute-start(f32[16,256]{1,0:T(8,128)S(1)} %slice_bitcast_fusion.5), channel_id=1, source_target_pairs={{0,16},{16,0},{1,17},{17,1},{2,18},{18,2},{3,19},{19,3},{4,20},{20... | collective-permute-start | bytes 49160 | tf_op jit(solution)/shard_map/ppermute | solution.py:180
  65.8 27.6 %all-to-all-start.2 = ((f32[8,168,128]{2,1,0:T(8,128)}), f32[8,168,128]{2,1,0:T(8,128)S(1)}, u32[]{:S(2)}, u32[]{:S(2)}) async-start(f32[8,168,128]{2,1,0:T(8,128)} %pad_maximum_fusion), calls=%async_computation.2 | async-start | bytes 1376256 | tf_op jit(solution)/shard_map/all_to_all | solution.py:190
  72.2 27.7 %collective-permute-start.17 = (f32[4,8,4,512]{3,2,1,0:T(4,128)S(1)}, f32[4,8,4,512]{3,2,1,0:T(4,128)}, u32[]{:S(2)}, u32[]{:S(2)}) collective-permute-start(f32[4,8,4,512]{3,2,1,0:T(4,128)S(1)} %pad_maximum_fusion.6), channel_id=1, source_target_pairs={{0,1},{1,0},{2,3},{3,2},{4,5},{5,4},{6,7},{7,6},{8,9},{9,8},{10,11... | collective-permute-start | bytes 786440 | tf_op jit(solution)/shard_map/ppermute | solution.py:180
  73.1 53.4 %collective-permute-start.25 = (f32[8,8,2,512]{3,2,1,0:T(2,128)S(1)}, f32[8,8,2,512]{3,2,1,0:T(2,128)}, u32[]{:S(2)}, u32[]{:S(2)}) collective-permute-start(f32[8,8,2,512]{3,2,1,0:T(2,128)S(1)} %pad_maximum_fusion.7), channel_id=1, source_target_pairs={{0,1},{1,0},{2,3},{3,2},{4,5},{5,4},{6,7},{7,6},{8,9},{9,8},{10,11... | collective-permute-start | bytes 786440 | tf_op jit(solution)/shard_map/ppermute | solution.py:180
  93.5 4.7 %collective-permute-start.6 = (f32[8,96,128]{2,1,0:T(8,128)S(1)}, f32[8,96,128]{2,1,0:T(8,128)S(1)}, u32[]{:S(2)}, u32[]{:S(2)}) collective-permute-start(f32[8,96,128]{2,1,0:T(8,128)S(1)} %slice.194), channel_id=1, source_target_pairs={{0,1},{1,0},{2,3},{3,2},{4,5},{5,4},{6,7},{7,6},{8,9},{9,8},{10,11... | collective-permute-start | bytes 1179656 | tf_op jit(solution)/shard_map/ppermute | solution.py:180
  94.8 13.6 %all-to-all-start.3 = ((f32[8,40,128]{2,1,0:T(8,128)}), f32[8,40,128]{2,1,0:T(8,128)S(1)}, u32[]{:S(2)}, u32[]{:S(2)}) async-start(f32[8,40,128]{2,1,0:T(8,128)} %broadcast_in_dim.32), calls=%async_computation.3 | async-start | bytes 327680 | tf_op jit(solution)/shard_map/all_to_all | solution.py:190
  98.5 2.7 %collective-permute-start.7 = (f32[16,256]{1,0:T(8,128)S(1)}, f32[16,256]{1,0:T(8,128)S(1)}, u32[]{:S(2)}, u32[]{:S(2)}) collective-permute-start(f32[16,256]{1,0:T(8,128)S(1)} %convolution_subtract_fusion.2), channel_id=1, source_target_pairs={{0,16},{16,0},{1,17},{17,1},{2,18},{18,2},{3,19},{19,3},{4,20},{20... | collective-permute-start | bytes 49160 | tf_op jit(solution)/shard_map/ppermute | solution.py:180
  101.2 7.7 %collective-permute-start.8 = (f32[16,256]{1,0:T(8,128)S(1)}, f32[16,256]{1,0:T(8,128)S(1)}, u32[]{:S(2)}, u32[]{:S(2)}) collective-permute-start(f32[16,256]{1,0:T(8,128)S(1)} %add.40), channel_id=1, source_target_pairs={{0,32},{32,0},{1,33},{33,1},{2,34},{34,2},{3,35},{35,3},{4,36},{36... | collective-permute-start | bytes 49160 | tf_op jit(solution)/shard_map/ppermute | solution.py:180
  108.4 1.5 collective-permute-start.11
  110.6 2.9 %collective-permute-start.12 = (f32[2,16,256]{2,1,0:T(8,128)S(1)}, f32[2,16,256]{2,1,0:T(8,128)S(1)}, u32[]{:S(2)}, u32[]{:S(2)}) collective-permute-start(f32[2,16,256]{2,1,0:T(8,128)S(1)} %pad_maximum_fusion.16), channel_id=1, source_target_pairs={{0,16},{16,0},{1,17},{17,1},{2,18},{18,2},{3,19},{19,3},{4,20},{20... | collective-permute-start | bytes 98312 | tf_op jit(solution)/shard_map/ppermute | solution.py:180
  113.5 4.9 %collective-permute-start.13 = (f32[2,16,256]{2,1,0:T(8,128)S(1)}, f32[2,16,256]{2,1,0:T(8,128)S(1)}, u32[]{:S(2)}, u32[]{:S(2)}) collective-permute-start(f32[2,16,256]{2,1,0:T(8,128)S(1)} %fusion.73), channel_id=1, source_target_pairs={{0,32},{32,0},{1,33},{33,1},{2,34},{34,2},{3,35},{35,3},{4,36},{36... | collective-permute-start | bytes 98312 | tf_op jit(solution)/shard_map/ppermute | solution.py:180
  117.1 3.4 %collective-permute-start.18 = (f32[16,8,128]{2,1,0:T(8,128)S(1)}, f32[16,8,128]{2,1,0:T(8,128)S(1)}, u32[]{:S(2)}, u32[]{:S(2)}) collective-permute-start(f32[16,8,128]{2,1,0:T(8,128)S(1)} %pad_maximum_fusion.12), channel_id=1, source_target_pairs={{0,16},{16,0},{1,17},{17,1},{2,18},{18,2},{3,19},{19,3},{4,20},{20... | collective-permute-start | bytes 196616 | tf_op jit(solution)/shard_map/ppermute | solution.py:180
  118.4 3.4 %collective-permute-start.14 = (f32[16,256]{1,0:T(8,128)S(1)}, f32[16,256]{1,0:T(8,128)S(1)}, u32[]{:S(2)}, u32[]{:S(2)}) collective-permute-start(f32[16,256]{1,0:T(8,128)S(1)} %slice_bitcast_fusion.4), channel_id=1, source_target_pairs={{0,64},{64,0},{1,65},{65,1},{2,66},{66,2},{3,67},{67,3},{4,68},{68... | collective-permute-start | bytes 49160 | tf_op jit(solution)/shard_map/ppermute | solution.py:180
  120.5 5.4 %collective-permute-start.19 = (f32[16,8,256]{2,1,0:T(8,128)S(1)}, f32[16,8,256]{2,1,0:T(8,128)S(1)}, u32[]{:S(2)}, u32[]{:S(2)}) collective-permute-start(f32[16,8,256]{2,1,0:T(8,128)S(1)} %pad_maximum_fusion.10), channel_id=1, source_target_pairs={{0,32},{32,0},{1,33},{33,1},{2,34},{34,2},{3,35},{35,3},{4,36},{36... | collective-permute-start | bytes 393224 | tf_op jit(solution)/shard_map/ppermute | solution.py:180
  126.2 3.0 %collective-permute-start.20 = (f32[16,256]{1,0:T(8,128)S(1)}, f32[16,256]{1,0:T(8,128)S(1)}, u32[]{:S(2)}, u32[]{:S(2)}) collective-permute-start(f32[16,256]{1,0:T(8,128)S(1)} %fusion.56), channel_id=1, source_target_pairs={{0,64},{64,0},{1,65},{65,1},{2,66},{66,2},{3,67},{67,3},{4,68},{68... | collective-permute-start | bytes 49160 | tf_op jit(solution)/shard_map/ppermute | solution.py:180
  129.1 4.1 %collective-permute-start.21 = (f32[16,256]{1,0:T(8,128)S(1)}, f32[16,256]{1,0:T(8,128)S(1)}, u32[]{:S(2)}, u32[]{:S(2)}) collective-permute-start(f32[16,256]{1,0:T(8,128)S(1)} %add.43), channel_id=1, source_target_pairs={{0,128},{128,0},{1,129},{129,1},{2,130},{130,2},{3,131},{131,3},{4... | collective-permute-start | bytes 49160 | tf_op jit(solution)/shard_map/ppermute | solution.py:180
  148.2 11.4 %copy-start.1 = (f32[8,4,16,256]{3,2,1,0:T(8,128)}, f32[8,4,16,256]{3,2,1,0:T(8,128)S(1)}, u32[]{:S(2)}) copy-start(f32[8,4,16,256]{3,2,1,0:T(8,128)S(1)} %all_to_all.25.own_ref) | copy-start | bytes 1572868
  148.2 11.4 %collective-permute-start.26 = (f32[8,4,16,256]{3,2,1,0:T(8,128)S(1)}, f32[8,4,16,256]{3,2,1,0:T(8,128)S(1)}, u32[]{:S(2)}, u32[]{:S(2)}) collective-permute-start(f32[8,4,16,256]{3,2,1,0:T(8,128)S(1)} %all_to_all.25.own_ref), channel_id=1, source_target_pairs={{0,1},{1,0},{2,3},{3,2},{4,5},{5,4},{6,7},{7,6},{8,9},{9,8},{10,11... | collective-permute-start | bytes 1572872 | tf_op jit(solution)/shard_map/ppermute | solution.py:180
  159.5 0.8 copy-start.4

commit v2 on v1

--- a/solution.py
+++ b/solution.py
@@ -40,7 +40,7 @@
 
 
 def leaf_kernel(
-    place_ref, inv_hbm, rhs_hbm, v_hbm, w_hbm, x_ref, keep_ref, give_ref, keep_shared_ref, give_shared_ref,
+    core_ref, pair_ref, inv_hbm, rhs_hbm, v_hbm, w_hbm, x_ref, keep_ref, give_ref, keep_shared_ref, give_shared_ref,
     inv_ref, rhs_ref, v_ref, w_ref, high_ref, low_ref, sems,
 ):
     rows = 1024 // STEPS
@@ -63,8 +63,8 @@
     parts = [pl.ds(step * rows, rows) for step in range(STEPS)]
     wait_inv = [load(inv_hbm.at[part], inv_ref.at[part]) for part in parts]
     wait_v[4] = load(v_hbm.at[3], v_ref.at[3])
-    first_core = place_ref[0] == 0
-    first_lanes = place_ref[1] == 0
+    first_core = core_ref[0] == 0
+    first_lanes = pair_ref[0] == 0
 
     def store(name, value):
         low, high = value[:128], value[128:]
@@ -111,11 +111,11 @@
         store(j, dot(high_ref[...], v, ((1,), (0,))) + dot(low_ref[...], v, ((1,), (0,))))
 
 
-def leaf(place, leaf_inv, right_side, right_basis, left_basis):
+def leaf(core, pair, leaf_inv, right_side, right_basis, left_basis):
     any_space = pl.BlockSpec(memory_space=pl.ANY)
     return pl.pallas_call(
         leaf_kernel,
-        in_specs=[pl.BlockSpec(memory_space=pltpu.SMEM)] + [any_space] * 4,
+        in_specs=[pl.BlockSpec(memory_space=pltpu.SMEM)] * 2 + [any_space] * 4,
         out_shape=[
             jax.ShapeDtypeStruct((1024, 256), F32),
             jax.ShapeDtypeStruct((Z, 4, 16, 256), F32),
@@ -133,47 +133,60 @@
             pltpu.SemaphoreType.DMA((8 + STEPS,)),
         ],
         name="leaf",
-    )(place, leaf_inv, right_side, right_basis, left_basis)
-
-
-def finish_kernel(core_ref, w_ref, x_ref, own_ref, other_ref, out_ref, high_ref, low_ref):
+    )(core.reshape(1), pair.reshape(1), leaf_inv, right_side, right_basis, left_basis)
+
+
+def assemble_kernel(
+    core_ref, yl_ref, yh_ref, xl_ref, rows, rows_c, a, a_c, b, b_c, e, e_c, k4_ref, k3_ref, k2_ref, k1_ref
+):
     first = core_ref[0] == 0
-
-    @pl.when(pl.program_id(0) == 0)
-    def _():
-        for n in range(4):
-            own = own_ref[:, n].reshape(128, 256)
-            other = other_ref[:, n].reshape(128, 256)
-            m = jnp.concatenate([jnp.where(first, own, other), jnp.where(first, other, own)], axis=0)
-            high = m.astype(BF16)
-            high_ref[n] = high
-            low_ref[n] = (m - high.astype(F32)).astype(BF16)
-
-    total = x_ref[...]
-    for n, level in enumerate((4, 3, 2, 1)):
-        w = w_ref[level - 1]
-        total = total - (dot(w, high_ref[n], ((1,), (1,))) + dot(w, low_ref[n], ((1,), (1,))))
-    out_ref[...] = total
-
-
-def finish(core, left_basis, x, own, other):
-    rows = 1024 // STEPS
-    whole = pl.BlockSpec((Z, 4, 16, 256), lambda s: (0, 0, 0, 0))
+    yl, yh, xl = yl_ref[0], yh_ref[0], xl_ref[0]
+    near, far = jnp.where(yl == 0, 0, 1), jnp.where(yl == 0, 1, 0)
+    up, down = jnp.where(yh == 0, 0, 2), jnp.where(yh == 0, 2, 0)
+    left, right = jnp.where(xl == 0, 0, 4), jnp.where(xl == 0, 4, 0)
+
+    def pair(own, other):
+        return jnp.where(first, own, other), jnp.where(first, other, own)
+
+    def both(own, other):
+        return jnp.concatenate(pair(own, other), axis=0)
+
+    for z in range(Z):
+        low, high = pair(rows[z, 0:16], rows_c[z, 0:16])
+        k4_ref[32 * z : 32 * z + 16] = low
+        k4_ref[32 * z + 16 : 32 * z + 32] = high
+        for t, own, other in ((near, rows[z, 16:24], rows_c[z, 16:24]), (far, a[z, 0:8], a_c[z, 0:8])):
+            k3_ref[pl.ds(pl.multiple_of(128 * t + 16 * z, 16), 16)] = both(own, other)
+        for t, own, other in (
+            (up + near, rows[z, 24:28], rows_c[z, 24:28]),
+            (up + far, a[z, 8:12], a_c[z, 8:12]),
+            (down + near, b[z, 0:4], b_c[z, 0:4]),
+            (down + far, b[z, 8:12], b_c[z, 8:12]),
+        ):
+            k2_ref[pl.ds(pl.multiple_of(64 * t + 8 * z, 8), 8)] = both(own, other)
+    for z in range(0, Z, 2):
+        for t, (own, other, row) in (
+            (left + up + near, (rows, rows_c, 28)),
+            (left + up + far, (a, a_c, 12)),
+            (left + down + near, (b, b_c, 4)),
+            (left + down + far, (b, b_c, 12)),
+            (right + up + near, (e, e_c, 0)),
+            (right + up + far, (e, e_c, 2)),
+            (right + down + near, (e, e_c, 4)),
+            (right + down + far, (e, e_c, 6)),
+        ):
+            tile = [both(own[y, row : row + 2], other[y, row : row + 2]) for y in (z, z + 1)]
+            k1_ref[pl.ds(pl.multiple_of(32 * t + 4 * z, 8), 8)] = jnp.concatenate(tile, axis=0)
+
+
+def assemble(at, pieces):
+    scalars = [at[axis].reshape(1) for axis in ("c", "yl", "yh", "xl")]
     return pl.pallas_call(
-        finish_kernel,
-        grid=(STEPS,),
-        in_specs=[
-            pl.BlockSpec(memory_space=pltpu.SMEM),
-            pl.BlockSpec((4, rows, 256), lambda s: (0, s, 0)),
-            pl.BlockSpec((rows, 256), lambda s: (s, 0)),
-            whole,
-            whole,
-        ],
-        out_specs=pl.BlockSpec((rows, 256), lambda s: (s, 0)),
-        out_shape=jax.ShapeDtypeStruct((1024, 256), F32),
-        scratch_shapes=[pltpu.VMEM((4, 256, 256), BF16), pltpu.VMEM((4, 256, 256), BF16)],
-        name="finish",
-    )(core.reshape(1), left_basis, x, own, other)
+        assemble_kernel,
+        in_specs=[pl.BlockSpec(memory_space=pltpu.SMEM)] * 4 + [pl.BlockSpec()] * len(pieces),
+        out_shape=[jax.ShapeDtypeStruct((256, 512), F32)] * 4,
+        name="assemble",
+    )(*scalars, *pieces)
 
 
 def partner(block, axis):
@@ -199,7 +212,7 @@
     core = at["c"]
     rows = exchange(pack(k4, k3, k2, k1), "z")
     x0, keep, give, keep_shared, give_shared = leaf(
-        jnp.stack([core, at["yl"]]), leaf_inv, right_side, right_basis, left_basis
+        core, at["yl"], leaf_inv, right_side, right_basis, left_basis
     )
     mine = keep + partner(give, "c")
     got_shared = partner(give_shared, "c")
@@ -207,35 +220,29 @@
     direct = exchange(mine, "z")
     pairs = (keep_shared[0] + got_shared[0]) + got
     upper = at["yh"] == 0
-    fours = pairs[:, 3:]
-    got = partner(jnp.where(upper, fours[:, :, 8:], fours[:, :, :8]), "yh")
-    fours = jnp.where(upper, fours[:, :, :8], fours[:, :, 8:]) + got
-    got, rows = lax.optimization_barrier((got, rows))
-    part4, part3, part2, part1 = rows[:, 0:16], rows[None, :, 16:24], rows[None, :, 24:28], rows[None, :, 28:30]
-
-    def widen(part, axis):
-        return ordered(at[axis], part, partner(part, axis), 0)
-
-    part3 = widen(part3, "yl")
-    part2 = widen(widen(part2, "yl"), "yh")
-    part1 = widen(widen(widen(part1, "yl"), "yh"), "xl")
-    other4 = partner(part4, "c")
-
-    def whole(part, other=None):
-        if other is None:
-            other = partner(part, "c")
-        low = jnp.where(core == 0, part, other)
-        high = jnp.where(core == 0, other, part)
-        return jnp.stack([low, high], axis=-3).reshape(256, 512)
+    fours = pairs[:, 3:5]
+    give = jnp.where(upper, fours[:, :, 8:], fours[:, :, :8]).reshape(Z, 1, 16, 128)
+    got = partner(jnp.concatenate([give, pairs[:, 5:]], axis=1), "yh")
+    keep = jnp.where(upper, fours[:, :, :8], fours[:, :, 8:]).reshape(Z, 1, 16, 128)
+    fours = jnp.concatenate([keep, pairs[:, 5:]], axis=1) + got
+    fours, rows = lax.optimization_barrier((fours, rows))
+    a0 = rows[:, 16:32]
+    a1 = partner(a0, "yl")
+    b0 = jnp.concatenate([a0[:, 8:], a1[:, 8:]], axis=1)
+    b1 = partner(b0, "yh")
+    e0 = jnp.concatenate([b0[:, 4:6], b0[:, 12:14], b1[:, 4:6], b1[:, 12:14]], axis=1)
+    e1 = partner(e0, "xl")
+    pieces = [piece for own in (rows, a1, b1, e1) for piece in (own, partner(own, "c"))]
+    reduced = assemble(at, pieces)
 
     def both_cores(own, other, first, count):
         own = own[:, first : first + count].reshape(Z * count, -1)
         other = other[:, first : first + count].reshape(Z * count, -1)
         return ordered(core, own, other, 0)
 
-    def mix(part, own, axis, other=None):
+    def mix(k, own, axis):
         stack = ordered(at[axis], own, partner(own, axis), 1)
-        return fdot(stack, whole(part, other), ((1,), (1,)))
+        return fdot(stack, k, ((1,), (1,)))
 
     def times(m, g):
         return fdot(m, g, ((1,), (0,)))
@@ -252,10 +259,10 @@
     direct = direct.sum(axis=0)
     to_all = jnp.broadcast_to(jnp.concatenate([direct[1:, :, :128], direct[1:, :, 128:]], axis=0)[None], (Z, 6, 16, 128))
     mixed = jnp.concatenate(
-        [to_all.reshape(Z, 96, 128), pairs[:, :3].reshape(Z, 48, 128), fours.reshape(Z, 24, 128)], axis=1
+        [to_all.reshape(Z, 96, 128), pairs[:, :3].reshape(Z, 48, 128), fours.reshape(Z, 32, 128)], axis=1
     )
     mixed = exchange(mixed, "z")
-    m4 = mix(part4, direct[0], "yl", other4)
+    m4 = mix(reduced[0], direct[0], "yl")
     own = mixed[:, :96]
     other = partner(own, "c")
     g34, g24, g14 = [
@@ -263,29 +270,37 @@
         for n in range(3)
     ]
     sums = mixed[:, 96:].sum(axis=0)
-    own = spread(jnp.concatenate([sums[16:48], sums[64:72]], axis=0), "z", Z)
+    third = spread(jnp.concatenate([sums[16:48], sums[64:80]], axis=0), "z", Z)
     t = in_lanes(sums[0:16]) - times(m4, g34)
     got = partner(t, "yl")
     t = t + got
-    m3 = mix(part3, t, "yh")
+    m3 = mix(reduced[1], t, "yh")
+    own, m3 = lax.optimization_barrier((third, m3))
     t2 = in_rows(in_lanes(sums[48:56])) - times(m4, g24)
     t1 = in_rows(in_lanes(sums[56:64])) - times(m4, g14)
     other = partner(own, "c")
     g23, g13 = both_cores(own, other, 0, 16), both_cores(own, other, 16, 16)
-    quarter = jnp.concatenate([own[:, 32:], other[:, 32:]], axis=0)
-    half = ordered(at["yl"], quarter, partner(quarter, "yl"), 2)
-    full = ordered(at["yh"], half, partner(half, "yh"), 1)
-    g12 = ordered(core, full[:Z].reshape(128, 256), full[Z:].reshape(128, 256), 0)
+    half = both_cores(own, other, 32, 16)
+    g12 = ordered(at["yl"], half, partner(half, "yl"), 1)
     t = jnp.stack([t2 - in_lanes(times(m3, g23)), t1 - in_lanes(times(m3, g13))])
     t = t + partner(t, "yl")
     t = t + partner(t, "yh")
-    m2 = mix(part2, t[0], "xl")
+    m2 = mix(reduced[2], t[0], "xl")
     t = t[1] - times(m2, g12)
     t = t + partner(t, "xl")
-    m1 = mix(part1, t, "xh")
-
-    last = spread(jnp.stack([m4, m3, m2, m1]), "z", Z)
-    return finish(core, left_basis, x0, last, partner(last, "c"))
+    m1 = mix(reduced[3], t, "xh")
+
+    own = spread(jnp.concatenate([m4, m3, m2, m1], axis=0), "z", Z)
+    other = partner(own, "c")
+    out = x0
+    for n, level in enumerate((4, 3, 2, 1)):
+        m = both_cores(own, other, 16 * n, 16)
+        high = lax.reduce_precision(m, 8, 7)
+        low = (m - high).astype(BF16)
+        high = high.astype(BF16)
+        left = left_basis[level - 1]
+        out = out - (dot(left, high, ((1,), (1,))) + dot(left, low, ((1,), (1,))))
+    return out
 
 
 def solution(mesh):

time: 166 us -> 161 us (0.970)
  other arithmetic: 12 us -> 4.32 us
  waiting for transfers between devices: 54.9 us -> 60.2 us
  starting transfers between devices: 63.5 us -> 58.7 us
  matrix products: 2.2 us -> 6.93 us
  Pallas kernels: 15.4 us -> 12.7 us
    another operation x10 -> x0, other arithmetic: 5.41 us -> none  [the longest x8 4.78 us: whole(): return jnp.stack([low, high], axis=-3).reshape(256, 512)]
    ppermute x27 -> x23, waiting for transfers between devices: 21.4 us -> 26.4 us  [partner(): return lax.ppermute(block, axis, [(0, 1), (1, 0)])]
    dot_general x0 -> x8, matrix products: none -> 3.63 us  [dot(): lax.dot_general(a, b, ((dims[0], dims[1]), ((), ())), preferred_element_t...]
    all_to_all x4, starting transfers between devices: 20.8 us -> 18.2 us  [exchange(): return lax.all_to_all(block, axes, 0, 0, tiled=True)]
    ppermute x27 -> x23, starting transfers between devices: 42.7 us -> 40.5 us  [partner(): return lax.ppermute(block, axis, [(0, 1), (1, 0)])]
    pallas_call x1, Pallas kernels: 5.15 us -> 3.14 us  [assemble(): pl.pallas_call(assemble_kernel, in_specs=[pl.BlockSpec(memory_space=pltpu...]
  transfers between devices with their start and end apart: 31 -> 27, of which waited for: 17 -> 16; matrix products, arithmetic and copies ran while one was open for 8% -> 4% of each run, Pallas kernels for 1% -> 3%
where the time goes in v2:
time: 161 us; the launch traced here: 160 us
  waiting for transfers between devices  60.2 us (37%)
  starting transfers between devices  58.7 us (36%)
  blocking collectives  14.8 us (9%)
  Pallas kernels  12.7 us (8%)
  matrix products  6.93 us (4%)
  other arithmetic  4.32 us (3%)
  local copies, waits for them, and re-layouts  2.15 us (1%)
    ppermute x23, starting transfers between devices, partner(): return lax.ppermute(block, axis, [(0, 1), (1, 0)])  40.5 us
    all_to_all x4, waiting for transfers between devices, exchange(): return lax.all_to_all(block, axes, 0, 0, tiled=True)  33.8 us
    ppermute x23, waiting for transfers between devices, partner(): return lax.ppermute(block, axis, [(0, 1), (1, 0)])  26.4 us
    all_to_all x4, starting transfers between devices, exchange(): return lax.all_to_all(block, axes, 0, 0, tiled=True)  18.2 us
    all_to_all x1, blocking collectives, exchange(): return lax.all_to_all(block, axes, 0, 0, tiled=True)  14.8 us
    pallas_call x1, Pallas kernels, leaf(): pl.pallas_call(leaf_kernel, in_specs=[pl.BlockSpec(memory_space=pltpu.SME...  7.98 us
    dot_general x8, matrix products, dot(): lax.dot_general(a, b, ((dims[0], dims[1]), ((), ())), preferred_element_t...  3.63 us
    dot_general x10, matrix products, fdot(): lax.dot_general(a, b, ((dims[0], dims[1]), ((), ())), precision=lax.Preci...  3.29 us
  transfers between devices with their start and end apart: 27, of which 16 were waited for; matrix products, arithmetic and copies ran while one was open for 4% of the time, Pallas kernels for 3%

profile of v2, /device:TPU:1, one launch (start us, length us, event | category | flops | bytes accessed | tf_op | source)
XLA Modules:
  0.0 160.4 jit_solution(17310572847241450829)
XLA Ops:
  0.0 8.0 %leaf.1 = (f32[1024,256]{1,0:T(8,128)}, f32[8,4,16,256]{3,2,1,0:T(8,128)}, f32[8,4,16,256]{3,2,1,0:T(8,128)}, f32[2,8,6,16,128]{4,3,2,1,0:T(8,128)}, f32[2,8,6,16,128]{4,3,2,1,0:T(8,128)}) custom-call(s32[1]{0:T(128)} %bitcast.core_ref, s32[1]{0:T(128)} %bitcast.1.pair_ref.yl_ref, bf16[1024,1024]{1,0:T(8,128)(2,1)} %inv_hbm.1, bf16[1024,256]{1,0:T(8,128)(2,1)} %rhs_hbm.1, ...), custom_call_target="tpu_custom_call" | custom-call | tf_op jit(solution)/shard_map/leaf/pallas_call | solution.py:116
  8.0 3.3 %collective-permute-start.2 = (f32[2,8,6,16,128]{4,3,2,1,0:T(8,128)}, f32[2,8,6,16,128]{4,3,2,1,0:T(8,128)S(1)}, u32[]{:S(2)}, u32[]{:S(2)}) collective-permute-start(f32[2,8,6,16,128]{4,3,2,1,0:T(8,128)} %get-tuple-element.22), channel_id=1, source_target_pairs={{0,1},{1,0},{2,3},{3,2},{4,5},{5,4},{6,7},{7,6},{8,9},{9,8},{10,11... | collective-permute-start | bytes 2359304 | tf_op jit(solution)/shard_map/ppermute | solution.py:193
  11.3 1.6 %pack.1 = f32[8,32,512]{2,1,0:T(8,128)} custom-call(f32[16,512]{1,0:T(8,128)} %a_ref.1, f32[8,512]{1,0:T(8,128)} %b_ref.1, f32[4,512]{1,0:T(4,128)} %c_ref.1, f32[2,512]{1,0:T(2,128)} %d_ref.1), custom_call_target="tpu_custom_call" | custom-call | tf_op jit(solution)/shard_map/pack/pallas_call | solution.py:39
  12.9 6.5 %all-to-all-start.1 = ((f32[8,32,512]{2,1,0:T(8,128)}), f32[8,32,512]{2,1,0:T(8,128)S(1)}, u32[]{:S(2)}, u32[]{:S(2)}) async-start(f32[8,32,512]{2,1,0:T(8,128)} %pack.1), calls=%async_computation.1 | async-start | bytes 1048576 | tf_op jit(solution)/shard_map/all_to_all | solution.py:203
  19.4 0.4 collective-permute-start
  19.8 1.8 %fusion.32 = f32[8,6,16,128]{3,2,1,0:T(8,128)} fusion(f32[2,8,6,16,128]{4,3,2,1,0:T(8,128)S(1)} %collective-permute-done.2, f32[2,8,6,16,128]{4,3,2,1,0:T(8,128)} %get-tuple-element.21), kind=kLoop, calls=%fused_computation.41 | loop fusion | flops 98304 | bytes 1179648 | tf_op jit(solution)/shard_map/add | solution.py:219
  21.6 1.3 collective-permute-start.3
  22.9 0.9 add.57
  23.8 13.5 %all-to-all-done.1.rows = f32[8,32,512]{2,1,0:T(8,128)S(1)} async-done(((f32[8,32,512]{2,1,0:T(8,128)}), f32[8,32,512]{2,1,0:T(8,128)S(1)}, u32[]{:S(2)}, u32[]{:S(2)}) %all-to-all-start.1) | async-done | bytes 524320 | tf_op jit(solution)/shard_map/all_to_all | solution.py:203
  37.4 3.5 %all-to-all-start = ((f32[8,4,16,256]{3,2,1,0:T(8,128)}), f32[8,4,16,256]{3,2,1,0:T(8,128)S(1)}, u32[]{:S(2)}, u32[]{:S(2)}) async-start(f32[8,4,16,256]{3,2,1,0:T(8,128)} %add.57), calls=%async_computation | async-start | bytes 1048576 | tf_op jit(solution)/shard_map/all_to_all | solution.py:203
  41.0 3.0 %collective-permute-start.4 = (f32[8,2,16,128]{3,2,1,0:T(8,128)S(1)}, f32[8,2,16,128]{3,2,1,0:T(8,128)S(1)}, u32[]{:S(2)}, u32[]{:S(2)}) collective-permute-start(f32[8,2,16,128]{3,2,1,0:T(8,128)S(1)} %pad_maximum_fusion.6), channel_id=1, source_target_pairs={{0,32},{32,0},{1,33},{33,1},{2,34},{34,2},{3,35},{35,3},{4,36},{36... | collective-permute-start | bytes 393224 | tf_op jit(solution)/shard_map/ppermute | solution.py:193
  44.1 3.2 %collective-permute-done.4 = f32[8,2,16,128]{3,2,1,0:T(8,128)S(1)} collective-permute-done((f32[8,2,16,128]{3,2,1,0:T(8,128)S(1)}, f32[8,2,16,128]{3,2,1,0:T(8,128)S(1)}, u32[]{:S(2)}, u32[]{:S(2)}) %collective-permute-start.4) | collective-permute-done | bytes 131104 | tf_op jit(solution)/shard_map/ppermute | solution.py:193
  47.3 1.4 collective-permute-start.6
  48.6 10.1 %all-to-all-done = f32[8,4,16,256]{3,2,1,0:T(8,128)S(1)} async-done(((f32[8,4,16,256]{3,2,1,0:T(8,128)}), f32[8,4,16,256]{3,2,1,0:T(8,128)S(1)}, u32[]{:S(2)}, u32[]{:S(2)}) %all-to-all-start) | async-done | bytes 524320 | tf_op jit(solution)/shard_map/all_to_all | solution.py:203
  58.9 0.9 pad_maximum_fusion
  59.8 3.5 %all-to-all-start.2 = ((f32[8,176,128]{2,1,0:T(8,128)}), f32[8,176,128]{2,1,0:T(8,128)S(1)}, u32[]{:S(2)}, u32[]{:S(2)}) async-start(f32[8,176,128]{2,1,0:T(8,128)} %pad_maximum_fusion), calls=%async_computation.2 | async-start | bytes 1441792 | tf_op jit(solution)/shard_map/all_to_all | solution.py:203
  63.4 3.0 %collective-permute-start.8 = (f32[8,16,512]{2,1,0:T(8,128)S(1)}, f32[8,16,512]{2,1,0:T(8,128)S(1)}, u32[]{:S(2)}, u32[]{:S(2)}) collective-permute-start(f32[8,16,512]{2,1,0:T(8,128)S(1)} %pad_maximum_fusion.1), channel_id=1, source_target_pairs={{0,32},{32,0},{1,33},{33,1},{2,34},{34,2},{3,35},{35,3},{4,36},{36... | collective-permute-start | bytes 786440 | tf_op jit(solution)/shard_map/ppermute | solution.py:193
  66.5 0.9 collective-permute-start.5
  67.4 5.0 %collective-permute-done.8.b = f32[8,16,512]{2,1,0:T(8,128)S(1)} collective-permute-done((f32[8,16,512]{2,1,0:T(8,128)S(1)}, f32[8,16,512]{2,1,0:T(8,128)S(1)}, u32[]{:S(2)}, u32[]{:S(2)}) %collective-permute-start.8) | collective-permute-done | bytes 262176 | tf_op jit(solution)/shard_map/ppermute | solution.py:193
  72.5 1.3 collective-permute-start.10
  73.8 1.6 %collective-permute-start.9 = (f32[8,16,512]{2,1,0:T(8,128)S(1)}, f32[8,16,512]{2,1,0:T(8,128)S(1)}, u32[]{:S(2)}, u32[]{:S(2)}) collective-permute-start(f32[8,16,512]{2,1,0:T(8,128)S(1)} %collective-permute-done.8.b), channel_id=1, source_target_pairs={{0,1},{1,0},{2,3},{3,2},{4,5},{5,4},{6,7},{7,6},{8,9},{9,8},{10,11... | collective-permute-start | bytes 786440 | tf_op jit(solution)/shard_map/ppermute | solution.py:193
  75.4 1.3 collective-permute-start.1
  76.7 2.2 %collective-permute-start.11 = (f32[8,8,512]{2,1,0:T(8,128)S(1)}, f32[8,8,512]{2,1,0:T(8,128)S(1)}, u32[]{:S(2)}, u32[]{:S(2)}) collective-permute-start(f32[8,8,512]{2,1,0:T(8,128)S(1)} %collective-permute-done.10.e), channel_id=1, source_target_pairs={{0,1},{1,0},{2,3},{3,2},{4,5},{5,4},{6,7},{7,6},{8,9},{9,8},{10,11... | collective-permute-start | bytes 393224 | tf_op jit(solution)/shard_map/ppermute | solution.py:193
  79.0 0.9 collective-permute-done.11.e_c
  79.9 0.6 copy-done.14
  80.5 3.1 %assemble.1 = (f32[256,512]{1,0:T(8,128)}, f32[256,512]{1,0:T(8,128)}, f32[256,512]{1,0:T(8,128)}, f32[256,512]{1,0:T(8,128)}) custom-call(s32[1]{0:T(128)} %bitcast.core_ref, s32[1]{0:T(128)} %bitcast.1.pair_ref.yl_ref, s32[1]{0:T(128)} %bitcast.3.yh_ref, s32[1]{0:T(128)} %bitcast.4.xl_ref, f32[8,32,512]{2,1,0:T(8,128)} %copy-done.1, ...), custom_call_target="tpu_custom_call" | custom-call | tf_op jit(solution)/shard_map/assemble/pallas_call | solution.py:184
  83.7 1.7 %all-to-all-done.2 = f32[8,176,128]{2,1,0:T(8,128)S(1)} async-done(((f32[8,176,128]{2,1,0:T(8,128)}), f32[8,176,128]{2,1,0:T(8,128)S(1)}, u32[]{:S(2)}, u32[]{:S(2)}) %all-to-all-start.2) | async-done | bytes 720928 | tf_op jit(solution)/shard_map/all_to_all | solution.py:203
  85.5 0.8 collective-permute-start.12
  86.2 1.4 fusion.77
  88.0 1.4 collective-permute-start.13
  89.3 1.3 collective-permute-done.13
  90.6 2.9 %collective-permute-start.14 = (f32[16,256]{1,0:T(8,128)S(1)}, f32[16,256]{1,0:T(8,128)S(1)}, u32[]{:S(2)}, u32[]{:S(2)}) collective-permute-start(f32[16,256]{1,0:T(8,128)S(1)} %add.64), channel_id=1, source_target_pairs={{0,32},{32,0},{1,33},{33,1},{2,34},{34,2},{3,35},{35,3},{4,36},{36... | collective-permute-start | bytes 49160 | tf_op jit(solution)/shard_map/ppermute | solution.py:193
  93.6 0.7 broadcast_in_dim.10
  94.3 4.7 %all-to-all-start.3 = ((f32[8,48,128]{2,1,0:T(8,128)}), f32[8,48,128]{2,1,0:T(8,128)S(1)}, u32[]{:S(2)}, u32[]{:S(2)}) async-start(f32[8,48,128]{2,1,0:T(8,128)} %broadcast_in_dim.10), calls=%async_computation.3 | async-start | bytes 393216 | tf_op jit(solution)/shard_map/all_to_all | solution.py:203
  99.0 0.3 fusion.81
  99.3 8.4 %all-to-all-done.3 = f32[8,48,128]{2,1,0:T(8,128)S(1)} async-done(((f32[8,48,128]{2,1,0:T(8,128)}), f32[8,48,128]{2,1,0:T(8,128)S(1)}, u32[]{:S(2)}, u32[]{:S(2)}) %all-to-all-start.3) | async-done | bytes 196640 | tf_op jit(solution)/shard_map/all_to_all | solution.py:203
  107.7 3.0 %collective-permute-start.15 = (f32[8,48,128]{2,1,0:T(8,128)S(1)}, f32[8,48,128]{2,1,0:T(8,128)S(1)}, u32[]{:S(2)}, u32[]{:S(2)}) collective-permute-start(f32[8,48,128]{2,1,0:T(8,128)S(1)} %all-to-all-done.3), channel_id=1, source_target_pairs={{0,1},{1,0},{2,3},{3,2},{4,5},{5,4},{6,7},{7,6},{8,9},{9,8},{10,11... | collective-permute-start | bytes 589832 | tf_op jit(solution)/shard_map/ppermute | solution.py:193
  110.7 1.0 collective-permute-done.15
  112.5 0.5 collective-permute-start.16
  113.0 2.4 %collective-permute-done.16 = f32[2,16,256]{2,1,0:T(8,128)S(1)} collective-permute-done((f32[2,16,256]{2,1,0:T(8,128)S(1)}, f32[2,16,256]{2,1,0:T(8,128)S(1)}, u32[]{:S(2)}, u32[]{:S(2)}) %collective-permute-start.16) | collective-permute-done | bytes 32800 | tf_op jit(solution)/shard_map/ppermute | solution.py:193
  115.4 0.5 collective-permute-start.17
  115.9 3.8 %collective-permute-done.17 = f32[2,16,256]{2,1,0:T(8,128)S(1)} collective-permute-done((f32[2,16,256]{2,1,0:T(8,128)S(1)}, f32[2,16,256]{2,1,0:T(8,128)S(1)}, u32[]{:S(2)}, u32[]{:S(2)}) %collective-permute-start.17) | collective-permute-done | bytes 32800 | tf_op jit(solution)/shard_map/ppermute | solution.py:193
  119.7 1.3 collective-permute-start.18
  121.0 0.5 collective-permute-start.19
  121.4 0.9 collective-permute-done.18
  122.3 0.3 fusion.85
  122.7 2.2 %collective-permute-done.19 = f32[256,128]{1,0:T(8,128)S(1)} collective-permute-done((f32[256,128]{1,0:T(8,128)S(1)}, f32[256,128]{1,0:T(8,128)S(1)}, u32[]{:S(2)}, u32[]{:S(2)}) %collective-permute-start.19) | collective-permute-done | bytes 131104 | tf_op jit(solution)/shard_map/ppermute | solution.py:193
  125.0 0.3 collective-permute-start.20
  125.4 2.6 %collective-permute-done.20 = f32[16,256]{1,0:T(8,128)S(1)} collective-permute-done((f32[16,256]{1,0:T(8,128)S(1)}, f32[16,256]{1,0:T(8,128)S(1)}, u32[]{:S(2)}, u32[]{:S(2)}) %collective-permute-start.20) | collective-permute-done | bytes 16416 | tf_op jit(solution)/shard_map/ppermute | solution.py:193
  128.0 2.5 %collective-permute-start.21 = (f32[16,256]{1,0:T(8,128)S(1)}, f32[16,256]{1,0:T(8,128)S(1)}, u32[]{:S(2)}, u32[]{:S(2)}) collective-permute-start(f32[16,256]{1,0:T(8,128)S(1)} %add.67), channel_id=1, source_target_pairs={{0,128},{128,0},{1,129},{129,1},{2,130},{130,2},{3,131},{131,3},{4... | collective-permute-start | bytes 49160 | tf_op jit(solution)/shard_map/ppermute | solution.py:193
  130.5 1.6 %collective-permute-done.21 = f32[16,256]{1,0:T(8,128)S(1)} collective-permute-done((f32[16,256]{1,0:T(8,128)S(1)}, f32[16,256]{1,0:T(8,128)S(1)}, u32[]{:S(2)}, u32[]{:S(2)}) %collective-permute-start.21) | collective-permute-done | bytes 16416 | tf_op jit(solution)/shard_map/ppermute | solution.py:193
  132.1 0.3 fusion.89
  132.5 14.8 %all_to_all.25 = f32[8,64,256]{2,1,0:T(8,128)S(1)} all-to-all(f32[8,64,256]{2,1,0:T(8,128)S(1)} %broadcast_in_dim.11), channel_id=1, replica_groups=mesh['xh'=2,'xl'=2,'yh'=2,'yl'=2,'z'=8,'c'=2] {'z'}, dimensions={0} | all-to-all | bytes 1048576 | tf_op jit(solution)/shard_map/all_to_all | solution.py:203
  147.3 7.1 %collective-permute-start.22 = (f32[8,64,256]{2,1,0:T(8,128)S(1)}, f32[8,64,256]{2,1,0:T(8,128)S(1)}, u32[]{:S(2)}, u32[]{:S(2)}) collective-permute-start(f32[8,64,256]{2,1,0:T(8,128)S(1)} %all_to_all.25), channel_id=1, source_target_pairs={{0,1},{1,0},{2,3},{3,2},{4,5},{5,4},{6,7},{7,6},{8,9},{9,8},{10,11... | collective-permute-start | bytes 1572872 | tf_op jit(solution)/shard_map/ppermute | solution.py:193
  154.4 1.5 collective-permute-done.22
  156.1 0.3 fusion.13
  156.5 0.3 fusion.16
  156.8 0.3 fusion.19
  157.1 0.3 fusion.22
  157.5 0.6 copy-done.2
  158.0 0.3 fusion.7
  158.4 0.3 fusion.5
  158.7 0.3 fusion.3
  159.0 1.3 fusion.1
  (90 shorter events, 2.1 us)
Async XLA Ops:
  8.0 14.9 %copy-start.5 = (f32[8,4,16,256]{3,2,1,0:T(8,128)S(1)}, f32[8,4,16,256]{3,2,1,0:T(8,128)}, u32[]{:S(2)}) copy-start(f32[8,4,16,256]{3,2,1,0:T(8,128)} %get-tuple-element.19) | copy-start | bytes 1572868
  8.0 11.8 %collective-permute-start.2 = (f32[2,8,6,16,128]{4,3,2,1,0:T(8,128)}, f32[2,8,6,16,128]{4,3,2,1,0:T(8,128)S(1)}, u32[]{:S(2)}, u32[]{:S(2)}) collective-permute-start(f32[2,8,6,16,128]{4,3,2,1,0:T(8,128)} %get-tuple-element.22), channel_id=1, source_target_pairs={{0,1},{1,0},{2,3},{3,2},{4,5},{5,4},{6,7},{7,6},{8,9},{9,8},{10,11... | collective-permute-start | bytes 2359304 | tf_op jit(solution)/shard_map/ppermute | solution.py:193
  12.9 24.5 %all-to-all-start.1 = ((f32[8,32,512]{2,1,0:T(8,128)}), f32[8,32,512]{2,1,0:T(8,128)S(1)}, u32[]{:S(2)}, u32[]{:S(2)}) async-start(f32[8,32,512]{2,1,0:T(8,128)} %pack.1), calls=%async_computation.1 | async-start | bytes 1048576 | tf_op jit(solution)/shard_map/all_to_all | solution.py:203
  19.4 21.5 %copy-start.3 = (f32[2,8,6,16,128]{4,3,2,1,0:T(8,128)S(1)}, f32[2,8,6,16,128]{4,3,2,1,0:T(8,128)}, u32[]{:S(2)}) copy-start(f32[2,8,6,16,128]{4,3,2,1,0:T(8,128)} %get-tuple-element.21) | copy-start | bytes 2359300
  19.4 3.5 %collective-permute-start = (f32[8,4,16,256]{3,2,1,0:T(8,128)}, f32[8,4,16,256]{3,2,1,0:T(8,128)S(1)}, u32[]{:S(2)}, u32[]{:S(2)}) collective-permute-start(f32[8,4,16,256]{3,2,1,0:T(8,128)} %get-tuple-element.20), channel_id=1, source_target_pairs={{0,1},{1,0},{2,3},{3,2},{4,5},{5,4},{6,7},{7,6},{8,9},{9,8},{10,11... | collective-permute-start | bytes 1572872 | tf_op jit(solution)/shard_map/ppermute | solution.py:193
  21.6 19.3 %collective-permute-start.3 = (f32[8,6,16,128]{3,2,1,0:T(8,128)}, f32[8,6,16,128]{3,2,1,0:T(8,128)S(1)}, u32[]{:S(2)}, u32[]{:S(2)}) collective-permute-start(f32[8,6,16,128]{3,2,1,0:T(8,128)} %fusion.32), channel_id=1, source_target_pairs={{0,16},{16,0},{1,17},{17,1},{2,18},{18,2},{3,19},{19,3},{4,20},{20... | collective-permute-start | bytes 1179656 | tf_op jit(solution)/shard_map/ppermute | solution.py:193
  37.4 29.1 %copy-start.1 = (f32[8,32,512]{2,1,0:T(8,128)}, f32[8,32,512]{2,1,0:T(8,128)S(1)}, u32[]{:S(2)}) copy-start(f32[8,32,512]{2,1,0:T(8,128)S(1)} %all-to-all-done.1.rows) | copy-start | bytes 1572868
  37.4 21.4 %all-to-all-start = ((f32[8,4,16,256]{3,2,1,0:T(8,128)}), f32[8,4,16,256]{3,2,1,0:T(8,128)S(1)}, u32[]{:S(2)}, u32[]{:S(2)}) async-start(f32[8,4,16,256]{3,2,1,0:T(8,128)} %add.57), calls=%async_computation | async-start | bytes 1048576 | tf_op jit(solution)/shard_map/all_to_all | solution.py:203
  41.0 6.2 %collective-permute-start.4 = (f32[8,2,16,128]{3,2,1,0:T(8,128)S(1)}, f32[8,2,16,128]{3,2,1,0:T(8,128)S(1)}, u32[]{:S(2)}, u32[]{:S(2)}) collective-permute-start(f32[8,2,16,128]{3,2,1,0:T(8,128)S(1)} %pad_maximum_fusion.6), channel_id=1, source_target_pairs={{0,32},{32,0},{1,33},{33,1},{2,34},{34,2},{3,35},{35,3},{4,36},{36... | collective-permute-start | bytes 393224 | tf_op jit(solution)/shard_map/ppermute | solution.py:193
  47.3 16.1 %collective-permute-start.6 = (f32[8,16,512]{2,1,0:T(8,128)S(1)}, f32[8,16,512]{2,1,0:T(8,128)S(1)}, u32[]{:S(2)}, u32[]{:S(2)}) collective-permute-start(f32[8,16,512]{2,1,0:T(8,128)S(1)} %slice.194), channel_id=1, source_target_pairs={{0,16},{16,0},{1,17},{17,1},{2,18},{18,2},{3,19},{19,3},{4,20},{20... | collective-permute-start | bytes 786440 | tf_op jit(solution)/shard_map/ppermute | solution.py:193
  59.8 25.6 %all-to-all-start.2 = ((f32[8,176,128]{2,1,0:T(8,128)}), f32[8,176,128]{2,1,0:T(8,128)S(1)}, u32[]{:S(2)}, u32[]{:S(2)}) async-start(f32[8,176,128]{2,1,0:T(8,128)} %pad_maximum_fusion), calls=%async_computation.2 | async-start | bytes 1441792 | tf_op jit(solution)/shard_map/all_to_all | solution.py:203
  63.4 16.5 %copy-start.4 = (f32[8,16,512]{2,1,0:T(8,128)}, f32[8,16,512]{2,1,0:T(8,128)S(1)}, u32[]{:S(2)}) copy-start(f32[8,16,512]{2,1,0:T(8,128)S(1)} %collective-permute-done.6.a) | copy-start | bytes 786436
  63.4 9.0 %collective-permute-start.8 = (f32[8,16,512]{2,1,0:T(8,128)S(1)}, f32[8,16,512]{2,1,0:T(8,128)S(1)}, u32[]{:S(2)}, u32[]{:S(2)}) collective-permute-start(f32[8,16,512]{2,1,0:T(8,128)S(1)} %pad_maximum_fusion.1), channel_id=1, source_target_pairs={{0,32},{32,0},{1,33},{33,1},{2,34},{34,2},{3,35},{35,3},{4,36},{36... | collective-permute-start | bytes 786440 | tf_op jit(solution)/shard_map/ppermute | solution.py:193
  66.5 12.5 %collective-permute-start.5 = (f32[8,32,512]{2,1,0:T(8,128)S(1)}, f32[8,32,512]{2,1,0:T(8,128)S(1)}, u32[]{:S(2)}, u32[]{:S(2)}) collective-permute-start(f32[8,32,512]{2,1,0:T(8,128)S(1)} %all-to-all-done.1.rows), channel_id=1, source_target_pairs={{0,1},{1,0},{2,3},{3,2},{4,5},{5,4},{6,7},{7,6},{8,9},{9,8},{10,11... | collective-permute-start | bytes 1572872 | tf_op jit(solution)/shard_map/ppermute | solution.py:193
  67.3 11.6 %collective-permute-start.7 = (f32[8,16,512]{2,1,0:T(8,128)S(1)}, f32[8,16,512]{2,1,0:T(8,128)S(1)}, u32[]{:S(2)}, u32[]{:S(2)}) collective-permute-start(f32[8,16,512]{2,1,0:T(8,128)S(1)} %collective-permute-done.6.a), channel_id=1, source_target_pairs={{0,1},{1,0},{2,3},{3,2},{4,5},{5,4},{6,7},{7,6},{8,9},{9,8},{10,11... | collective-permute-start | bytes 786440 | tf_op jit(solution)/shard_map/ppermute | solution.py:193
  72.4 7.5 %copy-start.10 = (f32[8,16,512]{2,1,0:T(8,128)}, f32[8,16,512]{2,1,0:T(8,128)S(1)}, u32[]{:S(2)}) copy-start(f32[8,16,512]{2,1,0:T(8,128)S(1)} %collective-permute-done.8.b) | copy-start | bytes 786436
  72.5 4.2 %collective-permute-start.10 = (f32[8,8,512]{2,1,0:T(8,128)S(1)}, f32[8,8,512]{2,1,0:T(8,128)S(1)}, u32[]{:S(2)}, u32[]{:S(2)}) collective-permute-start(f32[8,8,512]{2,1,0:T(8,128)S(1)} %pad_maximum_fusion.8), channel_id=1, source_target_pairs={{0,64},{64,0},{1,65},{65,1},{2,66},{66,2},{3,67},{67,3},{4,68},{68... | collective-permute-start | bytes 393224 | tf_op jit(solution)/shard_map/ppermute | solution.py:193
  73.8 5.2 %collective-permute-start.9 = (f32[8,16,512]{2,1,0:T(8,128)S(1)}, f32[8,16,512]{2,1,0:T(8,128)S(1)}, u32[]{:S(2)}, u32[]{:S(2)}) collective-permute-start(f32[8,16,512]{2,1,0:T(8,128)S(1)} %collective-permute-done.8.b), channel_id=1, source_target_pairs={{0,1},{1,0},{2,3},{3,2},{4,5},{5,4},{6,7},{7,6},{8,9},{9,8},{10,11... | collective-permute-start | bytes 786440 | tf_op jit(solution)/shard_map/ppermute | solution.py:193
  75.4 3.5 %collective-permute-start.1 = (f32[16,256]{1,0:T(8,128)S(1)}, f32[16,256]{1,0:T(8,128)S(1)}, u32[]{:S(2)}, u32[]{:S(2)}) collective-permute-start(f32[16,256]{1,0:T(8,128)S(1)} %slice_bitcast_fusion.2), channel_id=1, source_target_pairs={{0,16},{16,0},{1,17},{17,1},{2,18},{18,2},{3,19},{19,3},{4,20},{20... | collective-permute-start | bytes 49160 | tf_op jit(solution)/shard_map/ppermute | solution.py:193
  76.7 3.2 %copy-start.13 = (f32[8,8,512]{2,1,0:T(8,128)}, f32[8,8,512]{2,1,0:T(8,128)S(1)}, u32[]{:S(2)}) copy-start(f32[8,8,512]{2,1,0:T(8,128)S(1)} %collective-permute-done.10.e) | copy-start | bytes 393220
  76.7 3.2 %collective-permute-start.11 = (f32[8,8,512]{2,1,0:T(8,128)S(1)}, f32[8,8,512]{2,1,0:T(8,128)S(1)}, u32[]{:S(2)}, u32[]{:S(2)}) collective-permute-start(f32[8,8,512]{2,1,0:T(8,128)S(1)} %collective-permute-done.10.e), channel_id=1, source_target_pairs={{0,1},{1,0},{2,3},{3,2},{4,5},{5,4},{6,7},{7,6},{8,9},{9,8},{10,11... | collective-permute-start | bytes 393224 | tf_op jit(solution)/shard_map/ppermute | solution.py:193
  78.9 1.0 copy-start.11
  79.0 1.0 copy-start.9
  79.0 1.0 copy-start.12
  79.9 0.7 copy-start.14
  85.5 2.2 %collective-permute-start.12 = (f32[8,96,128]{2,1,0:T(8,128)S(1)}, f32[8,96,128]{2,1,0:T(8,128)S(1)}, u32[]{:S(2)}, u32[]{:S(2)}) collective-permute-start(f32[8,96,128]{2,1,0:T(8,128)S(1)} %slice.261), channel_id=1, source_target_pairs={{0,1},{1,0},{2,3},{3,2},{4,5},{5,4},{6,7},{7,6},{8,9},{9,8},{10,11... | collective-permute-start | bytes 1179656 | tf_op jit(solution)/shard_map/ppermute | solution.py:193
  86.2 12.8 %copy-start.8 = (f32[256,512]{1,0:T(8,128)S(1)}, f32[256,512]{1,0:T(8,128)}, u32[]{:S(2)}) copy-start(f32[256,512]{1,0:T(8,128)} %get-tuple-element.26) | copy-start | bytes 1572868
  88.0 2.7 %collective-permute-start.13 = (f32[16,256]{1,0:T(8,128)S(1)}, f32[16,256]{1,0:T(8,128)S(1)}, u32[]{:S(2)}, u32[]{:S(2)}) collective-permute-start(f32[16,256]{1,0:T(8,128)S(1)} %convolution_subtract_fusion.2), channel_id=1, source_target_pairs={{0,16},{16,0},{1,17},{17,1},{2,18},{18,2},{3,19},{19,3},{4,20},{20... | collective-permute-start | bytes 49160 | tf_op jit(solution)/shard_map/ppermute | solution.py:193
  90.6 31.7 %copy-start.7 = (f32[256,512]{1,0:T(8,128)S(1)}, f32[256,512]{1,0:T(8,128)}, u32[]{:S(2)}) copy-start(f32[256,512]{1,0:T(8,128)} %get-tuple-element.29) | copy-start | bytes 1572868
  90.6 8.3 %collective-permute-start.14 = (f32[16,256]{1,0:T(8,128)S(1)}, f32[16,256]{1,0:T(8,128)S(1)}, u32[]{:S(2)}, u32[]{:S(2)}) collective-permute-start(f32[16,256]{1,0:T(8,128)S(1)} %add.64), channel_id=1, source_target_pairs={{0,32},{32,0},{1,33},{33,1},{2,34},{34,2},{3,35},{35,3},{4,36},{36... | collective-permute-start | bytes 49160 | tf_op jit(solution)/shard_map/ppermute | solution.py:193
  94.3 13.4 %all-to-all-start.3 = ((f32[8,48,128]{2,1,0:T(8,128)}), f32[8,48,128]{2,1,0:T(8,128)S(1)}, u32[]{:S(2)}, u32[]{:S(2)}) async-start(f32[8,48,128]{2,1,0:T(8,128)} %broadcast_in_dim.10), calls=%async_computation.3 | async-start | bytes 393216 | tf_op jit(solution)/shard_map/all_to_all | solution.py:203
  107.7 4.1 %collective-permute-start.15 = (f32[8,48,128]{2,1,0:T(8,128)S(1)}, f32[8,48,128]{2,1,0:T(8,128)S(1)}, u32[]{:S(2)}, u32[]{:S(2)}) collective-permute-start(f32[8,48,128]{2,1,0:T(8,128)S(1)} %all-to-all-done.3), channel_id=1, source_target_pairs={{0,1},{1,0},{2,3},{3,2},{4,5},{5,4},{6,7},{7,6},{8,9},{9,8},{10,11... | collective-permute-start | bytes 589832 | tf_op jit(solution)/shard_map/ppermute | solution.py:193
  110.7 21.4 %copy-start.6 = (f32[256,512]{1,0:T(8,128)S(1)}, f32[256,512]{1,0:T(8,128)}, u32[]{:S(2)}) copy-start(f32[256,512]{1,0:T(8,128)} %get-tuple-element.30) | copy-start | bytes 1572868
  112.5 2.9 %collective-permute-start.16 = (f32[2,16,256]{2,1,0:T(8,128)S(1)}, f32[2,16,256]{2,1,0:T(8,128)S(1)}, u32[]{:S(2)}, u32[]{:S(2)}) collective-permute-start(f32[2,16,256]{2,1,0:T(8,128)S(1)} %pad_maximum_fusion.12), channel_id=1, source_target_pairs={{0,16},{16,0},{1,17},{17,1},{2,18},{18,2},{3,19},{19,3},{4,20},{20... | collective-permute-start | bytes 98312 | tf_op jit(solution)/shard_map/ppermute | solution.py:193
  115.4 4.3 %collective-permute-start.17 = (f32[2,16,256]{2,1,0:T(8,128)S(1)}, f32[2,16,256]{2,1,0:T(8,128)S(1)}, u32[]{:S(2)}, u32[]{:S(2)}) collective-permute-start(f32[2,16,256]{2,1,0:T(8,128)S(1)} %fusion.118), channel_id=1, source_target_pairs={{0,32},{32,0},{1,33},{33,1},{2,34},{34,2},{3,35},{35,3},{4,36},{36... | collective-permute-start | bytes 98312 | tf_op jit(solution)/shard_map/ppermute | solution.py:193
  119.7 2.7 %collective-permute-start.18 = (f32[16,256]{1,0:T(8,128)S(1)}, f32[16,256]{1,0:T(8,128)S(1)}, u32[]{:S(2)}, u32[]{:S(2)}) collective-permute-start(f32[16,256]{1,0:T(8,128)S(1)} %slice_bitcast_fusion.1), channel_id=1, source_target_pairs={{0,64},{64,0},{1,65},{65,1},{2,66},{66,2},{3,67},{67,3},{4,68},{68... | collective-permute-start | bytes 49160 | tf_op jit(solution)/shard_map/ppermute | solution.py:193
  121.0 3.9 %collective-permute-start.19 = (f32[256,128]{1,0:T(8,128)S(1)}, f32[256,128]{1,0:T(8,128)S(1)}, u32[]{:S(2)}, u32[]{:S(2)}) collective-permute-start(f32[256,128]{1,0:T(8,128)S(1)} %pad_maximum_fusion.9), channel_id=1, source_target_pairs={{0,16},{16,0},{1,17},{17,1},{2,18},{18,2},{3,19},{19,3},{4,20},{20... | collective-permute-start | bytes 393224 | tf_op jit(solution)/shard_map/ppermute | solution.py:193
  125.0 3.0 %collective-permute-start.20 = (f32[16,256]{1,0:T(8,128)S(1)}, f32[16,256]{1,0:T(8,128)S(1)}, u32[]{:S(2)}, u32[]{:S(2)}) collective-permute-start(f32[16,256]{1,0:T(8,128)S(1)} %fusion.93), channel_id=1, source_target_pairs={{0,64},{64,0},{1,65},{65,1},{2,66},{66,2},{3,67},{67,3},{4,68},{68... | collective-permute-start | bytes 49160 | tf_op jit(solution)/shard_map/ppermute | solution.py:193
  128.0 4.1 %collective-permute-start.21 = (f32[16,256]{1,0:T(8,128)S(1)}, f32[16,256]{1,0:T(8,128)S(1)}, u32[]{:S(2)}, u32[]{:S(2)}) collective-permute-start(f32[16,256]{1,0:T(8,128)S(1)} %add.67), channel_id=1, source_target_pairs={{0,128},{128,0},{1,129},{129,1},{2,130},{130,2},{3,131},{131,3},{4... | collective-permute-start | bytes 49160 | tf_op jit(solution)/shard_map/ppermute | solution.py:193
  132.1 24.0 %copy-start = (bf16[4,1024,256]{2,1,0:T(8,128)(2,1)S(1)}, bf16[4,1024,256]{2,1,0:T(8,128)(2,1)}, u32[]{:S(2)}) copy-start(bf16[4,1024,256]{2,1,0:T(8,128)(2,1)} %w_hbm.1) | copy-start | bytes 6291460
  147.3 8.7 %collective-permute-start.22 = (f32[8,64,256]{2,1,0:T(8,128)S(1)}, f32[8,64,256]{2,1,0:T(8,128)S(1)}, u32[]{:S(2)}, u32[]{:S(2)}) collective-permute-start(f32[8,64,256]{2,1,0:T(8,128)S(1)} %all_to_all.25), channel_id=1, source_target_pairs={{0,1},{1,0},{2,3},{3,2},{4,5},{5,4},{6,7},{7,6},{8,9},{9,8},{10,11... | collective-permute-start | bytes 1572872 | tf_op jit(solution)/shard_map/ppermute | solution.py:193
  156.8 1.2 copy-start.2

commit v3 on v2

--- a/solution.py
+++ b/solution.py
@@ -136,27 +136,35 @@
     )(core.reshape(1), pair.reshape(1), leaf_inv, right_side, right_basis, left_basis)
 
 
-def assemble_kernel(
-    core_ref, yl_ref, yh_ref, xl_ref, rows, rows_c, a, a_c, b, b_c, e, e_c, k4_ref, k3_ref, k2_ref, k1_ref
-):
+def offsets(bit, step):
+    return jnp.where(bit == 0, 0, step), jnp.where(bit == 0, step, 0)
+
+
+def pair(core_ref, own, other):
     first = core_ref[0] == 0
-    yl, yh, xl = yl_ref[0], yh_ref[0], xl_ref[0]
-    near, far = jnp.where(yl == 0, 0, 1), jnp.where(yl == 0, 1, 0)
-    up, down = jnp.where(yh == 0, 0, 2), jnp.where(yh == 0, 2, 0)
-    left, right = jnp.where(xl == 0, 0, 4), jnp.where(xl == 0, 4, 0)
-
-    def pair(own, other):
-        return jnp.where(first, own, other), jnp.where(first, other, own)
-
-    def both(own, other):
-        return jnp.concatenate(pair(own, other), axis=0)
-
+    return jnp.where(first, own, other), jnp.where(first, other, own)
+
+
+def fine_kernel(core_ref, yl_ref, rows, rows_c, a, a_c, k4_ref, k3_ref):
+    near, far = offsets(yl_ref[0], 1)
     for z in range(Z):
-        low, high = pair(rows[z, 0:16], rows_c[z, 0:16])
+        low, high = pair(core_ref, rows[z, 0:16], rows_c[z, 0:16])
         k4_ref[32 * z : 32 * z + 16] = low
         k4_ref[32 * z + 16 : 32 * z + 32] = high
         for t, own, other in ((near, rows[z, 16:24], rows_c[z, 16:24]), (far, a[z, 0:8], a_c[z, 0:8])):
-            k3_ref[pl.ds(pl.multiple_of(128 * t + 16 * z, 16), 16)] = both(own, other)
+            both = jnp.concatenate(pair(core_ref, own, other), axis=0)
+            k3_ref[pl.ds(pl.multiple_of(128 * t + 16 * z, 16), 16)] = both
+
+
+def coarse_kernel(core_ref, yl_ref, yh_ref, xl_ref, rows, rows_c, a, a_c, b, b_c, e, e_c, k2_ref, k1_ref):
+    near, far = offsets(yl_ref[0], 1)
+    up, down = offsets(yh_ref[0], 2)
+    left, right = offsets(xl_ref[0], 4)
+
+    def both(own, other):
+        return jnp.concatenate(pair(core_ref, own, other), axis=0)
+
+    for z in range(Z):
         for t, own, other in (
             (up + near, rows[z, 24:28], rows_c[z, 24:28]),
             (up + far, a[z, 8:12], a_c[z, 8:12]),
@@ -179,14 +187,12 @@
             k1_ref[pl.ds(pl.multiple_of(32 * t + 4 * z, 8), 8)] = jnp.concatenate(tile, axis=0)
 
 
-def assemble(at, pieces):
-    scalars = [at[axis].reshape(1) for axis in ("c", "yl", "yh", "xl")]
+def assemble(kernel, scalars, pieces):
     return pl.pallas_call(
-        assemble_kernel,
-        in_specs=[pl.BlockSpec(memory_space=pltpu.SMEM)] * 4 + [pl.BlockSpec()] * len(pieces),
-        out_shape=[jax.ShapeDtypeStruct((256, 512), F32)] * 4,
-        name="assemble",
-    )(*scalars, *pieces)
+        kernel,
+        in_specs=[pl.BlockSpec(memory_space=pltpu.SMEM)] * len(scalars) + [pl.BlockSpec()] * len(pieces),
+        out_shape=[jax.ShapeDtypeStruct((256, 512), F32)] * 2,
+    )(*[scalar.reshape(1) for scalar in scalars], *pieces)
 
 
 def partner(block, axis):
@@ -226,23 +232,31 @@
     keep = jnp.where(upper, fours[:, :, :8], fours[:, :, 8:]).reshape(Z, 1, 16, 128)
     fours = jnp.concatenate([keep, pairs[:, 5:]], axis=1) + got
     fours, rows = lax.optimization_barrier((fours, rows))
+    rows_c = partner(rows, "c")
     a0 = rows[:, 16:32]
     a1 = partner(a0, "yl")
+    a1_c = partner(a1, "c")
     b0 = jnp.concatenate([a0[:, 8:], a1[:, 8:]], axis=1)
     b1 = partner(b0, "yh")
+    b1_c = partner(b1, "c")
     e0 = jnp.concatenate([b0[:, 4:6], b0[:, 12:14], b1[:, 4:6], b1[:, 12:14]], axis=1)
     e1 = partner(e0, "xl")
-    pieces = [piece for own in (rows, a1, b1, e1) for piece in (own, partner(own, "c"))]
-    reduced = assemble(at, pieces)
+    e1_c = partner(e1, "c")
+    pieces = [rows, rows_c, a1, a1_c]
+    full4, full3 = assemble(fine_kernel, [core, at["yl"]], pieces)
+    scalars = [at[axis] for axis in ("c", "yl", "yh", "xl")]
+    full2, full1 = assemble(coarse_kernel, scalars, pieces + [b1, b1_c, e1, e1_c])
 
     def both_cores(own, other, first, count):
         own = own[:, first : first + count].reshape(Z * count, -1)
         other = other[:, first : first + count].reshape(Z * count, -1)
         return ordered(core, own, other, 0)
 
-    def mix(k, own, axis):
-        stack = ordered(at[axis], own, partner(own, axis), 1)
-        return fdot(stack, k, ((1,), (1,)))
+    def mix(k, own, other, axis):
+        return fdot(ordered(at[axis], own, other, 1), k, ((1,), (1,)))
+
+    def of_four(block, axes):
+        return [block] + [lax.ppermute(block, axes, [(i, i ^ k) for i in range(4)]) for k in (1, 2, 3)]
 
     def times(m, g):
         return fdot(m, g, ((1,), (0,)))
@@ -262,7 +276,7 @@
         [to_all.reshape(Z, 96, 128), pairs[:, :3].reshape(Z, 48, 128), fours.reshape(Z, 32, 128)], axis=1
     )
     mixed = exchange(mixed, "z")
-    m4 = mix(reduced[0], direct[0], "yl")
+    m4 = mix(full4, direct[0], partner(direct[0], "yl"), "yl")
     own = mixed[:, :96]
     other = partner(own, "c")
     g34, g24, g14 = [
@@ -274,7 +288,7 @@
     t = in_lanes(sums[0:16]) - times(m4, g34)
     got = partner(t, "yl")
     t = t + got
-    m3 = mix(reduced[1], t, "yh")
+    m3 = mix(full3, t, partner(t, "yh"), "yh")
     own, m3 = lax.optimization_barrier((third, m3))
     t2 = in_rows(in_lanes(sums[48:56])) - times(m4, g24)
     t1 = in_rows(in_lanes(sums[56:64])) - times(m4, g14)
@@ -283,24 +297,18 @@
     half = both_cores(own, other, 32, 16)
     g12 = ordered(at["yl"], half, partner(half, "yl"), 1)
     t = jnp.stack([t2 - in_lanes(times(m3, g23)), t1 - in_lanes(times(m3, g13))])
-    t = t + partner(t, "yl")
-    t = t + partner(t, "yh")
-    m2 = mix(reduced[2], t[0], "xl")
-    t = t[1] - times(m2, g12)
-    t = t + partner(t, "xl")
-    m1 = mix(reduced[3], t, "xh")
+    t = sum(of_four(t, ("yh", "yl")))
+    m2 = mix(full2, t[0], partner(t[0], "xl"), "xl")
+    four = of_four(t[1] - times(m2, g12), ("xh", "xl"))
+    m1 = mix(full1, four[0] + four[1], four[2] + four[3], "xh")
 
     own = spread(jnp.concatenate([m4, m3, m2, m1], axis=0), "z", Z)
     other = partner(own, "c")
-    out = x0
-    for n, level in enumerate((4, 3, 2, 1)):
-        m = both_cores(own, other, 16 * n, 16)
-        high = lax.reduce_precision(m, 8, 7)
-        low = (m - high).astype(BF16)
-        high = high.astype(BF16)
-        left = left_basis[level - 1]
-        out = out - (dot(left, high, ((1,), (1,))) + dot(left, low, ((1,), (1,))))
-    return out
+    m = jnp.stack([both_cores(own, other, 16 * n, 16) for n in (3, 2, 1, 0)])
+    high = lax.reduce_precision(m, 8, 7)
+    low = (m - high).astype(BF16)
+    dims = ((0, 2), (0, 2))
+    return x0 - (dot(left_basis, high.astype(BF16), dims) + dot(left_basis, low, dims))
 
 
 def solution(mesh):

time: 161 us -> 161 us (level)
  waiting for transfers between devices: 60.2 us -> 55.7 us
  Pallas kernels: 12.7 us -> 14.8 us
    ppermute x23 -> x19, starting transfers between devices: 40.5 us -> 31.6 us  [partner(): return lax.ppermute(block, axis, [(0, 1), (1, 0)])]
    ppermute x0 -> x6, starting transfers between devices: none -> 7.89 us  [of_four(): lax.ppermute(block, axes, [(i, i ^ k) for i in range(4)])]
    ppermute x23 -> x19, waiting for transfers between devices: 26.4 us -> 18.9 us  [partner(): return lax.ppermute(block, axis, [(0, 1), (1, 0)])]
    ppermute x0 -> x6, waiting for transfers between devices: none -> 3.32 us  [of_four(): lax.ppermute(block, axes, [(i, i ^ k) for i in range(4)])]
    pallas_call x1 -> x2, Pallas kernels: 3.14 us -> 5.2 us  [assemble(): pl.pallas_call(kernel, in_specs=[pl.BlockSpec(memory_space=pltpu.SMEM)] *...]
    dot_general x8 -> x2, matrix products: 3.63 us -> 2.46 us  [dot(): lax.dot_general(a, b, ((dims[0], dims[1]), ((), ())), preferred_element_t...]
  transfers between devices with their start and end apart: 27 -> 29, of which waited for: 16 -> 13; matrix products, arithmetic and copies ran while one was open for 4% -> 5% of each run, Pallas kernels for 3% -> 4%
where the time goes in v3:
time: 161 us; the launch traced here: 160 us
  starting transfers between devices  59.3 us (37%)
  waiting for transfers between devices  55.7 us (35%)
  blocking collectives  15.4 us (10%)
  Pallas kernels  14.8 us (9%)
  matrix products  6.79 us (4%)
  other arithmetic  4.37 us (3%)
  local copies, waits for them, and re-layouts  3.66 us (2%)
    all_to_all x4, waiting for transfers between devices, exchange(): return lax.all_to_all(block, axes, 0, 0, tiled=True)  33.4 us
    ppermute x19, starting transfers between devices, partner(): return lax.ppermute(block, axis, [(0, 1), (1, 0)])  31.6 us
    all_to_all x4, starting transfers between devices, exchange(): return lax.all_to_all(block, axes, 0, 0, tiled=True)  19.8 us
    ppermute x19, waiting for transfers between devices, partner(): return lax.ppermute(block, axis, [(0, 1), (1, 0)])  18.9 us
    all_to_all x1, blocking collectives, exchange(): return lax.all_to_all(block, axes, 0, 0, tiled=True)  15.4 us
    pallas_call x1, Pallas kernels, leaf(): pl.pallas_call(leaf_kernel, in_specs=[pl.BlockSpec(memory_space=pltpu.SME...  7.98 us
    ppermute x6, starting transfers between devices, of_four(): lax.ppermute(block, axes, [(i, i ^ k) for i in range(4)])  7.89 us
    pallas_call x2, Pallas kernels, assemble(): pl.pallas_call(kernel, in_specs=[pl.BlockSpec(memory_space=pltpu.SMEM)] *...  5.2 us
  transfers between devices with their start and end apart: 29, of which 13 were waited for; matrix products, arithmetic and copies ran while one was open for 5% of the time, Pallas kernels for 4%

profile of v3, /device:TPU:1, one launch (start us, length us, event | category | flops | bytes accessed | tf_op | source)
XLA Modules:
  0.0 160.5 jit_solution(714061479357836518)
XLA Ops:
  0.0 8.0 %leaf.1 = (f32[1024,256]{1,0:T(8,128)}, f32[8,4,16,256]{3,2,1,0:T(8,128)}, f32[8,4,16,256]{3,2,1,0:T(8,128)}, f32[2,8,6,16,128]{4,3,2,1,0:T(8,128)}, f32[2,8,6,16,128]{4,3,2,1,0:T(8,128)}) custom-call(s32[1]{0:T(128)} %bitcast.core_ref, s32[1]{0:T(128)} %bitcast.1.pair_ref.yl_ref, bf16[1024,1024]{1,0:T(8,128)(2,1)} %inv_hbm.1, bf16[1024,256]{1,0:T(8,128)(2,1)} %rhs_hbm.1, ...), custom_call_target="tpu_custom_call" | custom-call | tf_op jit(solution)/shard_map/leaf/pallas_call | solution.py:116
  8.0 3.3 %collective-permute-start.2 = (f32[2,8,6,16,128]{4,3,2,1,0:T(8,128)}, f32[2,8,6,16,128]{4,3,2,1,0:T(8,128)S(1)}, u32[]{:S(2)}, u32[]{:S(2)}) collective-permute-start(f32[2,8,6,16,128]{4,3,2,1,0:T(8,128)} %get-tuple-element.22), channel_id=1, source_target_pairs={{0,1},{1,0},{2,3},{3,2},{4,5},{5,4},{6,7},{7,6},{8,9},{9,8},{10,11... | collective-permute-start | bytes 2359304 | tf_op jit(solution)/shard_map/ppermute | solution.py:199
  11.3 1.6 %pack.1 = f32[8,32,512]{2,1,0:T(8,128)} custom-call(f32[16,512]{1,0:T(8,128)} %a_ref.1, f32[8,512]{1,0:T(8,128)} %b_ref.1, f32[4,512]{1,0:T(4,128)} %c_ref.1, f32[2,512]{1,0:T(2,128)} %d_ref.1), custom_call_target="tpu_custom_call" | custom-call | tf_op jit(solution)/shard_map/pack/pallas_call | solution.py:39
  12.9 6.5 %all-to-all-start.1 = ((f32[8,32,512]{2,1,0:T(8,128)}), f32[8,32,512]{2,1,0:T(8,128)S(1)}, u32[]{:S(2)}, u32[]{:S(2)}) async-start(f32[8,32,512]{2,1,0:T(8,128)} %pack.1), calls=%async_computation.1 | async-start | bytes 1048576 | tf_op jit(solution)/shard_map/all_to_all | solution.py:209
  19.4 0.4 collective-permute-start
  19.8 1.8 %fusion.9 = f32[8,6,16,128]{3,2,1,0:T(8,128)} fusion(f32[2,8,6,16,128]{4,3,2,1,0:T(8,128)S(1)} %collective-permute-done.2, f32[2,8,6,16,128]{4,3,2,1,0:T(8,128)} %get-tuple-element.21), kind=kLoop, calls=%fused_computation.18 | loop fusion | flops 98304 | bytes 1179648 | tf_op jit(solution)/shard_map/add | solution.py:225
  21.7 1.3 collective-permute-start.3
  23.0 0.9 add.45
  23.9 13.5 %all-to-all-done.1.rows = f32[8,32,512]{2,1,0:T(8,128)S(1)} async-done(((f32[8,32,512]{2,1,0:T(8,128)}), f32[8,32,512]{2,1,0:T(8,128)S(1)}, u32[]{:S(2)}, u32[]{:S(2)}) %all-to-all-start.1) | async-done | bytes 524320 | tf_op jit(solution)/shard_map/all_to_all | solution.py:209
  37.4 3.5 %all-to-all-start = ((f32[8,4,16,256]{3,2,1,0:T(8,128)}), f32[8,4,16,256]{3,2,1,0:T(8,128)S(1)}, u32[]{:S(2)}, u32[]{:S(2)}) async-start(f32[8,4,16,256]{3,2,1,0:T(8,128)} %add.45), calls=%async_computation | async-start | bytes 1048576 | tf_op jit(solution)/shard_map/all_to_all | solution.py:209
  41.1 3.0 %collective-permute-start.4 = (f32[8,2,16,128]{3,2,1,0:T(8,128)S(1)}, f32[8,2,16,128]{3,2,1,0:T(8,128)S(1)}, u32[]{:S(2)}, u32[]{:S(2)}) collective-permute-start(f32[8,2,16,128]{3,2,1,0:T(8,128)S(1)} %pad_maximum_fusion.3), channel_id=1, source_target_pairs={{0,32},{32,0},{1,33},{33,1},{2,34},{34,2},{3,35},{35,3},{4,36},{36... | collective-permute-start | bytes 393224 | tf_op jit(solution)/shard_map/ppermute | solution.py:199
  44.1 3.2 %collective-permute-done.4 = f32[8,2,16,128]{3,2,1,0:T(8,128)S(1)} collective-permute-done((f32[8,2,16,128]{3,2,1,0:T(8,128)S(1)}, f32[8,2,16,128]{3,2,1,0:T(8,128)S(1)}, u32[]{:S(2)}, u32[]{:S(2)}) %collective-permute-start.4) | collective-permute-done | bytes 131104 | tf_op jit(solution)/shard_map/ppermute | solution.py:199
  47.3 11.5 %all-to-all-done = f32[8,4,16,256]{3,2,1,0:T(8,128)S(1)} async-done(((f32[8,4,16,256]{3,2,1,0:T(8,128)}), f32[8,4,16,256]{3,2,1,0:T(8,128)S(1)}, u32[]{:S(2)}, u32[]{:S(2)}) %all-to-all-start) | async-done | bytes 524320 | tf_op jit(solution)/shard_map/all_to_all | solution.py:209
  58.9 0.9 pad_maximum_fusion.1
  59.8 3.5 %all-to-all-start.2 = ((f32[8,176,128]{2,1,0:T(8,128)}), f32[8,176,128]{2,1,0:T(8,128)S(1)}, u32[]{:S(2)}, u32[]{:S(2)}) async-start(f32[8,176,128]{2,1,0:T(8,128)} %pad_maximum_fusion.1), calls=%async_computation.2 | async-start | bytes 1441792 | tf_op jit(solution)/shard_map/all_to_all | solution.py:209
  63.4 1.4 collective-permute-start.6
  64.8 6.1 %collective-permute-done.6.a = f32[8,16,512]{2,1,0:T(8,128)S(1)} collective-permute-done((f32[8,16,512]{2,1,0:T(8,128)S(1)}, f32[8,16,512]{2,1,0:T(8,128)S(1)}, u32[]{:S(2)}, u32[]{:S(2)}) %collective-permute-start.6) | collective-permute-done | bytes 262176 | tf_op jit(solution)/shard_map/ppermute | solution.py:199
  70.9 3.0 %collective-permute-start.16 = (f32[8,16,512]{2,1,0:T(8,128)S(1)}, f32[8,16,512]{2,1,0:T(8,128)S(1)}, u32[]{:S(2)}, u32[]{:S(2)}) collective-permute-start(f32[8,16,512]{2,1,0:T(8,128)S(1)} %pad_maximum_fusion.2), channel_id=1, source_target_pairs={{0,32},{32,0},{1,33},{33,1},{2,34},{34,2},{3,35},{35,3},{4,36},{36... | collective-permute-start | bytes 786440 | tf_op jit(solution)/shard_map/ppermute | solution.py:199
  73.9 0.4 collective-permute-start.1
  74.3 1.9 %collective-permute-start.5 = (f32[8,32,512]{2,1,0:T(8,128)S(1)}, f32[8,32,512]{2,1,0:T(8,128)S(1)}, u32[]{:S(2)}, u32[]{:S(2)}) collective-permute-start(f32[8,32,512]{2,1,0:T(8,128)S(1)} %all-to-all-done.1.rows), channel_id=1, source_target_pairs={{0,1},{1,0},{2,3},{3,2},{4,5},{5,4},{6,7},{7,6},{8,9},{9,8},{10,11... | collective-permute-start | bytes 1572872 | tf_op jit(solution)/shard_map/ppermute | solution.py:199
  76.2 3.5 %collective-permute-done.1 = f32[16,256]{1,0:T(8,128)S(1)} collective-permute-done((f32[16,256]{1,0:T(8,128)S(1)}, f32[16,256]{1,0:T(8,128)S(1)}, u32[]{:S(2)}, u32[]{:S(2)}) %collective-permute-start.1) | collective-permute-done | bytes 16416 | tf_op jit(solution)/shard_map/ppermute | solution.py:199
  79.7 2.2 %collective-permute-start.7 = (f32[8,16,512]{2,1,0:T(8,128)S(1)}, f32[8,16,512]{2,1,0:T(8,128)S(1)}, u32[]{:S(2)}, u32[]{:S(2)}) collective-permute-start(f32[8,16,512]{2,1,0:T(8,128)S(1)} %collective-permute-done.6.a), channel_id=1, source_target_pairs={{0,1},{1,0},{2,3},{3,2},{4,5},{5,4},{6,7},{7,6},{8,9},{9,8},{10,11... | collective-permute-start | bytes 786440 | tf_op jit(solution)/shard_map/ppermute | solution.py:199
  82.0 1.3 collective-permute-start.18
  83.3 0.7 copy-done.5
  84.0 0.8 copy-done.2
  84.9 2.4 %shard_map.82 = (f32[256,512]{1,0:T(8,128)}, f32[256,512]{1,0:T(8,128)}) custom-call(s32[1]{0:T(128)} %bitcast.core_ref, s32[1]{0:T(128)} %bitcast.1.pair_ref.yl_ref, f32[8,32,512]{2,1,0:T(8,128)} %copy-done.1, f32[8,32,512]{2,1,0:T(8,128)} %copy-done.2, f32[8,16,512]{2,1,0:T(8,128)} %copy-done.3, f32[8,16,512]{2,1,0:T(8,128)} %copy-done.5), custom_call_target="tpu_custom_call" | custom-call | tf_op jit(solution)/shard_map/pallas_call | solution.py:191
  87.3 0.4 collective-permute-start.8
  87.7 1.4 fusion.46
  89.2 0.1 convolution_subtract_fusion.2
  89.4 1.1 collective-permute-start.9
  90.5 0.5 collective-permute-start.17
  91.2 0.9 collective-permute-done.9
  92.1 2.3 %collective-permute-start.10 = (f32[16,256]{1,0:T(8,128)S(1)}, f32[16,256]{1,0:T(8,128)S(1)}, u32[]{:S(2)}, u32[]{:S(2)}) collective-permute-start(f32[16,256]{1,0:T(8,128)S(1)} %add.52), channel_id=1, source_target_pairs={{0,32},{32,0},{1,33},{33,1},{2,34},{34,2},{3,35},{35,3},{4,36},{36... | collective-permute-start | bytes 49160 | tf_op jit(solution)/shard_map/ppermute | solution.py:199
  94.4 0.7 broadcast_in_dim.10
  95.1 6.3 %all-to-all-start.3 = ((f32[8,48,128]{2,1,0:T(8,128)}), f32[8,48,128]{2,1,0:T(8,128)S(1)}, u32[]{:S(2)}, u32[]{:S(2)}) async-start(f32[8,48,128]{2,1,0:T(8,128)} %broadcast_in_dim.10), calls=%async_computation.3 | async-start | bytes 393216 | tf_op jit(solution)/shard_map/all_to_all | solution.py:209
  101.4 0.3 fusion.50
  101.7 8.4 %all-to-all-done.3 = f32[8,48,128]{2,1,0:T(8,128)S(1)} async-done(((f32[8,48,128]{2,1,0:T(8,128)}), f32[8,48,128]{2,1,0:T(8,128)S(1)}, u32[]{:S(2)}, u32[]{:S(2)}) %all-to-all-start.3) | async-done | bytes 196640 | tf_op jit(solution)/shard_map/all_to_all | solution.py:209
  110.1 3.0 %collective-permute-start.11 = (f32[8,48,128]{2,1,0:T(8,128)S(1)}, f32[8,48,128]{2,1,0:T(8,128)S(1)}, u32[]{:S(2)}, u32[]{:S(2)}) collective-permute-start(f32[8,48,128]{2,1,0:T(8,128)S(1)} %all-to-all-done.3), channel_id=1, source_target_pairs={{0,1},{1,0},{2,3},{3,2},{4,5},{5,4},{6,7},{7,6},{8,9},{9,8},{10,11... | collective-permute-start | bytes 589832 | tf_op jit(solution)/shard_map/ppermute | solution.py:199
  113.1 1.1 collective-permute-done.11
  114.2 0.2 broadcast_select_fusion.13
  114.4 0.2 broadcast_select_fusion.11
  114.5 0.2 fusion.6
  114.7 0.2 fusion.4
  114.9 0.5 collective-permute-start.12
  115.4 1.9 %collective-permute-start.13 = (f32[2,16,256]{2,1,0:T(8,128)S(1)}, f32[2,16,256]{2,1,0:T(8,128)S(1)}, u32[]{:S(2)}, u32[]{:S(2)}) collective-permute-start(f32[2,16,256]{2,1,0:T(8,128)S(1)} %pad_maximum_fusion.9), channel_id=1, source_target_pairs={{0,32},{16,48},{32,0},{48,16},{1,33},{17,49},{33,1},{49,17},{2,34}... | collective-permute-start | bytes 98312 | tf_op jit(solution)/shard_map/ppermute | solution.py:259
  117.3 1.5 collective-permute-start.14
  118.9 0.7 copy-done.11
  119.6 2.8 %shard_map.83 = (f32[256,512]{1,0:T(8,128)}, f32[256,512]{1,0:T(8,128)}) custom-call(s32[1]{0:T(128)} %bitcast.core_ref, s32[1]{0:T(128)} %bitcast.1.pair_ref.yl_ref, s32[1]{0:T(128)} %bitcast.29.yh_ref, s32[1]{0:T(128)} %bitcast.30.xl_ref, f32[8,32,512]{2,1,0:T(8,128)} %copy-done.1, f32[8,32,512]{2,1,0:T(8,128)} %copy-done.2, f32[8,16,512]{2,1,0:T(8,128)} %copy-done.3, ...), custom_call_target="tpu_custom_call" | custom-call | tf_op jit(solution)/shard_map/pallas_call | solution.py:191
  122.5 0.3 collective-permute-start.15
  123.0 2.2 %collective-permute-done.15 = f32[16,256]{1,0:T(8,128)S(1)} collective-permute-done((f32[16,256]{1,0:T(8,128)S(1)}, f32[16,256]{1,0:T(8,128)S(1)}, u32[]{:S(2)}, u32[]{:S(2)}) %collective-permute-start.15) | collective-permute-done | bytes 16416 | tf_op jit(solution)/shard_map/ppermute | solution.py:199
  125.2 1.3 fusion.54
  126.6 0.5 collective-permute-done.20
  127.2 1.0 collective-permute-start.21
  128.2 2.5 %collective-permute-start.22 = (f32[16,256]{1,0:T(8,128)S(1)}, f32[16,256]{1,0:T(8,128)S(1)}, u32[]{:S(2)}, u32[]{:S(2)}) collective-permute-start(f32[16,256]{1,0:T(8,128)S(1)} %fusion.62), channel_id=1, source_target_pairs={{0,128},{64,192},{128,0},{192,64},{1,129},{65,193},{129,1},{193,65... | collective-permute-start | bytes 49160 | tf_op jit(solution)/shard_map/ppermute | solution.py:259
  130.7 0.5 collective-permute-start.23
  131.2 1.1 collective-permute-done.22
  132.3 2.2 %collective-permute-done.23 = f32[16,256]{1,0:T(8,128)S(1)} collective-permute-done((f32[16,256]{1,0:T(8,128)S(1)}, f32[16,256]{1,0:T(8,128)S(1)}, u32[]{:S(2)}, u32[]{:S(2)}) %collective-permute-start.23) | collective-permute-done | bytes 16416 | tf_op jit(solution)/shard_map/ppermute | solution.py:259
  134.5 0.3 fusion.58
  134.9 15.4 %all_to_all.25 = f32[8,64,256]{2,1,0:T(8,128)S(1)} all-to-all(f32[8,64,256]{2,1,0:T(8,128)S(1)} %broadcast_in_dim.11), channel_id=1, replica_groups=mesh['xh'=2,'xl'=2,'yh'=2,'yl'=2,'z'=8,'c'=2] {'z'}, dimensions={0} | all-to-all | bytes 1048576 | tf_op jit(solution)/shard_map/all_to_all | solution.py:209
  150.3 5.5 %collective-permute-start.24 = (f32[8,64,256]{2,1,0:T(8,128)S(1)}, f32[8,64,256]{2,1,0:T(8,128)S(1)}, u32[]{:S(2)}, u32[]{:S(2)}) collective-permute-start(f32[8,64,256]{2,1,0:T(8,128)S(1)} %all_to_all.25), channel_id=1, source_target_pairs={{0,1},{1,0},{2,3},{3,2},{4,5},{5,4},{6,7},{7,6},{8,9},{9,8},{10,11... | collective-permute-start | bytes 1572872 | tf_op jit(solution)/shard_map/ppermute | solution.py:199
  155.7 1.5 collective-permute-done.24
  157.5 0.7 convolution_bitcast_fusion
  158.3 0.5 copy-done.4
  158.8 1.7 %fusion.2 = f32[1024,256]{1,0:T(8,128)} fusion(f32[1024,256]{1,0:T(8,128)S(1)} %copy-done.4, f32[256,1024]{0,1:T(8,128)S(1)} %convolution_bitcast_fusion, bf16[4,1024,256]{2,1,0:T(8,128)(2,1)S(1)} %copy-done, f32[1,256,256]{2,1,0:T(8,128)S(1)} %maximum_bitcast_fusion.3, f32[1,256,256]{2,1,0:T(8,128)S(1)} %maximum_bitcast_fusion.2, ...), kind=kOutput, calls=%fused_computation.6 | convolution fusion | flops 538705920 | bytes 6291456 | tf_op jit(solution)/shard_map/dot_general | solution.py:20
  (89 shorter events, 1.4 us)
Async XLA Ops:
  8.0 15.0 %copy-start.7 = (f32[8,4,16,256]{3,2,1,0:T(8,128)S(1)}, f32[8,4,16,256]{3,2,1,0:T(8,128)}, u32[]{:S(2)}) copy-start(f32[8,4,16,256]{3,2,1,0:T(8,128)} %get-tuple-element.19) | copy-start | bytes 1572868
  8.0 11.8 %collective-permute-start.2 = (f32[2,8,6,16,128]{4,3,2,1,0:T(8,128)}, f32[2,8,6,16,128]{4,3,2,1,0:T(8,128)S(1)}, u32[]{:S(2)}, u32[]{:S(2)}) collective-permute-start(f32[2,8,6,16,128]{4,3,2,1,0:T(8,128)} %get-tuple-element.22), channel_id=1, source_target_pairs={{0,1},{1,0},{2,3},{3,2},{4,5},{5,4},{6,7},{7,6},{8,9},{9,8},{10,11... | collective-permute-start | bytes 2359304 | tf_op jit(solution)/shard_map/ppermute | solution.py:199
  12.9 24.5 %all-to-all-start.1 = ((f32[8,32,512]{2,1,0:T(8,128)}), f32[8,32,512]{2,1,0:T(8,128)S(1)}, u32[]{:S(2)}, u32[]{:S(2)}) async-start(f32[8,32,512]{2,1,0:T(8,128)} %pack.1), calls=%async_computation.1 | async-start | bytes 1048576 | tf_op jit(solution)/shard_map/all_to_all | solution.py:209
  19.4 21.5 %copy-start.6 = (f32[2,8,6,16,128]{4,3,2,1,0:T(8,128)S(1)}, f32[2,8,6,16,128]{4,3,2,1,0:T(8,128)}, u32[]{:S(2)}) copy-start(f32[2,8,6,16,128]{4,3,2,1,0:T(8,128)} %get-tuple-element.21) | copy-start | bytes 2359300
  19.4 3.5 %collective-permute-start = (f32[8,4,16,256]{3,2,1,0:T(8,128)}, f32[8,4,16,256]{3,2,1,0:T(8,128)S(1)}, u32[]{:S(2)}, u32[]{:S(2)}) collective-permute-start(f32[8,4,16,256]{3,2,1,0:T(8,128)} %get-tuple-element.20), channel_id=1, source_target_pairs={{0,1},{1,0},{2,3},{3,2},{4,5},{5,4},{6,7},{7,6},{8,9},{9,8},{10,11... | collective-permute-start | bytes 1572872 | tf_op jit(solution)/shard_map/ppermute | solution.py:199
  21.7 19.2 %collective-permute-start.3 = (f32[8,6,16,128]{3,2,1,0:T(8,128)}, f32[8,6,16,128]{3,2,1,0:T(8,128)S(1)}, u32[]{:S(2)}, u32[]{:S(2)}) collective-permute-start(f32[8,6,16,128]{3,2,1,0:T(8,128)} %fusion.9), channel_id=1, source_target_pairs={{0,16},{16,0},{1,17},{17,1},{2,18},{18,2},{3,19},{19,3},{4,20},{20... | collective-permute-start | bytes 1179656 | tf_op jit(solution)/shard_map/ppermute | solution.py:199
  37.4 38.8 %copy-start.1 = (f32[8,32,512]{2,1,0:T(8,128)}, f32[8,32,512]{2,1,0:T(8,128)S(1)}, u32[]{:S(2)}) copy-start(f32[8,32,512]{2,1,0:T(8,128)S(1)} %all-to-all-done.1.rows) | copy-start | bytes 1572868
  37.4 21.4 %all-to-all-start = ((f32[8,4,16,256]{3,2,1,0:T(8,128)}), f32[8,4,16,256]{3,2,1,0:T(8,128)S(1)}, u32[]{:S(2)}, u32[]{:S(2)}) async-start(f32[8,4,16,256]{3,2,1,0:T(8,128)} %add.45), calls=%async_computation | async-start | bytes 1048576 | tf_op jit(solution)/shard_map/all_to_all | solution.py:209
  41.1 6.2 %collective-permute-start.4 = (f32[8,2,16,128]{3,2,1,0:T(8,128)S(1)}, f32[8,2,16,128]{3,2,1,0:T(8,128)S(1)}, u32[]{:S(2)}, u32[]{:S(2)}) collective-permute-start(f32[8,2,16,128]{3,2,1,0:T(8,128)S(1)} %pad_maximum_fusion.3), channel_id=1, source_target_pairs={{0,32},{32,0},{1,33},{33,1},{2,34},{34,2},{3,35},{35,3},{4,36},{36... | collective-permute-start | bytes 393224 | tf_op jit(solution)/shard_map/ppermute | solution.py:199
  59.8 27.5 %all-to-all-start.2 = ((f32[8,176,128]{2,1,0:T(8,128)}), f32[8,176,128]{2,1,0:T(8,128)S(1)}, u32[]{:S(2)}, u32[]{:S(2)}) async-start(f32[8,176,128]{2,1,0:T(8,128)} %pad_maximum_fusion.1), calls=%async_computation.2 | async-start | bytes 1441792 | tf_op jit(solution)/shard_map/all_to_all | solution.py:209
  63.4 7.5 %collective-permute-start.6 = (f32[8,16,512]{2,1,0:T(8,128)S(1)}, f32[8,16,512]{2,1,0:T(8,128)S(1)}, u32[]{:S(2)}, u32[]{:S(2)}) collective-permute-start(f32[8,16,512]{2,1,0:T(8,128)S(1)} %slice.184), channel_id=1, source_target_pairs={{0,16},{16,0},{1,17},{17,1},{2,18},{18,2},{3,19},{19,3},{4,20},{20... | collective-permute-start | bytes 786440 | tf_op jit(solution)/shard_map/ppermute | solution.py:199
  70.8 12.5 %copy-start.3 = (f32[8,16,512]{2,1,0:T(8,128)}, f32[8,16,512]{2,1,0:T(8,128)S(1)}, u32[]{:S(2)}) copy-start(f32[8,16,512]{2,1,0:T(8,128)S(1)} %collective-permute-done.6.a) | copy-start | bytes 786436
  70.9 11.0 %collective-permute-start.16 = (f32[8,16,512]{2,1,0:T(8,128)S(1)}, f32[8,16,512]{2,1,0:T(8,128)S(1)}, u32[]{:S(2)}, u32[]{:S(2)}) collective-permute-start(f32[8,16,512]{2,1,0:T(8,128)S(1)} %pad_maximum_fusion.2), channel_id=1, source_target_pairs={{0,32},{32,0},{1,33},{33,1},{2,34},{34,2},{3,35},{35,3},{4,36},{36... | collective-permute-start | bytes 786440 | tf_op jit(solution)/shard_map/ppermute | solution.py:199
  73.9 5.8 %collective-permute-start.1 = (f32[16,256]{1,0:T(8,128)S(1)}, f32[16,256]{1,0:T(8,128)S(1)}, u32[]{:S(2)}, u32[]{:S(2)}) collective-permute-start(f32[16,256]{1,0:T(8,128)S(1)} %slice_bitcast_fusion.2), channel_id=1, source_target_pairs={{0,16},{16,0},{1,17},{17,1},{2,18},{18,2},{3,19},{19,3},{4,20},{20... | collective-permute-start | bytes 49160 | tf_op jit(solution)/shard_map/ppermute | solution.py:199
  74.3 9.1 %collective-permute-start.5 = (f32[8,32,512]{2,1,0:T(8,128)S(1)}, f32[8,32,512]{2,1,0:T(8,128)S(1)}, u32[]{:S(2)}, u32[]{:S(2)}) collective-permute-start(f32[8,32,512]{2,1,0:T(8,128)S(1)} %all-to-all-done.1.rows), channel_id=1, source_target_pairs={{0,1},{1,0},{2,3},{3,2},{4,5},{5,4},{6,7},{7,6},{8,9},{9,8},{10,11... | collective-permute-start | bytes 1572872 | tf_op jit(solution)/shard_map/ppermute | solution.py:199
  79.7 3.7 %collective-permute-start.7 = (f32[8,16,512]{2,1,0:T(8,128)S(1)}, f32[8,16,512]{2,1,0:T(8,128)S(1)}, u32[]{:S(2)}, u32[]{:S(2)}) collective-permute-start(f32[8,16,512]{2,1,0:T(8,128)S(1)} %collective-permute-done.6.a), channel_id=1, source_target_pairs={{0,1},{1,0},{2,3},{3,2},{4,5},{5,4},{6,7},{7,6},{8,9},{9,8},{10,11... | collective-permute-start | bytes 786440 | tf_op jit(solution)/shard_map/ppermute | solution.py:199
  81.9 8.6 %copy-start.10 = (f32[8,16,512]{2,1,0:T(8,128)}, f32[8,16,512]{2,1,0:T(8,128)S(1)}, u32[]{:S(2)}) copy-start(f32[8,16,512]{2,1,0:T(8,128)S(1)} %collective-permute-done.16.b) | copy-start | bytes 786436
  82.0 9.0 %collective-permute-start.18 = (f32[8,8,512]{2,1,0:T(8,128)S(1)}, f32[8,8,512]{2,1,0:T(8,128)S(1)}, u32[]{:S(2)}, u32[]{:S(2)}) collective-permute-start(f32[8,8,512]{2,1,0:T(8,128)S(1)} %pad_maximum_fusion.5), channel_id=1, source_target_pairs={{0,64},{64,0},{1,65},{65,1},{2,66},{66,2},{3,67},{67,3},{4,68},{68... | collective-permute-start | bytes 393224 | tf_op jit(solution)/shard_map/ppermute | solution.py:199
  83.3 0.7 copy-start.5
  84.0 0.8 copy-start.2
  87.3 1.9 %collective-permute-start.8 = (f32[8,96,128]{2,1,0:T(8,128)S(1)}, f32[8,96,128]{2,1,0:T(8,128)S(1)}, u32[]{:S(2)}, u32[]{:S(2)}) collective-permute-start(f32[8,96,128]{2,1,0:T(8,128)S(1)} %slice.243), channel_id=1, source_target_pairs={{0,1},{1,0},{2,3},{3,2},{4,5},{5,4},{6,7},{7,6},{8,9},{9,8},{10,11... | collective-permute-start | bytes 1179656 | tf_op jit(solution)/shard_map/ppermute | solution.py:199
  87.7 13.8 %copy-start.9 = (f32[256,512]{1,0:T(8,128)S(1)}, f32[256,512]{1,0:T(8,128)}, u32[]{:S(2)}) copy-start(f32[256,512]{1,0:T(8,128)} %get-tuple-element.26) | copy-start | bytes 1572868
  89.4 2.7 %collective-permute-start.9 = (f32[16,256]{1,0:T(8,128)S(1)}, f32[16,256]{1,0:T(8,128)S(1)}, u32[]{:S(2)}, u32[]{:S(2)}) collective-permute-start(f32[16,256]{1,0:T(8,128)S(1)} %convolution_subtract_fusion.2), channel_id=1, source_target_pairs={{0,16},{16,0},{1,17},{17,1},{2,18},{18,2},{3,19},{19,3},{4,20},{20... | collective-permute-start | bytes 49160 | tf_op jit(solution)/shard_map/ppermute | solution.py:199
  90.5 28.3 %collective-permute-start.17 = (f32[8,16,512]{2,1,0:T(8,128)S(1)}, f32[8,16,512]{2,1,0:T(8,128)S(1)}, u32[]{:S(2)}, u32[]{:S(2)}) collective-permute-start(f32[8,16,512]{2,1,0:T(8,128)S(1)} %collective-permute-done.16.b), channel_id=1, source_target_pairs={{0,1},{1,0},{2,3},{3,2},{4,5},{5,4},{6,7},{7,6},{8,9},{9,8},{10,11... | collective-permute-start | bytes 786440 | tf_op jit(solution)/shard_map/ppermute | solution.py:199
  91.1 27.8 %copy-start.12 = (f32[8,8,512]{2,1,0:T(8,128)}, f32[8,8,512]{2,1,0:T(8,128)S(1)}, u32[]{:S(2)}) copy-start(f32[8,8,512]{2,1,0:T(8,128)S(1)} %collective-permute-done.18.e) | copy-start | bytes 393220
  91.1 27.8 %collective-permute-start.19 = (f32[8,8,512]{2,1,0:T(8,128)S(1)}, f32[8,8,512]{2,1,0:T(8,128)S(1)}, u32[]{:S(2)}, u32[]{:S(2)}) collective-permute-start(f32[8,8,512]{2,1,0:T(8,128)S(1)} %collective-permute-done.18.e), channel_id=1, source_target_pairs={{0,1},{1,0},{2,3},{3,2},{4,5},{5,4},{6,7},{7,6},{8,9},{9,8},{10,11... | collective-permute-start | bytes 393224 | tf_op jit(solution)/shard_map/ppermute | solution.py:199
  92.1 9.3 %collective-permute-start.10 = (f32[16,256]{1,0:T(8,128)S(1)}, f32[16,256]{1,0:T(8,128)S(1)}, u32[]{:S(2)}, u32[]{:S(2)}) collective-permute-start(f32[16,256]{1,0:T(8,128)S(1)} %add.52), channel_id=1, source_target_pairs={{0,32},{32,0},{1,33},{33,1},{2,34},{34,2},{3,35},{35,3},{4,36},{36... | collective-permute-start | bytes 49160 | tf_op jit(solution)/shard_map/ppermute | solution.py:199
  95.1 15.0 %all-to-all-start.3 = ((f32[8,48,128]{2,1,0:T(8,128)}), f32[8,48,128]{2,1,0:T(8,128)S(1)}, u32[]{:S(2)}, u32[]{:S(2)}) async-start(f32[8,48,128]{2,1,0:T(8,128)} %broadcast_in_dim.10), calls=%async_computation.3 | async-start | bytes 393216 | tf_op jit(solution)/shard_map/all_to_all | solution.py:209
  110.1 4.1 %collective-permute-start.11 = (f32[8,48,128]{2,1,0:T(8,128)S(1)}, f32[8,48,128]{2,1,0:T(8,128)S(1)}, u32[]{:S(2)}, u32[]{:S(2)}) collective-permute-start(f32[8,48,128]{2,1,0:T(8,128)S(1)} %all-to-all-done.3), channel_id=1, source_target_pairs={{0,1},{1,0},{2,3},{3,2},{4,5},{5,4},{6,7},{7,6},{8,9},{9,8},{10,11... | collective-permute-start | bytes 589832 | tf_op jit(solution)/shard_map/ppermute | solution.py:199
  114.9 7.5 %collective-permute-start.12 = (f32[2,16,256]{2,1,0:T(8,128)S(1)}, f32[2,16,256]{2,1,0:T(8,128)S(1)}, u32[]{:S(2)}, u32[]{:S(2)}) collective-permute-start(f32[2,16,256]{2,1,0:T(8,128)S(1)} %pad_maximum_fusion.9), channel_id=1, source_target_pairs={{0,16},{16,0},{32,48},{48,32},{1,17},{17,1},{33,49},{49,33},{2,18}... | collective-permute-start | bytes 98312 | tf_op jit(solution)/shard_map/ppermute | solution.py:259
  115.4 7.0 %collective-permute-start.13 = (f32[2,16,256]{2,1,0:T(8,128)S(1)}, f32[2,16,256]{2,1,0:T(8,128)S(1)}, u32[]{:S(2)}, u32[]{:S(2)}) collective-permute-start(f32[2,16,256]{2,1,0:T(8,128)S(1)} %pad_maximum_fusion.9), channel_id=1, source_target_pairs={{0,32},{16,48},{32,0},{48,16},{1,33},{17,49},{33,1},{49,17},{2,34}... | collective-permute-start | bytes 98312 | tf_op jit(solution)/shard_map/ppermute | solution.py:259
  117.3 5.1 %collective-permute-start.14 = (f32[2,16,256]{2,1,0:T(8,128)S(1)}, f32[2,16,256]{2,1,0:T(8,128)S(1)}, u32[]{:S(2)}, u32[]{:S(2)}) collective-permute-start(f32[2,16,256]{2,1,0:T(8,128)S(1)} %pad_maximum_fusion.9), channel_id=1, source_target_pairs={{0,48},{16,32},{32,16},{48,0},{1,49},{17,33},{33,17},{49,1},{2,50}... | collective-permute-start | bytes 98312 | tf_op jit(solution)/shard_map/ppermute | solution.py:259
  118.9 0.7 copy-start.11
  118.9 0.7 copy-start.13
  122.4 12.1 %copy-start.8 = (f32[256,512]{1,0:T(8,128)S(1)}, f32[256,512]{1,0:T(8,128)}, u32[]{:S(2)}) copy-start(f32[256,512]{1,0:T(8,128)} %get-tuple-element.30) | copy-start | bytes 1572868
  122.5 2.7 %collective-permute-start.15 = (f32[16,256]{1,0:T(8,128)S(1)}, f32[16,256]{1,0:T(8,128)S(1)}, u32[]{:S(2)}, u32[]{:S(2)}) collective-permute-start(f32[16,256]{1,0:T(8,128)S(1)} %slice_bitcast_fusion.1), channel_id=1, source_target_pairs={{0,64},{64,0},{1,65},{65,1},{2,66},{66,2},{3,67},{67,3},{4,68},{68... | collective-permute-start | bytes 49160 | tf_op jit(solution)/shard_map/ppermute | solution.py:199
  122.9 4.2 %collective-permute-start.20 = (f32[256,128]{1,0:T(8,128)S(1)}, f32[256,128]{1,0:T(8,128)S(1)}, u32[]{:S(2)}, u32[]{:S(2)}) collective-permute-start(f32[256,128]{1,0:T(8,128)S(1)} %pad_maximum_fusion.6), channel_id=1, source_target_pairs={{0,16},{16,0},{1,17},{17,1},{2,18},{18,2},{3,19},{19,3},{4,20},{20... | collective-permute-start | bytes 393224 | tf_op jit(solution)/shard_map/ppermute | solution.py:199
  127.2 3.9 %collective-permute-start.21 = (f32[16,256]{1,0:T(8,128)S(1)}, f32[16,256]{1,0:T(8,128)S(1)}, u32[]{:S(2)}, u32[]{:S(2)}) collective-permute-start(f32[16,256]{1,0:T(8,128)S(1)} %fusion.62), channel_id=1, source_target_pairs={{0,64},{64,0},{128,192},{192,128},{1,65},{65,1},{129,193},{193,129... | collective-permute-start | bytes 49160 | tf_op jit(solution)/shard_map/ppermute | solution.py:259
  128.2 4.1 %collective-permute-start.22 = (f32[16,256]{1,0:T(8,128)S(1)}, f32[16,256]{1,0:T(8,128)S(1)}, u32[]{:S(2)}, u32[]{:S(2)}) collective-permute-start(f32[16,256]{1,0:T(8,128)S(1)} %fusion.62), channel_id=1, source_target_pairs={{0,128},{64,192},{128,0},{192,64},{1,129},{65,193},{129,1},{193,65... | collective-permute-start | bytes 49160 | tf_op jit(solution)/shard_map/ppermute | solution.py:259
  130.7 3.8 %collective-permute-start.23 = (f32[16,256]{1,0:T(8,128)S(1)}, f32[16,256]{1,0:T(8,128)S(1)}, u32[]{:S(2)}, u32[]{:S(2)}) collective-permute-start(f32[16,256]{1,0:T(8,128)S(1)} %fusion.62), channel_id=1, source_target_pairs={{0,192},{64,128},{128,64},{192,0},{1,193},{65,129},{129,65},{193,1... | collective-permute-start | bytes 49160 | tf_op jit(solution)/shard_map/ppermute | solution.py:259
  150.3 7.3 %copy-start = (bf16[4,1024,256]{2,1,0:T(8,128)(2,1)S(1)}, bf16[4,1024,256]{2,1,0:T(8,128)(2,1)}, u32[]{:S(2)}) copy-start(bf16[4,1024,256]{2,1,0:T(8,128)(2,1)} %w_hbm.1) | copy-start | bytes 6291460
  150.3 7.0 %collective-permute-start.24 = (f32[8,64,256]{2,1,0:T(8,128)S(1)}, f32[8,64,256]{2,1,0:T(8,128)S(1)}, u32[]{:S(2)}, u32[]{:S(2)}) collective-permute-start(f32[8,64,256]{2,1,0:T(8,128)S(1)} %all_to_all.25), channel_id=1, source_target_pairs={{0,1},{1,0},{2,3},{3,2},{4,5},{5,4},{6,7},{7,6},{8,9},{9,8},{10,11... | collective-permute-start | bytes 1572872 | tf_op jit(solution)/shard_map/ppermute | solution.py:199
  157.5 1.2 copy-start.4

commit v4 on v3

--- a/solution.py
+++ b/solution.py
@@ -220,18 +220,19 @@
     x0, keep, give, keep_shared, give_shared = leaf(
         core, at["yl"], leaf_inv, right_side, right_basis, left_basis
     )
-    mine = keep + partner(give, "c")
+    mine = partner(give, "c")
+    mine = keep + mine
     got_shared = partner(give_shared, "c")
     got = partner(keep_shared[1] + got_shared[1], "yl")
     direct = exchange(mine, "z")
     pairs = (keep_shared[0] + got_shared[0]) + got
+    pairs, rows = lax.optimization_barrier((pairs, rows))
     upper = at["yh"] == 0
     fours = pairs[:, 3:5]
     give = jnp.where(upper, fours[:, :, 8:], fours[:, :, :8]).reshape(Z, 1, 16, 128)
     got = partner(jnp.concatenate([give, pairs[:, 5:]], axis=1), "yh")
     keep = jnp.where(upper, fours[:, :, :8], fours[:, :, 8:]).reshape(Z, 1, 16, 128)
     fours = jnp.concatenate([keep, pairs[:, 5:]], axis=1) + got
-    fours, rows = lax.optimization_barrier((fours, rows))
     rows_c = partner(rows, "c")
     a0 = rows[:, 16:32]
     a1 = partner(a0, "yl")
@@ -290,6 +291,7 @@
     t = t + got
     m3 = mix(full3, t, partner(t, "yh"), "yh")
     own, m3 = lax.optimization_barrier((third, m3))
+    early = spread(jnp.concatenate([m4, m3], axis=0), "z", Z)
     t2 = in_rows(in_lanes(sums[48:56])) - times(m4, g24)
     t1 = in_rows(in_lanes(sums[56:64])) - times(m4, g14)
     other = partner(own, "c")
@@ -297,18 +299,23 @@
     half = both_cores(own, other, 32, 16)
     g12 = ordered(at["yl"], half, partner(half, "yl"), 1)
     t = jnp.stack([t2 - in_lanes(times(m3, g23)), t1 - in_lanes(times(m3, g13))])
-    t = sum(of_four(t, ("yh", "yl")))
+    four = of_four(t, ("yh", "yl"))
+    t = (four[0] + four[1]) + (four[2] + four[3])
     m2 = mix(full2, t[0], partner(t[0], "xl"), "xl")
     four = of_four(t[1] - times(m2, g12), ("xh", "xl"))
     m1 = mix(full1, four[0] + four[1], four[2] + four[3], "xh")
 
-    own = spread(jnp.concatenate([m4, m3, m2, m1], axis=0), "z", Z)
-    other = partner(own, "c")
-    m = jnp.stack([both_cores(own, other, 16 * n, 16) for n in (3, 2, 1, 0)])
-    high = lax.reduce_precision(m, 8, 7)
-    low = (m - high).astype(BF16)
-    dims = ((0, 2), (0, 2))
-    return x0 - (dot(left_basis, high.astype(BF16), dims) + dot(left_basis, low, dims))
+    def correct(out, own, other, levels):
+        m = jnp.stack([both_cores(own, other, row, 16) for row in (16, 0)])
+        high = lax.reduce_precision(m, 8, 7)
+        low = (m - high).astype(BF16)
+        left, dims = left_basis[levels], ((0, 2), (0, 2))
+        return out - (dot(left, high.astype(BF16), dims) + dot(left, low, dims))
+
+    last = spread(jnp.concatenate([m2, m1], axis=0), "z", Z)
+    out = correct(x0, early, partner(early, "c"), slice(2, 4))
+    out, last = lax.optimization_barrier((out, last))
+    return correct(out, last, partner(last, "c"), slice(0, 2))
 
 
 def solution(mesh):

time: 161 us -> 167 us (1.037)
  blocking collectives: 15.4 us -> 0 us
  waiting for transfers between devices: 55.7 us -> 66.9 us
  starting transfers between devices: 59.3 us -> 67.8 us
    all_to_all x1 -> x0, blocking collectives: 15.4 us -> none  [exchange(): return lax.all_to_all(block, axes, 0, 0, tiled=True)]
    all_to_all x4 -> x6, waiting for transfers between devices: 33.4 us -> 44.7 us  [exchange(): return lax.all_to_all(block, axes, 0, 0, tiled=True)]
    all_to_all x4 -> x6, starting transfers between devices: 19.8 us -> 30 us  [exchange(): return lax.all_to_all(block, axes, 0, 0, tiled=True)]
    ppermute x19 -> x20, starting transfers between devices: 31.6 us -> 29.9 us  [partner(): return lax.ppermute(block, axis, [(0, 1), (1, 0)])]
    ppermute x19 -> x20, waiting for transfers between devices: 18.9 us -> 18.6 us  [partner(): return lax.ppermute(block, axis, [(0, 1), (1, 0)])]
  transfers between devices with their start and end apart: 29 -> 32, of which waited for: 13 -> 14; matrix products, arithmetic and copies ran while one was open for 5% -> 5% of each run, Pallas kernels for 4% -> 4%
where the time goes in v4:
time: 167 us; the launch traced here: 166 us
  starting transfers between devices  67.8 us (41%)
  waiting for transfers between devices  66.9 us (40%)
  Pallas kernels  14.7 us (9%)
  matrix products  6.11 us (4%)
  local copies, waits for them, and re-layouts  5.25 us (3%)
  other arithmetic  4.31 us (3%)
    all_to_all x6, waiting for transfers between devices, exchange(): return lax.all_to_all(block, axes, 0, 0, tiled=True)  44.7 us
    all_to_all x6, starting transfers between devices, exchange(): return lax.all_to_all(block, axes, 0, 0, tiled=True)  30 us
    ppermute x20, starting transfers between devices, partner(): return lax.ppermute(block, axis, [(0, 1), (1, 0)])  29.9 us
    ppermute x20, waiting for transfers between devices, partner(): return lax.ppermute(block, axis, [(0, 1), (1, 0)])  18.6 us
    pallas_call x1, Pallas kernels, leaf(): pl.pallas_call(leaf_kernel, in_specs=[pl.BlockSpec(memory_space=pltpu.SME...  7.95 us
    ppermute x6, starting transfers between devices, of_four(): lax.ppermute(block, axes, [(i, i ^ k) for i in range(4)])  7.89 us
    pallas_call x2, Pallas kernels, assemble(): pl.pallas_call(kernel, in_specs=[pl.BlockSpec(memory_space=pltpu.SMEM)] *...  5.16 us
    ppermute x6, waiting for transfers between devices, of_four(): lax.ppermute(block, axes, [(i, i ^ k) for i in range(4)])  3.61 us
  transfers between devices with their start and end apart: 32, of which 14 were waited for; matrix products, arithmetic and copies ran while one was open for 5% of the time, Pallas kernels for 4%

profile of v4, /device:TPU:1, one launch (start us, length us, event | category | flops | bytes accessed | tf_op | source)
XLA Modules:
  0.0 165.7 jit_solution(5930794407959132688)
XLA Ops:
  0.0 8.0 %leaf.1 = (f32[1024,256]{1,0:T(8,128)}, f32[8,4,16,256]{3,2,1,0:T(8,128)}, f32[8,4,16,256]{3,2,1,0:T(8,128)}, f32[2,8,6,16,128]{4,3,2,1,0:T(8,128)}, f32[2,8,6,16,128]{4,3,2,1,0:T(8,128)}) custom-call(s32[1]{0:T(128)} %bitcast.core_ref, s32[1]{0:T(128)} %bitcast.1.pair_ref.yl_ref, bf16[1024,1024]{1,0:T(8,128)(2,1)} %inv_hbm.1, bf16[1024,256]{1,0:T(8,128)(2,1)} %rhs_hbm.1, ...), custom_call_target="tpu_custom_call" | custom-call | tf_op jit(solution)/shard_map/leaf/pallas_call | solution.py:116
  8.0 3.3 %collective-permute-start.2 = (f32[2,8,6,16,128]{4,3,2,1,0:T(8,128)}, f32[2,8,6,16,128]{4,3,2,1,0:T(8,128)S(1)}, u32[]{:S(2)}, u32[]{:S(2)}) collective-permute-start(f32[2,8,6,16,128]{4,3,2,1,0:T(8,128)} %get-tuple-element.24), channel_id=1, source_target_pairs={{0,1},{1,0},{2,3},{3,2},{4,5},{5,4},{6,7},{7,6},{8,9},{9,8},{10,11... | collective-permute-start | bytes 2359304 | tf_op jit(solution)/shard_map/ppermute | solution.py:199
  11.3 1.6 pack.1
  12.9 6.5 %all-to-all-start.1 = ((f32[8,32,512]{2,1,0:T(8,128)}), f32[8,32,512]{2,1,0:T(8,128)S(1)}, u32[]{:S(2)}, u32[]{:S(2)}) async-start(f32[8,32,512]{2,1,0:T(8,128)} %pack.1), calls=%async_computation.1 | async-start | bytes 1048576 | tf_op jit(solution)/shard_map/all_to_all | solution.py:209
  19.4 0.4 collective-permute-start
  19.8 1.8 %fusion.16 = f32[8,6,16,128]{3,2,1,0:T(8,128)} fusion(f32[2,8,6,16,128]{4,3,2,1,0:T(8,128)S(1)} %collective-permute-done.2, f32[2,8,6,16,128]{4,3,2,1,0:T(8,128)} %get-tuple-element.23), kind=kLoop, calls=%fused_computation.31 | loop fusion | flops 98304 | bytes 1179648 | tf_op jit(solution)/shard_map/add | solution.py:226
  21.6 1.3 collective-permute-start.3
  22.9 0.9 add.51
  23.8 13.6 %all-to-all-done.1.rows = f32[8,32,512]{2,1,0:T(8,128)S(1)} async-done(((f32[8,32,512]{2,1,0:T(8,128)}), f32[8,32,512]{2,1,0:T(8,128)S(1)}, u32[]{:S(2)}, u32[]{:S(2)}) %all-to-all-start.1) | async-done | bytes 524320 | tf_op jit(solution)/shard_map/all_to_all | solution.py:209
  37.4 3.5 %all-to-all-start = ((f32[8,4,16,256]{3,2,1,0:T(8,128)}), f32[8,4,16,256]{3,2,1,0:T(8,128)S(1)}, u32[]{:S(2)}, u32[]{:S(2)}) async-start(f32[8,4,16,256]{3,2,1,0:T(8,128)} %add.51), calls=%async_computation | async-start | bytes 1048576 | tf_op jit(solution)/shard_map/all_to_all | solution.py:209
  41.0 3.0 %collective-permute-start.7 = (f32[8,2,16,128]{3,2,1,0:T(8,128)S(1)}, f32[8,2,16,128]{3,2,1,0:T(8,128)S(1)}, u32[]{:S(2)}, u32[]{:S(2)}) collective-permute-start(f32[8,2,16,128]{3,2,1,0:T(8,128)S(1)} %pad_maximum_fusion.4), channel_id=1, source_target_pairs={{0,32},{32,0},{1,33},{33,1},{2,34},{34,2},{3,35},{35,3},{4,36},{36... | collective-permute-start | bytes 393224 | tf_op jit(solution)/shard_map/ppermute | solution.py:199
  44.0 3.2 %collective-permute-done.7 = f32[8,2,16,128]{3,2,1,0:T(8,128)S(1)} collective-permute-done((f32[8,2,16,128]{3,2,1,0:T(8,128)S(1)}, f32[8,2,16,128]{3,2,1,0:T(8,128)S(1)}, u32[]{:S(2)}, u32[]{:S(2)}) %collective-permute-start.7) | collective-permute-done | bytes 131104 | tf_op jit(solution)/shard_map/ppermute | solution.py:199
  47.2 11.5 %all-to-all-done = f32[8,4,16,256]{3,2,1,0:T(8,128)S(1)} async-done(((f32[8,4,16,256]{3,2,1,0:T(8,128)}), f32[8,4,16,256]{3,2,1,0:T(8,128)S(1)}, u32[]{:S(2)}, u32[]{:S(2)}) %all-to-all-start) | async-done | bytes 524320 | tf_op jit(solution)/shard_map/all_to_all | solution.py:209
  58.8 0.9 pad_maximum_fusion
  59.8 3.5 %all-to-all-start.2 = ((f32[8,176,128]{2,1,0:T(8,128)}), f32[8,176,128]{2,1,0:T(8,128)S(1)}, u32[]{:S(2)}, u32[]{:S(2)}) async-start(f32[8,176,128]{2,1,0:T(8,128)} %pad_maximum_fusion), calls=%async_computation.2 | async-start | bytes 1441792 | tf_op jit(solution)/shard_map/all_to_all | solution.py:209
  63.4 1.4 collective-permute-start.5
  64.7 6.1 %collective-permute-done.5.a = f32[8,16,512]{2,1,0:T(8,128)S(1)} collective-permute-done((f32[8,16,512]{2,1,0:T(8,128)S(1)}, f32[8,16,512]{2,1,0:T(8,128)S(1)}, u32[]{:S(2)}, u32[]{:S(2)}) %collective-permute-start.5) | collective-permute-done | bytes 262176 | tf_op jit(solution)/shard_map/ppermute | solution.py:199
  70.9 3.0 %collective-permute-start.17 = (f32[8,16,512]{2,1,0:T(8,128)S(1)}, f32[8,16,512]{2,1,0:T(8,128)S(1)}, u32[]{:S(2)}, u32[]{:S(2)}) collective-permute-start(f32[8,16,512]{2,1,0:T(8,128)S(1)} %pad_maximum_fusion.3), channel_id=1, source_target_pairs={{0,32},{32,0},{1,33},{33,1},{2,34},{34,2},{3,35},{35,3},{4,36},{36... | collective-permute-start | bytes 786440 | tf_op jit(solution)/shard_map/ppermute | solution.py:199
  73.9 0.4 collective-permute-start.1
  74.3 1.9 %collective-permute-start.4 = (f32[8,32,512]{2,1,0:T(8,128)S(1)}, f32[8,32,512]{2,1,0:T(8,128)S(1)}, u32[]{:S(2)}, u32[]{:S(2)}) collective-permute-start(f32[8,32,512]{2,1,0:T(8,128)S(1)} %all-to-all-done.1.rows), channel_id=1, source_target_pairs={{0,1},{1,0},{2,3},{3,2},{4,5},{5,4},{6,7},{7,6},{8,9},{9,8},{10,11... | collective-permute-start | bytes 1572872 | tf_op jit(solution)/shard_map/ppermute | solution.py:199
  76.3 3.4 %collective-permute-done.1 = f32[16,256]{1,0:T(8,128)S(1)} collective-permute-done((f32[16,256]{1,0:T(8,128)S(1)}, f32[16,256]{1,0:T(8,128)S(1)}, u32[]{:S(2)}, u32[]{:S(2)}) %collective-permute-start.1) | collective-permute-done | bytes 16416 | tf_op jit(solution)/shard_map/ppermute | solution.py:199
  79.8 1.3 collective-permute-start.19
  81.1 0.7 copy-done.5
  81.8 0.8 copy-done.2
  82.6 2.4 %shard_map.82 = (f32[256,512]{1,0:T(8,128)}, f32[256,512]{1,0:T(8,128)}) custom-call(s32[1]{0:T(128)} %bitcast.core_ref, s32[1]{0:T(128)} %bitcast.1.pair_ref.yl_ref, f32[8,32,512]{2,1,0:T(8,128)} %copy-done.1, f32[8,32,512]{2,1,0:T(8,128)} %copy-done.2, f32[8,16,512]{2,1,0:T(8,128)} %copy-done.3, f32[8,16,512]{2,1,0:T(8,128)} %copy-done.5), custom_call_target="tpu_custom_call" | custom-call | tf_op jit(solution)/shard_map/pallas_call | solution.py:191
  85.0 0.4 all-to-all-done.2
  85.4 2.1 %collective-permute-start.8 = (f32[8,96,128]{2,1,0:T(8,128)S(1)}, f32[8,96,128]{2,1,0:T(8,128)S(1)}, u32[]{:S(2)}, u32[]{:S(2)}) collective-permute-start(f32[8,96,128]{2,1,0:T(8,128)S(1)} %slice.247), channel_id=1, source_target_pairs={{0,1},{1,0},{2,3},{3,2},{4,5},{5,4},{6,7},{7,6},{8,9},{9,8},{10,11... | collective-permute-start | bytes 1179656 | tf_op jit(solution)/shard_map/ppermute | solution.py:199
  87.6 1.3 fusion.55
  89.1 0.5 collective-permute-start.20
  89.9 1.1 collective-permute-start.9
  91.0 0.7 copy-done.12
  91.7 2.8 %shard_map.83 = (f32[256,512]{1,0:T(8,128)}, f32[256,512]{1,0:T(8,128)}) custom-call(s32[1]{0:T(128)} %bitcast.core_ref, s32[1]{0:T(128)} %bitcast.1.pair_ref.yl_ref, s32[1]{0:T(128)} %bitcast.38.yh_ref, s32[1]{0:T(128)} %bitcast.39.xl_ref, f32[8,32,512]{2,1,0:T(8,128)} %copy-done.1, f32[8,32,512]{2,1,0:T(8,128)} %copy-done.2, f32[8,16,512]{2,1,0:T(8,128)} %copy-done.3, ...), custom_call_target="tpu_custom_call" | custom-call | tf_op jit(solution)/shard_map/pallas_call | solution.py:191
  94.6 2.4 %collective-permute-start.10 = (f32[16,256]{1,0:T(8,128)S(1)}, f32[16,256]{1,0:T(8,128)S(1)}, u32[]{:S(2)}, u32[]{:S(2)}) collective-permute-start(f32[16,256]{1,0:T(8,128)S(1)} %add.58), channel_id=1, source_target_pairs={{0,32},{32,0},{1,33},{33,1},{2,34},{34,2},{3,35},{35,3},{4,36},{36... | collective-permute-start | bytes 49160 | tf_op jit(solution)/shard_map/ppermute | solution.py:199
  97.0 0.7 broadcast_in_dim.12
  97.7 6.3 %all-to-all-start.3 = ((f32[8,48,128]{2,1,0:T(8,128)}), f32[8,48,128]{2,1,0:T(8,128)S(1)}, u32[]{:S(2)}, u32[]{:S(2)}) async-start(f32[8,48,128]{2,1,0:T(8,128)} %broadcast_in_dim.12), calls=%async_computation.3 | async-start | bytes 393216 | tf_op jit(solution)/shard_map/all_to_all | solution.py:209
  104.0 0.3 fusion.59
  104.3 8.6 %all-to-all-done.3 = f32[8,48,128]{2,1,0:T(8,128)S(1)} async-done(((f32[8,48,128]{2,1,0:T(8,128)}), f32[8,48,128]{2,1,0:T(8,128)S(1)}, u32[]{:S(2)}, u32[]{:S(2)}) %all-to-all-start.3) | async-done | bytes 196640 | tf_op jit(solution)/shard_map/all_to_all | solution.py:209
  112.9 2.5 %collective-permute-start.12 = (f32[8,48,128]{2,1,0:T(8,128)S(1)}, f32[8,48,128]{2,1,0:T(8,128)S(1)}, u32[]{:S(2)}, u32[]{:S(2)}) collective-permute-start(f32[8,48,128]{2,1,0:T(8,128)S(1)} %all-to-all-done.3), channel_id=1, source_target_pairs={{0,1},{1,0},{2,3},{3,2},{4,5},{5,4},{6,7},{7,6},{8,9},{9,8},{10,11... | collective-permute-start | bytes 589832 | tf_op jit(solution)/shard_map/ppermute | solution.py:199
  115.4 1.1 collective-permute-done.12
  117.4 1.9 %collective-permute-start.14 = (f32[2,16,256]{2,1,0:T(8,128)S(1)}, f32[2,16,256]{2,1,0:T(8,128)S(1)}, u32[]{:S(2)}, u32[]{:S(2)}) collective-permute-start(f32[2,16,256]{2,1,0:T(8,128)S(1)} %pad_maximum_fusion.10), channel_id=1, source_target_pairs={{0,32},{16,48},{32,0},{48,16},{1,33},{17,49},{33,1},{49,17},{2,34}... | collective-permute-start | bytes 98312 | tf_op jit(solution)/shard_map/ppermute | solution.py:260
  119.3 1.9 %collective-permute-start.15 = (f32[2,16,256]{2,1,0:T(8,128)S(1)}, f32[2,16,256]{2,1,0:T(8,128)S(1)}, u32[]{:S(2)}, u32[]{:S(2)}) collective-permute-start(f32[2,16,256]{2,1,0:T(8,128)S(1)} %pad_maximum_fusion.10), channel_id=1, source_target_pairs={{0,48},{16,32},{32,16},{48,0},{1,49},{17,33},{33,17},{49,1},{2,50}... | collective-permute-start | bytes 98312 | tf_op jit(solution)/shard_map/ppermute | solution.py:260
  121.1 0.7 broadcast_in_dim.13
  121.9 3.4 %all-to-all-start.4 = ((f32[8,32,256]{2,1,0:T(8,128)}), f32[8,32,256]{2,1,0:T(8,128)S(1)}, u32[]{:S(2)}, u32[]{:S(2)}) async-start(f32[8,32,256]{2,1,0:T(8,128)} %broadcast_in_dim.13), calls=%async_computation.4 | async-start | bytes 524288 | tf_op jit(solution)/shard_map/all_to_all | solution.py:209
  125.3 0.3 collective-permute-start.16
  125.8 2.2 %collective-permute-done.16 = f32[16,256]{1,0:T(8,128)S(1)} collective-permute-done((f32[16,256]{1,0:T(8,128)S(1)}, f32[16,256]{1,0:T(8,128)S(1)}, u32[]{:S(2)}, u32[]{:S(2)}) %collective-permute-start.16) | collective-permute-done | bytes 16416 | tf_op jit(solution)/shard_map/ppermute | solution.py:199
  128.0 0.3 fusion.63
  128.3 1.6 collective-permute-done.21
  130.1 1.0 collective-permute-start.22
  131.1 2.7 %collective-permute-start.23 = (f32[16,256]{1,0:T(8,128)S(1)}, f32[16,256]{1,0:T(8,128)S(1)}, u32[]{:S(2)}, u32[]{:S(2)}) collective-permute-start(f32[16,256]{1,0:T(8,128)S(1)} %fusion.71), channel_id=1, source_target_pairs={{0,128},{64,192},{128,0},{192,64},{1,129},{65,193},{129,1},{193,65... | collective-permute-start | bytes 49160 | tf_op jit(solution)/shard_map/ppermute | solution.py:260
  133.8 0.2 collective-permute-start.24
  134.0 1.1 collective-permute-done.23
  135.2 2.5 %collective-permute-done.24 = f32[16,256]{1,0:T(8,128)S(1)} collective-permute-done((f32[16,256]{1,0:T(8,128)S(1)}, f32[16,256]{1,0:T(8,128)S(1)}, u32[]{:S(2)}, u32[]{:S(2)}) %collective-permute-start.24) | collective-permute-done | bytes 16416 | tf_op jit(solution)/shard_map/ppermute | solution.py:260
  137.6 4.1 %collective-permute-start.11 = (f32[8,32,256]{2,1,0:T(8,128)S(1)}, f32[8,32,256]{2,1,0:T(8,128)S(1)}, u32[]{:S(2)}, u32[]{:S(2)}) collective-permute-start(f32[8,32,256]{2,1,0:T(8,128)S(1)} %all-to-all-done.4), channel_id=1, source_target_pairs={{0,1},{1,0},{2,3},{3,2},{4,5},{5,4},{6,7},{7,6},{8,9},{9,8},{10,11... | collective-permute-start | bytes 786440 | tf_op jit(solution)/shard_map/ppermute | solution.py:199
  141.8 0.3 fusion.67
  142.1 0.7 broadcast_in_dim.14
  142.8 6.8 %all-to-all-start.5 = ((f32[8,32,256]{2,1,0:T(8,128)}), f32[8,32,256]{2,1,0:T(8,128)S(1)}, u32[]{:S(2)}, u32[]{:S(2)}) async-start(f32[8,32,256]{2,1,0:T(8,128)} %broadcast_in_dim.14), calls=%async_computation.5 | async-start | bytes 524288 | tf_op jit(solution)/shard_map/all_to_all | solution.py:209
  149.8 0.5 convolution_bitcast_fusion.2
  150.3 0.7 copy-done.4
  151.0 0.5 fusion.2
  151.4 10.6 %all-to-all-done.5 = f32[8,32,256]{2,1,0:T(8,128)S(1)} async-done(((f32[8,32,256]{2,1,0:T(8,128)}), f32[8,32,256]{2,1,0:T(8,128)S(1)}, u32[]{:S(2)}, u32[]{:S(2)}) %all-to-all-start.5) | async-done | bytes 262176 | tf_op jit(solution)/shard_map/all_to_all | solution.py:209
  162.0 0.5 collective-permute-start.25
  162.5 1.2 collective-permute-done.25
  163.8 0.5 convolution_bitcast_fusion
  164.3 1.5 fusion.5
  (100 shorter events, 2.5 us)
Async XLA Ops:
  8.0 14.9 %copy-start.7 = (f32[8,4,16,256]{3,2,1,0:T(8,128)S(1)}, f32[8,4,16,256]{3,2,1,0:T(8,128)}, u32[]{:S(2)}) copy-start(f32[8,4,16,256]{3,2,1,0:T(8,128)} %get-tuple-element.21) | copy-start | bytes 1572868
  8.0 11.8 %collective-permute-start.2 = (f32[2,8,6,16,128]{4,3,2,1,0:T(8,128)}, f32[2,8,6,16,128]{4,3,2,1,0:T(8,128)S(1)}, u32[]{:S(2)}, u32[]{:S(2)}) collective-permute-start(f32[2,8,6,16,128]{4,3,2,1,0:T(8,128)} %get-tuple-element.24), channel_id=1, source_target_pairs={{0,1},{1,0},{2,3},{3,2},{4,5},{5,4},{6,7},{7,6},{8,9},{9,8},{10,11... | collective-permute-start | bytes 2359304 | tf_op jit(solution)/shard_map/ppermute | solution.py:199
  12.9 24.5 %all-to-all-start.1 = ((f32[8,32,512]{2,1,0:T(8,128)}), f32[8,32,512]{2,1,0:T(8,128)S(1)}, u32[]{:S(2)}, u32[]{:S(2)}) async-start(f32[8,32,512]{2,1,0:T(8,128)} %pack.1), calls=%async_computation.1 | async-start | bytes 1048576 | tf_op jit(solution)/shard_map/all_to_all | solution.py:209
  19.4 21.5 %copy-start.6 = (f32[2,8,6,16,128]{4,3,2,1,0:T(8,128)S(1)}, f32[2,8,6,16,128]{4,3,2,1,0:T(8,128)}, u32[]{:S(2)}) copy-start(f32[2,8,6,16,128]{4,3,2,1,0:T(8,128)} %get-tuple-element.23) | copy-start | bytes 2359300
  19.4 3.5 %collective-permute-start = (f32[8,4,16,256]{3,2,1,0:T(8,128)}, f32[8,4,16,256]{3,2,1,0:T(8,128)S(1)}, u32[]{:S(2)}, u32[]{:S(2)}) collective-permute-start(f32[8,4,16,256]{3,2,1,0:T(8,128)} %get-tuple-element.22), channel_id=1, source_target_pairs={{0,1},{1,0},{2,3},{3,2},{4,5},{5,4},{6,7},{7,6},{8,9},{9,8},{10,11... | collective-permute-start | bytes 1572872 | tf_op jit(solution)/shard_map/ppermute | solution.py:199
  21.6 19.3 %collective-permute-start.3 = (f32[8,6,16,128]{3,2,1,0:T(8,128)}, f32[8,6,16,128]{3,2,1,0:T(8,128)S(1)}, u32[]{:S(2)}, u32[]{:S(2)}) collective-permute-start(f32[8,6,16,128]{3,2,1,0:T(8,128)} %fusion.16), channel_id=1, source_target_pairs={{0,16},{16,0},{1,17},{17,1},{2,18},{18,2},{3,19},{19,3},{4,20},{20... | collective-permute-start | bytes 1179656 | tf_op jit(solution)/shard_map/ppermute | solution.py:199
  37.4 38.8 %copy-start.1 = (f32[8,32,512]{2,1,0:T(8,128)}, f32[8,32,512]{2,1,0:T(8,128)S(1)}, u32[]{:S(2)}) copy-start(f32[8,32,512]{2,1,0:T(8,128)S(1)} %all-to-all-done.1.rows) | copy-start | bytes 1572868
  37.4 21.4 %all-to-all-start = ((f32[8,4,16,256]{3,2,1,0:T(8,128)}), f32[8,4,16,256]{3,2,1,0:T(8,128)S(1)}, u32[]{:S(2)}, u32[]{:S(2)}) async-start(f32[8,4,16,256]{3,2,1,0:T(8,128)} %add.51), calls=%async_computation | async-start | bytes 1048576 | tf_op jit(solution)/shard_map/all_to_all | solution.py:209
  41.0 6.2 %collective-permute-start.7 = (f32[8,2,16,128]{3,2,1,0:T(8,128)S(1)}, f32[8,2,16,128]{3,2,1,0:T(8,128)S(1)}, u32[]{:S(2)}, u32[]{:S(2)}) collective-permute-start(f32[8,2,16,128]{3,2,1,0:T(8,128)S(1)} %pad_maximum_fusion.4), channel_id=1, source_target_pairs={{0,32},{32,0},{1,33},{33,1},{2,34},{34,2},{3,35},{35,3},{4,36},{36... | collective-permute-start | bytes 393224 | tf_op jit(solution)/shard_map/ppermute | solution.py:199
  59.8 25.6 %all-to-all-start.2 = ((f32[8,176,128]{2,1,0:T(8,128)}), f32[8,176,128]{2,1,0:T(8,128)S(1)}, u32[]{:S(2)}, u32[]{:S(2)}) async-start(f32[8,176,128]{2,1,0:T(8,128)} %pad_maximum_fusion), calls=%async_computation.2 | async-start | bytes 1441792 | tf_op jit(solution)/shard_map/all_to_all | solution.py:209
  63.4 7.5 %collective-permute-start.5 = (f32[8,16,512]{2,1,0:T(8,128)S(1)}, f32[8,16,512]{2,1,0:T(8,128)S(1)}, u32[]{:S(2)}, u32[]{:S(2)}) collective-permute-start(f32[8,16,512]{2,1,0:T(8,128)S(1)} %slice.187), channel_id=1, source_target_pairs={{0,16},{16,0},{1,17},{17,1},{2,18},{18,2},{3,19},{19,3},{4,20},{20... | collective-permute-start | bytes 786440 | tf_op jit(solution)/shard_map/ppermute | solution.py:199
  70.8 10.3 %copy-start.3 = (f32[8,16,512]{2,1,0:T(8,128)}, f32[8,16,512]{2,1,0:T(8,128)S(1)}, u32[]{:S(2)}) copy-start(f32[8,16,512]{2,1,0:T(8,128)S(1)} %collective-permute-done.5.a) | copy-start | bytes 786436
  70.9 8.8 %collective-permute-start.17 = (f32[8,16,512]{2,1,0:T(8,128)S(1)}, f32[8,16,512]{2,1,0:T(8,128)S(1)}, u32[]{:S(2)}, u32[]{:S(2)}) collective-permute-start(f32[8,16,512]{2,1,0:T(8,128)S(1)} %pad_maximum_fusion.3), channel_id=1, source_target_pairs={{0,32},{32,0},{1,33},{33,1},{2,34},{34,2},{3,35},{35,3},{4,36},{36... | collective-permute-start | bytes 786440 | tf_op jit(solution)/shard_map/ppermute | solution.py:199
  73.9 5.8 %collective-permute-start.1 = (f32[16,256]{1,0:T(8,128)S(1)}, f32[16,256]{1,0:T(8,128)S(1)}, u32[]{:S(2)}, u32[]{:S(2)}) collective-permute-start(f32[16,256]{1,0:T(8,128)S(1)} %slice_bitcast_fusion.2), channel_id=1, source_target_pairs={{0,16},{16,0},{1,17},{17,1},{2,18},{18,2},{3,19},{19,3},{4,20},{20... | collective-permute-start | bytes 49160 | tf_op jit(solution)/shard_map/ppermute | solution.py:199
  74.3 6.8 %collective-permute-start.4 = (f32[8,32,512]{2,1,0:T(8,128)S(1)}, f32[8,32,512]{2,1,0:T(8,128)S(1)}, u32[]{:S(2)}, u32[]{:S(2)}) collective-permute-start(f32[8,32,512]{2,1,0:T(8,128)S(1)} %all-to-all-done.1.rows), channel_id=1, source_target_pairs={{0,1},{1,0},{2,3},{3,2},{4,5},{5,4},{6,7},{7,6},{8,9},{9,8},{10,11... | collective-permute-start | bytes 1572872 | tf_op jit(solution)/shard_map/ppermute | solution.py:199
  76.2 4.9 %collective-permute-start.6 = (f32[8,16,512]{2,1,0:T(8,128)S(1)}, f32[8,16,512]{2,1,0:T(8,128)S(1)}, u32[]{:S(2)}, u32[]{:S(2)}) collective-permute-start(f32[8,16,512]{2,1,0:T(8,128)S(1)} %collective-permute-done.5.a), channel_id=1, source_target_pairs={{0,1},{1,0},{2,3},{3,2},{4,5},{5,4},{6,7},{7,6},{8,9},{9,8},{10,11... | collective-permute-start | bytes 786440 | tf_op jit(solution)/shard_map/ppermute | solution.py:199
  79.7 10.0 %copy-start.11 = (f32[8,16,512]{2,1,0:T(8,128)}, f32[8,16,512]{2,1,0:T(8,128)S(1)}, u32[]{:S(2)}) copy-start(f32[8,16,512]{2,1,0:T(8,128)S(1)} %collective-permute-done.17.b) | copy-start | bytes 786436
  79.8 9.2 %collective-permute-start.19 = (f32[8,8,512]{2,1,0:T(8,128)S(1)}, f32[8,8,512]{2,1,0:T(8,128)S(1)}, u32[]{:S(2)}, u32[]{:S(2)}) collective-permute-start(f32[8,8,512]{2,1,0:T(8,128)S(1)} %pad_maximum_fusion.6), channel_id=1, source_target_pairs={{0,64},{64,0},{1,65},{65,1},{2,66},{66,2},{3,67},{67,3},{4,68},{68... | collective-permute-start | bytes 393224 | tf_op jit(solution)/shard_map/ppermute | solution.py:199
  81.1 0.7 copy-start.5
  81.8 0.8 copy-start.2
  85.4 4.1 %collective-permute-start.8 = (f32[8,96,128]{2,1,0:T(8,128)S(1)}, f32[8,96,128]{2,1,0:T(8,128)S(1)}, u32[]{:S(2)}, u32[]{:S(2)}) collective-permute-start(f32[8,96,128]{2,1,0:T(8,128)S(1)} %slice.247), channel_id=1, source_target_pairs={{0,1},{1,0},{2,3},{3,2},{4,5},{5,4},{6,7},{7,6},{8,9},{9,8},{10,11... | collective-permute-start | bytes 1179656 | tf_op jit(solution)/shard_map/ppermute | solution.py:199
  88.9 2.1 %collective-permute-start.18 = (f32[8,16,512]{2,1,0:T(8,128)S(1)}, f32[8,16,512]{2,1,0:T(8,128)S(1)}, u32[]{:S(2)}, u32[]{:S(2)}) collective-permute-start(f32[8,16,512]{2,1,0:T(8,128)S(1)} %collective-permute-done.17.b), channel_id=1, source_target_pairs={{0,1},{1,0},{2,3},{3,2},{4,5},{5,4},{6,7},{7,6},{8,9},{9,8},{10,11... | collective-permute-start | bytes 786440 | tf_op jit(solution)/shard_map/ppermute | solution.py:199
  89.0 2.0 %copy-start.13 = (f32[8,8,512]{2,1,0:T(8,128)}, f32[8,8,512]{2,1,0:T(8,128)S(1)}, u32[]{:S(2)}) copy-start(f32[8,8,512]{2,1,0:T(8,128)S(1)} %collective-permute-done.19.e) | copy-start | bytes 393220
  89.1 2.0 %collective-permute-start.20 = (f32[8,8,512]{2,1,0:T(8,128)S(1)}, f32[8,8,512]{2,1,0:T(8,128)S(1)}, u32[]{:S(2)}, u32[]{:S(2)}) collective-permute-start(f32[8,8,512]{2,1,0:T(8,128)S(1)} %collective-permute-done.19.e), channel_id=1, source_target_pairs={{0,1},{1,0},{2,3},{3,2},{4,5},{5,4},{6,7},{7,6},{8,9},{9,8},{10,11... | collective-permute-start | bytes 393224 | tf_op jit(solution)/shard_map/ppermute | solution.py:199
  89.7 14.3 %copy-start.10 = (f32[256,512]{1,0:T(8,128)S(1)}, f32[256,512]{1,0:T(8,128)}, u32[]{:S(2)}) copy-start(f32[256,512]{1,0:T(8,128)} %get-tuple-element.28) | copy-start | bytes 1572868
  89.9 4.7 %collective-permute-start.9 = (f32[16,256]{1,0:T(8,128)S(1)}, f32[16,256]{1,0:T(8,128)S(1)}, u32[]{:S(2)}, u32[]{:S(2)}) collective-permute-start(f32[16,256]{1,0:T(8,128)S(1)} %convolution_subtract_fusion.2), channel_id=1, source_target_pairs={{0,16},{16,0},{1,17},{17,1},{2,18},{18,2},{3,19},{19,3},{4,20},{20... | collective-permute-start | bytes 49160 | tf_op jit(solution)/shard_map/ppermute | solution.py:199
  91.0 0.7 copy-start.12
  91.0 0.7 copy-start.14
  94.6 9.4 %collective-permute-start.10 = (f32[16,256]{1,0:T(8,128)S(1)}, f32[16,256]{1,0:T(8,128)S(1)}, u32[]{:S(2)}, u32[]{:S(2)}) collective-permute-start(f32[16,256]{1,0:T(8,128)S(1)} %add.58), channel_id=1, source_target_pairs={{0,32},{32,0},{1,33},{33,1},{2,34},{34,2},{3,35},{35,3},{4,36},{36... | collective-permute-start | bytes 49160 | tf_op jit(solution)/shard_map/ppermute | solution.py:199
  97.7 15.2 %all-to-all-start.3 = ((f32[8,48,128]{2,1,0:T(8,128)}), f32[8,48,128]{2,1,0:T(8,128)S(1)}, u32[]{:S(2)}, u32[]{:S(2)}) async-start(f32[8,48,128]{2,1,0:T(8,128)} %broadcast_in_dim.12), calls=%async_computation.3 | async-start | bytes 393216 | tf_op jit(solution)/shard_map/all_to_all | solution.py:209
  104.0 24.1 %copy-start.9 = (f32[256,512]{1,0:T(8,128)S(1)}, f32[256,512]{1,0:T(8,128)}, u32[]{:S(2)}) copy-start(f32[256,512]{1,0:T(8,128)} %get-tuple-element.31) | copy-start | bytes 1572868
  112.9 3.6 %collective-permute-start.12 = (f32[8,48,128]{2,1,0:T(8,128)S(1)}, f32[8,48,128]{2,1,0:T(8,128)S(1)}, u32[]{:S(2)}, u32[]{:S(2)}) collective-permute-start(f32[8,48,128]{2,1,0:T(8,128)S(1)} %all-to-all-done.3), channel_id=1, source_target_pairs={{0,1},{1,0},{2,3},{3,2},{4,5},{5,4},{6,7},{7,6},{8,9},{9,8},{10,11... | collective-permute-start | bytes 589832 | tf_op jit(solution)/shard_map/ppermute | solution.py:199
  116.6 25.2 %copy-start.8 = (f32[256,512]{1,0:T(8,128)S(1)}, f32[256,512]{1,0:T(8,128)}, u32[]{:S(2)}) copy-start(f32[256,512]{1,0:T(8,128)} %get-tuple-element.32) | copy-start | bytes 1572868
  117.2 8.1 %collective-permute-start.13 = (f32[2,16,256]{2,1,0:T(8,128)S(1)}, f32[2,16,256]{2,1,0:T(8,128)S(1)}, u32[]{:S(2)}, u32[]{:S(2)}) collective-permute-start(f32[2,16,256]{2,1,0:T(8,128)S(1)} %pad_maximum_fusion.10), channel_id=1, source_target_pairs={{0,16},{16,0},{32,48},{48,32},{1,17},{17,1},{33,49},{49,33},{2,18}... | collective-permute-start | bytes 98312 | tf_op jit(solution)/shard_map/ppermute | solution.py:260
  117.4 7.9 %collective-permute-start.14 = (f32[2,16,256]{2,1,0:T(8,128)S(1)}, f32[2,16,256]{2,1,0:T(8,128)S(1)}, u32[]{:S(2)}, u32[]{:S(2)}) collective-permute-start(f32[2,16,256]{2,1,0:T(8,128)S(1)} %pad_maximum_fusion.10), channel_id=1, source_target_pairs={{0,32},{16,48},{32,0},{48,16},{1,33},{17,49},{33,1},{49,17},{2,34}... | collective-permute-start | bytes 98312 | tf_op jit(solution)/shard_map/ppermute | solution.py:260
  119.3 6.0 %collective-permute-start.15 = (f32[2,16,256]{2,1,0:T(8,128)S(1)}, f32[2,16,256]{2,1,0:T(8,128)S(1)}, u32[]{:S(2)}, u32[]{:S(2)}) collective-permute-start(f32[2,16,256]{2,1,0:T(8,128)S(1)} %pad_maximum_fusion.10), channel_id=1, source_target_pairs={{0,48},{16,32},{32,16},{48,0},{1,49},{17,33},{33,17},{49,1},{2,50}... | collective-permute-start | bytes 98312 | tf_op jit(solution)/shard_map/ppermute | solution.py:260
  121.9 15.8 %all-to-all-start.4 = ((f32[8,32,256]{2,1,0:T(8,128)}), f32[8,32,256]{2,1,0:T(8,128)S(1)}, u32[]{:S(2)}, u32[]{:S(2)}) async-start(f32[8,32,256]{2,1,0:T(8,128)} %broadcast_in_dim.13), calls=%async_computation.4 | async-start | bytes 524288 | tf_op jit(solution)/shard_map/all_to_all | solution.py:209
  125.3 2.7 %collective-permute-start.16 = (f32[16,256]{1,0:T(8,128)S(1)}, f32[16,256]{1,0:T(8,128)S(1)}, u32[]{:S(2)}, u32[]{:S(2)}) collective-permute-start(f32[16,256]{1,0:T(8,128)S(1)} %slice_bitcast_fusion.1), channel_id=1, source_target_pairs={{0,64},{64,0},{1,65},{65,1},{2,66},{66,2},{3,67},{67,3},{4,68},{68... | collective-permute-start | bytes 49160 | tf_op jit(solution)/shard_map/ppermute | solution.py:199
  125.7 4.2 %collective-permute-start.21 = (f32[256,128]{1,0:T(8,128)S(1)}, f32[256,128]{1,0:T(8,128)S(1)}, u32[]{:S(2)}, u32[]{:S(2)}) collective-permute-start(f32[256,128]{1,0:T(8,128)S(1)} %pad_maximum_fusion.7), channel_id=1, source_target_pairs={{0,16},{16,0},{1,17},{17,1},{2,18},{18,2},{3,19},{19,3},{4,20},{20... | collective-permute-start | bytes 393224 | tf_op jit(solution)/shard_map/ppermute | solution.py:199
  129.9 19.9 %copy-start = (bf16[4,1024,256]{2,1,0:T(8,128)(2,1)S(1)}, bf16[4,1024,256]{2,1,0:T(8,128)(2,1)}, u32[]{:S(2)}) copy-start(bf16[4,1024,256]{2,1,0:T(8,128)(2,1)} %w_hbm.1) | copy-start | bytes 6291460
  130.1 3.9 %collective-permute-start.22 = (f32[16,256]{1,0:T(8,128)S(1)}, f32[16,256]{1,0:T(8,128)S(1)}, u32[]{:S(2)}, u32[]{:S(2)}) collective-permute-start(f32[16,256]{1,0:T(8,128)S(1)} %fusion.71), channel_id=1, source_target_pairs={{0,64},{64,0},{128,192},{192,128},{1,65},{65,1},{129,193},{193,129... | collective-permute-start | bytes 49160 | tf_op jit(solution)/shard_map/ppermute | solution.py:260
  131.1 4.1 %collective-permute-start.23 = (f32[16,256]{1,0:T(8,128)S(1)}, f32[16,256]{1,0:T(8,128)S(1)}, u32[]{:S(2)}, u32[]{:S(2)}) collective-permute-start(f32[16,256]{1,0:T(8,128)S(1)} %fusion.71), channel_id=1, source_target_pairs={{0,128},{64,192},{128,0},{192,64},{1,129},{65,193},{129,1},{193,65... | collective-permute-start | bytes 49160 | tf_op jit(solution)/shard_map/ppermute | solution.py:260
  133.8 3.8 %collective-permute-start.24 = (f32[16,256]{1,0:T(8,128)S(1)}, f32[16,256]{1,0:T(8,128)S(1)}, u32[]{:S(2)}, u32[]{:S(2)}) collective-permute-start(f32[16,256]{1,0:T(8,128)S(1)} %fusion.71), channel_id=1, source_target_pairs={{0,192},{64,128},{128,64},{192,0},{1,193},{65,129},{129,65},{193,1... | collective-permute-start | bytes 49160 | tf_op jit(solution)/shard_map/ppermute | solution.py:260
  137.6 12.0 %collective-permute-start.11 = (f32[8,32,256]{2,1,0:T(8,128)S(1)}, f32[8,32,256]{2,1,0:T(8,128)S(1)}, u32[]{:S(2)}, u32[]{:S(2)}) collective-permute-start(f32[8,32,256]{2,1,0:T(8,128)S(1)} %all-to-all-done.4), channel_id=1, source_target_pairs={{0,1},{1,0},{2,3},{3,2},{4,5},{5,4},{6,7},{7,6},{8,9},{9,8},{10,11... | collective-permute-start | bytes 786440 | tf_op jit(solution)/shard_map/ppermute | solution.py:199
  142.8 19.2 %all-to-all-start.5 = ((f32[8,32,256]{2,1,0:T(8,128)}), f32[8,32,256]{2,1,0:T(8,128)S(1)}, u32[]{:S(2)}, u32[]{:S(2)}) async-start(f32[8,32,256]{2,1,0:T(8,128)} %broadcast_in_dim.14), calls=%async_computation.5 | async-start | bytes 524288 | tf_op jit(solution)/shard_map/all_to_all | solution.py:209
  149.7 1.2 copy-start.4
  162.0 1.6 collective-permute-start.25

commit v5 on v3

--- a/solution.py
+++ b/solution.py
@@ -40,8 +40,8 @@
 
 
 def leaf_kernel(
-    core_ref, pair_ref, inv_hbm, rhs_hbm, v_hbm, w_hbm, x_ref, keep_ref, give_ref, keep_shared_ref, give_shared_ref,
-    inv_ref, rhs_ref, v_ref, w_ref, high_ref, low_ref, sems,
+    core_ref, pair_ref, inv_hbm, rhs_hbm, v_hbm, w_hbm, x_hbm, keep_hbm, give_hbm, keep_shared_hbm, give_shared_hbm,
+    x_ref, keep_ref, give_ref, keep_shared_ref, give_shared_ref, inv_ref, rhs_ref, v_ref, w_ref, high_ref, low_ref, sems,
 ):
     rows = 1024 // STEPS
     count = [0]
@@ -71,15 +71,21 @@
         keep = jnp.where(first_core, low, high).reshape(Z, 16, 256)
         give = jnp.where(first_core, high, low).reshape(Z, 16, 256)
         if name in DIRECT:
-            keep_ref[:, DIRECT.index(name)] = keep
-            give_ref[:, DIRECT.index(name)] = give
+            n = DIRECT.index(name)
+            keep_ref[:, n] = keep
+            give_ref[:, n] = give
+            stores.append(load(give_ref.at[:, n], give_hbm.at[:, n]))
+            stores.append(load(keep_ref.at[:, n], keep_hbm.at[:, n]))
             return
         n = SHARED.index(name)
         for value, ref in ((keep, keep_shared_ref), (give, give_shared_ref)):
             left, right = value[:, :, :128], value[:, :, 128:]
             ref[0, :, n] = jnp.where(first_lanes, left, right)
             ref[1, :, n] = jnp.where(first_lanes, right, left)
-
+        stores.append(load(give_shared_ref.at[:, :, n], give_shared_hbm.at[:, :, n]))
+        stores.append(load(keep_shared_ref.at[:, :, n], keep_shared_hbm.at[:, :, n]))
+
+    stores = []
     done = set()
 
     def ready(waits, level):
@@ -101,6 +107,7 @@
         wait_inv[step].wait()
         inv = inv_ref[part, :]
         x_ref[part, :] = jnp.dot(inv, rhs, preferred_element_type=F32)
+        stores.append(load(x_ref.at[part], x_hbm.at[part]))
         xt = dot(rhs_turned, inv, ((1,), (1,)))
         high = xt.astype(BF16)
         high_ref[:, part] = high
@@ -109,28 +116,28 @@
         ready(wait_v, j)
         v = v_ref[j - 1]
         store(j, dot(high_ref[...], v, ((1,), (0,))) + dot(low_ref[...], v, ((1,), (0,))))
+    for copy in stores:
+        copy.wait()
 
 
 def leaf(core, pair, leaf_inv, right_side, right_basis, left_basis):
     any_space = pl.BlockSpec(memory_space=pl.ANY)
+    direct, shared = (Z, 4, 16, 256), (2, Z, 6, 16, 128)
+    shapes = [(1024, 256), direct, direct, shared, shared]
     return pl.pallas_call(
         leaf_kernel,
         in_specs=[pl.BlockSpec(memory_space=pltpu.SMEM)] * 2 + [any_space] * 4,
-        out_shape=[
-            jax.ShapeDtypeStruct((1024, 256), F32),
-            jax.ShapeDtypeStruct((Z, 4, 16, 256), F32),
-            jax.ShapeDtypeStruct((Z, 4, 16, 256), F32),
-            jax.ShapeDtypeStruct((2, Z, 6, 16, 128), F32),
-            jax.ShapeDtypeStruct((2, Z, 6, 16, 128), F32),
-        ],
-        scratch_shapes=[
+        out_specs=[any_space] * 5,
+        out_shape=[jax.ShapeDtypeStruct(shape, F32) for shape in shapes],
+        scratch_shapes=[pltpu.VMEM(shape, F32) for shape in shapes]
+        + [
             pltpu.VMEM((1024, 1024), BF16),
             pltpu.VMEM((1024, 256), BF16),
             pltpu.VMEM((4, 1024, 256), BF16),
             pltpu.VMEM((3, 1024, 256), BF16),
             pltpu.VMEM((256, 1024), BF16),
             pltpu.VMEM((256, 1024), BF16),
-            pltpu.SemaphoreType.DMA((8 + STEPS,)),
+            pltpu.SemaphoreType.DMA((28 + 2 * STEPS,)),
         ],
         name="leaf",
     )(core.reshape(1), pair.reshape(1), leaf_inv, right_side, right_basis, left_basis)
@@ -220,18 +227,19 @@
     x0, keep, give, keep_shared, give_shared = leaf(
         core, at["yl"], leaf_inv, right_side, right_basis, left_basis
     )
-    mine = keep + partner(give, "c")
+    mine = partner(give, "c")
+    mine = keep + mine
     got_shared = partner(give_shared, "c")
     got = partner(keep_shared[1] + got_shared[1], "yl")
     direct = exchange(mine, "z")
     pairs = (keep_shared[0] + got_shared[0]) + got
+    pairs, rows = lax.optimization_barrier((pairs, rows))
     upper = at["yh"] == 0
     fours = pairs[:, 3:5]
     give = jnp.where(upper, fours[:, :, 8:], fours[:, :, :8]).reshape(Z, 1, 16, 128)
     got = partner(jnp.concatenate([give, pairs[:, 5:]], axis=1), "yh")
     keep = jnp.where(upper, fours[:, :, :8], fours[:, :, 8:]).reshape(Z, 1, 16, 128)
     fours = jnp.concatenate([keep, pairs[:, 5:]], axis=1) + got
-    fours, rows = lax.optimization_barrier((fours, rows))
     rows_c = partner(rows, "c")
     a0 = rows[:, 16:32]
     a1 = partner(a0, "yl")
@@ -256,7 +264,8 @@
         return fdot(ordered(at[axis], own, other, 1), k, ((1,), (1,)))
 
     def of_four(block, axes):
-        return [block] + [lax.ppermute(block, axes, [(i, i ^ k) for i in range(4)]) for k in (1, 2, 3)]
+        far, near, last = [lax.ppermute(block, axes, [(i, i ^ k) for i in range(4)]) for k in (2, 1, 3)]
+        return [block, near, far, last]
 
     def times(m, g):
         return fdot(m, g, ((1,), (0,)))
@@ -297,7 +306,8 @@
     half = both_cores(own, other, 32, 16)
     g12 = ordered(at["yl"], half, partner(half, "yl"), 1)
     t = jnp.stack([t2 - in_lanes(times(m3, g23)), t1 - in_lanes(times(m3, g13))])
-    t = sum(of_four(t, ("yh", "yl")))
+    four = of_four(t, ("yh", "yl"))
+    t = (four[0] + four[1]) + (four[2] + four[3])
     m2 = mix(full2, t[0], partner(t[0], "xl"), "xl")
     four = of_four(t[1] - times(m2, g12), ("xh", "xl"))
     m1 = mix(full1, four[0] + four[1], four[2] + four[3], "xh")

time: 161 us -> 161 us (level)
  transfers between devices with their start and end apart: 29 -> 29, of which waited for: 13 -> 14; matrix products, arithmetic and copies ran while one was open for 5% -> 5% of each run, Pallas kernels for 4% -> 4%
where the time goes in v5:
time: 161 us
  starting transfers between devices  59.2 us (37%)
  waiting for transfers between devices  55.9 us (35%)
  blocking collectives  15.4 us (10%)
  Pallas kernels  14.8 us (9%)
  matrix products  6.79 us (4%)
  other arithmetic  4.37 us (3%)
  local copies, waits for them, and re-layouts  3.66 us (2%)
    all_to_all x4, waiting for transfers between devices, exchange(): return lax.all_to_all(block, axes, 0, 0, tiled=True)  33.8 us
    ppermute x19, starting transfers between devices, partner(): return lax.ppermute(block, axis, [(0, 1), (1, 0)])  31.5 us
    all_to_all x4, starting transfers between devices, exchange(): return lax.all_to_all(block, axes, 0, 0, tiled=True)  19.8 us
    ppermute x19, waiting for transfers between devices, partner(): return lax.ppermute(block, axis, [(0, 1), (1, 0)])  18.8 us
    all_to_all x1, blocking collectives, exchange(): return lax.all_to_all(block, axes, 0, 0, tiled=True)  15.4 us
    pallas_call x1, Pallas kernels, leaf(): pl.pallas_call(leaf_kernel, in_specs=[pl.BlockSpec(memory_space=pltpu.SME...  7.92 us
    ppermute x6, starting transfers between devices, of_four(): lax.ppermute(block, axes, [(i, i ^ k) for i in range(4)])  7.89 us
    pallas_call x2, Pallas kernels, assemble(): pl.pallas_call(kernel, in_specs=[pl.BlockSpec(memory_space=pltpu.SMEM)] *...  5.2 us
  transfers between devices with their start and end apart: 29, of which 14 were waited for; matrix products, arithmetic and copies ran while one was open for 5% of the time, Pallas kernels for 4%

profile of v5, /device:TPU:1, one launch (start us, length us, event | category | flops | bytes accessed | tf_op | source)
XLA Modules:
  0.0 160.6 jit_solution(471057038476962435)
XLA Ops:
  0.0 7.9 %leaf.1 = (f32[1024,256]{1,0:T(8,128)}, f32[8,4,16,256]{3,2,1,0:T(8,128)}, f32[8,4,16,256]{3,2,1,0:T(8,128)}, f32[2,8,6,16,128]{4,3,2,1,0:T(8,128)}, f32[2,8,6,16,128]{4,3,2,1,0:T(8,128)}) custom-call(s32[1]{0:T(128)} %bitcast.core_ref, s32[1]{0:T(128)} %bitcast.1.pair_ref.yl_ref, bf16[1024,1024]{1,0:T(8,128)(2,1)} %inv_hbm.1, bf16[1024,256]{1,0:T(8,128)(2,1)} %rhs_hbm.1, ...), custom_call_target="tpu_custom_call" | custom-call | tf_op jit(solution)/shard_map/leaf/pallas_call | solution.py:127
  7.9 3.3 %collective-permute-start.2 = (f32[2,8,6,16,128]{4,3,2,1,0:T(8,128)}, f32[2,8,6,16,128]{4,3,2,1,0:T(8,128)S(1)}, u32[]{:S(2)}, u32[]{:S(2)}) collective-permute-start(f32[2,8,6,16,128]{4,3,2,1,0:T(8,128)} %get-tuple-element.22), channel_id=1, source_target_pairs={{0,1},{1,0},{2,3},{3,2},{4,5},{5,4},{6,7},{7,6},{8,9},{9,8},{10,11... | collective-permute-start | bytes 2359304 | tf_op jit(solution)/shard_map/ppermute | solution.py:206
  11.2 1.6 %pack.1 = f32[8,32,512]{2,1,0:T(8,128)} custom-call(f32[16,512]{1,0:T(8,128)} %a_ref.1, f32[8,512]{1,0:T(8,128)} %b_ref.1, f32[4,512]{1,0:T(4,128)} %c_ref.1, f32[2,512]{1,0:T(2,128)} %d_ref.1), custom_call_target="tpu_custom_call" | custom-call | tf_op jit(solution)/shard_map/pack/pallas_call | solution.py:39
  12.9 6.5 %all-to-all-start.1 = ((f32[8,32,512]{2,1,0:T(8,128)}), f32[8,32,512]{2,1,0:T(8,128)S(1)}, u32[]{:S(2)}, u32[]{:S(2)}) async-start(f32[8,32,512]{2,1,0:T(8,128)} %pack.1), calls=%async_computation.1 | async-start | bytes 1048576 | tf_op jit(solution)/shard_map/all_to_all | solution.py:216
  19.3 0.4 collective-permute-start
  19.8 1.8 %fusion.9 = f32[8,6,16,128]{3,2,1,0:T(8,128)} fusion(f32[2,8,6,16,128]{4,3,2,1,0:T(8,128)S(1)} %collective-permute-done.2, f32[2,8,6,16,128]{4,3,2,1,0:T(8,128)} %get-tuple-element.21), kind=kLoop, calls=%fused_computation.18 | loop fusion | flops 98304 | bytes 1179648 | tf_op jit(solution)/shard_map/add | solution.py:233
  21.6 1.3 collective-permute-start.3
  22.9 0.9 add.45
  23.8 13.5 %all-to-all-done.1.rows = f32[8,32,512]{2,1,0:T(8,128)S(1)} async-done(((f32[8,32,512]{2,1,0:T(8,128)}), f32[8,32,512]{2,1,0:T(8,128)S(1)}, u32[]{:S(2)}, u32[]{:S(2)}) %all-to-all-start.1) | async-done | bytes 524320 | tf_op jit(solution)/shard_map/all_to_all | solution.py:216
  37.3 3.5 %all-to-all-start = ((f32[8,4,16,256]{3,2,1,0:T(8,128)}), f32[8,4,16,256]{3,2,1,0:T(8,128)S(1)}, u32[]{:S(2)}, u32[]{:S(2)}) async-start(f32[8,4,16,256]{3,2,1,0:T(8,128)} %add.45), calls=%async_computation | async-start | bytes 1048576 | tf_op jit(solution)/shard_map/all_to_all | solution.py:216
  41.0 3.0 %collective-permute-start.7 = (f32[8,2,16,128]{3,2,1,0:T(8,128)S(1)}, f32[8,2,16,128]{3,2,1,0:T(8,128)S(1)}, u32[]{:S(2)}, u32[]{:S(2)}) collective-permute-start(f32[8,2,16,128]{3,2,1,0:T(8,128)S(1)} %pad_maximum_fusion.3), channel_id=1, source_target_pairs={{0,32},{32,0},{1,33},{33,1},{2,34},{34,2},{3,35},{35,3},{4,36},{36... | collective-permute-start | bytes 393224 | tf_op jit(solution)/shard_map/ppermute | solution.py:206
  44.0 3.2 %collective-permute-done.7 = f32[8,2,16,128]{3,2,1,0:T(8,128)S(1)} collective-permute-done((f32[8,2,16,128]{3,2,1,0:T(8,128)S(1)}, f32[8,2,16,128]{3,2,1,0:T(8,128)S(1)}, u32[]{:S(2)}, u32[]{:S(2)}) %collective-permute-start.7) | collective-permute-done | bytes 131104 | tf_op jit(solution)/shard_map/ppermute | solution.py:206
  47.2 11.5 %all-to-all-done = f32[8,4,16,256]{3,2,1,0:T(8,128)S(1)} async-done(((f32[8,4,16,256]{3,2,1,0:T(8,128)}), f32[8,4,16,256]{3,2,1,0:T(8,128)S(1)}, u32[]{:S(2)}, u32[]{:S(2)}) %all-to-all-start) | async-done | bytes 524320 | tf_op jit(solution)/shard_map/all_to_all | solution.py:216
  58.8 0.9 pad_maximum_fusion.1
  59.7 3.5 %all-to-all-start.2 = ((f32[8,176,128]{2,1,0:T(8,128)}), f32[8,176,128]{2,1,0:T(8,128)S(1)}, u32[]{:S(2)}, u32[]{:S(2)}) async-start(f32[8,176,128]{2,1,0:T(8,128)} %pad_maximum_fusion.1), calls=%async_computation.2 | async-start | bytes 1441792 | tf_op jit(solution)/shard_map/all_to_all | solution.py:216
  63.3 1.4 collective-permute-start.5
  64.7 6.1 %collective-permute-done.5.a = f32[8,16,512]{2,1,0:T(8,128)S(1)} collective-permute-done((f32[8,16,512]{2,1,0:T(8,128)S(1)}, f32[8,16,512]{2,1,0:T(8,128)S(1)}, u32[]{:S(2)}, u32[]{:S(2)}) %collective-permute-start.5) | collective-permute-done | bytes 262176 | tf_op jit(solution)/shard_map/ppermute | solution.py:206
  70.8 3.0 %collective-permute-start.16 = (f32[8,16,512]{2,1,0:T(8,128)S(1)}, f32[8,16,512]{2,1,0:T(8,128)S(1)}, u32[]{:S(2)}, u32[]{:S(2)}) collective-permute-start(f32[8,16,512]{2,1,0:T(8,128)S(1)} %pad_maximum_fusion.2), channel_id=1, source_target_pairs={{0,32},{32,0},{1,33},{33,1},{2,34},{34,2},{3,35},{35,3},{4,36},{36... | collective-permute-start | bytes 786440 | tf_op jit(solution)/shard_map/ppermute | solution.py:206
  73.8 0.4 collective-permute-start.1
  74.2 1.9 %collective-permute-start.4 = (f32[8,32,512]{2,1,0:T(8,128)S(1)}, f32[8,32,512]{2,1,0:T(8,128)S(1)}, u32[]{:S(2)}, u32[]{:S(2)}) collective-permute-start(f32[8,32,512]{2,1,0:T(8,128)S(1)} %all-to-all-done.1.rows), channel_id=1, source_target_pairs={{0,1},{1,0},{2,3},{3,2},{4,5},{5,4},{6,7},{7,6},{8,9},{9,8},{10,11... | collective-permute-start | bytes 1572872 | tf_op jit(solution)/shard_map/ppermute | solution.py:206
  76.2 3.4 %collective-permute-done.1 = f32[16,256]{1,0:T(8,128)S(1)} collective-permute-done((f32[16,256]{1,0:T(8,128)S(1)}, f32[16,256]{1,0:T(8,128)S(1)}, u32[]{:S(2)}, u32[]{:S(2)}) %collective-permute-start.1) | collective-permute-done | bytes 16416 | tf_op jit(solution)/shard_map/ppermute | solution.py:206
  79.7 1.3 collective-permute-start.18
  81.1 0.7 copy-done.5
  81.8 0.8 copy-done.2
  82.6 2.4 %shard_map.82 = (f32[256,512]{1,0:T(8,128)}, f32[256,512]{1,0:T(8,128)}) custom-call(s32[1]{0:T(128)} %bitcast.core_ref, s32[1]{0:T(128)} %bitcast.1.pair_ref.yl_ref, f32[8,32,512]{2,1,0:T(8,128)} %copy-done.1, f32[8,32,512]{2,1,0:T(8,128)} %copy-done.2, f32[8,16,512]{2,1,0:T(8,128)} %copy-done.3, f32[8,16,512]{2,1,0:T(8,128)} %copy-done.5), custom_call_target="tpu_custom_call" | custom-call | tf_op jit(solution)/shard_map/pallas_call | solution.py:198
  85.0 0.4 all-to-all-done.2
  85.4 2.2 %collective-permute-start.8 = (f32[8,96,128]{2,1,0:T(8,128)S(1)}, f32[8,96,128]{2,1,0:T(8,128)S(1)}, u32[]{:S(2)}, u32[]{:S(2)}) collective-permute-start(f32[8,96,128]{2,1,0:T(8,128)S(1)} %slice.239), channel_id=1, source_target_pairs={{0,1},{1,0},{2,3},{3,2},{4,5},{5,4},{6,7},{7,6},{8,9},{9,8},{10,11... | collective-permute-start | bytes 1179656 | tf_op jit(solution)/shard_map/ppermute | solution.py:206
  87.6 1.4 fusion.46
  89.1 0.1 convolution_subtract_fusion.2
  89.3 1.3 collective-permute-start.9
  90.6 0.5 collective-permute-start.17
  91.2 0.9 collective-permute-done.9
  92.1 2.4 %collective-permute-start.10 = (f32[16,256]{1,0:T(8,128)S(1)}, f32[16,256]{1,0:T(8,128)S(1)}, u32[]{:S(2)}, u32[]{:S(2)}) collective-permute-start(f32[16,256]{1,0:T(8,128)S(1)} %add.52), channel_id=1, source_target_pairs={{0,32},{32,0},{1,33},{33,1},{2,34},{34,2},{3,35},{35,3},{4,36},{36... | collective-permute-start | bytes 49160 | tf_op jit(solution)/shard_map/ppermute | solution.py:206
  94.5 0.7 broadcast_in_dim.10
  95.2 6.3 %all-to-all-start.3 = ((f32[8,48,128]{2,1,0:T(8,128)}), f32[8,48,128]{2,1,0:T(8,128)S(1)}, u32[]{:S(2)}, u32[]{:S(2)}) async-start(f32[8,48,128]{2,1,0:T(8,128)} %broadcast_in_dim.10), calls=%async_computation.3 | async-start | bytes 393216 | tf_op jit(solution)/shard_map/all_to_all | solution.py:216
  101.5 0.3 fusion.50
  101.9 8.4 %all-to-all-done.3 = f32[8,48,128]{2,1,0:T(8,128)S(1)} async-done(((f32[8,48,128]{2,1,0:T(8,128)}), f32[8,48,128]{2,1,0:T(8,128)S(1)}, u32[]{:S(2)}, u32[]{:S(2)}) %all-to-all-start.3) | async-done | bytes 196640 | tf_op jit(solution)/shard_map/all_to_all | solution.py:216
  110.2 3.0 %collective-permute-start.11 = (f32[8,48,128]{2,1,0:T(8,128)S(1)}, f32[8,48,128]{2,1,0:T(8,128)S(1)}, u32[]{:S(2)}, u32[]{:S(2)}) collective-permute-start(f32[8,48,128]{2,1,0:T(8,128)S(1)} %all-to-all-done.3), channel_id=1, source_target_pairs={{0,1},{1,0},{2,3},{3,2},{4,5},{5,4},{6,7},{7,6},{8,9},{9,8},{10,11... | collective-permute-start | bytes 589832 | tf_op jit(solution)/shard_map/ppermute | solution.py:206
  113.3 1.1 collective-permute-done.11
  114.3 0.2 broadcast_select_fusion.13
  114.5 0.2 broadcast_select_fusion.11
  114.6 0.2 fusion.6
  114.8 0.2 fusion.4
  115.1 0.5 collective-permute-start.12
  115.5 1.9 %collective-permute-start.13 = (f32[2,16,256]{2,1,0:T(8,128)S(1)}, f32[2,16,256]{2,1,0:T(8,128)S(1)}, u32[]{:S(2)}, u32[]{:S(2)}) collective-permute-start(f32[2,16,256]{2,1,0:T(8,128)S(1)} %pad_maximum_fusion.9), channel_id=1, source_target_pairs={{0,32},{16,48},{32,0},{48,16},{1,33},{17,49},{33,1},{49,17},{2,34}... | collective-permute-start | bytes 98312 | tf_op jit(solution)/shard_map/ppermute | solution.py:267
  117.4 1.6 collective-permute-start.14
  119.0 0.7 copy-done.11
  119.7 2.8 %shard_map.83 = (f32[256,512]{1,0:T(8,128)}, f32[256,512]{1,0:T(8,128)}) custom-call(s32[1]{0:T(128)} %bitcast.core_ref, s32[1]{0:T(128)} %bitcast.1.pair_ref.yl_ref, s32[1]{0:T(128)} %bitcast.29.yh_ref, s32[1]{0:T(128)} %bitcast.30.xl_ref, f32[8,32,512]{2,1,0:T(8,128)} %copy-done.1, f32[8,32,512]{2,1,0:T(8,128)} %copy-done.2, f32[8,16,512]{2,1,0:T(8,128)} %copy-done.3, ...), custom_call_target="tpu_custom_call" | custom-call | tf_op jit(solution)/shard_map/pallas_call | solution.py:198
  122.6 0.3 collective-permute-start.15
  123.1 2.2 %collective-permute-done.15 = f32[16,256]{1,0:T(8,128)S(1)} collective-permute-done((f32[16,256]{1,0:T(8,128)S(1)}, f32[16,256]{1,0:T(8,128)S(1)}, u32[]{:S(2)}, u32[]{:S(2)}) %collective-permute-start.15) | collective-permute-done | bytes 16416 | tf_op jit(solution)/shard_map/ppermute | solution.py:206
  125.3 1.3 fusion.54
  126.7 0.5 collective-permute-done.20
  127.3 1.0 collective-permute-start.21
  128.3 2.5 %collective-permute-start.22 = (f32[16,256]{1,0:T(8,128)S(1)}, f32[16,256]{1,0:T(8,128)S(1)}, u32[]{:S(2)}, u32[]{:S(2)}) collective-permute-start(f32[16,256]{1,0:T(8,128)S(1)} %fusion.62), channel_id=1, source_target_pairs={{0,128},{64,192},{128,0},{192,64},{1,129},{65,193},{129,1},{193,65... | collective-permute-start | bytes 49160 | tf_op jit(solution)/shard_map/ppermute | solution.py:267
  130.8 0.5 collective-permute-start.23
  131.3 1.1 collective-permute-done.22
  132.4 2.2 %collective-permute-done.23 = f32[16,256]{1,0:T(8,128)S(1)} collective-permute-done((f32[16,256]{1,0:T(8,128)S(1)}, f32[16,256]{1,0:T(8,128)S(1)}, u32[]{:S(2)}, u32[]{:S(2)}) %collective-permute-start.23) | collective-permute-done | bytes 16416 | tf_op jit(solution)/shard_map/ppermute | solution.py:267
  134.6 0.3 fusion.58
  135.0 15.4 %all_to_all.25 = f32[8,64,256]{2,1,0:T(8,128)S(1)} all-to-all(f32[8,64,256]{2,1,0:T(8,128)S(1)} %broadcast_in_dim.11), channel_id=1, replica_groups=mesh['xh'=2,'xl'=2,'yh'=2,'yl'=2,'z'=8,'c'=2] {'z'}, dimensions={0} | all-to-all | bytes 1048576 | tf_op jit(solution)/shard_map/all_to_all | solution.py:216
  150.4 5.5 %collective-permute-start.24 = (f32[8,64,256]{2,1,0:T(8,128)S(1)}, f32[8,64,256]{2,1,0:T(8,128)S(1)}, u32[]{:S(2)}, u32[]{:S(2)}) collective-permute-start(f32[8,64,256]{2,1,0:T(8,128)S(1)} %all_to_all.25), channel_id=1, source_target_pairs={{0,1},{1,0},{2,3},{3,2},{4,5},{5,4},{6,7},{7,6},{8,9},{9,8},{10,11... | collective-permute-start | bytes 1572872 | tf_op jit(solution)/shard_map/ppermute | solution.py:206
  155.9 1.5 collective-permute-done.24
  157.7 0.7 convolution_bitcast_fusion
  158.4 0.5 copy-done.4
  158.9 1.7 %fusion.2 = f32[1024,256]{1,0:T(8,128)} fusion(f32[1024,256]{1,0:T(8,128)S(1)} %copy-done.4, f32[256,1024]{0,1:T(8,128)S(1)} %convolution_bitcast_fusion, bf16[4,1024,256]{2,1,0:T(8,128)(2,1)S(1)} %copy-done, f32[1,256,256]{2,1,0:T(8,128)S(1)} %maximum_bitcast_fusion.3, f32[1,256,256]{2,1,0:T(8,128)S(1)} %maximum_bitcast_fusion.2, ...), kind=kOutput, calls=%fused_computation.6 | convolution fusion | flops 538705920 | bytes 6291456 | tf_op jit(solution)/shard_map/dot_general | solution.py:20
  (89 shorter events, 1.5 us)
Async XLA Ops:
  7.9 15.0 %copy-start.7 = (f32[8,4,16,256]{3,2,1,0:T(8,128)S(1)}, f32[8,4,16,256]{3,2,1,0:T(8,128)}, u32[]{:S(2)}) copy-start(f32[8,4,16,256]{3,2,1,0:T(8,128)} %get-tuple-element.19) | copy-start | bytes 1572868
  7.9 11.8 %collective-permute-start.2 = (f32[2,8,6,16,128]{4,3,2,1,0:T(8,128)}, f32[2,8,6,16,128]{4,3,2,1,0:T(8,128)S(1)}, u32[]{:S(2)}, u32[]{:S(2)}) collective-permute-start(f32[2,8,6,16,128]{4,3,2,1,0:T(8,128)} %get-tuple-element.22), channel_id=1, source_target_pairs={{0,1},{1,0},{2,3},{3,2},{4,5},{5,4},{6,7},{7,6},{8,9},{9,8},{10,11... | collective-permute-start | bytes 2359304 | tf_op jit(solution)/shard_map/ppermute | solution.py:206
  12.9 24.5 %all-to-all-start.1 = ((f32[8,32,512]{2,1,0:T(8,128)}), f32[8,32,512]{2,1,0:T(8,128)S(1)}, u32[]{:S(2)}, u32[]{:S(2)}) async-start(f32[8,32,512]{2,1,0:T(8,128)} %pack.1), calls=%async_computation.1 | async-start | bytes 1048576 | tf_op jit(solution)/shard_map/all_to_all | solution.py:216
  19.3 21.5 %copy-start.6 = (f32[2,8,6,16,128]{4,3,2,1,0:T(8,128)S(1)}, f32[2,8,6,16,128]{4,3,2,1,0:T(8,128)}, u32[]{:S(2)}) copy-start(f32[2,8,6,16,128]{4,3,2,1,0:T(8,128)} %get-tuple-element.21) | copy-start | bytes 2359300
  19.3 3.5 %collective-permute-start = (f32[8,4,16,256]{3,2,1,0:T(8,128)}, f32[8,4,16,256]{3,2,1,0:T(8,128)S(1)}, u32[]{:S(2)}, u32[]{:S(2)}) collective-permute-start(f32[8,4,16,256]{3,2,1,0:T(8,128)} %get-tuple-element.20), channel_id=1, source_target_pairs={{0,1},{1,0},{2,3},{3,2},{4,5},{5,4},{6,7},{7,6},{8,9},{9,8},{10,11... | collective-permute-start | bytes 1572872 | tf_op jit(solution)/shard_map/ppermute | solution.py:206
  21.6 19.2 %collective-permute-start.3 = (f32[8,6,16,128]{3,2,1,0:T(8,128)}, f32[8,6,16,128]{3,2,1,0:T(8,128)S(1)}, u32[]{:S(2)}, u32[]{:S(2)}) collective-permute-start(f32[8,6,16,128]{3,2,1,0:T(8,128)} %fusion.9), channel_id=1, source_target_pairs={{0,16},{16,0},{1,17},{17,1},{2,18},{18,2},{3,19},{19,3},{4,20},{20... | collective-permute-start | bytes 1179656 | tf_op jit(solution)/shard_map/ppermute | solution.py:206
  37.3 38.8 %copy-start.1 = (f32[8,32,512]{2,1,0:T(8,128)}, f32[8,32,512]{2,1,0:T(8,128)S(1)}, u32[]{:S(2)}) copy-start(f32[8,32,512]{2,1,0:T(8,128)S(1)} %all-to-all-done.1.rows) | copy-start | bytes 1572868
  37.3 21.4 %all-to-all-start = ((f32[8,4,16,256]{3,2,1,0:T(8,128)}), f32[8,4,16,256]{3,2,1,0:T(8,128)S(1)}, u32[]{:S(2)}, u32[]{:S(2)}) async-start(f32[8,4,16,256]{3,2,1,0:T(8,128)} %add.45), calls=%async_computation | async-start | bytes 1048576 | tf_op jit(solution)/shard_map/all_to_all | solution.py:216
  41.0 6.2 %collective-permute-start.7 = (f32[8,2,16,128]{3,2,1,0:T(8,128)S(1)}, f32[8,2,16,128]{3,2,1,0:T(8,128)S(1)}, u32[]{:S(2)}, u32[]{:S(2)}) collective-permute-start(f32[8,2,16,128]{3,2,1,0:T(8,128)S(1)} %pad_maximum_fusion.3), channel_id=1, source_target_pairs={{0,32},{32,0},{1,33},{33,1},{2,34},{34,2},{3,35},{35,3},{4,36},{36... | collective-permute-start | bytes 393224 | tf_op jit(solution)/shard_map/ppermute | solution.py:206
  59.7 25.6 %all-to-all-start.2 = ((f32[8,176,128]{2,1,0:T(8,128)}), f32[8,176,128]{2,1,0:T(8,128)S(1)}, u32[]{:S(2)}, u32[]{:S(2)}) async-start(f32[8,176,128]{2,1,0:T(8,128)} %pad_maximum_fusion.1), calls=%async_computation.2 | async-start | bytes 1441792 | tf_op jit(solution)/shard_map/all_to_all | solution.py:216
  63.3 7.5 %collective-permute-start.5 = (f32[8,16,512]{2,1,0:T(8,128)S(1)}, f32[8,16,512]{2,1,0:T(8,128)S(1)}, u32[]{:S(2)}, u32[]{:S(2)}) collective-permute-start(f32[8,16,512]{2,1,0:T(8,128)S(1)} %slice.181), channel_id=1, source_target_pairs={{0,16},{16,0},{1,17},{17,1},{2,18},{18,2},{3,19},{19,3},{4,20},{20... | collective-permute-start | bytes 786440 | tf_op jit(solution)/shard_map/ppermute | solution.py:206
  70.8 10.3 %copy-start.3 = (f32[8,16,512]{2,1,0:T(8,128)}, f32[8,16,512]{2,1,0:T(8,128)S(1)}, u32[]{:S(2)}) copy-start(f32[8,16,512]{2,1,0:T(8,128)S(1)} %collective-permute-done.5.a) | copy-start | bytes 786436
  70.8 8.8 %collective-permute-start.16 = (f32[8,16,512]{2,1,0:T(8,128)S(1)}, f32[8,16,512]{2,1,0:T(8,128)S(1)}, u32[]{:S(2)}, u32[]{:S(2)}) collective-permute-start(f32[8,16,512]{2,1,0:T(8,128)S(1)} %pad_maximum_fusion.2), channel_id=1, source_target_pairs={{0,32},{32,0},{1,33},{33,1},{2,34},{34,2},{3,35},{35,3},{4,36},{36... | collective-permute-start | bytes 786440 | tf_op jit(solution)/shard_map/ppermute | solution.py:206
  73.8 5.8 %collective-permute-start.1 = (f32[16,256]{1,0:T(8,128)S(1)}, f32[16,256]{1,0:T(8,128)S(1)}, u32[]{:S(2)}, u32[]{:S(2)}) collective-permute-start(f32[16,256]{1,0:T(8,128)S(1)} %slice_bitcast_fusion.2), channel_id=1, source_target_pairs={{0,16},{16,0},{1,17},{17,1},{2,18},{18,2},{3,19},{19,3},{4,20},{20... | collective-permute-start | bytes 49160 | tf_op jit(solution)/shard_map/ppermute | solution.py:206
  74.2 6.8 %collective-permute-start.4 = (f32[8,32,512]{2,1,0:T(8,128)S(1)}, f32[8,32,512]{2,1,0:T(8,128)S(1)}, u32[]{:S(2)}, u32[]{:S(2)}) collective-permute-start(f32[8,32,512]{2,1,0:T(8,128)S(1)} %all-to-all-done.1.rows), channel_id=1, source_target_pairs={{0,1},{1,0},{2,3},{3,2},{4,5},{5,4},{6,7},{7,6},{8,9},{9,8},{10,11... | collective-permute-start | bytes 1572872 | tf_op jit(solution)/shard_map/ppermute | solution.py:206
  76.1 4.9 %collective-permute-start.6 = (f32[8,16,512]{2,1,0:T(8,128)S(1)}, f32[8,16,512]{2,1,0:T(8,128)S(1)}, u32[]{:S(2)}, u32[]{:S(2)}) collective-permute-start(f32[8,16,512]{2,1,0:T(8,128)S(1)} %collective-permute-done.5.a), channel_id=1, source_target_pairs={{0,1},{1,0},{2,3},{3,2},{4,5},{5,4},{6,7},{7,6},{8,9},{9,8},{10,11... | collective-permute-start | bytes 786440 | tf_op jit(solution)/shard_map/ppermute | solution.py:206
  79.6 11.0 %copy-start.10 = (f32[8,16,512]{2,1,0:T(8,128)}, f32[8,16,512]{2,1,0:T(8,128)S(1)}, u32[]{:S(2)}) copy-start(f32[8,16,512]{2,1,0:T(8,128)S(1)} %collective-permute-done.16.b) | copy-start | bytes 786436
  79.7 11.4 %collective-permute-start.18 = (f32[8,8,512]{2,1,0:T(8,128)S(1)}, f32[8,8,512]{2,1,0:T(8,128)S(1)}, u32[]{:S(2)}, u32[]{:S(2)}) collective-permute-start(f32[8,8,512]{2,1,0:T(8,128)S(1)} %pad_maximum_fusion.5), channel_id=1, source_target_pairs={{0,64},{64,0},{1,65},{65,1},{2,66},{66,2},{3,67},{67,3},{4,68},{68... | collective-permute-start | bytes 393224 | tf_op jit(solution)/shard_map/ppermute | solution.py:206
  81.0 0.7 copy-start.5
  81.8 0.8 copy-start.2
  85.4 3.7 %collective-permute-start.8 = (f32[8,96,128]{2,1,0:T(8,128)S(1)}, f32[8,96,128]{2,1,0:T(8,128)S(1)}, u32[]{:S(2)}, u32[]{:S(2)}) collective-permute-start(f32[8,96,128]{2,1,0:T(8,128)S(1)} %slice.239), channel_id=1, source_target_pairs={{0,1},{1,0},{2,3},{3,2},{4,5},{5,4},{6,7},{7,6},{8,9},{9,8},{10,11... | collective-permute-start | bytes 1179656 | tf_op jit(solution)/shard_map/ppermute | solution.py:206
  87.6 14.0 %copy-start.9 = (f32[256,512]{1,0:T(8,128)S(1)}, f32[256,512]{1,0:T(8,128)}, u32[]{:S(2)}) copy-start(f32[256,512]{1,0:T(8,128)} %get-tuple-element.26) | copy-start | bytes 1572868
  89.3 2.9 %collective-permute-start.9 = (f32[16,256]{1,0:T(8,128)S(1)}, f32[16,256]{1,0:T(8,128)S(1)}, u32[]{:S(2)}, u32[]{:S(2)}) collective-permute-start(f32[16,256]{1,0:T(8,128)S(1)} %convolution_subtract_fusion.2), channel_id=1, source_target_pairs={{0,16},{16,0},{1,17},{17,1},{2,18},{18,2},{3,19},{19,3},{4,20},{20... | collective-permute-start | bytes 49160 | tf_op jit(solution)/shard_map/ppermute | solution.py:206
  90.6 28.4 %collective-permute-start.17 = (f32[8,16,512]{2,1,0:T(8,128)S(1)}, f32[8,16,512]{2,1,0:T(8,128)S(1)}, u32[]{:S(2)}, u32[]{:S(2)}) collective-permute-start(f32[8,16,512]{2,1,0:T(8,128)S(1)} %collective-permute-done.16.b), channel_id=1, source_target_pairs={{0,1},{1,0},{2,3},{3,2},{4,5},{5,4},{6,7},{7,6},{8,9},{9,8},{10,11... | collective-permute-start | bytes 786440 | tf_op jit(solution)/shard_map/ppermute | solution.py:206
  91.1 27.9 %copy-start.12 = (f32[8,8,512]{2,1,0:T(8,128)}, f32[8,8,512]{2,1,0:T(8,128)S(1)}, u32[]{:S(2)}) copy-start(f32[8,8,512]{2,1,0:T(8,128)S(1)} %collective-permute-done.18.e) | copy-start | bytes 393220
  91.1 27.9 %collective-permute-start.19 = (f32[8,8,512]{2,1,0:T(8,128)S(1)}, f32[8,8,512]{2,1,0:T(8,128)S(1)}, u32[]{:S(2)}, u32[]{:S(2)}) collective-permute-start(f32[8,8,512]{2,1,0:T(8,128)S(1)} %collective-permute-done.18.e), channel_id=1, source_target_pairs={{0,1},{1,0},{2,3},{3,2},{4,5},{5,4},{6,7},{7,6},{8,9},{9,8},{10,11... | collective-permute-start | bytes 393224 | tf_op jit(solution)/shard_map/ppermute | solution.py:206
  92.1 9.4 %collective-permute-start.10 = (f32[16,256]{1,0:T(8,128)S(1)}, f32[16,256]{1,0:T(8,128)S(1)}, u32[]{:S(2)}, u32[]{:S(2)}) collective-permute-start(f32[16,256]{1,0:T(8,128)S(1)} %add.52), channel_id=1, source_target_pairs={{0,32},{32,0},{1,33},{33,1},{2,34},{34,2},{3,35},{35,3},{4,36},{36... | collective-permute-start | bytes 49160 | tf_op jit(solution)/shard_map/ppermute | solution.py:206
  95.2 15.0 %all-to-all-start.3 = ((f32[8,48,128]{2,1,0:T(8,128)}), f32[8,48,128]{2,1,0:T(8,128)S(1)}, u32[]{:S(2)}, u32[]{:S(2)}) async-start(f32[8,48,128]{2,1,0:T(8,128)} %broadcast_in_dim.10), calls=%async_computation.3 | async-start | bytes 393216 | tf_op jit(solution)/shard_map/all_to_all | solution.py:216
  110.2 4.1 %collective-permute-start.11 = (f32[8,48,128]{2,1,0:T(8,128)S(1)}, f32[8,48,128]{2,1,0:T(8,128)S(1)}, u32[]{:S(2)}, u32[]{:S(2)}) collective-permute-start(f32[8,48,128]{2,1,0:T(8,128)S(1)} %all-to-all-done.3), channel_id=1, source_target_pairs={{0,1},{1,0},{2,3},{3,2},{4,5},{5,4},{6,7},{7,6},{8,9},{9,8},{10,11... | collective-permute-start | bytes 589832 | tf_op jit(solution)/shard_map/ppermute | solution.py:206
  115.1 7.5 %collective-permute-start.12 = (f32[2,16,256]{2,1,0:T(8,128)S(1)}, f32[2,16,256]{2,1,0:T(8,128)S(1)}, u32[]{:S(2)}, u32[]{:S(2)}) collective-permute-start(f32[2,16,256]{2,1,0:T(8,128)S(1)} %pad_maximum_fusion.9), channel_id=1, source_target_pairs={{0,16},{16,0},{32,48},{48,32},{1,17},{17,1},{33,49},{49,33},{2,18}... | collective-permute-start | bytes 98312 | tf_op jit(solution)/shard_map/ppermute | solution.py:267
  115.5 7.0 %collective-permute-start.13 = (f32[2,16,256]{2,1,0:T(8,128)S(1)}, f32[2,16,256]{2,1,0:T(8,128)S(1)}, u32[]{:S(2)}, u32[]{:S(2)}) collective-permute-start(f32[2,16,256]{2,1,0:T(8,128)S(1)} %pad_maximum_fusion.9), channel_id=1, source_target_pairs={{0,32},{16,48},{32,0},{48,16},{1,33},{17,49},{33,1},{49,17},{2,34}... | collective-permute-start | bytes 98312 | tf_op jit(solution)/shard_map/ppermute | solution.py:267
  117.4 5.2 %collective-permute-start.14 = (f32[2,16,256]{2,1,0:T(8,128)S(1)}, f32[2,16,256]{2,1,0:T(8,128)S(1)}, u32[]{:S(2)}, u32[]{:S(2)}) collective-permute-start(f32[2,16,256]{2,1,0:T(8,128)S(1)} %pad_maximum_fusion.9), channel_id=1, source_target_pairs={{0,48},{16,32},{32,16},{48,0},{1,49},{17,33},{33,17},{49,1},{2,50}... | collective-permute-start | bytes 98312 | tf_op jit(solution)/shard_map/ppermute | solution.py:267
  119.0 0.7 copy-start.11
  119.0 0.7 copy-start.13
  122.6 12.1 %copy-start.8 = (f32[256,512]{1,0:T(8,128)S(1)}, f32[256,512]{1,0:T(8,128)}, u32[]{:S(2)}) copy-start(f32[256,512]{1,0:T(8,128)} %get-tuple-element.30) | copy-start | bytes 1572868
  122.6 2.7 %collective-permute-start.15 = (f32[16,256]{1,0:T(8,128)S(1)}, f32[16,256]{1,0:T(8,128)S(1)}, u32[]{:S(2)}, u32[]{:S(2)}) collective-permute-start(f32[16,256]{1,0:T(8,128)S(1)} %slice_bitcast_fusion.1), channel_id=1, source_target_pairs={{0,64},{64,0},{1,65},{65,1},{2,66},{66,2},{3,67},{67,3},{4,68},{68... | collective-permute-start | bytes 49160 | tf_op jit(solution)/shard_map/ppermute | solution.py:206
  123.0 4.2 %collective-permute-start.20 = (f32[256,128]{1,0:T(8,128)S(1)}, f32[256,128]{1,0:T(8,128)S(1)}, u32[]{:S(2)}, u32[]{:S(2)}) collective-permute-start(f32[256,128]{1,0:T(8,128)S(1)} %pad_maximum_fusion.6), channel_id=1, source_target_pairs={{0,16},{16,0},{1,17},{17,1},{2,18},{18,2},{3,19},{19,3},{4,20},{20... | collective-permute-start | bytes 393224 | tf_op jit(solution)/shard_map/ppermute | solution.py:206
  127.3 3.9 %collective-permute-start.21 = (f32[16,256]{1,0:T(8,128)S(1)}, f32[16,256]{1,0:T(8,128)S(1)}, u32[]{:S(2)}, u32[]{:S(2)}) collective-permute-start(f32[16,256]{1,0:T(8,128)S(1)} %fusion.62), channel_id=1, source_target_pairs={{0,64},{64,0},{128,192},{192,128},{1,65},{65,1},{129,193},{193,129... | collective-permute-start | bytes 49160 | tf_op jit(solution)/shard_map/ppermute | solution.py:267
  128.3 4.1 %collective-permute-start.22 = (f32[16,256]{1,0:T(8,128)S(1)}, f32[16,256]{1,0:T(8,128)S(1)}, u32[]{:S(2)}, u32[]{:S(2)}) collective-permute-start(f32[16,256]{1,0:T(8,128)S(1)} %fusion.62), channel_id=1, source_target_pairs={{0,128},{64,192},{128,0},{192,64},{1,129},{65,193},{129,1},{193,65... | collective-permute-start | bytes 49160 | tf_op jit(solution)/shard_map/ppermute | solution.py:267
  130.8 3.8 %collective-permute-start.23 = (f32[16,256]{1,0:T(8,128)S(1)}, f32[16,256]{1,0:T(8,128)S(1)}, u32[]{:S(2)}, u32[]{:S(2)}) collective-permute-start(f32[16,256]{1,0:T(8,128)S(1)} %fusion.62), channel_id=1, source_target_pairs={{0,192},{64,128},{128,64},{192,0},{1,193},{65,129},{129,65},{193,1... | collective-permute-start | bytes 49160 | tf_op jit(solution)/shard_map/ppermute | solution.py:267
  150.4 7.3 %copy-start = (bf16[4,1024,256]{2,1,0:T(8,128)(2,1)S(1)}, bf16[4,1024,256]{2,1,0:T(8,128)(2,1)}, u32[]{:S(2)}) copy-start(bf16[4,1024,256]{2,1,0:T(8,128)(2,1)} %w_hbm.1) | copy-start | bytes 6291460
  150.4 7.0 %collective-permute-start.24 = (f32[8,64,256]{2,1,0:T(8,128)S(1)}, f32[8,64,256]{2,1,0:T(8,128)S(1)}, u32[]{:S(2)}, u32[]{:S(2)}) collective-permute-start(f32[8,64,256]{2,1,0:T(8,128)S(1)} %all_to_all.25), channel_id=1, source_target_pairs={{0,1},{1,0},{2,3},{3,2},{4,5},{5,4},{6,7},{7,6},{8,9},{9,8},{10,11... | collective-permute-start | bytes 1572872 | tf_op jit(solution)/shard_map/ppermute | solution.py:206
  157.6 1.2 copy-start.4

commit v6 on v5

--- a/solution.py
+++ b/solution.py
@@ -11,7 +11,6 @@
 STEPS = 4
 F32 = jnp.float32
 BF16 = jnp.bfloat16
-PAIRS = ((3, 4), (2, 4), (1, 4), (2, 3), (1, 3), (1, 2))
 DIRECT = (4, (3, 4), (2, 4), (1, 4))
 SHARED = (3, (2, 3), (1, 3), 2, 1, (1, 2))
 
@@ -41,7 +40,7 @@
 
 def leaf_kernel(
     core_ref, pair_ref, inv_hbm, rhs_hbm, v_hbm, w_hbm, x_hbm, keep_hbm, give_hbm, keep_shared_hbm, give_shared_hbm,
-    x_ref, keep_ref, give_ref, keep_shared_ref, give_shared_ref, inv_ref, rhs_ref, v_ref, w_ref, high_ref, low_ref, sems,
+    x_ref, keep_ref, give_ref, keep_shared_ref, give_shared_ref, inv_ref, rhs_ref, v_ref, w_ref, left_ref, split_ref, sems,
 ):
     rows = 1024 // STEPS
     count = [0]
@@ -93,13 +92,16 @@
             done.add((id(waits), level))
             waits[level].wait()
 
-    turned = {}
-    for j, k in PAIRS:
-        ready(wait_w, k)
-        if k not in turned:
-            turned[k] = w_ref[k - 2].T
+    for j in (3, 2, 1):
+        for k in range(4, j, -1):
+            if ("turned", k) not in done:
+                done.add(("turned", k))
+                ready(wait_w, k)
+                left_ref[pl.ds(256 * (k - 2), 256), :] = w_ref[k - 2].T
         ready(wait_v, j)
-        store((j, k), dot(turned[k], v_ref[j - 1], ((1,), (0,))))
+        value = dot(left_ref[pl.ds(256 * (j - 1), 256 * (4 - j)), :], v_ref[j - 1], ((1,), (0,)))
+        for k in range(j + 1, 5):
+            store((j, k), value[256 * (k - j - 1) : 256 * (k - j)])
     wait_rhs.wait()
     rhs = rhs_ref[...]
     rhs_turned = rhs.T
@@ -110,12 +112,13 @@
         stores.append(load(x_ref.at[part], x_hbm.at[part]))
         xt = dot(rhs_turned, inv, ((1,), (1,)))
         high = xt.astype(BF16)
-        high_ref[:, part] = high
-        low_ref[:, part] = (xt - high.astype(F32)).astype(BF16)
+        split_ref[0:256, part] = high
+        split_ref[256:512, part] = (xt - high.astype(F32)).astype(BF16)
     for j in (4, 3, 2, 1):
         ready(wait_v, j)
         v = v_ref[j - 1]
-        store(j, dot(high_ref[...], v, ((1,), (0,))) + dot(low_ref[...], v, ((1,), (0,))))
+        both = dot(split_ref[...], v, ((1,), (0,)))
+        store(j, both[:256] + both[256:])
     for copy in stores:
         copy.wait()
 
@@ -135,8 +138,8 @@
             pltpu.VMEM((1024, 256), BF16),
             pltpu.VMEM((4, 1024, 256), BF16),
             pltpu.VMEM((3, 1024, 256), BF16),
-            pltpu.VMEM((256, 1024), BF16),
-            pltpu.VMEM((256, 1024), BF16),
+            pltpu.VMEM((768, 1024), BF16),
+            pltpu.VMEM((512, 1024), BF16),
             pltpu.SemaphoreType.DMA((28 + 2 * STEPS,)),
         ],
         name="leaf",
@@ -158,7 +161,7 @@
         low, high = pair(core_ref, rows[z, 0:16], rows_c[z, 0:16])
         k4_ref[32 * z : 32 * z + 16] = low
         k4_ref[32 * z + 16 : 32 * z + 32] = high
-        for t, own, other in ((near, rows[z, 16:24], rows_c[z, 16:24]), (far, a[z, 0:8], a_c[z, 0:8])):
+        for t, own, other in ((near, rows[z, 16:24], rows_c[z, 16:24]), (far, a[z], a_c[z])):
             both = jnp.concatenate(pair(core_ref, own, other), axis=0)
             k3_ref[pl.ds(pl.multiple_of(128 * t + 16 * z, 16), 16)] = both
 
@@ -173,16 +176,16 @@
 
     for z in range(Z):
         for t, own, other in (
-            (up + near, rows[z, 24:28], rows_c[z, 24:28]),
-            (up + far, a[z, 8:12], a_c[z, 8:12]),
+            (up + near, rows[z, 0:4], rows_c[z, 0:4]),
+            (up + far, a[z, 0:4], a_c[z, 0:4]),
             (down + near, b[z, 0:4], b_c[z, 0:4]),
             (down + far, b[z, 8:12], b_c[z, 8:12]),
         ):
             k2_ref[pl.ds(pl.multiple_of(64 * t + 8 * z, 8), 8)] = both(own, other)
     for z in range(0, Z, 2):
         for t, (own, other, row) in (
-            (left + up + near, (rows, rows_c, 28)),
-            (left + up + far, (a, a_c, 12)),
+            (left + up + near, (rows, rows_c, 4)),
+            (left + up + far, (a, a_c, 4)),
             (left + down + near, (b, b_c, 4)),
             (left + down + far, (b, b_c, 12)),
             (right + up + near, (e, e_c, 0)),
@@ -194,10 +197,14 @@
             k1_ref[pl.ds(pl.multiple_of(32 * t + 4 * z, 8), 8)] = jnp.concatenate(tile, axis=0)
 
 
-def assemble(kernel, scalars, pieces):
+def assemble(kernel, scalars, pieces, blocks):
+    specs = [pl.BlockSpec((Z, count, 512), lambda i, index=index: (0, index, 0)) for count, index in blocks]
+    full = pl.BlockSpec((256, 512), lambda i: (0, 0))
     return pl.pallas_call(
         kernel,
-        in_specs=[pl.BlockSpec(memory_space=pltpu.SMEM)] * len(scalars) + [pl.BlockSpec()] * len(pieces),
+        grid=(1,),
+        in_specs=[pl.BlockSpec(memory_space=pltpu.SMEM)] * len(scalars) + specs,
+        out_specs=[full, full],
         out_shape=[jax.ShapeDtypeStruct((256, 512), F32)] * 2,
     )(*[scalar.reshape(1) for scalar in scalars], *pieces)
 
@@ -251,9 +258,11 @@
     e1 = partner(e0, "xl")
     e1_c = partner(e1, "c")
     pieces = [rows, rows_c, a1, a1_c]
-    full4, full3 = assemble(fine_kernel, [core, at["yl"]], pieces)
+    full4, full3 = assemble(fine_kernel, [core, at["yl"]], pieces, [(32, 0)] * 2 + [(8, 0)] * 2)
     scalars = [at[axis] for axis in ("c", "yl", "yh", "xl")]
-    full2, full1 = assemble(coarse_kernel, scalars, pieces + [b1, b1_c, e1, e1_c])
+    full2, full1 = assemble(
+        coarse_kernel, scalars, pieces + [b1, b1_c, e1, e1_c], [(8, 3)] * 2 + [(8, 1)] * 2 + [(16, 0)] * 2 + [(8, 0)] * 2
+    )
 
     def both_cores(own, other, first, count):
         own = own[:, first : first + count].reshape(Z * count, -1)
@@ -264,8 +273,10 @@
         return fdot(ordered(at[axis], own, other, 1), k, ((1,), (1,)))
 
     def of_four(block, axes):
-        far, near, last = [lax.ppermute(block, axes, [(i, i ^ k) for i in range(4)]) for k in (2, 1, 3)]
-        return [block, near, far, last]
+        got = {}
+        for k in (2, 1, 3):
+            got[k] = lax.ppermute(block, axes, [(i, i ^ k) for i in range(4)])
+        return [block, got[1], got[2], got[3]]
 
     def times(m, g):
         return fdot(m, g, ((1,), (0,)))
@@ -304,7 +315,8 @@
     other = partner(own, "c")
     g23, g13 = both_cores(own, other, 0, 16), both_cores(own, other, 16, 16)
     half = both_cores(own, other, 32, 16)
-    g12 = ordered(at["yl"], half, partner(half, "yl"), 1)
+    got = partner(half, "yl")
+    g12 = ordered(at["yl"], half, got, 1)
     t = jnp.stack([t2 - in_lanes(times(m3, g23)), t1 - in_lanes(times(m3, g13))])
     four = of_four(t, ("yh", "yl"))
     t = (four[0] + four[1]) + (four[2] + four[3])

time: 161 us -> 161 us (level)
  no operation moved by 1% of the time
where the time goes in v6:
time: 161 us
  starting transfers between devices  59.1 us (37%)
  waiting for transfers between devices  56 us (35%)
  blocking collectives  15.4 us (10%)
  Pallas kernels  14.9 us (9%)
  matrix products  6.79 us (4%)
  other arithmetic  4.37 us (3%)
  local copies, waits for them, and re-layouts  3.66 us (2%)
    all_to_all x4, waiting for transfers between devices, exchange(): return lax.all_to_all(block, axes, 0, 0, tiled=True)  33.9 us
    ppermute x19, starting transfers between devices, partner(): return lax.ppermute(block, axis, [(0, 1), (1, 0)])  31.4 us
    all_to_all x4, starting transfers between devices, exchange(): return lax.all_to_all(block, axes, 0, 0, tiled=True)  19.8 us
    ppermute x19, waiting for transfers between devices, partner(): return lax.ppermute(block, axis, [(0, 1), (1, 0)])  18.8 us
    all_to_all x1, blocking collectives, exchange(): return lax.all_to_all(block, axes, 0, 0, tiled=True)  15.4 us
    pallas_call x1, Pallas kernels, leaf(): pl.pallas_call(leaf_kernel, in_specs=[pl.BlockSpec(memory_space=pltpu.SME...  8.42 us
    ppermute x6, starting transfers between devices, of_four(): got[k] = lax.ppermute(block, axes, [(i, i ^ k) for i in range(4)])  7.89 us
    pallas_call x2, Pallas kernels, assemble(): pl.pallas_call(kernel, grid=(1,), in_specs=[pl.BlockSpec(memory_space=plt...  4.86 us
  transfers between devices with their start and end apart: 29, of which 14 were waited for; matrix products, arithmetic and copies ran while one was open for 5% of the time, Pallas kernels for 4%

profile of v6, /device:TPU:1, one launch (start us, length us, event | category | flops | bytes accessed | tf_op | source)
XLA Modules:
  0.0 160.7 jit_solution(14004651925553124071)
XLA Ops:
  0.0 8.4 %leaf.1 = (f32[1024,256]{1,0:T(8,128)}, f32[8,4,16,256]{3,2,1,0:T(8,128)}, f32[8,4,16,256]{3,2,1,0:T(8,128)}, f32[2,8,6,16,128]{4,3,2,1,0:T(8,128)}, f32[2,8,6,16,128]{4,3,2,1,0:T(8,128)}) custom-call(s32[1]{0:T(128)} %bitcast.core_ref, s32[1]{0:T(128)} %bitcast.1.pair_ref.yl_ref, bf16[1024,1024]{1,0:T(8,128)(2,1)} %inv_hbm.1, bf16[1024,256]{1,0:T(8,128)(2,1)} %rhs_hbm.1, ...), custom_call_target="tpu_custom_call" | custom-call | tf_op jit(solution)/shard_map/leaf/pallas_call | solution.py:130
  8.4 3.3 %collective-permute-start.2 = (f32[2,8,6,16,128]{4,3,2,1,0:T(8,128)}, f32[2,8,6,16,128]{4,3,2,1,0:T(8,128)S(1)}, u32[]{:S(2)}, u32[]{:S(2)}) collective-permute-start(f32[2,8,6,16,128]{4,3,2,1,0:T(8,128)} %get-tuple-element.22), channel_id=1, source_target_pairs={{0,1},{1,0},{2,3},{3,2},{4,5},{5,4},{6,7},{7,6},{8,9},{9,8},{10,11... | collective-permute-start | bytes 2359304 | tf_op jit(solution)/shard_map/ppermute | solution.py:213
  11.7 1.6 %pack.1 = f32[8,32,512]{2,1,0:T(8,128)} custom-call(f32[16,512]{1,0:T(8,128)} %a_ref.1, f32[8,512]{1,0:T(8,128)} %b_ref.1, f32[4,512]{1,0:T(4,128)} %c_ref.1, f32[2,512]{1,0:T(2,128)} %d_ref.1), custom_call_target="tpu_custom_call" | custom-call | tf_op jit(solution)/shard_map/pack/pallas_call | solution.py:38
  13.4 6.5 %all-to-all-start.1 = ((f32[8,32,512]{2,1,0:T(8,128)}), f32[8,32,512]{2,1,0:T(8,128)S(1)}, u32[]{:S(2)}, u32[]{:S(2)}) async-start(f32[8,32,512]{2,1,0:T(8,128)} %pack.1), calls=%async_computation.1 | async-start | bytes 1048576 | tf_op jit(solution)/shard_map/all_to_all | solution.py:223
  19.8 0.4 collective-permute-start
  20.3 1.8 %fusion.9 = f32[8,6,16,128]{3,2,1,0:T(8,128)} fusion(f32[2,8,6,16,128]{4,3,2,1,0:T(8,128)S(1)} %collective-permute-done.2, f32[2,8,6,16,128]{4,3,2,1,0:T(8,128)} %get-tuple-element.21), kind=kLoop, calls=%fused_computation.18 | loop fusion | flops 98304 | bytes 1179648 | tf_op jit(solution)/shard_map/add | solution.py:240
  22.1 1.3 collective-permute-start.3
  23.4 0.9 add.45
  24.3 13.5 %all-to-all-done.1.rows = f32[8,32,512]{2,1,0:T(8,128)S(1)} async-done(((f32[8,32,512]{2,1,0:T(8,128)}), f32[8,32,512]{2,1,0:T(8,128)S(1)}, u32[]{:S(2)}, u32[]{:S(2)}) %all-to-all-start.1) | async-done | bytes 524320 | tf_op jit(solution)/shard_map/all_to_all | solution.py:223
  37.8 3.5 %all-to-all-start = ((f32[8,4,16,256]{3,2,1,0:T(8,128)}), f32[8,4,16,256]{3,2,1,0:T(8,128)S(1)}, u32[]{:S(2)}, u32[]{:S(2)}) async-start(f32[8,4,16,256]{3,2,1,0:T(8,128)} %add.45), calls=%async_computation | async-start | bytes 1048576 | tf_op jit(solution)/shard_map/all_to_all | solution.py:223
  41.5 3.0 %collective-permute-start.7 = (f32[8,2,16,128]{3,2,1,0:T(8,128)S(1)}, f32[8,2,16,128]{3,2,1,0:T(8,128)S(1)}, u32[]{:S(2)}, u32[]{:S(2)}) collective-permute-start(f32[8,2,16,128]{3,2,1,0:T(8,128)S(1)} %pad_maximum_fusion.3), channel_id=1, source_target_pairs={{0,32},{32,0},{1,33},{33,1},{2,34},{34,2},{3,35},{35,3},{4,36},{36... | collective-permute-start | bytes 393224 | tf_op jit(solution)/shard_map/ppermute | solution.py:213
  44.5 3.2 %collective-permute-done.7 = f32[8,2,16,128]{3,2,1,0:T(8,128)S(1)} collective-permute-done((f32[8,2,16,128]{3,2,1,0:T(8,128)S(1)}, f32[8,2,16,128]{3,2,1,0:T(8,128)S(1)}, u32[]{:S(2)}, u32[]{:S(2)}) %collective-permute-start.7) | collective-permute-done | bytes 131104 | tf_op jit(solution)/shard_map/ppermute | solution.py:213
  47.7 11.5 %all-to-all-done = f32[8,4,16,256]{3,2,1,0:T(8,128)S(1)} async-done(((f32[8,4,16,256]{3,2,1,0:T(8,128)}), f32[8,4,16,256]{3,2,1,0:T(8,128)S(1)}, u32[]{:S(2)}, u32[]{:S(2)}) %all-to-all-start) | async-done | bytes 524320 | tf_op jit(solution)/shard_map/all_to_all | solution.py:223
  59.3 0.9 pad_maximum_fusion.1
  60.2 3.5 %all-to-all-start.2 = ((f32[8,176,128]{2,1,0:T(8,128)}), f32[8,176,128]{2,1,0:T(8,128)S(1)}, u32[]{:S(2)}, u32[]{:S(2)}) async-start(f32[8,176,128]{2,1,0:T(8,128)} %pad_maximum_fusion.1), calls=%async_computation.2 | async-start | bytes 1441792 | tf_op jit(solution)/shard_map/all_to_all | solution.py:223
  63.8 1.4 collective-permute-start.5
  65.2 6.1 %collective-permute-done.5.a = f32[8,16,512]{2,1,0:T(8,128)S(1)} collective-permute-done((f32[8,16,512]{2,1,0:T(8,128)S(1)}, f32[8,16,512]{2,1,0:T(8,128)S(1)}, u32[]{:S(2)}, u32[]{:S(2)}) %collective-permute-start.5) | collective-permute-done | bytes 262176 | tf_op jit(solution)/shard_map/ppermute | solution.py:213
  71.3 3.0 %collective-permute-start.16 = (f32[8,16,512]{2,1,0:T(8,128)S(1)}, f32[8,16,512]{2,1,0:T(8,128)S(1)}, u32[]{:S(2)}, u32[]{:S(2)}) collective-permute-start(f32[8,16,512]{2,1,0:T(8,128)S(1)} %pad_maximum_fusion.2), channel_id=1, source_target_pairs={{0,32},{32,0},{1,33},{33,1},{2,34},{34,2},{3,35},{35,3},{4,36},{36... | collective-permute-start | bytes 786440 | tf_op jit(solution)/shard_map/ppermute | solution.py:213
  74.3 0.4 collective-permute-start.1
  74.7 1.9 %collective-permute-start.4 = (f32[8,32,512]{2,1,0:T(8,128)S(1)}, f32[8,32,512]{2,1,0:T(8,128)S(1)}, u32[]{:S(2)}, u32[]{:S(2)}) collective-permute-start(f32[8,32,512]{2,1,0:T(8,128)S(1)} %all-to-all-done.1.rows), channel_id=1, source_target_pairs={{0,1},{1,0},{2,3},{3,2},{4,5},{5,4},{6,7},{7,6},{8,9},{9,8},{10,11... | collective-permute-start | bytes 1572872 | tf_op jit(solution)/shard_map/ppermute | solution.py:213
  76.8 3.4 %collective-permute-done.1 = f32[16,256]{1,0:T(8,128)S(1)} collective-permute-done((f32[16,256]{1,0:T(8,128)S(1)}, f32[16,256]{1,0:T(8,128)S(1)}, u32[]{:S(2)}, u32[]{:S(2)}) %collective-permute-start.1) | collective-permute-done | bytes 16416 | tf_op jit(solution)/shard_map/ppermute | solution.py:213
  80.2 1.3 collective-permute-start.18
  81.6 0.7 copy-done.5
  82.3 0.8 copy-done.2
  83.1 2.3 %shard_map.82 = (f32[256,512]{1,0:T(8,128)}, f32[256,512]{1,0:T(8,128)}) custom-call(s32[1]{0:T(128)} %bitcast.core_ref, s32[1]{0:T(128)} %bitcast.1.pair_ref.yl_ref, f32[8,32,512]{2,1,0:T(8,128)} %copy-done.1, f32[8,32,512]{2,1,0:T(8,128)} %copy-done.2, f32[8,16,512]{2,1,0:T(8,128)} %copy-done.3, f32[8,16,512]{2,1,0:T(8,128)} %copy-done.5), custom_call_target="tpu_custom_call" | custom-call | tf_op jit(solution)/shard_map/pallas_call | solution.py:203
  85.4 0.5 all-to-all-done.2
  85.9 2.1 %collective-permute-start.8 = (f32[8,96,128]{2,1,0:T(8,128)S(1)}, f32[8,96,128]{2,1,0:T(8,128)S(1)}, u32[]{:S(2)}, u32[]{:S(2)}) collective-permute-start(f32[8,96,128]{2,1,0:T(8,128)S(1)} %slice.239), channel_id=1, source_target_pairs={{0,1},{1,0},{2,3},{3,2},{4,5},{5,4},{6,7},{7,6},{8,9},{9,8},{10,11... | collective-permute-start | bytes 1179656 | tf_op jit(solution)/shard_map/ppermute | solution.py:213
  88.0 1.4 fusion.46
  89.6 0.1 convolution_subtract_fusion.2
  89.7 1.3 collective-permute-start.9
  91.0 0.5 collective-permute-start.17
  91.7 0.9 collective-permute-done.9
  92.6 2.4 %collective-permute-start.10 = (f32[16,256]{1,0:T(8,128)S(1)}, f32[16,256]{1,0:T(8,128)S(1)}, u32[]{:S(2)}, u32[]{:S(2)}) collective-permute-start(f32[16,256]{1,0:T(8,128)S(1)} %add.52), channel_id=1, source_target_pairs={{0,32},{32,0},{1,33},{33,1},{2,34},{34,2},{3,35},{35,3},{4,36},{36... | collective-permute-start | bytes 49160 | tf_op jit(solution)/shard_map/ppermute | solution.py:213
  94.9 0.7 broadcast_in_dim.10
  95.6 6.3 %all-to-all-start.3 = ((f32[8,48,128]{2,1,0:T(8,128)}), f32[8,48,128]{2,1,0:T(8,128)S(1)}, u32[]{:S(2)}, u32[]{:S(2)}) async-start(f32[8,48,128]{2,1,0:T(8,128)} %broadcast_in_dim.10), calls=%async_computation.3 | async-start | bytes 393216 | tf_op jit(solution)/shard_map/all_to_all | solution.py:223
  102.0 0.3 fusion.50
  102.3 8.4 %all-to-all-done.3 = f32[8,48,128]{2,1,0:T(8,128)S(1)} async-done(((f32[8,48,128]{2,1,0:T(8,128)}), f32[8,48,128]{2,1,0:T(8,128)S(1)}, u32[]{:S(2)}, u32[]{:S(2)}) %all-to-all-start.3) | async-done | bytes 196640 | tf_op jit(solution)/shard_map/all_to_all | solution.py:223
  110.7 3.0 %collective-permute-start.11 = (f32[8,48,128]{2,1,0:T(8,128)S(1)}, f32[8,48,128]{2,1,0:T(8,128)S(1)}, u32[]{:S(2)}, u32[]{:S(2)}) collective-permute-start(f32[8,48,128]{2,1,0:T(8,128)S(1)} %all-to-all-done.3), channel_id=1, source_target_pairs={{0,1},{1,0},{2,3},{3,2},{4,5},{5,4},{6,7},{7,6},{8,9},{9,8},{10,11... | collective-permute-start | bytes 589832 | tf_op jit(solution)/shard_map/ppermute | solution.py:213
  113.7 1.1 collective-permute-done.11
  114.8 0.2 broadcast_select_fusion.13
  114.9 0.2 broadcast_select_fusion.11
  115.1 0.2 fusion.6
  115.2 0.2 fusion.4
  115.5 0.5 collective-permute-start.12
  116.0 1.9 %collective-permute-start.13 = (f32[2,16,256]{2,1,0:T(8,128)S(1)}, f32[2,16,256]{2,1,0:T(8,128)S(1)}, u32[]{:S(2)}, u32[]{:S(2)}) collective-permute-start(f32[2,16,256]{2,1,0:T(8,128)S(1)} %pad_maximum_fusion.9), channel_id=1, source_target_pairs={{0,32},{16,48},{32,0},{48,16},{1,33},{17,49},{33,1},{49,17},{2,34}... | collective-permute-start | bytes 98312 | tf_op jit(solution)/shard_map/ppermute | solution.py:278
  117.8 1.6 collective-permute-start.14
  119.4 0.7 copy-done.11
  120.2 2.5 %shard_map.83 = (f32[256,512]{1,0:T(8,128)}, f32[256,512]{1,0:T(8,128)}) custom-call(s32[1]{0:T(128)} %bitcast.core_ref, s32[1]{0:T(128)} %bitcast.1.pair_ref.yl_ref, s32[1]{0:T(128)} %bitcast.29.yh_ref, s32[1]{0:T(128)} %bitcast.30.xl_ref, f32[8,32,512]{2,1,0:T(8,128)} %copy-done.1, f32[8,32,512]{2,1,0:T(8,128)} %copy-done.2, f32[8,16,512]{2,1,0:T(8,128)} %copy-done.3, ...), custom_call_target="tpu_custom_call" | custom-call | tf_op jit(solution)/shard_map/pallas_call | solution.py:203
  122.8 0.3 collective-permute-start.15
  123.2 2.2 %collective-permute-done.15 = f32[16,256]{1,0:T(8,128)S(1)} collective-permute-done((f32[16,256]{1,0:T(8,128)S(1)}, f32[16,256]{1,0:T(8,128)S(1)}, u32[]{:S(2)}, u32[]{:S(2)}) %collective-permute-start.15) | collective-permute-done | bytes 16416 | tf_op jit(solution)/shard_map/ppermute | solution.py:213
  125.5 1.3 fusion.54
  126.8 0.5 collective-permute-done.20
  127.5 1.0 collective-permute-start.21
  128.5 2.5 %collective-permute-start.22 = (f32[16,256]{1,0:T(8,128)S(1)}, f32[16,256]{1,0:T(8,128)S(1)}, u32[]{:S(2)}, u32[]{:S(2)}) collective-permute-start(f32[16,256]{1,0:T(8,128)S(1)} %fusion.62), channel_id=1, source_target_pairs={{0,128},{64,192},{128,0},{192,64},{1,129},{65,193},{129,1},{193,65... | collective-permute-start | bytes 49160 | tf_op jit(solution)/shard_map/ppermute | solution.py:278
  131.0 0.5 collective-permute-start.23
  131.5 1.1 collective-permute-done.22
  132.6 2.2 %collective-permute-done.23 = f32[16,256]{1,0:T(8,128)S(1)} collective-permute-done((f32[16,256]{1,0:T(8,128)S(1)}, f32[16,256]{1,0:T(8,128)S(1)}, u32[]{:S(2)}, u32[]{:S(2)}) %collective-permute-start.23) | collective-permute-done | bytes 16416 | tf_op jit(solution)/shard_map/ppermute | solution.py:278
  134.8 0.3 fusion.58
  135.2 15.4 %all_to_all.25 = f32[8,64,256]{2,1,0:T(8,128)S(1)} all-to-all(f32[8,64,256]{2,1,0:T(8,128)S(1)} %broadcast_in_dim.11), channel_id=1, replica_groups=mesh['xh'=2,'xl'=2,'yh'=2,'yl'=2,'z'=8,'c'=2] {'z'}, dimensions={0} | all-to-all | bytes 1048576 | tf_op jit(solution)/shard_map/all_to_all | solution.py:223
  150.5 5.5 %collective-permute-start.24 = (f32[8,64,256]{2,1,0:T(8,128)S(1)}, f32[8,64,256]{2,1,0:T(8,128)S(1)}, u32[]{:S(2)}, u32[]{:S(2)}) collective-permute-start(f32[8,64,256]{2,1,0:T(8,128)S(1)} %all_to_all.25), channel_id=1, source_target_pairs={{0,1},{1,0},{2,3},{3,2},{4,5},{5,4},{6,7},{7,6},{8,9},{9,8},{10,11... | collective-permute-start | bytes 1572872 | tf_op jit(solution)/shard_map/ppermute | solution.py:213
  156.0 1.5 collective-permute-done.24
  157.8 0.7 convolution_bitcast_fusion
  158.6 0.5 copy-done.4
  159.0 1.7 %fusion.2 = f32[1024,256]{1,0:T(8,128)} fusion(f32[1024,256]{1,0:T(8,128)S(1)} %copy-done.4, f32[256,1024]{0,1:T(8,128)S(1)} %convolution_bitcast_fusion, bf16[4,1024,256]{2,1,0:T(8,128)(2,1)S(1)} %copy-done, f32[1,256,256]{2,1,0:T(8,128)S(1)} %maximum_bitcast_fusion.3, f32[1,256,256]{2,1,0:T(8,128)S(1)} %maximum_bitcast_fusion.2, ...), kind=kOutput, calls=%fused_computation.6 | convolution fusion | flops 538705920 | bytes 6291456 | tf_op jit(solution)/shard_map/dot_general | solution.py:19
  (89 shorter events, 1.5 us)
Async XLA Ops:
  8.4 15.0 %copy-start.7 = (f32[8,4,16,256]{3,2,1,0:T(8,128)S(1)}, f32[8,4,16,256]{3,2,1,0:T(8,128)}, u32[]{:S(2)}) copy-start(f32[8,4,16,256]{3,2,1,0:T(8,128)} %get-tuple-element.19) | copy-start | bytes 1572868
  8.4 11.8 %collective-permute-start.2 = (f32[2,8,6,16,128]{4,3,2,1,0:T(8,128)}, f32[2,8,6,16,128]{4,3,2,1,0:T(8,128)S(1)}, u32[]{:S(2)}, u32[]{:S(2)}) collective-permute-start(f32[2,8,6,16,128]{4,3,2,1,0:T(8,128)} %get-tuple-element.22), channel_id=1, source_target_pairs={{0,1},{1,0},{2,3},{3,2},{4,5},{5,4},{6,7},{7,6},{8,9},{9,8},{10,11... | collective-permute-start | bytes 2359304 | tf_op jit(solution)/shard_map/ppermute | solution.py:213
  13.4 24.5 %all-to-all-start.1 = ((f32[8,32,512]{2,1,0:T(8,128)}), f32[8,32,512]{2,1,0:T(8,128)S(1)}, u32[]{:S(2)}, u32[]{:S(2)}) async-start(f32[8,32,512]{2,1,0:T(8,128)} %pack.1), calls=%async_computation.1 | async-start | bytes 1048576 | tf_op jit(solution)/shard_map/all_to_all | solution.py:223
  19.8 21.5 %copy-start.6 = (f32[2,8,6,16,128]{4,3,2,1,0:T(8,128)S(1)}, f32[2,8,6,16,128]{4,3,2,1,0:T(8,128)}, u32[]{:S(2)}) copy-start(f32[2,8,6,16,128]{4,3,2,1,0:T(8,128)} %get-tuple-element.21) | copy-start | bytes 2359300
  19.8 3.5 %collective-permute-start = (f32[8,4,16,256]{3,2,1,0:T(8,128)}, f32[8,4,16,256]{3,2,1,0:T(8,128)S(1)}, u32[]{:S(2)}, u32[]{:S(2)}) collective-permute-start(f32[8,4,16,256]{3,2,1,0:T(8,128)} %get-tuple-element.20), channel_id=1, source_target_pairs={{0,1},{1,0},{2,3},{3,2},{4,5},{5,4},{6,7},{7,6},{8,9},{9,8},{10,11... | collective-permute-start | bytes 1572872 | tf_op jit(solution)/shard_map/ppermute | solution.py:213
  22.1 19.2 %collective-permute-start.3 = (f32[8,6,16,128]{3,2,1,0:T(8,128)}, f32[8,6,16,128]{3,2,1,0:T(8,128)S(1)}, u32[]{:S(2)}, u32[]{:S(2)}) collective-permute-start(f32[8,6,16,128]{3,2,1,0:T(8,128)} %fusion.9), channel_id=1, source_target_pairs={{0,16},{16,0},{1,17},{17,1},{2,18},{18,2},{3,19},{19,3},{4,20},{20... | collective-permute-start | bytes 1179656 | tf_op jit(solution)/shard_map/ppermute | solution.py:213
  37.8 38.8 %copy-start.1 = (f32[8,32,512]{2,1,0:T(8,128)}, f32[8,32,512]{2,1,0:T(8,128)S(1)}, u32[]{:S(2)}) copy-start(f32[8,32,512]{2,1,0:T(8,128)S(1)} %all-to-all-done.1.rows) | copy-start | bytes 1572868
  37.8 21.4 %all-to-all-start = ((f32[8,4,16,256]{3,2,1,0:T(8,128)}), f32[8,4,16,256]{3,2,1,0:T(8,128)S(1)}, u32[]{:S(2)}, u32[]{:S(2)}) async-start(f32[8,4,16,256]{3,2,1,0:T(8,128)} %add.45), calls=%async_computation | async-start | bytes 1048576 | tf_op jit(solution)/shard_map/all_to_all | solution.py:223
  41.5 6.2 %collective-permute-start.7 = (f32[8,2,16,128]{3,2,1,0:T(8,128)S(1)}, f32[8,2,16,128]{3,2,1,0:T(8,128)S(1)}, u32[]{:S(2)}, u32[]{:S(2)}) collective-permute-start(f32[8,2,16,128]{3,2,1,0:T(8,128)S(1)} %pad_maximum_fusion.3), channel_id=1, source_target_pairs={{0,32},{32,0},{1,33},{33,1},{2,34},{34,2},{3,35},{35,3},{4,36},{36... | collective-permute-start | bytes 393224 | tf_op jit(solution)/shard_map/ppermute | solution.py:213
  60.2 25.6 %all-to-all-start.2 = ((f32[8,176,128]{2,1,0:T(8,128)}), f32[8,176,128]{2,1,0:T(8,128)S(1)}, u32[]{:S(2)}, u32[]{:S(2)}) async-start(f32[8,176,128]{2,1,0:T(8,128)} %pad_maximum_fusion.1), calls=%async_computation.2 | async-start | bytes 1441792 | tf_op jit(solution)/shard_map/all_to_all | solution.py:223
  63.8 7.5 %collective-permute-start.5 = (f32[8,16,512]{2,1,0:T(8,128)S(1)}, f32[8,16,512]{2,1,0:T(8,128)S(1)}, u32[]{:S(2)}, u32[]{:S(2)}) collective-permute-start(f32[8,16,512]{2,1,0:T(8,128)S(1)} %slice.181), channel_id=1, source_target_pairs={{0,16},{16,0},{1,17},{17,1},{2,18},{18,2},{3,19},{19,3},{4,20},{20... | collective-permute-start | bytes 786440 | tf_op jit(solution)/shard_map/ppermute | solution.py:213
  71.3 10.3 %copy-start.3 = (f32[8,16,512]{2,1,0:T(8,128)}, f32[8,16,512]{2,1,0:T(8,128)S(1)}, u32[]{:S(2)}) copy-start(f32[8,16,512]{2,1,0:T(8,128)S(1)} %collective-permute-done.5.a) | copy-start | bytes 786436
  71.3 8.8 %collective-permute-start.16 = (f32[8,16,512]{2,1,0:T(8,128)S(1)}, f32[8,16,512]{2,1,0:T(8,128)S(1)}, u32[]{:S(2)}, u32[]{:S(2)}) collective-permute-start(f32[8,16,512]{2,1,0:T(8,128)S(1)} %pad_maximum_fusion.2), channel_id=1, source_target_pairs={{0,32},{32,0},{1,33},{33,1},{2,34},{34,2},{3,35},{35,3},{4,36},{36... | collective-permute-start | bytes 786440 | tf_op jit(solution)/shard_map/ppermute | solution.py:213
  74.3 5.8 %collective-permute-start.1 = (f32[16,256]{1,0:T(8,128)S(1)}, f32[16,256]{1,0:T(8,128)S(1)}, u32[]{:S(2)}, u32[]{:S(2)}) collective-permute-start(f32[16,256]{1,0:T(8,128)S(1)} %slice_bitcast_fusion.2), channel_id=1, source_target_pairs={{0,16},{16,0},{1,17},{17,1},{2,18},{18,2},{3,19},{19,3},{4,20},{20... | collective-permute-start | bytes 49160 | tf_op jit(solution)/shard_map/ppermute | solution.py:213
  74.7 6.8 %collective-permute-start.4 = (f32[8,32,512]{2,1,0:T(8,128)S(1)}, f32[8,32,512]{2,1,0:T(8,128)S(1)}, u32[]{:S(2)}, u32[]{:S(2)}) collective-permute-start(f32[8,32,512]{2,1,0:T(8,128)S(1)} %all-to-all-done.1.rows), channel_id=1, source_target_pairs={{0,1},{1,0},{2,3},{3,2},{4,5},{5,4},{6,7},{7,6},{8,9},{9,8},{10,11... | collective-permute-start | bytes 1572872 | tf_op jit(solution)/shard_map/ppermute | solution.py:213
  76.6 4.9 %collective-permute-start.6 = (f32[8,16,512]{2,1,0:T(8,128)S(1)}, f32[8,16,512]{2,1,0:T(8,128)S(1)}, u32[]{:S(2)}, u32[]{:S(2)}) collective-permute-start(f32[8,16,512]{2,1,0:T(8,128)S(1)} %collective-permute-done.5.a), channel_id=1, source_target_pairs={{0,1},{1,0},{2,3},{3,2},{4,5},{5,4},{6,7},{7,6},{8,9},{9,8},{10,11... | collective-permute-start | bytes 786440 | tf_op jit(solution)/shard_map/ppermute | solution.py:213
  80.1 10.9 %copy-start.10 = (f32[8,16,512]{2,1,0:T(8,128)}, f32[8,16,512]{2,1,0:T(8,128)S(1)}, u32[]{:S(2)}) copy-start(f32[8,16,512]{2,1,0:T(8,128)S(1)} %collective-permute-done.16.b) | copy-start | bytes 786436
  80.2 11.3 %collective-permute-start.18 = (f32[8,8,512]{2,1,0:T(8,128)S(1)}, f32[8,8,512]{2,1,0:T(8,128)S(1)}, u32[]{:S(2)}, u32[]{:S(2)}) collective-permute-start(f32[8,8,512]{2,1,0:T(8,128)S(1)} %pad_maximum_fusion.5), channel_id=1, source_target_pairs={{0,64},{64,0},{1,65},{65,1},{2,66},{66,2},{3,67},{67,3},{4,68},{68... | collective-permute-start | bytes 393224 | tf_op jit(solution)/shard_map/ppermute | solution.py:213
  81.5 0.7 copy-start.5
  82.3 0.8 copy-start.2
  85.9 3.6 %collective-permute-start.8 = (f32[8,96,128]{2,1,0:T(8,128)S(1)}, f32[8,96,128]{2,1,0:T(8,128)S(1)}, u32[]{:S(2)}, u32[]{:S(2)}) collective-permute-start(f32[8,96,128]{2,1,0:T(8,128)S(1)} %slice.239), channel_id=1, source_target_pairs={{0,1},{1,0},{2,3},{3,2},{4,5},{5,4},{6,7},{7,6},{8,9},{9,8},{10,11... | collective-permute-start | bytes 1179656 | tf_op jit(solution)/shard_map/ppermute | solution.py:213
  88.0 14.0 %copy-start.9 = (f32[256,512]{1,0:T(8,128)S(1)}, f32[256,512]{1,0:T(8,128)}, u32[]{:S(2)}) copy-start(f32[256,512]{1,0:T(8,128)} %get-tuple-element.26) | copy-start | bytes 1572868
  89.7 2.9 %collective-permute-start.9 = (f32[16,256]{1,0:T(8,128)S(1)}, f32[16,256]{1,0:T(8,128)S(1)}, u32[]{:S(2)}, u32[]{:S(2)}) collective-permute-start(f32[16,256]{1,0:T(8,128)S(1)} %convolution_subtract_fusion.2), channel_id=1, source_target_pairs={{0,16},{16,0},{1,17},{17,1},{2,18},{18,2},{3,19},{19,3},{4,20},{20... | collective-permute-start | bytes 49160 | tf_op jit(solution)/shard_map/ppermute | solution.py:213
  91.0 28.4 %collective-permute-start.17 = (f32[8,16,512]{2,1,0:T(8,128)S(1)}, f32[8,16,512]{2,1,0:T(8,128)S(1)}, u32[]{:S(2)}, u32[]{:S(2)}) collective-permute-start(f32[8,16,512]{2,1,0:T(8,128)S(1)} %collective-permute-done.16.b), channel_id=1, source_target_pairs={{0,1},{1,0},{2,3},{3,2},{4,5},{5,4},{6,7},{7,6},{8,9},{9,8},{10,11... | collective-permute-start | bytes 786440 | tf_op jit(solution)/shard_map/ppermute | solution.py:213
  91.6 27.9 %copy-start.12 = (f32[8,8,512]{2,1,0:T(8,128)}, f32[8,8,512]{2,1,0:T(8,128)S(1)}, u32[]{:S(2)}) copy-start(f32[8,8,512]{2,1,0:T(8,128)S(1)} %collective-permute-done.18.e) | copy-start | bytes 393220
  91.6 27.9 %collective-permute-start.19 = (f32[8,8,512]{2,1,0:T(8,128)S(1)}, f32[8,8,512]{2,1,0:T(8,128)S(1)}, u32[]{:S(2)}, u32[]{:S(2)}) collective-permute-start(f32[8,8,512]{2,1,0:T(8,128)S(1)} %collective-permute-done.18.e), channel_id=1, source_target_pairs={{0,1},{1,0},{2,3},{3,2},{4,5},{5,4},{6,7},{7,6},{8,9},{9,8},{10,11... | collective-permute-start | bytes 393224 | tf_op jit(solution)/shard_map/ppermute | solution.py:213
  92.6 9.4 %collective-permute-start.10 = (f32[16,256]{1,0:T(8,128)S(1)}, f32[16,256]{1,0:T(8,128)S(1)}, u32[]{:S(2)}, u32[]{:S(2)}) collective-permute-start(f32[16,256]{1,0:T(8,128)S(1)} %add.52), channel_id=1, source_target_pairs={{0,32},{32,0},{1,33},{33,1},{2,34},{34,2},{3,35},{35,3},{4,36},{36... | collective-permute-start | bytes 49160 | tf_op jit(solution)/shard_map/ppermute | solution.py:213
  95.6 15.0 %all-to-all-start.3 = ((f32[8,48,128]{2,1,0:T(8,128)}), f32[8,48,128]{2,1,0:T(8,128)S(1)}, u32[]{:S(2)}, u32[]{:S(2)}) async-start(f32[8,48,128]{2,1,0:T(8,128)} %broadcast_in_dim.10), calls=%async_computation.3 | async-start | bytes 393216 | tf_op jit(solution)/shard_map/all_to_all | solution.py:223
  110.7 4.1 %collective-permute-start.11 = (f32[8,48,128]{2,1,0:T(8,128)S(1)}, f32[8,48,128]{2,1,0:T(8,128)S(1)}, u32[]{:S(2)}, u32[]{:S(2)}) collective-permute-start(f32[8,48,128]{2,1,0:T(8,128)S(1)} %all-to-all-done.3), channel_id=1, source_target_pairs={{0,1},{1,0},{2,3},{3,2},{4,5},{5,4},{6,7},{7,6},{8,9},{9,8},{10,11... | collective-permute-start | bytes 589832 | tf_op jit(solution)/shard_map/ppermute | solution.py:213
  115.5 7.2 %collective-permute-start.12 = (f32[2,16,256]{2,1,0:T(8,128)S(1)}, f32[2,16,256]{2,1,0:T(8,128)S(1)}, u32[]{:S(2)}, u32[]{:S(2)}) collective-permute-start(f32[2,16,256]{2,1,0:T(8,128)S(1)} %pad_maximum_fusion.9), channel_id=1, source_target_pairs={{0,16},{16,0},{32,48},{48,32},{1,17},{17,1},{33,49},{49,33},{2,18}... | collective-permute-start | bytes 98312 | tf_op jit(solution)/shard_map/ppermute | solution.py:278
  116.0 6.8 %collective-permute-start.13 = (f32[2,16,256]{2,1,0:T(8,128)S(1)}, f32[2,16,256]{2,1,0:T(8,128)S(1)}, u32[]{:S(2)}, u32[]{:S(2)}) collective-permute-start(f32[2,16,256]{2,1,0:T(8,128)S(1)} %pad_maximum_fusion.9), channel_id=1, source_target_pairs={{0,32},{16,48},{32,0},{48,16},{1,33},{17,49},{33,1},{49,17},{2,34}... | collective-permute-start | bytes 98312 | tf_op jit(solution)/shard_map/ppermute | solution.py:278
  117.8 4.9 %collective-permute-start.14 = (f32[2,16,256]{2,1,0:T(8,128)S(1)}, f32[2,16,256]{2,1,0:T(8,128)S(1)}, u32[]{:S(2)}, u32[]{:S(2)}) collective-permute-start(f32[2,16,256]{2,1,0:T(8,128)S(1)} %pad_maximum_fusion.9), channel_id=1, source_target_pairs={{0,48},{16,32},{32,16},{48,0},{1,49},{17,33},{33,17},{49,1},{2,50}... | collective-permute-start | bytes 98312 | tf_op jit(solution)/shard_map/ppermute | solution.py:278
  119.4 0.7 copy-start.11
  119.4 0.7 copy-start.13
  122.7 12.1 %copy-start.8 = (f32[256,512]{1,0:T(8,128)S(1)}, f32[256,512]{1,0:T(8,128)}, u32[]{:S(2)}) copy-start(f32[256,512]{1,0:T(8,128)} %get-tuple-element.30) | copy-start | bytes 1572868
  122.8 2.7 %collective-permute-start.15 = (f32[16,256]{1,0:T(8,128)S(1)}, f32[16,256]{1,0:T(8,128)S(1)}, u32[]{:S(2)}, u32[]{:S(2)}) collective-permute-start(f32[16,256]{1,0:T(8,128)S(1)} %slice_bitcast_fusion.1), channel_id=1, source_target_pairs={{0,64},{64,0},{1,65},{65,1},{2,66},{66,2},{3,67},{67,3},{4,68},{68... | collective-permute-start | bytes 49160 | tf_op jit(solution)/shard_map/ppermute | solution.py:213
  123.1 4.2 %collective-permute-start.20 = (f32[256,128]{1,0:T(8,128)S(1)}, f32[256,128]{1,0:T(8,128)S(1)}, u32[]{:S(2)}, u32[]{:S(2)}) collective-permute-start(f32[256,128]{1,0:T(8,128)S(1)} %pad_maximum_fusion.6), channel_id=1, source_target_pairs={{0,16},{16,0},{1,17},{17,1},{2,18},{18,2},{3,19},{19,3},{4,20},{20... | collective-permute-start | bytes 393224 | tf_op jit(solution)/shard_map/ppermute | solution.py:213
  127.5 3.9 %collective-permute-start.21 = (f32[16,256]{1,0:T(8,128)S(1)}, f32[16,256]{1,0:T(8,128)S(1)}, u32[]{:S(2)}, u32[]{:S(2)}) collective-permute-start(f32[16,256]{1,0:T(8,128)S(1)} %fusion.62), channel_id=1, source_target_pairs={{0,64},{64,0},{128,192},{192,128},{1,65},{65,1},{129,193},{193,129... | collective-permute-start | bytes 49160 | tf_op jit(solution)/shard_map/ppermute | solution.py:278
  128.5 4.1 %collective-permute-start.22 = (f32[16,256]{1,0:T(8,128)S(1)}, f32[16,256]{1,0:T(8,128)S(1)}, u32[]{:S(2)}, u32[]{:S(2)}) collective-permute-start(f32[16,256]{1,0:T(8,128)S(1)} %fusion.62), channel_id=1, source_target_pairs={{0,128},{64,192},{128,0},{192,64},{1,129},{65,193},{129,1},{193,65... | collective-permute-start | bytes 49160 | tf_op jit(solution)/shard_map/ppermute | solution.py:278
  131.0 3.8 %collective-permute-start.23 = (f32[16,256]{1,0:T(8,128)S(1)}, f32[16,256]{1,0:T(8,128)S(1)}, u32[]{:S(2)}, u32[]{:S(2)}) collective-permute-start(f32[16,256]{1,0:T(8,128)S(1)} %fusion.62), channel_id=1, source_target_pairs={{0,192},{64,128},{128,64},{192,0},{1,193},{65,129},{129,65},{193,1... | collective-permute-start | bytes 49160 | tf_op jit(solution)/shard_map/ppermute | solution.py:278
  150.5 7.3 %copy-start = (bf16[4,1024,256]{2,1,0:T(8,128)(2,1)S(1)}, bf16[4,1024,256]{2,1,0:T(8,128)(2,1)}, u32[]{:S(2)}) copy-start(bf16[4,1024,256]{2,1,0:T(8,128)(2,1)} %w_hbm.1) | copy-start | bytes 6291460
  150.5 7.0 %collective-permute-start.24 = (f32[8,64,256]{2,1,0:T(8,128)S(1)}, f32[8,64,256]{2,1,0:T(8,128)S(1)}, u32[]{:S(2)}, u32[]{:S(2)}) collective-permute-start(f32[8,64,256]{2,1,0:T(8,128)S(1)} %all_to_all.25), channel_id=1, source_target_pairs={{0,1},{1,0},{2,3},{3,2},{4,5},{5,4},{6,7},{7,6},{8,9},{9,8},{10,11... | collective-permute-start | bytes 1572872 | tf_op jit(solution)/shard_map/ppermute | solution.py:213
  157.8 1.2 copy-start.4

commit v7 on v6

--- a/solution.py
+++ b/solution.py
@@ -11,6 +11,7 @@
 STEPS = 4
 F32 = jnp.float32
 BF16 = jnp.bfloat16
+PAIRS = ((3, 4), (2, 4), (1, 4), (2, 3), (1, 3), (1, 2))
 DIRECT = (4, (3, 4), (2, 4), (1, 4))
 SHARED = (3, (2, 3), (1, 3), 2, 1, (1, 2))
 
@@ -40,7 +41,7 @@
 
 def leaf_kernel(
     core_ref, pair_ref, inv_hbm, rhs_hbm, v_hbm, w_hbm, x_hbm, keep_hbm, give_hbm, keep_shared_hbm, give_shared_hbm,
-    x_ref, keep_ref, give_ref, keep_shared_ref, give_shared_ref, inv_ref, rhs_ref, v_ref, w_ref, left_ref, split_ref, sems,
+    x_ref, keep_ref, give_ref, keep_shared_ref, give_shared_ref, inv_ref, rhs_ref, v_ref, w_ref, high_ref, low_ref, sems,
 ):
     rows = 1024 // STEPS
     count = [0]
@@ -92,16 +93,13 @@
             done.add((id(waits), level))
             waits[level].wait()
 
-    for j in (3, 2, 1):
-        for k in range(4, j, -1):
-            if ("turned", k) not in done:
-                done.add(("turned", k))
-                ready(wait_w, k)
-                left_ref[pl.ds(256 * (k - 2), 256), :] = w_ref[k - 2].T
+    turned = {}
+    for j, k in PAIRS:
+        ready(wait_w, k)
+        if k not in turned:
+            turned[k] = w_ref[k - 2].T
         ready(wait_v, j)
-        value = dot(left_ref[pl.ds(256 * (j - 1), 256 * (4 - j)), :], v_ref[j - 1], ((1,), (0,)))
-        for k in range(j + 1, 5):
-            store((j, k), value[256 * (k - j - 1) : 256 * (k - j)])
+        store((j, k), dot(turned[k], v_ref[j - 1], ((1,), (0,))))
     wait_rhs.wait()
     rhs = rhs_ref[...]
     rhs_turned = rhs.T
@@ -112,13 +110,12 @@
         stores.append(load(x_ref.at[part], x_hbm.at[part]))
         xt = dot(rhs_turned, inv, ((1,), (1,)))
         high = xt.astype(BF16)
-        split_ref[0:256, part] = high
-        split_ref[256:512, part] = (xt - high.astype(F32)).astype(BF16)
+        high_ref[:, part] = high
+        low_ref[:, part] = (xt - high.astype(F32)).astype(BF16)
     for j in (4, 3, 2, 1):
         ready(wait_v, j)
         v = v_ref[j - 1]
-        both = dot(split_ref[...], v, ((1,), (0,)))
-        store(j, both[:256] + both[256:])
+        store(j, dot(high_ref[...], v, ((1,), (0,))) + dot(low_ref[...], v, ((1,), (0,))))
     for copy in stores:
         copy.wait()
 
@@ -138,8 +135,8 @@
             pltpu.VMEM((1024, 256), BF16),
             pltpu.VMEM((4, 1024, 256), BF16),
             pltpu.VMEM((3, 1024, 256), BF16),
-            pltpu.VMEM((768, 1024), BF16),
-            pltpu.VMEM((512, 1024), BF16),
+            pltpu.VMEM((256, 1024), BF16),
+            pltpu.VMEM((256, 1024), BF16),
             pltpu.SemaphoreType.DMA((28 + 2 * STEPS,)),
         ],
         name="leaf",

time: 161 us -> 161 us (level)
  no operation moved by 1% of the time
where the time goes in v7:
time: 161 us; the launch traced here: 160 us
  starting transfers between devices  59.1 us (37%)
  waiting for transfers between devices  56 us (35%)
  blocking collectives  15.4 us (10%)
  Pallas kernels  14.4 us (9%)
  matrix products  6.79 us (4%)
  other arithmetic  4.37 us (3%)
  local copies, waits for them, and re-layouts  3.66 us (2%)
    all_to_all x4, waiting for transfers between devices, exchange(): return lax.all_to_all(block, axes, 0, 0, tiled=True)  33.9 us
    ppermute x19, starting transfers between devices, partner(): return lax.ppermute(block, axis, [(0, 1), (1, 0)])  31.4 us
    all_to_all x4, starting transfers between devices, exchange(): return lax.all_to_all(block, axes, 0, 0, tiled=True)  19.8 us
    ppermute x19, waiting for transfers between devices, partner(): return lax.ppermute(block, axis, [(0, 1), (1, 0)])  18.8 us
    all_to_all x1, blocking collectives, exchange(): return lax.all_to_all(block, axes, 0, 0, tiled=True)  15.4 us
    pallas_call x1, Pallas kernels, leaf(): pl.pallas_call(leaf_kernel, in_specs=[pl.BlockSpec(memory_space=pltpu.SME...  7.92 us
    ppermute x6, starting transfers between devices, of_four(): got[k] = lax.ppermute(block, axes, [(i, i ^ k) for i in range(4)])  7.89 us
    pallas_call x2, Pallas kernels, assemble(): pl.pallas_call(kernel, grid=(1,), in_specs=[pl.BlockSpec(memory_space=plt...  4.86 us
  transfers between devices with their start and end apart: 29, of which 14 were waited for; matrix products, arithmetic and copies ran while one was open for 5% of the time, Pallas kernels for 4%

profile of v7, /device:TPU:1, one launch (start us, length us, event | category | flops | bytes accessed | tf_op | source)
XLA Modules:
  0.0 160.2 jit_solution(13427657139548343749)
XLA Ops:
  0.0 7.9 %leaf.1 = (f32[1024,256]{1,0:T(8,128)}, f32[8,4,16,256]{3,2,1,0:T(8,128)}, f32[8,4,16,256]{3,2,1,0:T(8,128)}, f32[2,8,6,16,128]{4,3,2,1,0:T(8,128)}, f32[2,8,6,16,128]{4,3,2,1,0:T(8,128)}) custom-call(s32[1]{0:T(128)} %bitcast.core_ref, s32[1]{0:T(128)} %bitcast.1.pair_ref.yl_ref, bf16[1024,1024]{1,0:T(8,128)(2,1)} %inv_hbm.1, bf16[1024,256]{1,0:T(8,128)(2,1)} %rhs_hbm.1, ...), custom_call_target="tpu_custom_call" | custom-call | tf_op jit(solution)/shard_map/leaf/pallas_call | solution.py:127
  7.9 3.3 %collective-permute-start.2 = (f32[2,8,6,16,128]{4,3,2,1,0:T(8,128)}, f32[2,8,6,16,128]{4,3,2,1,0:T(8,128)S(1)}, u32[]{:S(2)}, u32[]{:S(2)}) collective-permute-start(f32[2,8,6,16,128]{4,3,2,1,0:T(8,128)} %get-tuple-element.22), channel_id=1, source_target_pairs={{0,1},{1,0},{2,3},{3,2},{4,5},{5,4},{6,7},{7,6},{8,9},{9,8},{10,11... | collective-permute-start | bytes 2359304 | tf_op jit(solution)/shard_map/ppermute | solution.py:210
  11.2 1.6 %pack.1 = f32[8,32,512]{2,1,0:T(8,128)} custom-call(f32[16,512]{1,0:T(8,128)} %a_ref.1, f32[8,512]{1,0:T(8,128)} %b_ref.1, f32[4,512]{1,0:T(4,128)} %c_ref.1, f32[2,512]{1,0:T(2,128)} %d_ref.1), custom_call_target="tpu_custom_call" | custom-call | tf_op jit(solution)/shard_map/pack/pallas_call | solution.py:39
  12.9 6.5 %all-to-all-start.1 = ((f32[8,32,512]{2,1,0:T(8,128)}), f32[8,32,512]{2,1,0:T(8,128)S(1)}, u32[]{:S(2)}, u32[]{:S(2)}) async-start(f32[8,32,512]{2,1,0:T(8,128)} %pack.1), calls=%async_computation.1 | async-start | bytes 1048576 | tf_op jit(solution)/shard_map/all_to_all | solution.py:220
  19.3 0.4 collective-permute-start
  19.8 1.8 %fusion.9 = f32[8,6,16,128]{3,2,1,0:T(8,128)} fusion(f32[2,8,6,16,128]{4,3,2,1,0:T(8,128)S(1)} %collective-permute-done.2, f32[2,8,6,16,128]{4,3,2,1,0:T(8,128)} %get-tuple-element.21), kind=kLoop, calls=%fused_computation.18 | loop fusion | flops 98304 | bytes 1179648 | tf_op jit(solution)/shard_map/add | solution.py:237
  21.6 1.3 collective-permute-start.3
  22.9 0.9 add.45
  23.8 13.5 %all-to-all-done.1.rows = f32[8,32,512]{2,1,0:T(8,128)S(1)} async-done(((f32[8,32,512]{2,1,0:T(8,128)}), f32[8,32,512]{2,1,0:T(8,128)S(1)}, u32[]{:S(2)}, u32[]{:S(2)}) %all-to-all-start.1) | async-done | bytes 524320 | tf_op jit(solution)/shard_map/all_to_all | solution.py:220
  37.3 3.5 %all-to-all-start = ((f32[8,4,16,256]{3,2,1,0:T(8,128)}), f32[8,4,16,256]{3,2,1,0:T(8,128)S(1)}, u32[]{:S(2)}, u32[]{:S(2)}) async-start(f32[8,4,16,256]{3,2,1,0:T(8,128)} %add.45), calls=%async_computation | async-start | bytes 1048576 | tf_op jit(solution)/shard_map/all_to_all | solution.py:220
  41.0 3.0 %collective-permute-start.7 = (f32[8,2,16,128]{3,2,1,0:T(8,128)S(1)}, f32[8,2,16,128]{3,2,1,0:T(8,128)S(1)}, u32[]{:S(2)}, u32[]{:S(2)}) collective-permute-start(f32[8,2,16,128]{3,2,1,0:T(8,128)S(1)} %pad_maximum_fusion.3), channel_id=1, source_target_pairs={{0,32},{32,0},{1,33},{33,1},{2,34},{34,2},{3,35},{35,3},{4,36},{36... | collective-permute-start | bytes 393224 | tf_op jit(solution)/shard_map/ppermute | solution.py:210
  44.0 3.2 %collective-permute-done.7 = f32[8,2,16,128]{3,2,1,0:T(8,128)S(1)} collective-permute-done((f32[8,2,16,128]{3,2,1,0:T(8,128)S(1)}, f32[8,2,16,128]{3,2,1,0:T(8,128)S(1)}, u32[]{:S(2)}, u32[]{:S(2)}) %collective-permute-start.7) | collective-permute-done | bytes 131104 | tf_op jit(solution)/shard_map/ppermute | solution.py:210
  47.2 11.5 %all-to-all-done = f32[8,4,16,256]{3,2,1,0:T(8,128)S(1)} async-done(((f32[8,4,16,256]{3,2,1,0:T(8,128)}), f32[8,4,16,256]{3,2,1,0:T(8,128)S(1)}, u32[]{:S(2)}, u32[]{:S(2)}) %all-to-all-start) | async-done | bytes 524320 | tf_op jit(solution)/shard_map/all_to_all | solution.py:220
  58.8 0.9 pad_maximum_fusion.1
  59.7 3.5 %all-to-all-start.2 = ((f32[8,176,128]{2,1,0:T(8,128)}), f32[8,176,128]{2,1,0:T(8,128)S(1)}, u32[]{:S(2)}, u32[]{:S(2)}) async-start(f32[8,176,128]{2,1,0:T(8,128)} %pad_maximum_fusion.1), calls=%async_computation.2 | async-start | bytes 1441792 | tf_op jit(solution)/shard_map/all_to_all | solution.py:220
  63.3 1.4 collective-permute-start.5
  64.7 6.1 %collective-permute-done.5.a = f32[8,16,512]{2,1,0:T(8,128)S(1)} collective-permute-done((f32[8,16,512]{2,1,0:T(8,128)S(1)}, f32[8,16,512]{2,1,0:T(8,128)S(1)}, u32[]{:S(2)}, u32[]{:S(2)}) %collective-permute-start.5) | collective-permute-done | bytes 262176 | tf_op jit(solution)/shard_map/ppermute | solution.py:210
  70.8 3.0 %collective-permute-start.16 = (f32[8,16,512]{2,1,0:T(8,128)S(1)}, f32[8,16,512]{2,1,0:T(8,128)S(1)}, u32[]{:S(2)}, u32[]{:S(2)}) collective-permute-start(f32[8,16,512]{2,1,0:T(8,128)S(1)} %pad_maximum_fusion.2), channel_id=1, source_target_pairs={{0,32},{32,0},{1,33},{33,1},{2,34},{34,2},{3,35},{35,3},{4,36},{36... | collective-permute-start | bytes 786440 | tf_op jit(solution)/shard_map/ppermute | solution.py:210
  73.8 0.4 collective-permute-start.1
  74.2 1.9 %collective-permute-start.4 = (f32[8,32,512]{2,1,0:T(8,128)S(1)}, f32[8,32,512]{2,1,0:T(8,128)S(1)}, u32[]{:S(2)}, u32[]{:S(2)}) collective-permute-start(f32[8,32,512]{2,1,0:T(8,128)S(1)} %all-to-all-done.1.rows), channel_id=1, source_target_pairs={{0,1},{1,0},{2,3},{3,2},{4,5},{5,4},{6,7},{7,6},{8,9},{9,8},{10,11... | collective-permute-start | bytes 1572872 | tf_op jit(solution)/shard_map/ppermute | solution.py:210
  76.2 3.4 %collective-permute-done.1 = f32[16,256]{1,0:T(8,128)S(1)} collective-permute-done((f32[16,256]{1,0:T(8,128)S(1)}, f32[16,256]{1,0:T(8,128)S(1)}, u32[]{:S(2)}, u32[]{:S(2)}) %collective-permute-start.1) | collective-permute-done | bytes 16416 | tf_op jit(solution)/shard_map/ppermute | solution.py:210
  79.7 1.3 collective-permute-start.18
  81.1 0.7 copy-done.5
  81.8 0.8 copy-done.2
  82.6 2.3 %shard_map.82 = (f32[256,512]{1,0:T(8,128)}, f32[256,512]{1,0:T(8,128)}) custom-call(s32[1]{0:T(128)} %bitcast.core_ref, s32[1]{0:T(128)} %bitcast.1.pair_ref.yl_ref, f32[8,32,512]{2,1,0:T(8,128)} %copy-done.1, f32[8,32,512]{2,1,0:T(8,128)} %copy-done.2, f32[8,16,512]{2,1,0:T(8,128)} %copy-done.3, f32[8,16,512]{2,1,0:T(8,128)} %copy-done.5), custom_call_target="tpu_custom_call" | custom-call | tf_op jit(solution)/shard_map/pallas_call | solution.py:200
  84.9 0.5 all-to-all-done.2
  85.4 2.1 %collective-permute-start.8 = (f32[8,96,128]{2,1,0:T(8,128)S(1)}, f32[8,96,128]{2,1,0:T(8,128)S(1)}, u32[]{:S(2)}, u32[]{:S(2)}) collective-permute-start(f32[8,96,128]{2,1,0:T(8,128)S(1)} %slice.239), channel_id=1, source_target_pairs={{0,1},{1,0},{2,3},{3,2},{4,5},{5,4},{6,7},{7,6},{8,9},{9,8},{10,11... | collective-permute-start | bytes 1179656 | tf_op jit(solution)/shard_map/ppermute | solution.py:210
  87.5 1.4 fusion.46
  89.0 0.1 convolution_subtract_fusion.2
  89.2 1.3 collective-permute-start.9
  90.5 0.5 collective-permute-start.17
  91.2 0.9 collective-permute-done.9
  92.1 2.4 %collective-permute-start.10 = (f32[16,256]{1,0:T(8,128)S(1)}, f32[16,256]{1,0:T(8,128)S(1)}, u32[]{:S(2)}, u32[]{:S(2)}) collective-permute-start(f32[16,256]{1,0:T(8,128)S(1)} %add.52), channel_id=1, source_target_pairs={{0,32},{32,0},{1,33},{33,1},{2,34},{34,2},{3,35},{35,3},{4,36},{36... | collective-permute-start | bytes 49160 | tf_op jit(solution)/shard_map/ppermute | solution.py:210
  94.4 0.7 broadcast_in_dim.10
  95.1 6.3 %all-to-all-start.3 = ((f32[8,48,128]{2,1,0:T(8,128)}), f32[8,48,128]{2,1,0:T(8,128)S(1)}, u32[]{:S(2)}, u32[]{:S(2)}) async-start(f32[8,48,128]{2,1,0:T(8,128)} %broadcast_in_dim.10), calls=%async_computation.3 | async-start | bytes 393216 | tf_op jit(solution)/shard_map/all_to_all | solution.py:220
  101.5 0.3 fusion.50
  101.8 8.4 %all-to-all-done.3 = f32[8,48,128]{2,1,0:T(8,128)S(1)} async-done(((f32[8,48,128]{2,1,0:T(8,128)}), f32[8,48,128]{2,1,0:T(8,128)S(1)}, u32[]{:S(2)}, u32[]{:S(2)}) %all-to-all-start.3) | async-done | bytes 196640 | tf_op jit(solution)/shard_map/all_to_all | solution.py:220
  110.2 3.0 %collective-permute-start.11 = (f32[8,48,128]{2,1,0:T(8,128)S(1)}, f32[8,48,128]{2,1,0:T(8,128)S(1)}, u32[]{:S(2)}, u32[]{:S(2)}) collective-permute-start(f32[8,48,128]{2,1,0:T(8,128)S(1)} %all-to-all-done.3), channel_id=1, source_target_pairs={{0,1},{1,0},{2,3},{3,2},{4,5},{5,4},{6,7},{7,6},{8,9},{9,8},{10,11... | collective-permute-start | bytes 589832 | tf_op jit(solution)/shard_map/ppermute | solution.py:210
  113.2 1.1 collective-permute-done.11
  114.3 0.2 broadcast_select_fusion.13
  114.4 0.2 broadcast_select_fusion.11
  114.6 0.2 fusion.6
  114.7 0.2 fusion.4
  115.0 0.5 collective-permute-start.12
  115.5 1.9 %collective-permute-start.13 = (f32[2,16,256]{2,1,0:T(8,128)S(1)}, f32[2,16,256]{2,1,0:T(8,128)S(1)}, u32[]{:S(2)}, u32[]{:S(2)}) collective-permute-start(f32[2,16,256]{2,1,0:T(8,128)S(1)} %pad_maximum_fusion.9), channel_id=1, source_target_pairs={{0,32},{16,48},{32,0},{48,16},{1,33},{17,49},{33,1},{49,17},{2,34}... | collective-permute-start | bytes 98312 | tf_op jit(solution)/shard_map/ppermute | solution.py:275
  117.3 1.6 collective-permute-start.14
  118.9 0.7 copy-done.11
  119.7 2.5 %shard_map.83 = (f32[256,512]{1,0:T(8,128)}, f32[256,512]{1,0:T(8,128)}) custom-call(s32[1]{0:T(128)} %bitcast.core_ref, s32[1]{0:T(128)} %bitcast.1.pair_ref.yl_ref, s32[1]{0:T(128)} %bitcast.29.yh_ref, s32[1]{0:T(128)} %bitcast.30.xl_ref, f32[8,32,512]{2,1,0:T(8,128)} %copy-done.1, f32[8,32,512]{2,1,0:T(8,128)} %copy-done.2, f32[8,16,512]{2,1,0:T(8,128)} %copy-done.3, ...), custom_call_target="tpu_custom_call" | custom-call | tf_op jit(solution)/shard_map/pallas_call | solution.py:200
  122.3 0.3 collective-permute-start.15
  122.7 2.2 %collective-permute-done.15 = f32[16,256]{1,0:T(8,128)S(1)} collective-permute-done((f32[16,256]{1,0:T(8,128)S(1)}, f32[16,256]{1,0:T(8,128)S(1)}, u32[]{:S(2)}, u32[]{:S(2)}) %collective-permute-start.15) | collective-permute-done | bytes 16416 | tf_op jit(solution)/shard_map/ppermute | solution.py:210
  125.0 1.3 fusion.54
  126.3 0.5 collective-permute-done.20
  127.0 1.0 collective-permute-start.21
  128.0 2.5 %collective-permute-start.22 = (f32[16,256]{1,0:T(8,128)S(1)}, f32[16,256]{1,0:T(8,128)S(1)}, u32[]{:S(2)}, u32[]{:S(2)}) collective-permute-start(f32[16,256]{1,0:T(8,128)S(1)} %fusion.62), channel_id=1, source_target_pairs={{0,128},{64,192},{128,0},{192,64},{1,129},{65,193},{129,1},{193,65... | collective-permute-start | bytes 49160 | tf_op jit(solution)/shard_map/ppermute | solution.py:275
  130.5 0.5 collective-permute-start.23
  130.9 1.1 collective-permute-done.22
  132.1 2.2 %collective-permute-done.23 = f32[16,256]{1,0:T(8,128)S(1)} collective-permute-done((f32[16,256]{1,0:T(8,128)S(1)}, f32[16,256]{1,0:T(8,128)S(1)}, u32[]{:S(2)}, u32[]{:S(2)}) %collective-permute-start.23) | collective-permute-done | bytes 16416 | tf_op jit(solution)/shard_map/ppermute | solution.py:275
  134.3 0.3 fusion.58
  134.7 15.4 %all_to_all.25 = f32[8,64,256]{2,1,0:T(8,128)S(1)} all-to-all(f32[8,64,256]{2,1,0:T(8,128)S(1)} %broadcast_in_dim.11), channel_id=1, replica_groups=mesh['xh'=2,'xl'=2,'yh'=2,'yl'=2,'z'=8,'c'=2] {'z'}, dimensions={0} | all-to-all | bytes 1048576 | tf_op jit(solution)/shard_map/all_to_all | solution.py:220
  150.0 5.5 %collective-permute-start.24 = (f32[8,64,256]{2,1,0:T(8,128)S(1)}, f32[8,64,256]{2,1,0:T(8,128)S(1)}, u32[]{:S(2)}, u32[]{:S(2)}) collective-permute-start(f32[8,64,256]{2,1,0:T(8,128)S(1)} %all_to_all.25), channel_id=1, source_target_pairs={{0,1},{1,0},{2,3},{3,2},{4,5},{5,4},{6,7},{7,6},{8,9},{9,8},{10,11... | collective-permute-start | bytes 1572872 | tf_op jit(solution)/shard_map/ppermute | solution.py:210
  155.5 1.5 collective-permute-done.24
  157.3 0.7 convolution_bitcast_fusion
  158.1 0.5 copy-done.4
  158.5 1.7 %fusion.2 = f32[1024,256]{1,0:T(8,128)} fusion(f32[1024,256]{1,0:T(8,128)S(1)} %copy-done.4, f32[256,1024]{0,1:T(8,128)S(1)} %convolution_bitcast_fusion, bf16[4,1024,256]{2,1,0:T(8,128)(2,1)S(1)} %copy-done, f32[1,256,256]{2,1,0:T(8,128)S(1)} %maximum_bitcast_fusion.3, f32[1,256,256]{2,1,0:T(8,128)S(1)} %maximum_bitcast_fusion.2, ...), kind=kOutput, calls=%fused_computation.6 | convolution fusion | flops 538705920 | bytes 6291456 | tf_op jit(solution)/shard_map/dot_general | solution.py:20
  (89 shorter events, 1.5 us)
Async XLA Ops:
  7.9 15.0 %copy-start.7 = (f32[8,4,16,256]{3,2,1,0:T(8,128)S(1)}, f32[8,4,16,256]{3,2,1,0:T(8,128)}, u32[]{:S(2)}) copy-start(f32[8,4,16,256]{3,2,1,0:T(8,128)} %get-tuple-element.19) | copy-start | bytes 1572868
  7.9 11.8 %collective-permute-start.2 = (f32[2,8,6,16,128]{4,3,2,1,0:T(8,128)}, f32[2,8,6,16,128]{4,3,2,1,0:T(8,128)S(1)}, u32[]{:S(2)}, u32[]{:S(2)}) collective-permute-start(f32[2,8,6,16,128]{4,3,2,1,0:T(8,128)} %get-tuple-element.22), channel_id=1, source_target_pairs={{0,1},{1,0},{2,3},{3,2},{4,5},{5,4},{6,7},{7,6},{8,9},{9,8},{10,11... | collective-permute-start | bytes 2359304 | tf_op jit(solution)/shard_map/ppermute | solution.py:210
  12.9 24.5 %all-to-all-start.1 = ((f32[8,32,512]{2,1,0:T(8,128)}), f32[8,32,512]{2,1,0:T(8,128)S(1)}, u32[]{:S(2)}, u32[]{:S(2)}) async-start(f32[8,32,512]{2,1,0:T(8,128)} %pack.1), calls=%async_computation.1 | async-start | bytes 1048576 | tf_op jit(solution)/shard_map/all_to_all | solution.py:220
  19.3 21.5 %copy-start.6 = (f32[2,8,6,16,128]{4,3,2,1,0:T(8,128)S(1)}, f32[2,8,6,16,128]{4,3,2,1,0:T(8,128)}, u32[]{:S(2)}) copy-start(f32[2,8,6,16,128]{4,3,2,1,0:T(8,128)} %get-tuple-element.21) | copy-start | bytes 2359300
  19.3 3.5 %collective-permute-start = (f32[8,4,16,256]{3,2,1,0:T(8,128)}, f32[8,4,16,256]{3,2,1,0:T(8,128)S(1)}, u32[]{:S(2)}, u32[]{:S(2)}) collective-permute-start(f32[8,4,16,256]{3,2,1,0:T(8,128)} %get-tuple-element.20), channel_id=1, source_target_pairs={{0,1},{1,0},{2,3},{3,2},{4,5},{5,4},{6,7},{7,6},{8,9},{9,8},{10,11... | collective-permute-start | bytes 1572872 | tf_op jit(solution)/shard_map/ppermute | solution.py:210
  21.6 19.2 %collective-permute-start.3 = (f32[8,6,16,128]{3,2,1,0:T(8,128)}, f32[8,6,16,128]{3,2,1,0:T(8,128)S(1)}, u32[]{:S(2)}, u32[]{:S(2)}) collective-permute-start(f32[8,6,16,128]{3,2,1,0:T(8,128)} %fusion.9), channel_id=1, source_target_pairs={{0,16},{16,0},{1,17},{17,1},{2,18},{18,2},{3,19},{19,3},{4,20},{20... | collective-permute-start | bytes 1179656 | tf_op jit(solution)/shard_map/ppermute | solution.py:210
  37.3 38.8 %copy-start.1 = (f32[8,32,512]{2,1,0:T(8,128)}, f32[8,32,512]{2,1,0:T(8,128)S(1)}, u32[]{:S(2)}) copy-start(f32[8,32,512]{2,1,0:T(8,128)S(1)} %all-to-all-done.1.rows) | copy-start | bytes 1572868
  37.3 21.4 %all-to-all-start = ((f32[8,4,16,256]{3,2,1,0:T(8,128)}), f32[8,4,16,256]{3,2,1,0:T(8,128)S(1)}, u32[]{:S(2)}, u32[]{:S(2)}) async-start(f32[8,4,16,256]{3,2,1,0:T(8,128)} %add.45), calls=%async_computation | async-start | bytes 1048576 | tf_op jit(solution)/shard_map/all_to_all | solution.py:220
  41.0 6.2 %collective-permute-start.7 = (f32[8,2,16,128]{3,2,1,0:T(8,128)S(1)}, f32[8,2,16,128]{3,2,1,0:T(8,128)S(1)}, u32[]{:S(2)}, u32[]{:S(2)}) collective-permute-start(f32[8,2,16,128]{3,2,1,0:T(8,128)S(1)} %pad_maximum_fusion.3), channel_id=1, source_target_pairs={{0,32},{32,0},{1,33},{33,1},{2,34},{34,2},{3,35},{35,3},{4,36},{36... | collective-permute-start | bytes 393224 | tf_op jit(solution)/shard_map/ppermute | solution.py:210
  59.7 25.6 %all-to-all-start.2 = ((f32[8,176,128]{2,1,0:T(8,128)}), f32[8,176,128]{2,1,0:T(8,128)S(1)}, u32[]{:S(2)}, u32[]{:S(2)}) async-start(f32[8,176,128]{2,1,0:T(8,128)} %pad_maximum_fusion.1), calls=%async_computation.2 | async-start | bytes 1441792 | tf_op jit(solution)/shard_map/all_to_all | solution.py:220
  63.3 7.5 %collective-permute-start.5 = (f32[8,16,512]{2,1,0:T(8,128)S(1)}, f32[8,16,512]{2,1,0:T(8,128)S(1)}, u32[]{:S(2)}, u32[]{:S(2)}) collective-permute-start(f32[8,16,512]{2,1,0:T(8,128)S(1)} %slice.181), channel_id=1, source_target_pairs={{0,16},{16,0},{1,17},{17,1},{2,18},{18,2},{3,19},{19,3},{4,20},{20... | collective-permute-start | bytes 786440 | tf_op jit(solution)/shard_map/ppermute | solution.py:210
  70.8 10.3 %copy-start.3 = (f32[8,16,512]{2,1,0:T(8,128)}, f32[8,16,512]{2,1,0:T(8,128)S(1)}, u32[]{:S(2)}) copy-start(f32[8,16,512]{2,1,0:T(8,128)S(1)} %collective-permute-done.5.a) | copy-start | bytes 786436
  70.8 8.8 %collective-permute-start.16 = (f32[8,16,512]{2,1,0:T(8,128)S(1)}, f32[8,16,512]{2,1,0:T(8,128)S(1)}, u32[]{:S(2)}, u32[]{:S(2)}) collective-permute-start(f32[8,16,512]{2,1,0:T(8,128)S(1)} %pad_maximum_fusion.2), channel_id=1, source_target_pairs={{0,32},{32,0},{1,33},{33,1},{2,34},{34,2},{3,35},{35,3},{4,36},{36... | collective-permute-start | bytes 786440 | tf_op jit(solution)/shard_map/ppermute | solution.py:210
  73.8 5.8 %collective-permute-start.1 = (f32[16,256]{1,0:T(8,128)S(1)}, f32[16,256]{1,0:T(8,128)S(1)}, u32[]{:S(2)}, u32[]{:S(2)}) collective-permute-start(f32[16,256]{1,0:T(8,128)S(1)} %slice_bitcast_fusion.2), channel_id=1, source_target_pairs={{0,16},{16,0},{1,17},{17,1},{2,18},{18,2},{3,19},{19,3},{4,20},{20... | collective-permute-start | bytes 49160 | tf_op jit(solution)/shard_map/ppermute | solution.py:210
  74.2 6.8 %collective-permute-start.4 = (f32[8,32,512]{2,1,0:T(8,128)S(1)}, f32[8,32,512]{2,1,0:T(8,128)S(1)}, u32[]{:S(2)}, u32[]{:S(2)}) collective-permute-start(f32[8,32,512]{2,1,0:T(8,128)S(1)} %all-to-all-done.1.rows), channel_id=1, source_target_pairs={{0,1},{1,0},{2,3},{3,2},{4,5},{5,4},{6,7},{7,6},{8,9},{9,8},{10,11... | collective-permute-start | bytes 1572872 | tf_op jit(solution)/shard_map/ppermute | solution.py:210
  76.1 4.9 %collective-permute-start.6 = (f32[8,16,512]{2,1,0:T(8,128)S(1)}, f32[8,16,512]{2,1,0:T(8,128)S(1)}, u32[]{:S(2)}, u32[]{:S(2)}) collective-permute-start(f32[8,16,512]{2,1,0:T(8,128)S(1)} %collective-permute-done.5.a), channel_id=1, source_target_pairs={{0,1},{1,0},{2,3},{3,2},{4,5},{5,4},{6,7},{7,6},{8,9},{9,8},{10,11... | collective-permute-start | bytes 786440 | tf_op jit(solution)/shard_map/ppermute | solution.py:210
  79.6 10.9 %copy-start.10 = (f32[8,16,512]{2,1,0:T(8,128)}, f32[8,16,512]{2,1,0:T(8,128)S(1)}, u32[]{:S(2)}) copy-start(f32[8,16,512]{2,1,0:T(8,128)S(1)} %collective-permute-done.16.b) | copy-start | bytes 786436
  79.7 11.3 %collective-permute-start.18 = (f32[8,8,512]{2,1,0:T(8,128)S(1)}, f32[8,8,512]{2,1,0:T(8,128)S(1)}, u32[]{:S(2)}, u32[]{:S(2)}) collective-permute-start(f32[8,8,512]{2,1,0:T(8,128)S(1)} %pad_maximum_fusion.5), channel_id=1, source_target_pairs={{0,64},{64,0},{1,65},{65,1},{2,66},{66,2},{3,67},{67,3},{4,68},{68... | collective-permute-start | bytes 393224 | tf_op jit(solution)/shard_map/ppermute | solution.py:210
  81.0 0.7 copy-start.5
  81.8 0.8 copy-start.2
  85.4 3.6 %collective-permute-start.8 = (f32[8,96,128]{2,1,0:T(8,128)S(1)}, f32[8,96,128]{2,1,0:T(8,128)S(1)}, u32[]{:S(2)}, u32[]{:S(2)}) collective-permute-start(f32[8,96,128]{2,1,0:T(8,128)S(1)} %slice.239), channel_id=1, source_target_pairs={{0,1},{1,0},{2,3},{3,2},{4,5},{5,4},{6,7},{7,6},{8,9},{9,8},{10,11... | collective-permute-start | bytes 1179656 | tf_op jit(solution)/shard_map/ppermute | solution.py:210
  87.5 14.0 %copy-start.9 = (f32[256,512]{1,0:T(8,128)S(1)}, f32[256,512]{1,0:T(8,128)}, u32[]{:S(2)}) copy-start(f32[256,512]{1,0:T(8,128)} %get-tuple-element.26) | copy-start | bytes 1572868
  89.2 2.9 %collective-permute-start.9 = (f32[16,256]{1,0:T(8,128)S(1)}, f32[16,256]{1,0:T(8,128)S(1)}, u32[]{:S(2)}, u32[]{:S(2)}) collective-permute-start(f32[16,256]{1,0:T(8,128)S(1)} %convolution_subtract_fusion.2), channel_id=1, source_target_pairs={{0,16},{16,0},{1,17},{17,1},{2,18},{18,2},{3,19},{19,3},{4,20},{20... | collective-permute-start | bytes 49160 | tf_op jit(solution)/shard_map/ppermute | solution.py:210
  90.5 28.4 %collective-permute-start.17 = (f32[8,16,512]{2,1,0:T(8,128)S(1)}, f32[8,16,512]{2,1,0:T(8,128)S(1)}, u32[]{:S(2)}, u32[]{:S(2)}) collective-permute-start(f32[8,16,512]{2,1,0:T(8,128)S(1)} %collective-permute-done.16.b), channel_id=1, source_target_pairs={{0,1},{1,0},{2,3},{3,2},{4,5},{5,4},{6,7},{7,6},{8,9},{9,8},{10,11... | collective-permute-start | bytes 786440 | tf_op jit(solution)/shard_map/ppermute | solution.py:210
  91.1 27.9 %copy-start.12 = (f32[8,8,512]{2,1,0:T(8,128)}, f32[8,8,512]{2,1,0:T(8,128)S(1)}, u32[]{:S(2)}) copy-start(f32[8,8,512]{2,1,0:T(8,128)S(1)} %collective-permute-done.18.e) | copy-start | bytes 393220
  91.1 27.9 %collective-permute-start.19 = (f32[8,8,512]{2,1,0:T(8,128)S(1)}, f32[8,8,512]{2,1,0:T(8,128)S(1)}, u32[]{:S(2)}, u32[]{:S(2)}) collective-permute-start(f32[8,8,512]{2,1,0:T(8,128)S(1)} %collective-permute-done.18.e), channel_id=1, source_target_pairs={{0,1},{1,0},{2,3},{3,2},{4,5},{5,4},{6,7},{7,6},{8,9},{9,8},{10,11... | collective-permute-start | bytes 393224 | tf_op jit(solution)/shard_map/ppermute | solution.py:210
  92.1 9.4 %collective-permute-start.10 = (f32[16,256]{1,0:T(8,128)S(1)}, f32[16,256]{1,0:T(8,128)S(1)}, u32[]{:S(2)}, u32[]{:S(2)}) collective-permute-start(f32[16,256]{1,0:T(8,128)S(1)} %add.52), channel_id=1, source_target_pairs={{0,32},{32,0},{1,33},{33,1},{2,34},{34,2},{3,35},{35,3},{4,36},{36... | collective-permute-start | bytes 49160 | tf_op jit(solution)/shard_map/ppermute | solution.py:210
  95.1 15.0 %all-to-all-start.3 = ((f32[8,48,128]{2,1,0:T(8,128)}), f32[8,48,128]{2,1,0:T(8,128)S(1)}, u32[]{:S(2)}, u32[]{:S(2)}) async-start(f32[8,48,128]{2,1,0:T(8,128)} %broadcast_in_dim.10), calls=%async_computation.3 | async-start | bytes 393216 | tf_op jit(solution)/shard_map/all_to_all | solution.py:220
  110.2 4.1 %collective-permute-start.11 = (f32[8,48,128]{2,1,0:T(8,128)S(1)}, f32[8,48,128]{2,1,0:T(8,128)S(1)}, u32[]{:S(2)}, u32[]{:S(2)}) collective-permute-start(f32[8,48,128]{2,1,0:T(8,128)S(1)} %all-to-all-done.3), channel_id=1, source_target_pairs={{0,1},{1,0},{2,3},{3,2},{4,5},{5,4},{6,7},{7,6},{8,9},{9,8},{10,11... | collective-permute-start | bytes 589832 | tf_op jit(solution)/shard_map/ppermute | solution.py:210
  115.0 7.2 %collective-permute-start.12 = (f32[2,16,256]{2,1,0:T(8,128)S(1)}, f32[2,16,256]{2,1,0:T(8,128)S(1)}, u32[]{:S(2)}, u32[]{:S(2)}) collective-permute-start(f32[2,16,256]{2,1,0:T(8,128)S(1)} %pad_maximum_fusion.9), channel_id=1, source_target_pairs={{0,16},{16,0},{32,48},{48,32},{1,17},{17,1},{33,49},{49,33},{2,18}... | collective-permute-start | bytes 98312 | tf_op jit(solution)/shard_map/ppermute | solution.py:275
  115.5 6.8 %collective-permute-start.13 = (f32[2,16,256]{2,1,0:T(8,128)S(1)}, f32[2,16,256]{2,1,0:T(8,128)S(1)}, u32[]{:S(2)}, u32[]{:S(2)}) collective-permute-start(f32[2,16,256]{2,1,0:T(8,128)S(1)} %pad_maximum_fusion.9), channel_id=1, source_target_pairs={{0,32},{16,48},{32,0},{48,16},{1,33},{17,49},{33,1},{49,17},{2,34}... | collective-permute-start | bytes 98312 | tf_op jit(solution)/shard_map/ppermute | solution.py:275
  117.3 4.9 %collective-permute-start.14 = (f32[2,16,256]{2,1,0:T(8,128)S(1)}, f32[2,16,256]{2,1,0:T(8,128)S(1)}, u32[]{:S(2)}, u32[]{:S(2)}) collective-permute-start(f32[2,16,256]{2,1,0:T(8,128)S(1)} %pad_maximum_fusion.9), channel_id=1, source_target_pairs={{0,48},{16,32},{32,16},{48,0},{1,49},{17,33},{33,17},{49,1},{2,50}... | collective-permute-start | bytes 98312 | tf_op jit(solution)/shard_map/ppermute | solution.py:275
  118.9 0.7 copy-start.11
  118.9 0.7 copy-start.13
  122.2 12.1 %copy-start.8 = (f32[256,512]{1,0:T(8,128)S(1)}, f32[256,512]{1,0:T(8,128)}, u32[]{:S(2)}) copy-start(f32[256,512]{1,0:T(8,128)} %get-tuple-element.30) | copy-start | bytes 1572868
  122.3 2.7 %collective-permute-start.15 = (f32[16,256]{1,0:T(8,128)S(1)}, f32[16,256]{1,0:T(8,128)S(1)}, u32[]{:S(2)}, u32[]{:S(2)}) collective-permute-start(f32[16,256]{1,0:T(8,128)S(1)} %slice_bitcast_fusion.1), channel_id=1, source_target_pairs={{0,64},{64,0},{1,65},{65,1},{2,66},{66,2},{3,67},{67,3},{4,68},{68... | collective-permute-start | bytes 49160 | tf_op jit(solution)/shard_map/ppermute | solution.py:210
  122.6 4.2 %collective-permute-start.20 = (f32[256,128]{1,0:T(8,128)S(1)}, f32[256,128]{1,0:T(8,128)S(1)}, u32[]{:S(2)}, u32[]{:S(2)}) collective-permute-start(f32[256,128]{1,0:T(8,128)S(1)} %pad_maximum_fusion.6), channel_id=1, source_target_pairs={{0,16},{16,0},{1,17},{17,1},{2,18},{18,2},{3,19},{19,3},{4,20},{20... | collective-permute-start | bytes 393224 | tf_op jit(solution)/shard_map/ppermute | solution.py:210
  127.0 3.9 %collective-permute-start.21 = (f32[16,256]{1,0:T(8,128)S(1)}, f32[16,256]{1,0:T(8,128)S(1)}, u32[]{:S(2)}, u32[]{:S(2)}) collective-permute-start(f32[16,256]{1,0:T(8,128)S(1)} %fusion.62), channel_id=1, source_target_pairs={{0,64},{64,0},{128,192},{192,128},{1,65},{65,1},{129,193},{193,129... | collective-permute-start | bytes 49160 | tf_op jit(solution)/shard_map/ppermute | solution.py:275
  128.0 4.1 %collective-permute-start.22 = (f32[16,256]{1,0:T(8,128)S(1)}, f32[16,256]{1,0:T(8,128)S(1)}, u32[]{:S(2)}, u32[]{:S(2)}) collective-permute-start(f32[16,256]{1,0:T(8,128)S(1)} %fusion.62), channel_id=1, source_target_pairs={{0,128},{64,192},{128,0},{192,64},{1,129},{65,193},{129,1},{193,65... | collective-permute-start | bytes 49160 | tf_op jit(solution)/shard_map/ppermute | solution.py:275
  130.5 3.8 %collective-permute-start.23 = (f32[16,256]{1,0:T(8,128)S(1)}, f32[16,256]{1,0:T(8,128)S(1)}, u32[]{:S(2)}, u32[]{:S(2)}) collective-permute-start(f32[16,256]{1,0:T(8,128)S(1)} %fusion.62), channel_id=1, source_target_pairs={{0,192},{64,128},{128,64},{192,0},{1,193},{65,129},{129,65},{193,1... | collective-permute-start | bytes 49160 | tf_op jit(solution)/shard_map/ppermute | solution.py:275
  150.0 7.3 %copy-start = (bf16[4,1024,256]{2,1,0:T(8,128)(2,1)S(1)}, bf16[4,1024,256]{2,1,0:T(8,128)(2,1)}, u32[]{:S(2)}) copy-start(bf16[4,1024,256]{2,1,0:T(8,128)(2,1)} %w_hbm.1) | copy-start | bytes 6291460
  150.0 7.0 %collective-permute-start.24 = (f32[8,64,256]{2,1,0:T(8,128)S(1)}, f32[8,64,256]{2,1,0:T(8,128)S(1)}, u32[]{:S(2)}, u32[]{:S(2)}) collective-permute-start(f32[8,64,256]{2,1,0:T(8,128)S(1)} %all_to_all.25), channel_id=1, source_target_pairs={{0,1},{1,0},{2,3},{3,2},{4,5},{5,4},{6,7},{7,6},{8,9},{9,8},{10,11... | collective-permute-start | bytes 1572872 | tf_op jit(solution)/shard_map/ppermute | solution.py:210
  157.3 1.2 copy-start.4

commit v8 on v7

--- a/solution.py
+++ b/solution.py
@@ -244,9 +244,9 @@
     got = partner(jnp.concatenate([give, pairs[:, 5:]], axis=1), "yh")
     keep = jnp.where(upper, fours[:, :, :8], fours[:, :, 8:]).reshape(Z, 1, 16, 128)
     fours = jnp.concatenate([keep, pairs[:, 5:]], axis=1) + got
-    rows_c = partner(rows, "c")
     a0 = rows[:, 16:32]
     a1 = partner(a0, "yl")
+    rows_c = partner(rows, "c")
     a1_c = partner(a1, "c")
     b0 = jnp.concatenate([a0[:, 8:], a1[:, 8:]], axis=1)
     b1 = partner(b0, "yh")
@@ -303,9 +303,8 @@
     sums = mixed[:, 96:].sum(axis=0)
     third = spread(jnp.concatenate([sums[16:48], sums[64:80]], axis=0), "z", Z)
     t = in_lanes(sums[0:16]) - times(m4, g34)
-    got = partner(t, "yl")
-    t = t + got
-    m3 = mix(full3, t, partner(t, "yh"), "yh")
+    four = of_four(t, ("yh", "yl"))
+    m3 = mix(full3, four[0] + four[1], four[2] + four[3], "yh")
     own, m3 = lax.optimization_barrier((third, m3))
     t2 = in_rows(in_lanes(sums[48:56])) - times(m4, g24)
     t1 = in_rows(in_lanes(sums[56:64])) - times(m4, g14)

time: 161 us -> 160 us (level)
    ppermute x6 -> x9, starting transfers between devices: 7.89 us -> 11.5 us  [of_four(): got[k] = lax.ppermute(block, axes, [(i, i ^ k) for i in range(4)])]
    ppermute x19 -> x17, starting transfers between devices: 31.4 us -> 27.9 us  [partner(): return lax.ppermute(block, axis, [(0, 1), (1, 0)])]
    ppermute x19 -> x17, waiting for transfers between devices: 18.8 us -> 17.5 us  [partner(): return lax.ppermute(block, axis, [(0, 1), (1, 0)])]
    ppermute x6 -> x9, waiting for transfers between devices: 3.32 us -> 3.67 us  [of_four(): got[k] = lax.ppermute(block, axes, [(i, i ^ k) for i in range(4)])]
  transfers between devices with their start and end apart: 29 -> 30, of which waited for: 14 -> 13; matrix products, arithmetic and copies ran while one was open for 5% -> 5% of each run, Pallas kernels for 4% -> 4%
where the time goes in v8:
time: 160 us; the launch traced here: 159 us
  starting transfers between devices  59.2 us (37%)
  waiting for transfers between devices  55.2 us (34%)
  blocking collectives  14.8 us (9%)
  Pallas kernels  14.4 us (9%)
  matrix products  6.78 us (4%)
  other arithmetic  4.36 us (3%)
  local copies, waits for them, and re-layouts  3.66 us (2%)
    all_to_all x4, waiting for transfers between devices, exchange(): return lax.all_to_all(block, axes, 0, 0, tiled=True)  34.1 us
    ppermute x17, starting transfers between devices, partner(): return lax.ppermute(block, axis, [(0, 1), (1, 0)])  27.9 us
    all_to_all x4, starting transfers between devices, exchange(): return lax.all_to_all(block, axes, 0, 0, tiled=True)  19.8 us
    ppermute x17, waiting for transfers between devices, partner(): return lax.ppermute(block, axis, [(0, 1), (1, 0)])  17.5 us
    all_to_all x1, blocking collectives, exchange(): return lax.all_to_all(block, axes, 0, 0, tiled=True)  14.8 us
    ppermute x9, starting transfers between devices, of_four(): got[k] = lax.ppermute(block, axes, [(i, i ^ k) for i in range(4)])  11.5 us
    pallas_call x1, Pallas kernels, leaf(): pl.pallas_call(leaf_kernel, in_specs=[pl.BlockSpec(memory_space=pltpu.SME...  7.9 us
    pallas_call x2, Pallas kernels, assemble(): pl.pallas_call(kernel, grid=(1,), in_specs=[pl.BlockSpec(memory_space=plt...  4.84 us
  transfers between devices with their start and end apart: 30, of which 13 were waited for; matrix products, arithmetic and copies ran while one was open for 5% of the time, Pallas kernels for 4%

profile of v8, /device:TPU:1, one launch (start us, length us, event | category | flops | bytes accessed | tf_op | source)
XLA Modules:
  0.0 158.9 jit_solution(15034457079623928861)
XLA Ops:
  0.0 7.9 %leaf.1 = (f32[1024,256]{1,0:T(8,128)}, f32[8,4,16,256]{3,2,1,0:T(8,128)}, f32[8,4,16,256]{3,2,1,0:T(8,128)}, f32[2,8,6,16,128]{4,3,2,1,0:T(8,128)}, f32[2,8,6,16,128]{4,3,2,1,0:T(8,128)}) custom-call(s32[1]{0:T(128)} %bitcast.core_ref, s32[1]{0:T(128)} %bitcast.1.pair_ref.yl_ref, bf16[1024,1024]{1,0:T(8,128)(2,1)} %inv_hbm.1, bf16[1024,256]{1,0:T(8,128)(2,1)} %rhs_hbm.1, ...), custom_call_target="tpu_custom_call" | custom-call | tf_op jit(solution)/shard_map/leaf/pallas_call | solution.py:127
  7.9 3.3 %collective-permute-start.2 = (f32[2,8,6,16,128]{4,3,2,1,0:T(8,128)}, f32[2,8,6,16,128]{4,3,2,1,0:T(8,128)S(1)}, u32[]{:S(2)}, u32[]{:S(2)}) collective-permute-start(f32[2,8,6,16,128]{4,3,2,1,0:T(8,128)} %get-tuple-element.22), channel_id=1, source_target_pairs={{0,1},{1,0},{2,3},{3,2},{4,5},{5,4},{6,7},{7,6},{8,9},{9,8},{10,11... | collective-permute-start | bytes 2359304 | tf_op jit(solution)/shard_map/ppermute | solution.py:210
  11.2 1.6 %pack.1 = f32[8,32,512]{2,1,0:T(8,128)} custom-call(f32[16,512]{1,0:T(8,128)} %a_ref.1, f32[8,512]{1,0:T(8,128)} %b_ref.1, f32[4,512]{1,0:T(4,128)} %c_ref.1, f32[2,512]{1,0:T(2,128)} %d_ref.1), custom_call_target="tpu_custom_call" | custom-call | tf_op jit(solution)/shard_map/pack/pallas_call | solution.py:39
  12.8 6.5 %all-to-all-start.1 = ((f32[8,32,512]{2,1,0:T(8,128)}), f32[8,32,512]{2,1,0:T(8,128)S(1)}, u32[]{:S(2)}, u32[]{:S(2)}) async-start(f32[8,32,512]{2,1,0:T(8,128)} %pack.1), calls=%async_computation.1 | async-start | bytes 1048576 | tf_op jit(solution)/shard_map/all_to_all | solution.py:220
  19.3 0.4 collective-permute-start
  19.7 1.8 %fusion.9 = f32[8,6,16,128]{3,2,1,0:T(8,128)} fusion(f32[2,8,6,16,128]{4,3,2,1,0:T(8,128)S(1)} %collective-permute-done.2, f32[2,8,6,16,128]{4,3,2,1,0:T(8,128)} %get-tuple-element.21), kind=kLoop, calls=%fused_computation.18 | loop fusion | flops 98304 | bytes 1179648 | tf_op jit(solution)/shard_map/add | solution.py:237
  21.5 1.3 collective-permute-start.3
  22.9 0.9 add.48
  23.8 13.5 %all-to-all-done.1.rows = f32[8,32,512]{2,1,0:T(8,128)S(1)} async-done(((f32[8,32,512]{2,1,0:T(8,128)}), f32[8,32,512]{2,1,0:T(8,128)S(1)}, u32[]{:S(2)}, u32[]{:S(2)}) %all-to-all-start.1) | async-done | bytes 524320 | tf_op jit(solution)/shard_map/all_to_all | solution.py:220
  37.3 3.5 %all-to-all-start = ((f32[8,4,16,256]{3,2,1,0:T(8,128)}), f32[8,4,16,256]{3,2,1,0:T(8,128)S(1)}, u32[]{:S(2)}, u32[]{:S(2)}) async-start(f32[8,4,16,256]{3,2,1,0:T(8,128)} %add.48), calls=%async_computation | async-start | bytes 1048576 | tf_op jit(solution)/shard_map/all_to_all | solution.py:220
  41.0 3.0 %collective-permute-start.7 = (f32[8,2,16,128]{3,2,1,0:T(8,128)S(1)}, f32[8,2,16,128]{3,2,1,0:T(8,128)S(1)}, u32[]{:S(2)}, u32[]{:S(2)}) collective-permute-start(f32[8,2,16,128]{3,2,1,0:T(8,128)S(1)} %pad_maximum_fusion.3), channel_id=1, source_target_pairs={{0,32},{32,0},{1,33},{33,1},{2,34},{34,2},{3,35},{35,3},{4,36},{36... | collective-permute-start | bytes 393224 | tf_op jit(solution)/shard_map/ppermute | solution.py:210
  44.0 3.2 %collective-permute-done.7 = f32[8,2,16,128]{3,2,1,0:T(8,128)S(1)} collective-permute-done((f32[8,2,16,128]{3,2,1,0:T(8,128)S(1)}, f32[8,2,16,128]{3,2,1,0:T(8,128)S(1)}, u32[]{:S(2)}, u32[]{:S(2)}) %collective-permute-start.7) | collective-permute-done | bytes 131104 | tf_op jit(solution)/shard_map/ppermute | solution.py:210
  47.2 11.5 %all-to-all-done = f32[8,4,16,256]{3,2,1,0:T(8,128)S(1)} async-done(((f32[8,4,16,256]{3,2,1,0:T(8,128)}), f32[8,4,16,256]{3,2,1,0:T(8,128)S(1)}, u32[]{:S(2)}, u32[]{:S(2)}) %all-to-all-start) | async-done | bytes 524320 | tf_op jit(solution)/shard_map/all_to_all | solution.py:220
  58.8 0.9 pad_maximum_fusion.1
  59.7 3.5 %all-to-all-start.2 = ((f32[8,176,128]{2,1,0:T(8,128)}), f32[8,176,128]{2,1,0:T(8,128)S(1)}, u32[]{:S(2)}, u32[]{:S(2)}) async-start(f32[8,176,128]{2,1,0:T(8,128)} %pad_maximum_fusion.1), calls=%async_computation.2 | async-start | bytes 1441792 | tf_op jit(solution)/shard_map/all_to_all | solution.py:220
  63.3 1.4 collective-permute-start.5
  64.7 6.1 %collective-permute-done.5.a = f32[8,16,512]{2,1,0:T(8,128)S(1)} collective-permute-done((f32[8,16,512]{2,1,0:T(8,128)S(1)}, f32[8,16,512]{2,1,0:T(8,128)S(1)}, u32[]{:S(2)}, u32[]{:S(2)}) %collective-permute-start.5) | collective-permute-done | bytes 262176 | tf_op jit(solution)/shard_map/ppermute | solution.py:210
  70.8 3.0 %collective-permute-start.17 = (f32[8,16,512]{2,1,0:T(8,128)S(1)}, f32[8,16,512]{2,1,0:T(8,128)S(1)}, u32[]{:S(2)}, u32[]{:S(2)}) collective-permute-start(f32[8,16,512]{2,1,0:T(8,128)S(1)} %pad_maximum_fusion.2), channel_id=1, source_target_pairs={{0,32},{32,0},{1,33},{33,1},{2,34},{34,2},{3,35},{35,3},{4,36},{36... | collective-permute-start | bytes 786440 | tf_op jit(solution)/shard_map/ppermute | solution.py:210
  73.8 0.4 collective-permute-start.1
  74.2 1.9 %collective-permute-start.4 = (f32[8,32,512]{2,1,0:T(8,128)S(1)}, f32[8,32,512]{2,1,0:T(8,128)S(1)}, u32[]{:S(2)}, u32[]{:S(2)}) collective-permute-start(f32[8,32,512]{2,1,0:T(8,128)S(1)} %all-to-all-done.1.rows), channel_id=1, source_target_pairs={{0,1},{1,0},{2,3},{3,2},{4,5},{5,4},{6,7},{7,6},{8,9},{9,8},{10,11... | collective-permute-start | bytes 1572872 | tf_op jit(solution)/shard_map/ppermute | solution.py:210
  76.2 3.4 %collective-permute-done.1 = f32[16,256]{1,0:T(8,128)S(1)} collective-permute-done((f32[16,256]{1,0:T(8,128)S(1)}, f32[16,256]{1,0:T(8,128)S(1)}, u32[]{:S(2)}, u32[]{:S(2)}) %collective-permute-start.1) | collective-permute-done | bytes 16416 | tf_op jit(solution)/shard_map/ppermute | solution.py:210
  79.7 1.3 collective-permute-start.19
  81.0 0.7 copy-done.5
  81.7 0.8 copy-done.2
  82.5 2.3 %shard_map.82 = (f32[256,512]{1,0:T(8,128)}, f32[256,512]{1,0:T(8,128)}) custom-call(s32[1]{0:T(128)} %bitcast.core_ref, s32[1]{0:T(128)} %bitcast.1.pair_ref.yl_ref, f32[8,32,512]{2,1,0:T(8,128)} %copy-done.1, f32[8,32,512]{2,1,0:T(8,128)} %copy-done.2, f32[8,16,512]{2,1,0:T(8,128)} %copy-done.3, f32[8,16,512]{2,1,0:T(8,128)} %copy-done.5), custom_call_target="tpu_custom_call" | custom-call | tf_op jit(solution)/shard_map/pallas_call | solution.py:200
  84.8 0.5 all-to-all-done.2
  85.3 2.1 %collective-permute-start.8 = (f32[8,96,128]{2,1,0:T(8,128)S(1)}, f32[8,96,128]{2,1,0:T(8,128)S(1)}, u32[]{:S(2)}, u32[]{:S(2)}) collective-permute-start(f32[8,96,128]{2,1,0:T(8,128)S(1)} %slice.239), channel_id=1, source_target_pairs={{0,1},{1,0},{2,3},{3,2},{4,5},{5,4},{6,7},{7,6},{8,9},{9,8},{10,11... | collective-permute-start | bytes 1179656 | tf_op jit(solution)/shard_map/ppermute | solution.py:210
  87.4 1.4 fusion.46
  89.0 0.5 collective-permute-start.20
  89.6 0.1 convolution_subtract_fusion.2
  89.8 2.5 %collective-permute-start.10 = (f32[16,256]{1,0:T(8,128)S(1)}, f32[16,256]{1,0:T(8,128)S(1)}, u32[]{:S(2)}, u32[]{:S(2)}) collective-permute-start(f32[16,256]{1,0:T(8,128)S(1)} %convolution_subtract_fusion.2), channel_id=1, source_target_pairs={{0,32},{16,48},{32,0},{48,16},{1,33},{17,49},{33,1},{49,17},{2,34}... | collective-permute-start | bytes 49160 | tf_op jit(solution)/shard_map/ppermute | solution.py:275
  92.2 1.1 collective-permute-start.11
  93.3 0.7 broadcast_in_dim.10
  94.0 6.3 %all-to-all-start.3 = ((f32[8,48,128]{2,1,0:T(8,128)}), f32[8,48,128]{2,1,0:T(8,128)S(1)}, u32[]{:S(2)}, u32[]{:S(2)}) async-start(f32[8,48,128]{2,1,0:T(8,128)} %broadcast_in_dim.10), calls=%async_computation.3 | async-start | bytes 393216 | tf_op jit(solution)/shard_map/all_to_all | solution.py:220
  100.3 0.3 fusion.50
  100.7 8.5 %all-to-all-done.3 = f32[8,48,128]{2,1,0:T(8,128)S(1)} async-done(((f32[8,48,128]{2,1,0:T(8,128)}), f32[8,48,128]{2,1,0:T(8,128)S(1)}, u32[]{:S(2)}, u32[]{:S(2)}) %all-to-all-start.3) | async-done | bytes 196640 | tf_op jit(solution)/shard_map/all_to_all | solution.py:220
  109.2 2.5 %collective-permute-start.12 = (f32[8,48,128]{2,1,0:T(8,128)S(1)}, f32[8,48,128]{2,1,0:T(8,128)S(1)}, u32[]{:S(2)}, u32[]{:S(2)}) collective-permute-start(f32[8,48,128]{2,1,0:T(8,128)S(1)} %all-to-all-done.3), channel_id=1, source_target_pairs={{0,1},{1,0},{2,3},{3,2},{4,5},{5,4},{6,7},{7,6},{8,9},{9,8},{10,11... | collective-permute-start | bytes 589832 | tf_op jit(solution)/shard_map/ppermute | solution.py:210
  111.7 1.1 collective-permute-done.12
  112.8 0.2 broadcast_select_fusion.13
  113.0 0.2 broadcast_select_fusion.11
  113.1 0.2 fusion.6
  113.3 0.2 fusion.4
  113.5 1.5 collective-permute-start.13
  115.1 1.4 collective-permute-start.14
  116.5 1.1 collective-permute-start.15
  117.6 0.7 copy-done.11
  118.3 2.5 %shard_map.83 = (f32[256,512]{1,0:T(8,128)}, f32[256,512]{1,0:T(8,128)}) custom-call(s32[1]{0:T(128)} %bitcast.core_ref, s32[1]{0:T(128)} %bitcast.1.pair_ref.yl_ref, s32[1]{0:T(128)} %bitcast.29.yh_ref, s32[1]{0:T(128)} %bitcast.30.xl_ref, f32[8,32,512]{2,1,0:T(8,128)} %copy-done.1, f32[8,32,512]{2,1,0:T(8,128)} %copy-done.2, f32[8,16,512]{2,1,0:T(8,128)} %copy-done.3, ...), custom_call_target="tpu_custom_call" | custom-call | tf_op jit(solution)/shard_map/pallas_call | solution.py:200
  120.9 0.3 collective-permute-start.16
  121.3 0.2 collective-permute-start.21
  121.5 2.1 %collective-permute-done.16 = f32[16,256]{1,0:T(8,128)S(1)} collective-permute-done((f32[16,256]{1,0:T(8,128)S(1)}, f32[16,256]{1,0:T(8,128)S(1)}, u32[]{:S(2)}, u32[]{:S(2)}) %collective-permute-start.16) | collective-permute-done | bytes 16416 | tf_op jit(solution)/shard_map/ppermute | solution.py:210
  123.6 1.3 fusion.54
  125.0 0.2 collective-permute-done.21
  125.2 0.1 fusion.62
  125.4 1.3 collective-permute-start.22
  126.7 2.5 %collective-permute-start.23 = (f32[16,256]{1,0:T(8,128)S(1)}, f32[16,256]{1,0:T(8,128)S(1)}, u32[]{:S(2)}, u32[]{:S(2)}) collective-permute-start(f32[16,256]{1,0:T(8,128)S(1)} %fusion.62), channel_id=1, source_target_pairs={{0,128},{64,192},{128,0},{192,64},{1,129},{65,193},{129,1},{193,65... | collective-permute-start | bytes 49160 | tf_op jit(solution)/shard_map/ppermute | solution.py:275
  129.3 1.4 collective-permute-done.23
  130.7 2.2 %collective-permute-done.24 = f32[16,256]{1,0:T(8,128)S(1)} collective-permute-done((f32[16,256]{1,0:T(8,128)S(1)}, f32[16,256]{1,0:T(8,128)S(1)}, u32[]{:S(2)}, u32[]{:S(2)}) %collective-permute-start.24) | collective-permute-done | bytes 16416 | tf_op jit(solution)/shard_map/ppermute | solution.py:275
  133.0 0.3 fusion.58
  133.4 14.8 %all_to_all.25 = f32[8,64,256]{2,1,0:T(8,128)S(1)} all-to-all(f32[8,64,256]{2,1,0:T(8,128)S(1)} %broadcast_in_dim.11), channel_id=1, replica_groups=mesh['xh'=2,'xl'=2,'yh'=2,'yl'=2,'z'=8,'c'=2] {'z'}, dimensions={0} | all-to-all | bytes 1048576 | tf_op jit(solution)/shard_map/all_to_all | solution.py:220
  148.2 6.0 %collective-permute-start.25 = (f32[8,64,256]{2,1,0:T(8,128)S(1)}, f32[8,64,256]{2,1,0:T(8,128)S(1)}, u32[]{:S(2)}, u32[]{:S(2)}) collective-permute-start(f32[8,64,256]{2,1,0:T(8,128)S(1)} %all_to_all.25), channel_id=1, source_target_pairs={{0,1},{1,0},{2,3},{3,2},{4,5},{5,4},{6,7},{7,6},{8,9},{9,8},{10,11... | collective-permute-start | bytes 1572872 | tf_op jit(solution)/shard_map/ppermute | solution.py:210
  154.2 1.5 collective-permute-done.25
  156.0 0.7 convolution_bitcast_fusion
  156.8 0.5 copy-done.4
  157.2 1.7 %fusion.2 = f32[1024,256]{1,0:T(8,128)} fusion(f32[1024,256]{1,0:T(8,128)S(1)} %copy-done.4, f32[256,1024]{0,1:T(8,128)S(1)} %convolution_bitcast_fusion, bf16[4,1024,256]{2,1,0:T(8,128)(2,1)S(1)} %copy-done, f32[1,256,256]{2,1,0:T(8,128)S(1)} %maximum_bitcast_fusion.3, f32[1,256,256]{2,1,0:T(8,128)S(1)} %maximum_bitcast_fusion.2, ...), kind=kOutput, calls=%fused_computation.6 | convolution fusion | flops 538705920 | bytes 6291456 | tf_op jit(solution)/shard_map/dot_general | solution.py:20
  (90 shorter events, 1.5 us)
Async XLA Ops:
  7.9 14.9 %copy-start.7 = (f32[8,4,16,256]{3,2,1,0:T(8,128)S(1)}, f32[8,4,16,256]{3,2,1,0:T(8,128)}, u32[]{:S(2)}) copy-start(f32[8,4,16,256]{3,2,1,0:T(8,128)} %get-tuple-element.19) | copy-start | bytes 1572868
  7.9 11.8 %collective-permute-start.2 = (f32[2,8,6,16,128]{4,3,2,1,0:T(8,128)}, f32[2,8,6,16,128]{4,3,2,1,0:T(8,128)S(1)}, u32[]{:S(2)}, u32[]{:S(2)}) collective-permute-start(f32[2,8,6,16,128]{4,3,2,1,0:T(8,128)} %get-tuple-element.22), channel_id=1, source_target_pairs={{0,1},{1,0},{2,3},{3,2},{4,5},{5,4},{6,7},{7,6},{8,9},{9,8},{10,11... | collective-permute-start | bytes 2359304 | tf_op jit(solution)/shard_map/ppermute | solution.py:210
  12.8 24.5 %all-to-all-start.1 = ((f32[8,32,512]{2,1,0:T(8,128)}), f32[8,32,512]{2,1,0:T(8,128)S(1)}, u32[]{:S(2)}, u32[]{:S(2)}) async-start(f32[8,32,512]{2,1,0:T(8,128)} %pack.1), calls=%async_computation.1 | async-start | bytes 1048576 | tf_op jit(solution)/shard_map/all_to_all | solution.py:220
  19.3 21.5 %copy-start.6 = (f32[2,8,6,16,128]{4,3,2,1,0:T(8,128)S(1)}, f32[2,8,6,16,128]{4,3,2,1,0:T(8,128)}, u32[]{:S(2)}) copy-start(f32[2,8,6,16,128]{4,3,2,1,0:T(8,128)} %get-tuple-element.21) | copy-start | bytes 2359300
  19.3 3.5 %collective-permute-start = (f32[8,4,16,256]{3,2,1,0:T(8,128)}, f32[8,4,16,256]{3,2,1,0:T(8,128)S(1)}, u32[]{:S(2)}, u32[]{:S(2)}) collective-permute-start(f32[8,4,16,256]{3,2,1,0:T(8,128)} %get-tuple-element.20), channel_id=1, source_target_pairs={{0,1},{1,0},{2,3},{3,2},{4,5},{5,4},{6,7},{7,6},{8,9},{9,8},{10,11... | collective-permute-start | bytes 1572872 | tf_op jit(solution)/shard_map/ppermute | solution.py:210
  21.5 19.2 %collective-permute-start.3 = (f32[8,6,16,128]{3,2,1,0:T(8,128)}, f32[8,6,16,128]{3,2,1,0:T(8,128)S(1)}, u32[]{:S(2)}, u32[]{:S(2)}) collective-permute-start(f32[8,6,16,128]{3,2,1,0:T(8,128)} %fusion.9), channel_id=1, source_target_pairs={{0,16},{16,0},{1,17},{17,1},{2,18},{18,2},{3,19},{19,3},{4,20},{20... | collective-permute-start | bytes 1179656 | tf_op jit(solution)/shard_map/ppermute | solution.py:210
  37.3 38.8 %copy-start.1 = (f32[8,32,512]{2,1,0:T(8,128)}, f32[8,32,512]{2,1,0:T(8,128)S(1)}, u32[]{:S(2)}) copy-start(f32[8,32,512]{2,1,0:T(8,128)S(1)} %all-to-all-done.1.rows) | copy-start | bytes 1572868
  37.3 21.4 %all-to-all-start = ((f32[8,4,16,256]{3,2,1,0:T(8,128)}), f32[8,4,16,256]{3,2,1,0:T(8,128)S(1)}, u32[]{:S(2)}, u32[]{:S(2)}) async-start(f32[8,4,16,256]{3,2,1,0:T(8,128)} %add.48), calls=%async_computation | async-start | bytes 1048576 | tf_op jit(solution)/shard_map/all_to_all | solution.py:220
  41.0 6.2 %collective-permute-start.7 = (f32[8,2,16,128]{3,2,1,0:T(8,128)S(1)}, f32[8,2,16,128]{3,2,1,0:T(8,128)S(1)}, u32[]{:S(2)}, u32[]{:S(2)}) collective-permute-start(f32[8,2,16,128]{3,2,1,0:T(8,128)S(1)} %pad_maximum_fusion.3), channel_id=1, source_target_pairs={{0,32},{32,0},{1,33},{33,1},{2,34},{34,2},{3,35},{35,3},{4,36},{36... | collective-permute-start | bytes 393224 | tf_op jit(solution)/shard_map/ppermute | solution.py:210
  59.7 25.6 %all-to-all-start.2 = ((f32[8,176,128]{2,1,0:T(8,128)}), f32[8,176,128]{2,1,0:T(8,128)S(1)}, u32[]{:S(2)}, u32[]{:S(2)}) async-start(f32[8,176,128]{2,1,0:T(8,128)} %pad_maximum_fusion.1), calls=%async_computation.2 | async-start | bytes 1441792 | tf_op jit(solution)/shard_map/all_to_all | solution.py:220
  63.3 7.5 %collective-permute-start.5 = (f32[8,16,512]{2,1,0:T(8,128)S(1)}, f32[8,16,512]{2,1,0:T(8,128)S(1)}, u32[]{:S(2)}, u32[]{:S(2)}) collective-permute-start(f32[8,16,512]{2,1,0:T(8,128)S(1)} %slice.181), channel_id=1, source_target_pairs={{0,16},{16,0},{1,17},{17,1},{2,18},{18,2},{3,19},{19,3},{4,20},{20... | collective-permute-start | bytes 786440 | tf_op jit(solution)/shard_map/ppermute | solution.py:210
  70.7 10.3 %copy-start.3 = (f32[8,16,512]{2,1,0:T(8,128)}, f32[8,16,512]{2,1,0:T(8,128)S(1)}, u32[]{:S(2)}) copy-start(f32[8,16,512]{2,1,0:T(8,128)S(1)} %collective-permute-done.5.a) | copy-start | bytes 786436
  70.8 8.8 %collective-permute-start.17 = (f32[8,16,512]{2,1,0:T(8,128)S(1)}, f32[8,16,512]{2,1,0:T(8,128)S(1)}, u32[]{:S(2)}, u32[]{:S(2)}) collective-permute-start(f32[8,16,512]{2,1,0:T(8,128)S(1)} %pad_maximum_fusion.2), channel_id=1, source_target_pairs={{0,32},{32,0},{1,33},{33,1},{2,34},{34,2},{3,35},{35,3},{4,36},{36... | collective-permute-start | bytes 786440 | tf_op jit(solution)/shard_map/ppermute | solution.py:210
  73.8 5.8 %collective-permute-start.1 = (f32[16,256]{1,0:T(8,128)S(1)}, f32[16,256]{1,0:T(8,128)S(1)}, u32[]{:S(2)}, u32[]{:S(2)}) collective-permute-start(f32[16,256]{1,0:T(8,128)S(1)} %slice_bitcast_fusion.2), channel_id=1, source_target_pairs={{0,16},{16,0},{1,17},{17,1},{2,18},{18,2},{3,19},{19,3},{4,20},{20... | collective-permute-start | bytes 49160 | tf_op jit(solution)/shard_map/ppermute | solution.py:210
  74.2 6.8 %collective-permute-start.4 = (f32[8,32,512]{2,1,0:T(8,128)S(1)}, f32[8,32,512]{2,1,0:T(8,128)S(1)}, u32[]{:S(2)}, u32[]{:S(2)}) collective-permute-start(f32[8,32,512]{2,1,0:T(8,128)S(1)} %all-to-all-done.1.rows), channel_id=1, source_target_pairs={{0,1},{1,0},{2,3},{3,2},{4,5},{5,4},{6,7},{7,6},{8,9},{9,8},{10,11... | collective-permute-start | bytes 1572872 | tf_op jit(solution)/shard_map/ppermute | solution.py:210
  76.1 4.9 %collective-permute-start.6 = (f32[8,16,512]{2,1,0:T(8,128)S(1)}, f32[8,16,512]{2,1,0:T(8,128)S(1)}, u32[]{:S(2)}, u32[]{:S(2)}) collective-permute-start(f32[8,16,512]{2,1,0:T(8,128)S(1)} %collective-permute-done.5.a), channel_id=1, source_target_pairs={{0,1},{1,0},{2,3},{3,2},{4,5},{5,4},{6,7},{7,6},{8,9},{9,8},{10,11... | collective-permute-start | bytes 786440 | tf_op jit(solution)/shard_map/ppermute | solution.py:210
  79.6 10.0 %copy-start.10 = (f32[8,16,512]{2,1,0:T(8,128)}, f32[8,16,512]{2,1,0:T(8,128)S(1)}, u32[]{:S(2)}) copy-start(f32[8,16,512]{2,1,0:T(8,128)S(1)} %collective-permute-done.17.b) | copy-start | bytes 786436
  79.7 9.3 %collective-permute-start.19 = (f32[8,8,512]{2,1,0:T(8,128)S(1)}, f32[8,8,512]{2,1,0:T(8,128)S(1)}, u32[]{:S(2)}, u32[]{:S(2)}) collective-permute-start(f32[8,8,512]{2,1,0:T(8,128)S(1)} %pad_maximum_fusion.5), channel_id=1, source_target_pairs={{0,64},{64,0},{1,65},{65,1},{2,66},{66,2},{3,67},{67,3},{4,68},{68... | collective-permute-start | bytes 393224 | tf_op jit(solution)/shard_map/ppermute | solution.py:210
  81.0 0.7 copy-start.5
  81.7 0.8 copy-start.2
  85.3 4.2 %collective-permute-start.8 = (f32[8,96,128]{2,1,0:T(8,128)S(1)}, f32[8,96,128]{2,1,0:T(8,128)S(1)}, u32[]{:S(2)}, u32[]{:S(2)}) collective-permute-start(f32[8,96,128]{2,1,0:T(8,128)S(1)} %slice.239), channel_id=1, source_target_pairs={{0,1},{1,0},{2,3},{3,2},{4,5},{5,4},{6,7},{7,6},{8,9},{9,8},{10,11... | collective-permute-start | bytes 1179656 | tf_op jit(solution)/shard_map/ppermute | solution.py:210
  87.4 12.9 %copy-start.9 = (f32[256,512]{1,0:T(8,128)S(1)}, f32[256,512]{1,0:T(8,128)}, u32[]{:S(2)}) copy-start(f32[256,512]{1,0:T(8,128)} %get-tuple-element.26) | copy-start | bytes 1572868
  88.8 28.7 %collective-permute-start.18 = (f32[8,16,512]{2,1,0:T(8,128)S(1)}, f32[8,16,512]{2,1,0:T(8,128)S(1)}, u32[]{:S(2)}, u32[]{:S(2)}) collective-permute-start(f32[8,16,512]{2,1,0:T(8,128)S(1)} %collective-permute-done.17.b), channel_id=1, source_target_pairs={{0,1},{1,0},{2,3},{3,2},{4,5},{5,4},{6,7},{7,6},{8,9},{9,8},{10,11... | collective-permute-start | bytes 786440 | tf_op jit(solution)/shard_map/ppermute | solution.py:210
  89.0 11.7 %copy-start.12 = (f32[8,8,512]{2,1,0:T(8,128)}, f32[8,8,512]{2,1,0:T(8,128)S(1)}, u32[]{:S(2)}) copy-start(f32[8,8,512]{2,1,0:T(8,128)S(1)} %collective-permute-done.19.e) | copy-start | bytes 393220
  89.0 28.6 %collective-permute-start.20 = (f32[8,8,512]{2,1,0:T(8,128)S(1)}, f32[8,8,512]{2,1,0:T(8,128)S(1)}, u32[]{:S(2)}, u32[]{:S(2)}) collective-permute-start(f32[8,8,512]{2,1,0:T(8,128)S(1)} %collective-permute-done.19.e), channel_id=1, source_target_pairs={{0,1},{1,0},{2,3},{3,2},{4,5},{5,4},{6,7},{7,6},{8,9},{9,8},{10,11... | collective-permute-start | bytes 393224 | tf_op jit(solution)/shard_map/ppermute | solution.py:210
  89.8 10.5 %collective-permute-start.10 = (f32[16,256]{1,0:T(8,128)S(1)}, f32[16,256]{1,0:T(8,128)S(1)}, u32[]{:S(2)}, u32[]{:S(2)}) collective-permute-start(f32[16,256]{1,0:T(8,128)S(1)} %convolution_subtract_fusion.2), channel_id=1, source_target_pairs={{0,32},{16,48},{32,0},{48,16},{1,33},{17,49},{33,1},{49,17},{2,34}... | collective-permute-start | bytes 49160 | tf_op jit(solution)/shard_map/ppermute | solution.py:275
  92.2 8.1 %collective-permute-start.11 = (f32[16,256]{1,0:T(8,128)S(1)}, f32[16,256]{1,0:T(8,128)S(1)}, u32[]{:S(2)}, u32[]{:S(2)}) collective-permute-start(f32[16,256]{1,0:T(8,128)S(1)} %convolution_subtract_fusion.2), channel_id=1, source_target_pairs={{0,48},{16,32},{32,16},{48,0},{1,49},{17,33},{33,17},{49,1},{2,50}... | collective-permute-start | bytes 49160 | tf_op jit(solution)/shard_map/ppermute | solution.py:275
  93.3 7.0 %collective-permute-start.9 = (f32[16,256]{1,0:T(8,128)S(1)}, f32[16,256]{1,0:T(8,128)S(1)}, u32[]{:S(2)}, u32[]{:S(2)}) collective-permute-start(f32[16,256]{1,0:T(8,128)S(1)} %convolution_subtract_fusion.2), channel_id=1, source_target_pairs={{0,16},{16,0},{32,48},{48,32},{1,17},{17,1},{33,49},{49,33},{2,18}... | collective-permute-start | bytes 49160 | tf_op jit(solution)/shard_map/ppermute | solution.py:275
  94.0 15.2 %all-to-all-start.3 = ((f32[8,48,128]{2,1,0:T(8,128)}), f32[8,48,128]{2,1,0:T(8,128)S(1)}, u32[]{:S(2)}, u32[]{:S(2)}) async-start(f32[8,48,128]{2,1,0:T(8,128)} %broadcast_in_dim.10), calls=%async_computation.3 | async-start | bytes 393216 | tf_op jit(solution)/shard_map/all_to_all | solution.py:220
  109.2 3.6 %collective-permute-start.12 = (f32[8,48,128]{2,1,0:T(8,128)S(1)}, f32[8,48,128]{2,1,0:T(8,128)S(1)}, u32[]{:S(2)}, u32[]{:S(2)}) collective-permute-start(f32[8,48,128]{2,1,0:T(8,128)S(1)} %all-to-all-done.3), channel_id=1, source_target_pairs={{0,1},{1,0},{2,3},{3,2},{4,5},{5,4},{6,7},{7,6},{8,9},{9,8},{10,11... | collective-permute-start | bytes 589832 | tf_op jit(solution)/shard_map/ppermute | solution.py:210
  113.5 7.3 %collective-permute-start.13 = (f32[2,16,256]{2,1,0:T(8,128)S(1)}, f32[2,16,256]{2,1,0:T(8,128)S(1)}, u32[]{:S(2)}, u32[]{:S(2)}) collective-permute-start(f32[2,16,256]{2,1,0:T(8,128)S(1)} %pad_maximum_fusion.9), channel_id=1, source_target_pairs={{0,16},{16,0},{32,48},{48,32},{1,17},{17,1},{33,49},{49,33},{2,18}... | collective-permute-start | bytes 98312 | tf_op jit(solution)/shard_map/ppermute | solution.py:275
  115.1 5.8 %collective-permute-start.14 = (f32[2,16,256]{2,1,0:T(8,128)S(1)}, f32[2,16,256]{2,1,0:T(8,128)S(1)}, u32[]{:S(2)}, u32[]{:S(2)}) collective-permute-start(f32[2,16,256]{2,1,0:T(8,128)S(1)} %pad_maximum_fusion.9), channel_id=1, source_target_pairs={{0,32},{16,48},{32,0},{48,16},{1,33},{17,49},{33,1},{49,17},{2,34}... | collective-permute-start | bytes 98312 | tf_op jit(solution)/shard_map/ppermute | solution.py:275
  116.5 4.4 %collective-permute-start.15 = (f32[2,16,256]{2,1,0:T(8,128)S(1)}, f32[2,16,256]{2,1,0:T(8,128)S(1)}, u32[]{:S(2)}, u32[]{:S(2)}) collective-permute-start(f32[2,16,256]{2,1,0:T(8,128)S(1)} %pad_maximum_fusion.9), channel_id=1, source_target_pairs={{0,48},{16,32},{32,16},{48,0},{1,49},{17,33},{33,17},{49,1},{2,50}... | collective-permute-start | bytes 98312 | tf_op jit(solution)/shard_map/ppermute | solution.py:275
  117.6 0.7 copy-start.11
  117.6 0.7 copy-start.13
  120.9 12.1 %copy-start.8 = (f32[256,512]{1,0:T(8,128)S(1)}, f32[256,512]{1,0:T(8,128)}, u32[]{:S(2)}) copy-start(f32[256,512]{1,0:T(8,128)} %get-tuple-element.30) | copy-start | bytes 1572868
  120.9 2.7 %collective-permute-start.16 = (f32[16,256]{1,0:T(8,128)S(1)}, f32[16,256]{1,0:T(8,128)S(1)}, u32[]{:S(2)}, u32[]{:S(2)}) collective-permute-start(f32[16,256]{1,0:T(8,128)S(1)} %slice_bitcast_fusion.1), channel_id=1, source_target_pairs={{0,64},{64,0},{1,65},{65,1},{2,66},{66,2},{3,67},{67,3},{4,68},{68... | collective-permute-start | bytes 49160 | tf_op jit(solution)/shard_map/ppermute | solution.py:210
  121.3 3.9 %collective-permute-start.21 = (f32[256,128]{1,0:T(8,128)S(1)}, f32[256,128]{1,0:T(8,128)S(1)}, u32[]{:S(2)}, u32[]{:S(2)}) collective-permute-start(f32[256,128]{1,0:T(8,128)S(1)} %pad_maximum_fusion.6), channel_id=1, source_target_pairs={{0,16},{16,0},{1,17},{17,1},{2,18},{18,2},{3,19},{19,3},{4,20},{20... | collective-permute-start | bytes 393224 | tf_op jit(solution)/shard_map/ppermute | solution.py:210
  125.4 3.9 %collective-permute-start.22 = (f32[16,256]{1,0:T(8,128)S(1)}, f32[16,256]{1,0:T(8,128)S(1)}, u32[]{:S(2)}, u32[]{:S(2)}) collective-permute-start(f32[16,256]{1,0:T(8,128)S(1)} %fusion.62), channel_id=1, source_target_pairs={{0,64},{64,0},{128,192},{192,128},{1,65},{65,1},{129,193},{193,129... | collective-permute-start | bytes 49160 | tf_op jit(solution)/shard_map/ppermute | solution.py:275
  126.7 4.1 %collective-permute-start.23 = (f32[16,256]{1,0:T(8,128)S(1)}, f32[16,256]{1,0:T(8,128)S(1)}, u32[]{:S(2)}, u32[]{:S(2)}) collective-permute-start(f32[16,256]{1,0:T(8,128)S(1)} %fusion.62), channel_id=1, source_target_pairs={{0,128},{64,192},{128,0},{192,64},{1,129},{65,193},{129,1},{193,65... | collective-permute-start | bytes 49160 | tf_op jit(solution)/shard_map/ppermute | solution.py:275
  129.2 3.8 %collective-permute-start.24 = (f32[16,256]{1,0:T(8,128)S(1)}, f32[16,256]{1,0:T(8,128)S(1)}, u32[]{:S(2)}, u32[]{:S(2)}) collective-permute-start(f32[16,256]{1,0:T(8,128)S(1)} %fusion.62), channel_id=1, source_target_pairs={{0,192},{64,128},{128,64},{192,0},{1,193},{65,129},{129,65},{193,1... | collective-permute-start | bytes 49160 | tf_op jit(solution)/shard_map/ppermute | solution.py:275
  148.2 7.8 %copy-start = (bf16[4,1024,256]{2,1,0:T(8,128)(2,1)S(1)}, bf16[4,1024,256]{2,1,0:T(8,128)(2,1)}, u32[]{:S(2)}) copy-start(bf16[4,1024,256]{2,1,0:T(8,128)(2,1)} %w_hbm.1) | copy-start | bytes 6291460
  148.2 7.6 %collective-permute-start.25 = (f32[8,64,256]{2,1,0:T(8,128)S(1)}, f32[8,64,256]{2,1,0:T(8,128)S(1)}, u32[]{:S(2)}, u32[]{:S(2)}) collective-permute-start(f32[8,64,256]{2,1,0:T(8,128)S(1)} %all_to_all.25), channel_id=1, source_target_pairs={{0,1},{1,0},{2,3},{3,2},{4,5},{5,4},{6,7},{7,6},{8,9},{9,8},{10,11... | collective-permute-start | bytes 1572872 | tf_op jit(solution)/shard_map/ppermute | solution.py:210
  156.0 1.2 copy-start.4
